TPU v7x, 128 devices: a whole 4x4x4 slice. The times are simulated.
128 devices in a mesh: curve: 32 (over y, z, core), split: 4 (over x).
Axes of the slice: x: 4, y: 4, z: 4, core: 2. Of those that a mesh axis runs over, the one named last changes fastest.
Arguments:
- velocity: float32 [3, 1015808], P(None, ('curve', 'split')), may hold values from -6 to 6
- energy: float32 [27, 32768], P(None, ('curve', 'split')), may hold values from 0.1 to 1
- point_mass: float32 [216, 32768], P(None, ('curve', 'split')), may hold values from 0.5 to 2
- inv_jacobian: float32 [1944, 32768], P(None, ('curve', 'split')), may hold values from -6 to 6
- energy_mass_inv: float32 [729, 32768], P(None, ('curve', 'split')), may hold values from -0.2 to 6
- send_rows: int32 [128, 36], P(('curve', 'split')), may hold values from 0 to 255, as said below
- arrive_rows: int32 [128, 36], P(('curve', 'split')), may hold values from 0 to 255, as said below
- zone_nodes: int32 [64, 32768], P(None, ('curve', 'split')), may hold values from 0 to 7935, as said below
- shared_nodes: int32 [128, 4, 256], P(('curve', 'split')), may hold values from 0 to 7935, as said below
Outputs:
- velocity_next: float32 [3, 1015808], P(None, ('curve', 'split'))
- energy_next: float32 [27, 32768], P(None, ('curve', 'split'))
Inputs may be any that keep to these rules, and one draw needn't show every extreme that they name: `send_rows`: entry p * 9 + m of a device's row is the local zone row leaving for peer p in slot m; a row's entries are distinct. `arrive_rows`: A device's row holds the same local rows as its row of send_rows, in another order; entry p * 9 + m is where the zone from peer p, slot m, lands. `zone_nodes`: every local node of a device belongs to some zone of that device. `shared_nodes`: the four lists of a device are disjoint with distinct entries; entry m of list 0 of device (c, s) and entry m of list 1 of device (c + 1, s) are one node, likewise list 2 and list 3 of the next device along split.
All inputs are finite; a program needn't handle non-finite values.
Results may differ from a plain program's by a relative error of at most 0.00011.
Values sent between devices are 32-bit elements; how exact they have to be, the bound alone decides.
No kernel may reach another device: no remote copies, remote signals or barrier semaphores. Data moves between devices by JAX's collectives and lax.ppermute only.
A program may use at most 128 MiB of HBM per device.

v0:
```python
import math

import jax
import jax.numpy as jnp
import numpy as np
from jax import lax
from jax.sharding import PartitionSpec as P

H1D = 4
Q1D = 6
L1D = 3
SWEEPS = 3


GAMMA_LESS = 0.4
STEP_SIZE = 0.25
LOWER_BOUND = 0.15
UPPER_BOUND = 1.0
HIGH = lax.Precision.HIGHEST


def passed_along(x, axis, by):
    size = lax.axis_size(axis)
    pairs = [(i, i + by) for i in range(size) if 0 <= i + by < size]
    return lax.ppermute(x, axis, pairs)


def padded(block, sides, width):
    for axis, dim in sides:
        count = lax.axis_size(axis)
        forward = [(i, i + 1) for i in range(count - 1)]
        backward = [(target, source) for source, target in forward]
        low = lax.ppermute(
            lax.slice_in_dim(block, block.shape[dim] - width, None, axis=dim), axis, forward
        )
        high = lax.ppermute(lax.slice_in_dim(block, 0, width, axis=dim), axis, backward)
        block = jnp.concatenate([low, block, high], axis=dim)
    return block


def gauss_points():
    on_line = [
        -0.932469514203152,
        -0.6612093864662645,
        -0.2386191860831909,
        0.2386191860831909,
        0.6612093864662645,
        0.932469514203152,
    ]
    return [0.5 * (v + 1.0) for v in on_line]


def lobatto_points():
    on_line = [-1.0, -0.4472135954999579, 0.4472135954999579, 1.0]
    return [0.5 * (v + 1.0) for v in on_line]


def basis_tables(nodes_line, points_line, energy_line):
    points = gauss_points()
    lobatto = lobatto_points()
    value_table = np.zeros((points_line, nodes_line))
    slope_table = np.zeros((points_line, nodes_line))
    for i in range(nodes_line):
        others = [lobatto[j] for j in range(nodes_line) if j != i]
        scaling = np.prod([lobatto[i] - o for o in others])
        for q in range(points_line):
            t = points[q]
            value_table[q, i] = np.prod([t - o for o in others]) / scaling
            summed = 0.0
            for m in range(len(others)):
                summed += np.prod([t - others[n] for n in range(len(others)) if n != m])
            slope_table[q, i] = summed / scaling
    degree = energy_line - 1
    bern_table = np.zeros((points_line, energy_line))
    for q in range(points_line):
        t = points[q]
        for j in range(energy_line):
            bern_table[q, j] = math.comb(degree, j) * t**j * (1.0 - t) ** (degree - j)
    return (value_table, slope_table, bern_table)


def tables():
    value_table, slope_table, bern_table = basis_tables(H1D, Q1D, L1D)
    return (
        jnp.asarray(value_table, jnp.float32),
        jnp.asarray(slope_table, jnp.float32),
        jnp.asarray(bern_table, jnp.float32),
    )


def apply_along(matrix, tensor, which_axis):
    einsum_forms = ("ai,cijkz->cajkz", "aj,cijkz->ciakz", "ak,cijkz->cijaz")
    return jnp.einsum(einsum_forms[which_axis], matrix, tensor, precision=HIGH)


def through(tensor, matrices):
    return apply_along(
        matrices[2], apply_along(matrices[1], apply_along(matrices[0], tensor, 0), 1), 2
    )


def scatter_nodes(terms, connect, node_count):
    return jnp.zeros((terms.shape[0], node_count), jnp.float32).at[:, connect].add(terms)


def zone_force(velocity_nodes, connect, energy_dofs, mass, jacobian):
    value_table, slope_table, bern_table = tables()
    zone_count = connect.shape[1]
    vel_zone = velocity_nodes[:, connect].reshape(3, H1D, H1D, H1D, zone_count)
    energy_points = through(
        energy_dofs.reshape(1, L1D, L1D, L1D, zone_count), (bern_table, bern_table, bern_table)
    )[0]
    pressure_weight = GAMMA_LESS * energy_points * mass.reshape(Q1D, Q1D, Q1D, zone_count)
    stress_flux = jacobian.reshape(3, 3, Q1D, Q1D, Q1D, zone_count) * pressure_weight
    value_t = value_table.T
    slope_t = slope_table.T
    rhs_zone = (
        through(stress_flux[0], (slope_t, value_t, value_t))
        + through(stress_flux[1], (value_t, slope_t, value_t))
        + through(stress_flux[2], (value_t, value_t, slope_t))
    )
    first_b = apply_along(value_table, vel_zone, 0)
    first_g = apply_along(slope_table, vel_zone, 0)
    grad_x = apply_along(value_table, apply_along(value_table, first_g, 1), 2)
    grad_y = apply_along(value_table, apply_along(slope_table, first_b, 1), 2)
    grad_z = apply_along(slope_table, apply_along(value_table, first_b, 1), 2)
    work_density = jnp.sum(
        stress_flux[0] * grad_x + stress_flux[1] * grad_y + stress_flux[2] * grad_z, axis=0
    )
    bern_t = bern_table.T
    rhs_energy = -through(work_density[None], (bern_t, bern_t, bern_t)).reshape(L1D**3, zone_count)
    rhs_nodes = scatter_nodes(
        rhs_zone.reshape(3, H1D**3, zone_count), connect, velocity_nodes.shape[1]
    )
    return (rhs_nodes, rhs_energy)


def zone_mass(direction_nodes, connect, mass):
    value_table, slope_table, bern_table = tables()
    zone_count = connect.shape[1]
    dir_zone = direction_nodes[:, connect].reshape(3, H1D, H1D, H1D, zone_count)
    at_points = through(dir_zone, (value_table, value_table, value_table))
    weighted = at_points * mass.reshape(Q1D, Q1D, Q1D, zone_count)
    value_t = value_table.T
    back = through(weighted, (value_t, value_t, value_t))
    return scatter_nodes(back.reshape(3, H1D**3, zone_count), connect, direction_nodes.shape[1])


def bound_term(connect, mass, node_count):
    value_table, slope_table, bern_table = tables()
    zone_count = connect.shape[1]
    abs_table = jnp.abs(value_table)
    row_total = jnp.sum(abs_table, axis=1)
    point_weight = row_total[:, None, None] * row_total[None, :, None] * row_total[None, None, :]
    weighted = (mass.reshape(Q1D, Q1D, Q1D, zone_count) * point_weight[:, :, :, None])[None]
    abs_t = abs_table.T
    term = through(weighted, (abs_t, abs_t, abs_t))
    return scatter_nodes(term.reshape(1, H1D**3, zone_count), connect, node_count)


def apply_inverse(inverse, rhs_energy):
    return jnp.einsum(
        "jlz,lz->jz", inverse.reshape(L1D**3, L1D**3, inverse.shape[1]), rhs_energy, precision=HIGH
    )


def chebyshev(rhs_nodes, bound, apply_mass):
    theta = 0.5 * (UPPER_BOUND + LOWER_BOUND)
    delta = 0.5 * (UPPER_BOUND - LOWER_BOUND)
    sigma = theta / delta
    rho_now = 1.0 / sigma
    residual = rhs_nodes
    direction = residual / bound / theta
    solution = jnp.zeros_like(rhs_nodes)
    for sweep in range(SWEEPS):
        solution = solution + direction
        residual = residual - apply_mass(direction)
        rho_new = 1.0 / (2.0 * sigma - rho_now)
        direction = rho_new * rho_now * direction + 2.0 * rho_new / delta * (residual / bound)
        rho_now = rho_new
    return solution + direction


def per_device(
    velocity,
    energy,
    point_mass,
    inv_jacobian,
    energy_mass_inv,
    send_rows,
    arrive_rows,
    zone_nodes,
    shared_nodes,
):
    slots = send_rows.shape[1]
    per_peer = slots // 4
    leaving = send_rows[0]
    landing = arrive_rows[0]
    lists = shared_nodes[0]
    node_count = velocity.shape[1]
    fields = (point_mass, inv_jacobian, energy_mass_inv, energy)
    packs = tuple((f[:, leaving].reshape(f.shape[0], 4, per_peer) for f in fields))
    offsets = (1, -1, 2, -2)
    received = []
    for peer in range(4):
        got = passed_along(tuple((p[:, peer] for p in packs)), ("curve", "split"), offsets[peer])
        received.append(got)
    arrived = tuple((jnp.stack([received[peer][f] for peer in range(4)], 1) for f in range(4)))
    devices = lax.axis_size("curve") * lax.axis_size("split")
    me = lax.axis_index("curve") * lax.axis_size("split") + lax.axis_index("split")
    peer_offset = jnp.repeat(jnp.array(offsets, dtype=jnp.int32), per_peer)
    source = me - peer_offset
    valid = (source >= 0) & (source < devices)
    moved = []
    for f in range(4):
        incoming = arrived[f].reshape(fields[f].shape[0], slots)
        placed = jnp.where(valid[None, :], incoming, fields[f][:, landing])
        moved.append(fields[f].at[:, landing].set(placed))
    mass, jacobian, inverse, energy_now = moved

    def assemble(values):
        picked = values[:, lists]
        curve_send = jnp.stack((picked[:, 1], picked[:, 0]), 1)
        split_send = jnp.stack((picked[:, 3], picked[:, 2]), 1)
        curve_got = padded(curve_send, (("curve", 1),), 1)
        split_got = padded(split_send, (("split", 1),), 1)
        result = values.at[:, lists[1]].add(curve_got[:, 0]).at[:, lists[0]].add(curve_got[:, 3])
        return result.at[:, lists[3]].add(split_got[:, 0]).at[:, lists[2]].add(split_got[:, 3])

    def apply_mass(direction):
        return assemble(zone_mass(direction, zone_nodes, mass))

    local_bound = bound_term(zone_nodes, mass, node_count)
    rhs_first, energy_rhs_first = zone_force(velocity, zone_nodes, energy_now, mass, jacobian)
    bound = assemble(local_bound)
    rhs_first = assemble(rhs_first)
    accel_one = chebyshev(rhs_first, bound, apply_mass)
    change_one = apply_inverse(inverse, energy_rhs_first)
    vel_half = velocity + 0.5 * STEP_SIZE * accel_one
    energy_half = energy_now + 0.5 * STEP_SIZE * change_one
    rhs_second, energy_rhs_second = zone_force(vel_half, zone_nodes, energy_half, mass, jacobian)
    accel_two = chebyshev(assemble(rhs_second), bound, apply_mass)
    change_two = apply_inverse(inverse, energy_rhs_second)
    velocity_next = velocity + STEP_SIZE * accel_two
    energy_next = energy_now + STEP_SIZE * change_two
    return (velocity_next, energy_next)


def solution(mesh):
    in_specs = (
        P(None, ("curve", "split")),
        P(None, ("curve", "split")),
        P(None, ("curve", "split")),
        P(None, ("curve", "split")),
        P(None, ("curve", "split")),
        P(("curve", "split"), None),
        P(("curve", "split"), None),
        P(None, ("curve", "split")),
        P(("curve", "split"), None, None),
    )
    out_specs = (P(None, ("curve", "split")), P(None, ("curve", "split")))
    return jax.shard_map(
        per_device, mesh=mesh, in_specs=in_specs, out_specs=out_specs, check_vma=False
    )
```

profile of v0, /device:TPU:26, one launch (start us, length us, event | category | flops | bytes accessed | tf_op | source)
XLA Modules:
  0.0 2022.9 jit_solution(770842795739132860)
XLA Ops:
  17.5 7.5 collective-permute-start.7
  30.0 56.6 %gather_fusion.3 = f32[16384,3]{1,0:T(8,128)} fusion(f32[3,7936]{0,1:T(8,128)} %copy.414, s32[16384]{0:T(1024)S(1)} %broadcast_clamp_fusion), kind=kCustom, calls=%fused_computation.6 | custom fusion | bytes 458752 | tf_op jit(solution)/shard_map/gather | solution.py:109
  109.2 6.4 collective-permute-start.9
  117.6 8.2 collective-permute-start.11
  141.3 85.9 %scatter_custom_fusion.9 = f32[7936]{0:T(1024)S(1)} fusion(s32[16384]{0:T(1024)} %bitcast.784, f32[16384]{0:T(1024)} %bitcast.796, f32[]{:T(128)} %constant.23.clone.1), kind=kCustom, calls=%fused_computation.403 | custom fusion | flops 16384 | bytes 32256 | tf_op jit(solution)/shard_map/scatter-add | solution.py:103
  245.9 8.2 collective-permute-start.15
  276.9 8.2 collective-permute-start.3
  328.4 89.8 %scatter_custom_fusion.4 = f32[3,7936]{0,1:T(8,128)} fusion(s32[16384]{0:T(1024)} %bitcast.785, f32[16384,3]{1,0:T(8,128)} %bitcast.748, f32[]{:T(128)} %constant.23.clone.1), kind=kCustom, calls=%fused_computation.89 | custom fusion | flops 49152 | bytes 95744 | tf_op jit(solution)/shard_map/scatter-add | solution.py:103
  440.5 89.7 %scatter_custom_fusion.29 = f32[3,7936]{0,1:T(8,128)} fusion(s32[16384]{0:T(1024)} %bitcast.786, f32[16384,3]{1,0:T(8,128)} %bitcast.749, f32[]{:T(128)} %constant.23.clone.1), kind=kCustom, calls=%fused_computation.81 | custom fusion | flops 49152 | bytes 95744 | tf_op jit(solution)/shard_map/scatter-add | solution.py:103
  562.7 6.6 scatter_custom_fusion.30
  599.6 56.6 %gather_fusion.14 = f32[16384,3]{1,0:T(8,128)} fusion(f32[3,7936]{0,1:T(8,128)} %copy.490, s32[16384]{0:T(1024)S(1)} %broadcast_clamp_fusion), kind=kCustom, calls=%fused_computation.18 | custom fusion | bytes 458752 | tf_op jit(solution)/shard_map/gather | solution.py:141
  674.2 89.7 %scatter_custom_fusion.34 = f32[3,7936]{0,1:T(8,128)} fusion(s32[16384]{0:T(1024)} %bitcast.787, f32[16384,3]{1,0:T(8,128)} %bitcast.750, f32[]{:T(128)} %constant.23.clone.1), kind=kCustom, calls=%fused_computation.79 | custom fusion | flops 49152 | bytes 95744 | tf_op jit(solution)/shard_map/scatter-add | solution.py:103
  786.2 6.2 scatter_custom_fusion.5
  798.7 6.4 scatter_custom_fusion.7
  814.1 6.2 scatter_custom_fusion.35
  847.4 56.6 %gather_fusion.7 = f32[16384,3]{1,0:T(8,128)} fusion(f32[3,7936]{0,1:T(8,128)} %copy.448, s32[16384]{0:T(1024)S(1)} %broadcast_clamp_fusion), kind=kCustom, calls=%fused_computation.11 | custom fusion | bytes 458752 | tf_op jit(solution)/shard_map/gather | solution.py:141
  925.3 89.8 %scatter_custom_fusion.14 = f32[3,7936]{0,1:T(8,128)} fusion(s32[16384]{0:T(1024)} %bitcast.788, f32[16384,3]{1,0:T(8,128)} %bitcast.751, f32[]{:T(128)} %constant.23.clone.1), kind=kCustom, calls=%fused_computation.87 | custom fusion | flops 49152 | bytes 95744 | tf_op jit(solution)/shard_map/scatter-add | solution.py:103
  1041.1 56.6 %gather_fusion.16 = f32[16384,3]{1,0:T(8,128)} fusion(f32[3,7936]{0,1:T(8,128)} %copy.501, s32[16384]{0:T(1024)S(1)} %broadcast_clamp_fusion), kind=kCustom, calls=%fused_computation.20 | custom fusion | bytes 458752 | tf_op jit(solution)/shard_map/gather | solution.py:141
  1118.9 89.7 %scatter_custom_fusion.39 = f32[3,7936]{0,1:T(8,128)} fusion(s32[16384]{0:T(1024)} %bitcast.789, f32[16384,3]{1,0:T(8,128)} %bitcast.752, f32[]{:T(128)} %constant.23.clone.1), kind=kCustom, calls=%fused_computation.77 | custom fusion | flops 49152 | bytes 95744 | tf_op jit(solution)/shard_map/scatter-add | solution.py:103
  1230.9 6.2 scatter_custom_fusion.15
  1249.5 6.4 scatter_custom_fusion.18
  1292.9 56.6 %gather_fusion.9 = f32[16384,3]{1,0:T(8,128)} fusion(f32[3,7936]{0,1:T(8,128)} %copy.459, s32[16384]{0:T(1024)S(1)} %broadcast_clamp_fusion), kind=kCustom, calls=%fused_computation.13 | custom fusion | bytes 458752 | tf_op jit(solution)/shard_map/gather | solution.py:141
  1367.6 89.7 %scatter_custom_fusion.19 = f32[3,7936]{0,1:T(8,128)} fusion(s32[16384]{0:T(1024)} %bitcast.790, f32[16384,3]{1,0:T(8,128)} %bitcast.753, f32[]{:T(128)} %constant.23.clone.1), kind=kCustom, calls=%fused_computation.85 | custom fusion | flops 49152 | bytes 95744 | tf_op jit(solution)/shard_map/scatter-add | solution.py:103
  1482.5 56.6 %gather_fusion.18 = f32[16384,3]{1,0:T(8,128)} fusion(f32[3,7936]{0,1:T(8,128)} %copy.511, s32[16384]{0:T(1024)S(1)} %broadcast_clamp_fusion), kind=kCustom, calls=%fused_computation.22 | custom fusion | bytes 458752 | tf_op jit(solution)/shard_map/gather | solution.py:141
  1557.2 89.8 %scatter_custom_fusion.44 = f32[3,7936]{0,1:T(8,128)} fusion(s32[16384]{0:T(1024)} %bitcast.791, f32[16384,3]{1,0:T(8,128)} %bitcast.754, f32[]{:T(128)} %constant.23.clone.1), kind=kCustom, calls=%fused_computation.75 | custom fusion | flops 49152 | bytes 95744 | tf_op jit(solution)/shard_map/scatter-add | solution.py:103
  1687.7 6.4 scatter_custom_fusion.23
  1702.7 56.6 %gather_fusion.11 = f32[16384,3]{1,0:T(8,128)} fusion(f32[3,7936]{0,1:T(8,128)} %copy.469, s32[16384]{0:T(1024)S(1)} %broadcast_clamp_fusion), kind=kCustom, calls=%fused_computation.15 | custom fusion | bytes 458752 | tf_op jit(solution)/shard_map/gather | solution.py:141
  1775.7 89.7 %scatter_custom_fusion.24 = f32[3,7936]{0,1:T(8,128)} fusion(s32[16384]{0:T(1024)} %bitcast.792, f32[16384,3]{1,0:T(8,128)} %bitcast.747, f32[]{:T(128)} %constant.23.clone.1), kind=kCustom, calls=%fused_computation.83 | custom fusion | flops 49152 | bytes 95744 | tf_op jit(solution)/shard_map/scatter-add | solution.py:103
  1884.7 6.2 scatter_custom_fusion.45
  1891.0 6.4 scatter_custom_fusion.46
  1931.1 6.2 scatter_custom_fusion.28
  1946.6 56.6 %gather_fusion.20 = f32[16384,3]{1,0:T(8,128)} fusion(f32[3,7936]{0,1:T(8,128)} %copy.521, s32[16384]{0:T(1024)S(1)} %broadcast_clamp_fusion), kind=kCustom, calls=%fused_computation.24 | custom fusion | bytes 458752 | tf_op jit(solution)/shard_map/gather | solution.py:109
  (412 shorter events, 661.9 us)
Async XLA Ops:
  3.6 126.1 %collective-permute-start.8 = (f32[216,9]{0,1:T(8,128)}, f32[216,9]{0,1:T(8,128)}, u32[]{:S(2)}, u32[]{:S(2)}) collective-permute-start(f32[216,9]{0,1:T(8,128)} %get-tuple-element.65), channel_id=1, source_target_pairs={{0,1},{1,2},{2,3},{3,4},{4,5},{5,6},{6,7},{7,8},{8,9},{9,10},{10,1... | collective-permute-start | bytes 23336 | tf_op jit(solution)/shard_map/ppermute | solution.py:25
  9.1 100.1 %collective-permute-start.4 = (f32[27,9]{0,1:T(8,128)}, f32[27,9]{0,1:T(8,128)}, u32[]{:S(2)}, u32[]{:S(2)}) collective-permute-start(f32[27,9]{0,1:T(8,128)} %get-tuple-element.72), channel_id=1, source_target_pairs={{0,1},{1,2},{2,3},{3,4},{4,5},{5,6},{6,7},{7,8},{8,9},{9,10},{10,1... | collective-permute-start | bytes 2924 | tf_op jit(solution)/shard_map/ppermute | solution.py:25
  12.2 103.4 %collective-permute-start.5 = (f32[27,9]{0,1:T(8,128)}, f32[27,9]{0,1:T(8,128)}, u32[]{:S(2)}, u32[]{:S(2)}) collective-permute-start(f32[27,9]{0,1:T(8,128)} %get-tuple-element.75), channel_id=1, source_target_pairs={{1,0},{2,1},{3,2},{4,3},{5,4},{6,5},{7,6},{8,7},{9,8},{10,9},{11,1... | collective-permute-start | bytes 2924 | tf_op jit(solution)/shard_map/ppermute | solution.py:25
  14.9 102.6 %collective-permute-start.6 = (f32[27,9]{0,1:T(8,128)}, f32[27,9]{0,1:T(8,128)}, u32[]{:S(2)}, u32[]{:S(2)}) collective-permute-start(f32[27,9]{0,1:T(8,128)} %get-tuple-element.74), channel_id=1, source_target_pairs={{0,2},{1,3},{2,4},{3,5},{4,6},{5,7},{6,8},{7,9},{8,10},{9,11},{10,... | collective-permute-start | bytes 2924 | tf_op jit(solution)/shard_map/ppermute | solution.py:25
  17.5 108.2 %collective-permute-start.7 = (f32[27,9]{0,1:T(8,128)}, f32[27,9]{0,1:T(8,128)}, u32[]{:S(2)}, u32[]{:S(2)}) collective-permute-start(f32[27,9]{0,1:T(8,128)} %get-tuple-element.73), channel_id=1, source_target_pairs={{2,0},{3,1},{4,2},{5,3},{6,4},{7,5},{8,6},{9,7},{10,8},{11,9},{12,... | collective-permute-start | bytes 2924 | tf_op jit(solution)/shard_map/ppermute | solution.py:25
  125.7 145.2 %collective-permute-start.12 = (f32[729,9]{0,1:T(8,128)}, f32[729,9]{0,1:T(8,128)}, u32[]{:S(2)}, u32[]{:S(2)}) collective-permute-start(f32[729,9]{0,1:T(8,128)} %get-tuple-element.59), channel_id=1, source_target_pairs={{0,1},{1,2},{2,3},{3,4},{4,5},{5,6},{6,7},{7,8},{8,9},{9,10},{10,1... | collective-permute-start | bytes 78740 | tf_op jit(solution)/shard_map/ppermute | solution.py:25
  129.7 145.2 %collective-permute-start.13 = (f32[729,9]{0,1:T(8,128)}, f32[729,9]{0,1:T(8,128)}, u32[]{:S(2)}, u32[]{:S(2)}) collective-permute-start(f32[729,9]{0,1:T(8,128)} %get-tuple-element.62), channel_id=1, source_target_pairs={{1,0},{2,1},{3,2},{4,3},{5,4},{6,5},{7,6},{8,7},{9,8},{10,9},{11,1... | collective-permute-start | bytes 78740 | tf_op jit(solution)/shard_map/ppermute | solution.py:25
  555.0 218.9 %collective-permute-start.16 = (f32[3,1,256]{0,2,1:T(8,128)}, f32[3,1,256]{0,2,1:T(8,128)}, u32[]{:S(2)}, u32[]{:S(2)}) collective-permute-start(f32[3,1,256]{0,2,1:T(8,128)} %get-tuple-element.54), channel_id=1, source_target_pairs={{0,4},{4,8},{8,12},{12,16},{16,20},{20,24},{24,28},{28,32},{32,36}... | collective-permute-start | bytes 9224 | tf_op jit(solution)/shard_map/ppermute | solution.py:33
  556.9 222.8 %collective-permute-start.17 = (f32[3,1,256]{0,2,1:T(8,128)}, f32[3,1,256]{0,2,1:T(8,128)}, u32[]{:S(2)}, u32[]{:S(2)}) collective-permute-start(f32[3,1,256]{0,2,1:T(8,128)} %get-tuple-element.53), channel_id=1, source_target_pairs={{4,0},{8,4},{12,8},{16,12},{20,16},{24,20},{28,24},{32,28},{36,32}... | collective-permute-start | bytes 9224 | tf_op jit(solution)/shard_map/ppermute | solution.py:36
  569.3 212.4 %collective-permute-start.18 = (f32[3,1,256]{0,2,1:T(8,128)}, f32[3,1,256]{0,2,1:T(8,128)}, u32[]{:S(2)}, u32[]{:S(2)}) collective-permute-start(f32[3,1,256]{0,2,1:T(8,128)} %get-tuple-element.52), channel_id=1, source_target_pairs={{0,1},{1,2},{2,3},{4,5},{5,6},{6,7},{8,9},{9,10},{10,11},{12,13},{... | collective-permute-start | bytes 9224 | tf_op jit(solution)/shard_map/ppermute | solution.py:33
  577.4 227.6 %collective-permute-start.19 = (f32[3,1,256]{0,2,1:T(8,128)}, f32[3,1,256]{0,2,1:T(8,128)}, u32[]{:S(2)}, u32[]{:S(2)}) collective-permute-start(f32[3,1,256]{0,2,1:T(8,128)} %get-tuple-element.51), channel_id=1, source_target_pairs={{1,0},{2,1},{3,2},{5,4},{6,5},{7,6},{9,8},{10,9},{11,10},{13,12},{... | collective-permute-start | bytes 9224 | tf_op jit(solution)/shard_map/ppermute | solution.py:36
  773.9 46.4 %collective-permute-start.41 = (f32[3,1,256]{0,2,1:T(8,128)}, f32[3,1,256]{0,2,1:T(8,128)}, u32[]{:S(2)}, u32[]{:S(2)}) collective-permute-start(f32[3,1,256]{0,2,1:T(8,128)} %get-tuple-element.33), channel_id=1, source_target_pairs={{4,0},{8,4},{12,8},{16,12},{20,16},{24,20},{28,24},{32,28},{36,32}... | collective-permute-start | bytes 9224 | tf_op jit(solution)/shard_map/ppermute | solution.py:36
  779.7 46.8 %collective-permute-start.42 = (f32[3,1,256]{0,2,1:T(8,128)}, f32[3,1,256]{0,2,1:T(8,128)}, u32[]{:S(2)}, u32[]{:S(2)}) collective-permute-start(f32[3,1,256]{0,2,1:T(8,128)} %get-tuple-element.32), channel_id=1, source_target_pairs={{0,1},{1,2},{2,3},{4,5},{5,6},{6,7},{8,9},{9,10},{10,11},{12,13},{... | collective-permute-start | bytes 9224 | tf_op jit(solution)/shard_map/ppermute | solution.py:33
  781.7 51.1 %collective-permute-start.43 = (f32[3,1,256]{0,2,1:T(8,128)}, f32[3,1,256]{0,2,1:T(8,128)}, u32[]{:S(2)}, u32[]{:S(2)}) collective-permute-start(f32[3,1,256]{0,2,1:T(8,128)} %get-tuple-element.31), channel_id=1, source_target_pairs={{1,0},{2,1},{3,2},{5,4},{6,5},{7,6},{9,8},{10,9},{11,10},{13,12},{... | collective-permute-start | bytes 9224 | tf_op jit(solution)/shard_map/ppermute | solution.py:36
  1023.1 195.5 %collective-permute-start.24 = (f32[3,1,256]{0,2,1:T(8,128)}, f32[3,1,256]{0,2,1:T(8,128)}, u32[]{:S(2)}, u32[]{:S(2)}) collective-permute-start(f32[3,1,256]{0,2,1:T(8,128)} %get-tuple-element.50), channel_id=1, source_target_pairs={{0,4},{4,8},{8,12},{12,16},{16,20},{20,24},{24,28},{28,32},{32,36}... | collective-permute-start | bytes 9224 | tf_op jit(solution)/shard_map/ppermute | solution.py:33
  1025.0 199.4 %collective-permute-start.25 = (f32[3,1,256]{0,2,1:T(8,128)}, f32[3,1,256]{0,2,1:T(8,128)}, u32[]{:S(2)}, u32[]{:S(2)}) collective-permute-start(f32[3,1,256]{0,2,1:T(8,128)} %get-tuple-element.49), channel_id=1, source_target_pairs={{4,0},{8,4},{12,8},{16,12},{20,16},{24,20},{28,24},{32,28},{36,32}... | collective-permute-start | bytes 9224 | tf_op jit(solution)/shard_map/ppermute | solution.py:36
  1030.8 195.5 %collective-permute-start.26 = (f32[3,1,256]{0,2,1:T(8,128)}, f32[3,1,256]{0,2,1:T(8,128)}, u32[]{:S(2)}, u32[]{:S(2)}) collective-permute-start(f32[3,1,256]{0,2,1:T(8,128)} %get-tuple-element.48), channel_id=1, source_target_pairs={{0,1},{1,2},{2,3},{4,5},{5,6},{6,7},{8,9},{9,10},{10,11},{12,13},{... | collective-permute-start | bytes 9224 | tf_op jit(solution)/shard_map/ppermute | solution.py:33
  1032.7 216.8 %collective-permute-start.27 = (f32[3,1,256]{0,2,1:T(8,128)}, f32[3,1,256]{0,2,1:T(8,128)}, u32[]{:S(2)}, u32[]{:S(2)}) collective-permute-start(f32[3,1,256]{0,2,1:T(8,128)} %get-tuple-element.47), channel_id=1, source_target_pairs={{1,0},{2,1},{3,2},{5,4},{6,5},{7,6},{9,8},{10,9},{11,10},{13,12},{... | collective-permute-start | bytes 9224 | tf_op jit(solution)/shard_map/ppermute | solution.py:36
  1218.6 46.9 %collective-permute-start.45 = (f32[3,1,256]{0,2,1:T(8,128)}, f32[3,1,256]{0,2,1:T(8,128)}, u32[]{:S(2)}, u32[]{:S(2)}) collective-permute-start(f32[3,1,256]{0,2,1:T(8,128)} %get-tuple-element.29), channel_id=1, source_target_pairs={{4,0},{8,4},{12,8},{16,12},{20,16},{24,20},{28,24},{32,28},{36,32}... | collective-permute-start | bytes 9224 | tf_op jit(solution)/shard_map/ppermute | solution.py:36
  1224.4 47.4 %collective-permute-start.46 = (f32[3,1,256]{0,2,1:T(8,128)}, f32[3,1,256]{0,2,1:T(8,128)}, u32[]{:S(2)}, u32[]{:S(2)}) collective-permute-start(f32[3,1,256]{0,2,1:T(8,128)} %get-tuple-element.28), channel_id=1, source_target_pairs={{0,1},{1,2},{2,3},{4,5},{5,6},{6,7},{8,9},{9,10},{10,11},{12,13},{... | collective-permute-start | bytes 9224 | tf_op jit(solution)/shard_map/ppermute | solution.py:33
  1226.3 51.6 %collective-permute-start.47 = (f32[3,1,256]{0,2,1:T(8,128)}, f32[3,1,256]{0,2,1:T(8,128)}, u32[]{:S(2)}, u32[]{:S(2)}) collective-permute-start(f32[3,1,256]{0,2,1:T(8,128)} %get-tuple-element.27), channel_id=1, source_target_pairs={{1,0},{2,1},{3,2},{5,4},{6,5},{7,6},{9,8},{10,9},{11,10},{13,12},{... | collective-permute-start | bytes 9224 | tf_op jit(solution)/shard_map/ppermute | solution.py:36
  1465.3 191.6 %collective-permute-start.28 = (f32[3,1,256]{0,2,1:T(8,128)}, f32[3,1,256]{0,2,1:T(8,128)}, u32[]{:S(2)}, u32[]{:S(2)}) collective-permute-start(f32[3,1,256]{0,2,1:T(8,128)} %get-tuple-element.46), channel_id=1, source_target_pairs={{0,4},{4,8},{8,12},{12,16},{16,20},{20,24},{24,28},{28,32},{32,36}... | collective-permute-start | bytes 9224 | tf_op jit(solution)/shard_map/ppermute | solution.py:33
  1467.3 201.6 %collective-permute-start.29 = (f32[3,1,256]{0,2,1:T(8,128)}, f32[3,1,256]{0,2,1:T(8,128)}, u32[]{:S(2)}, u32[]{:S(2)}) collective-permute-start(f32[3,1,256]{0,2,1:T(8,128)} %get-tuple-element.45), channel_id=1, source_target_pairs={{4,0},{8,4},{12,8},{16,12},{20,16},{24,20},{28,24},{32,28},{36,32}... | collective-permute-start | bytes 9224 | tf_op jit(solution)/shard_map/ppermute | solution.py:36
  1473.0 204.0 %collective-permute-start.30 = (f32[3,1,256]{0,2,1:T(8,128)}, f32[3,1,256]{0,2,1:T(8,128)}, u32[]{:S(2)}, u32[]{:S(2)}) collective-permute-start(f32[3,1,256]{0,2,1:T(8,128)} %get-tuple-element.44), channel_id=1, source_target_pairs={{0,1},{1,2},{2,3},{4,5},{5,6},{6,7},{8,9},{9,10},{10,11},{12,13},{... | collective-permute-start | bytes 9224 | tf_op jit(solution)/shard_map/ppermute | solution.py:33
  1475.0 212.8 %collective-permute-start.31 = (f32[3,1,256]{0,2,1:T(8,128)}, f32[3,1,256]{0,2,1:T(8,128)}, u32[]{:S(2)}, u32[]{:S(2)}) collective-permute-start(f32[3,1,256]{0,2,1:T(8,128)} %get-tuple-element.43), channel_id=1, source_target_pairs={{1,0},{2,1},{3,2},{5,4},{6,5},{7,6},{9,8},{10,9},{11,10},{13,12},{... | collective-permute-start | bytes 9224 | tf_op jit(solution)/shard_map/ppermute | solution.py:36
  1655.0 218.1 %collective-permute-start.48 = (f32[3,1,256]{0,2,1:T(8,128)}, f32[3,1,256]{0,2,1:T(8,128)}, u32[]{:S(2)}, u32[]{:S(2)}) collective-permute-start(f32[3,1,256]{0,2,1:T(8,128)} %get-tuple-element.26), channel_id=1, source_target_pairs={{0,4},{4,8},{8,12},{12,16},{16,20},{20,24},{24,28},{28,32},{32,36}... | collective-permute-start | bytes 9224 | tf_op jit(solution)/shard_map/ppermute | solution.py:33
  1656.9 221.9 %collective-permute-start.49 = (f32[3,1,256]{0,2,1:T(8,128)}, f32[3,1,256]{0,2,1:T(8,128)}, u32[]{:S(2)}, u32[]{:S(2)}) collective-permute-start(f32[3,1,256]{0,2,1:T(8,128)} %get-tuple-element.25), channel_id=1, source_target_pairs={{4,0},{8,4},{12,8},{16,12},{20,16},{24,20},{28,24},{32,28},{36,32}... | collective-permute-start | bytes 9224 | tf_op jit(solution)/shard_map/ppermute | solution.py:36
  1668.9 211.9 %collective-permute-start.50 = (f32[3,1,256]{0,2,1:T(8,128)}, f32[3,1,256]{0,2,1:T(8,128)}, u32[]{:S(2)}, u32[]{:S(2)}) collective-permute-start(f32[3,1,256]{0,2,1:T(8,128)} %get-tuple-element.24), channel_id=1, source_target_pairs={{0,1},{1,2},{2,3},{4,5},{5,6},{6,7},{8,9},{9,10},{10,11},{12,13},{... | collective-permute-start | bytes 9224 | tf_op jit(solution)/shard_map/ppermute | solution.py:33
  1677.0 226.6 %collective-permute-start.51 = (f32[3,1,256]{0,2,1:T(8,128)}, f32[3,1,256]{0,2,1:T(8,128)}, u32[]{:S(2)}, u32[]{:S(2)}) collective-permute-start(f32[3,1,256]{0,2,1:T(8,128)} %get-tuple-element.23), channel_id=1, source_target_pairs={{1,0},{2,1},{3,2},{5,4},{6,5},{7,6},{9,8},{10,9},{11,10},{13,12},{... | collective-permute-start | bytes 9224 | tf_op jit(solution)/shard_map/ppermute | solution.py:36
  1873.1 46.1 %collective-permute-start.33 = (f32[3,1,256]{0,2,1:T(8,128)}, f32[3,1,256]{0,2,1:T(8,128)S(1)}, u32[]{:S(2)}, u32[]{:S(2)}) collective-permute-start(f32[3,1,256]{0,2,1:T(8,128)} %get-tuple-element.41), channel_id=1, source_target_pairs={{4,0},{8,4},{12,8},{16,12},{20,16},{24,20},{28,24},{32,28},{36,32}... | collective-permute-start | bytes 9224 | tf_op jit(solution)/shard_map/ppermute | solution.py:36
  1878.9 46.3 %collective-permute-start.34 = (f32[3,1,256]{0,2,1:T(8,128)}, f32[3,1,256]{0,2,1:T(8,128)S(1)}, u32[]{:S(2)}, u32[]{:S(2)}) collective-permute-start(f32[3,1,256]{0,2,1:T(8,128)} %get-tuple-element.40), channel_id=1, source_target_pairs={{0,1},{1,2},{2,3},{4,5},{5,6},{6,7},{8,9},{9,10},{10,11},{12,13},{... | collective-permute-start | bytes 9224 | tf_op jit(solution)/shard_map/ppermute | solution.py:33
  1880.8 50.3 %collective-permute-start.35 = (f32[3,1,256]{0,2,1:T(8,128)}, f32[3,1,256]{0,2,1:T(8,128)}, u32[]{:S(2)}, u32[]{:S(2)}) collective-permute-start(f32[3,1,256]{0,2,1:T(8,128)} %get-tuple-element.39), channel_id=1, source_target_pairs={{1,0},{2,1},{3,2},{5,4},{6,5},{7,6},{9,8},{10,9},{11,10},{13,12},{... | collective-permute-start | bytes 9224 | tf_op jit(solution)/shard_map/ppermute | solution.py:36
  (50 other events, 1790.9 us)
where the time goes:
time: 2040 us; the launch traced here: 2020 us
  other arithmetic  1040 us (51%)
  local copies, waits for them, and re-layouts  710 us (35%)
  starting transfers between devices  196 us (10%)
  matrix products  71.4 us (4%)
    scatter-add x9, other arithmetic, scatter_nodes(): jnp.zeros((terms.shape[0], node_count), jnp.float32).at[:, connect]  804 us
    gather x12, local copies, waits for them, and re-layouts, zone_mass(): dir_zone = direction_nodes[:, connect].reshape(3, H1D, H1D, H1D, zone_count)  375 us
    gather x4, local copies, waits for them, and re-layouts, zone_force(): vel_zone = velocity_nodes[:, connect].reshape(3, H1D, H1D, H1D, zone_count)  124 us
    scatter-add x18, other arithmetic, assemble(): result.at[:, lists[3]].add(split_got[:, 0]).at[:, lists[2]]  104 us
    scatter-add x18, other arithmetic, assemble(): values.at[:, lists[1]].add(curve_got[:, 0]).at[:, lists[0]]  104 us
    ppermute x18, starting transfers between devices, padded(): lax.ppermute(lax.slice_in_dim(block, 0, width, axis=dim), axis, backward)  93.5 us
    dot_general x85, matrix products, apply_along(): return jnp.einsum(einsum_forms[which_axis], matrix, tensor, precision=HIGH)  71.4 us
    ppermute x16, starting transfers between devices, passed_along(): return lax.ppermute(x, axis, pairs)  67.6 us
  transfers between devices with their start and end apart: 52, of which 0 were waited for; matrix products, arithmetic and copies ran while one was open for 55% of the time, Pallas kernels for 0%

commit v1 on v0

v1 whole, which is shorter than its diff:
```python
import functools
import math

import jax
import jax.numpy as jnp
import numpy as np
from jax import lax
from jax.experimental import pallas as pl
from jax.experimental.pallas import tpu as pltpu
from jax.sharding import PartitionSpec as P

H1D, Q1D, L1D, SWEEPS = 4, 6, 3, 3
NPZ, QP, LD = 64, 216, 27
GAMMA_LESS = 0.4
STEP_SIZE = 0.25
THETA, DELTA = 0.575, 0.425
SIGMA = THETA / DELTA
AXES = ("curve", "split")
CAP = 9
HALF = 128
WIDE = 256
ROWS = 32
AT_JAC, AT_MASS, AT_INV, AT_EN, AT_FLAG, MSG = 0, 2048, 2304, 3072, 3100, 3200
TAIL = 512
BF, F32 = jnp.bfloat16, jnp.float32
NT = (((1,), (1,)), ((), ()))
TN = (((0,), (0,)), ((), ()))


def line_tables():
    on_line = [-0.9324695142031521, -0.6612093864662645, -0.2386191860831909]
    on_line = on_line + [-v for v in reversed(on_line)]
    points = [0.5 * (v + 1.0) for v in on_line]
    lobatto = [0.5 * (v + 1.0) for v in [-1.0, -0.4472135954999579, 0.4472135954999579, 1.0]]
    value, slope, bern = np.zeros((Q1D, H1D)), np.zeros((Q1D, H1D)), np.zeros((Q1D, L1D))
    for i in range(H1D):
        others = [lobatto[j] for j in range(H1D) if j != i]
        scaling = np.prod([lobatto[i] - o for o in others])
        for q, t in enumerate(points):
            value[q, i] = np.prod([t - o for o in others]) / scaling
            slope[q, i] = sum(
                np.prod([t - others[n] for n in range(3) if n != m]) for m in range(3)
            ) / scaling
    for q, t in enumerate(points):
        for j in range(L1D):
            bern[q, j] = math.comb(2, j) * t**j * (1.0 - t) ** (2 - j)
    return [np.float32(t).astype(np.float64) for t in (value, slope, bern)]


def halves(table):
    high = table.astype(np.float32).astype(BF)
    low = (table - high.astype(np.float64)).astype(np.float32).astype(BF)
    return high, low


def beside(table):
    high, low = halves(table)
    return np.concatenate([high, high, low], 1)


def above(table):
    return np.concatenate(halves(table), 0)


def constants():
    b, g, p = line_tables()
    kron = lambda x, y, z: np.kron(np.kron(x, y), z)
    bbb, ppp = kron(b, b, b), kron(p, p, p)
    grads = [kron(g, b, b), kron(b, g, b), kron(b, b, g)]
    r = np.abs(b).sum(1, keepdims=True)
    limit = kron(np.abs(b), np.abs(b), np.abs(b)) * kron(r, r, r)
    spread = np.kron(np.ones((LD, 1)), np.eye(LD))
    gather = np.kron(np.eye(LD), np.ones((1, LD)))
    return dict(
        mass_up=beside(bbb),
        mass_down=above(bbb.T),
        grad_up=np.concatenate([beside(t) for t in grads], 0),
        grad_down=np.stack([above(t.T) for t in grads], 0),
        limit=above(limit.T),
        bern_up=np.stack(halves(ppp), 0),
        bern_down=np.stack(halves(ppp.T), 0),
        spread=spread.astype(BF),
        gather=gather.astype(BF),
    )


def split2(x):
    high = x.astype(BF)
    return high, (x - high.astype(F32)).astype(BF)


def split3(x):
    high = x.astype(BF)
    rest = x - high.astype(F32)
    mid = rest.astype(BF)
    return high, mid, (rest - mid.astype(F32)).astype(BF)


def dot(a, b, dims=None):
    if dims is None:
        return jnp.dot(a, b, preferred_element_type=F32)
    return lax.dot_general(a, b, dims, preferred_element_type=F32)


def up(table, x):
    high, low = split2(x)
    return dot(table[...], jnp.concatenate([high, low, high], 0))


def down(table, x):
    high, low = split2(x)
    table = table[...]
    half = table.shape[0] // 2
    both = dot(table, high)
    return both[:half] + both[half:] + dot(table[:half], low)


def pick(tables, chunk_of, lane_of, shape):
    acc = [jnp.zeros(shape, F32) for _ in tables]
    for k in range(62):
        here = chunk_of == k
        for c, row in enumerate(tables):
            got = jnp.take_along_axis(jnp.broadcast_to(row(k), shape), lane_of, axis=1)
            acc[c] = jnp.where(here, got, acc[c])
    return acc


def table_rows(ref, count):
    def row(c, k):
        return ref[c * ROWS + k // 2 : c * ROWS + k // 2 + 1, (k % 2) * HALF : (k % 2 + 1) * HALF]

    return [functools.partial(row, c) for c in range(count)]


def gather_zones(idx_ref, tab_ref, out_ref):
    @pl.loop(0, 8)
    def _(t):
        r0 = pl.multiple_of(t * 8, 8)
        for h in range(2):
            lanes = slice(h * HALF, (h + 1) * HALF)
            idx = idx_ref[pl.ds(r0, 8), lanes]
            got = pick(table_rows(tab_ref, 3), idx >> 7, idx & 127, (8, HALF))
            for c in range(3):
                out_ref[c, pl.ds(r0, 8), lanes] = got[c]


def scatter_tile(acc, idx, rows):
    lane = jnp.where(
        lax.broadcasted_iota(jnp.int32, (WIDE, WIDE), 0) == (idx & 255), 1.0, 0.0
    ).astype(BF)
    here = lax.broadcasted_iota(jnp.int32, (ROWS, WIDE), 0) == (idx >> 8)
    parts = []
    for x in rows:
        high = x.astype(BF).astype(F32)
        for part in (high, x - high):
            parts.append(jnp.where(here, part, 0.0).astype(BF))
    return acc + dot(jnp.concatenate(parts, 0), lane, NT)


def joined(acc):
    acc = acc.reshape(acc.shape[0] // (2 * ROWS), 2, ROWS, WIDE)
    return (acc[:, 0] + acc[:, 1]).reshape(-1, WIDE)


def scatter_zones(idx_ref, term_ref, count):
    def eight(t, acc):
        r0 = pl.multiple_of(t * 8, 8)
        idx = idx_ref[pl.ds(r0, 8), :]
        terms = [term_ref[c, pl.ds(r0, 8), :] for c in range(count)]
        for a in range(8):
            acc = scatter_tile(acc, idx[a : a + 1], [x[a : a + 1] for x in terms])
        return acc

    return joined(lax.fori_loop(0, 8, eight, jnp.zeros((2 * ROWS * count, WIDE), F32)))


def flat_row(ref, first):
    return jnp.concatenate([ref[first : first + 1, :], ref[first + 1 : first + 2, :]], 1)


def received(lists_ref, got_refs, count):
    acc = jnp.zeros((2 * ROWS * count, WIDE), F32)
    for k, got in enumerate(got_refs):
        acc = scatter_tile(acc, flat_row(lists_ref, 2 * k), [flat_row(got, 2 * c) for c in range(count)])
    return joined(acc)


def send_shared(lists_ref, tab_ref, send_refs, count):
    idx = lists_ref[...]
    got = pick(table_rows(tab_ref, count), idx >> 7, idx & 127, (8, HALF))
    for k, send in enumerate(send_refs):
        send[...] = jnp.concatenate(
            [got[min(c, count - 1)][2 * k : 2 * k + 2] for c in range(4)], 0
        )


def force(v_ref, en, jac_ref, mass, t_ref, work_ref, cst):
    bu = cst["bern_up"]
    eh, el = split2(en)
    e_q = dot(bu[0], eh) + dot(bu[0], el) + dot(bu[1], eh)
    pressure = GAMMA_LESS * e_q * mass
    for c in range(3):
        high, low = split2(v_ref[c])
        vc = jnp.concatenate([high, low, high], 0)
        term = jnp.zeros((NPZ, WIDE), F32)
        for k in range(3):
            w = jac_ref[(3 * k + c) * QP : (3 * k + c + 1) * QP, :] * pressure
            dv = dot(cst["grad_up"][k * QP : (k + 1) * QP, :], vc)
            if c == 0 and k == 0:
                work_ref[...] = w * dv
            else:
                work_ref[...] += w * dv
            term = term + down(cst["grad_down"][k], w)
        t_ref[c] = term
    wh, wl = split2(work_ref[...])
    bd = cst["bern_down"]
    return -(dot(bd[0], wh) + dot(bd[0], wl) + dot(bd[1], wh))


def energy_change(rhs_e, inv, cst):
    rh, rl = split2(rhs_e)
    prod = inv * (dot(cst["spread"][...], rh) + dot(cst["spread"][...], rl))
    ph, pl_ = split2(prod)
    return dot(cst["gather"][...], ph) + dot(cst["gather"][...], pl_)


def nodes_in(vel_ref, tab_ref):
    for c in range(3):
        for r in range(31):
            tab_ref[c * ROWS + r : c * ROWS + r + 1, :] = vel_ref[c : c + 1, r * WIDE : (r + 1) * WIDE]
        tab_ref[c * ROWS + 31 : (c + 1) * ROWS, :] = jnp.zeros((1, WIDE), F32)


def pack_kernel(send_ref, jac_ref, mass_ref, inv_ref, en_ref, *refs):
    msgs, (oh,) = refs[:4], refs[4:]
    lane = lax.broadcasted_iota(jnp.int32, (1, WIDE), 1)
    for m in range(4 * CAP):
        p, j = divmod(m, CAP)
        at = p * 8 + j if j < 8 else 32 + p
        oh[at : at + 1, :] = jnp.where(lane == send_ref[0, m], 1.0, 0.0)
    oh[36:40, :] = jnp.zeros((4, WIDE), F32)
    hot = oh[...].astype(BF)

    def put(at, n, block):
        for p in range(4):
            msgs[p][:, at : at + n] = block[p * 8 : (p + 1) * 8]
            done = 0
            while done < n:
                piece, off = divmod(at + done, TAIL)
                step = min(n - done, TAIL - off)
                msgs[p][piece : piece + 1, MSG + off : MSG + off + step] = block[
                    32 + p : 33 + p, done : done + step
                ]
                done += step

    for ref, at in ((jac_ref, AT_JAC), (mass_ref, AT_MASS), (inv_ref, AT_INV), (en_ref, AT_EN)):
        total = ref.shape[0]
        for i in range(0, total, WIDE):
            n = min(WIDE, total - i)
            parts = split3(ref[i : i + n, :])
            put(at + i, n, sum(dot(hot, part, NT) for part in parts))
    for p in range(4):
        msgs[p][:, AT_FLAG:MSG] = jnp.ones((8, MSG - AT_FLAG), F32)


def first_kernel(
    arrive_ref, m0, m1, m2, m3, jac_ref, mass_ref, inv_ref, en_ref, vel_ref, zn_ref, lists_ref,
    limit, grad_up, grad_down, bern_up, bern_down, spread, gather,
    jac_out, mass_out, inv_out, en_out, vel_out, ehalf_out, y_out, s0, s1, s2, s3,
    oh, arr, vz, terms, work,
):
    cst = dict(grad_up=grad_up, grad_down=grad_down, bern_up=bern_up, bern_down=bern_down,
               spread=spread, gather=gather)
    msgs = (m0, m1, m2, m3)
    lane = lax.broadcasted_iota(jnp.int32, (1, WIDE), 1)
    oh[...] = jnp.zeros(oh.shape, F32)
    for m in range(4 * CAP):
        p, j = divmod(m, CAP)
        at = p * 8 + j if j < 8 else 32 + p
        flag = msgs[p][0:1, AT_FLAG : AT_FLAG + 1]
        oh[at : at + 1, :] = jnp.where(lane == arrive_ref[0, m], 1.0, 0.0) * flag
    lands = jnp.sum(oh[...], axis=0, keepdims=True) > 0.5
    hot = oh[...].astype(BF)
    hot3 = jnp.concatenate([hot, hot, hot], 0)
    for p in range(4):
        arr[p * 8 : (p + 1) * 8, :] = msgs[p][:, :MSG]
        for piece in range(7):
            n = min(TAIL, MSG - piece * TAIL)
            arr[32 + p : 33 + p, piece * TAIL : piece * TAIL + n] = msgs[p][
                piece : piece + 1, MSG : MSG + n
            ]
    arr[36:48, :] = jnp.zeros((12, MSG), F32)
    for ref, out, at in (
        (jac_ref, jac_out, AT_JAC), (mass_ref, mass_out, AT_MASS),
        (inv_ref, inv_out, AT_INV), (en_ref, en_out, AT_EN),
    ):
        total = ref.shape[0]
        for i in range(0, total, WIDE):
            n = min(WIDE, total - i)
            wide = min(WIDE, -(-n // HALF) * HALF)
            came = jnp.concatenate(split3(arr[:, at + i : at + i + wide]), 0)
            out[i : i + n, :] = jnp.where(lands, dot(came, hot3, TN)[:n], ref[i : i + n, :])
    nodes_in(vel_ref, vel_out)
    gather_zones(zn_ref, vel_out, vz)
    mass = mass_out[...]
    rhs_e = force(vz, en_out[...], jac_out, mass, terms, work, cst)
    terms[3] = down(limit, mass)
    ehalf_out[...] = en_out[...] + 0.5 * STEP_SIZE * energy_change(rhs_e, inv_out[...], cst)
    y_out[...] = scatter_zones(zn_ref, terms, 4)
    send_shared(lists_ref, y_out, (s0, s1, s2, s3), 4)


def rhos():
    rho, out = 1.0 / SIGMA, []
    for _ in range(SWEEPS):
        new = 1.0 / (2.0 * SIGMA - rho)
        out.append((new * rho, 2.0 * new / DELTA))
        rho = new
    return out


def three(x):
    return jnp.concatenate([x, x, x], 0)


def update(y, r_ref, d_ref, a_ref, ib_ref, step):
    keep, add = rhos()[step]
    r = r_ref[...] - y
    d = keep * d_ref[...] + add * (r * three(ib_ref[...]))
    return r, d, a_ref[...] + d


def apply_mass(zn_ref, mass_ref, mass_up, mass_down, d_ref, y_out, zone, terms):
    gather_zones(zn_ref, d_ref, zone)
    mass = mass_ref[...]
    for c in range(3):
        terms[c] = down(mass_down, up(mass_up[...], zone[c]) * mass)
    y_out[...] = scatter_zones(zn_ref, terms, 3)


def start_kernel(
    g0, g1, g2, g3, y_ref, *refs, first
):
    if first:
        lists, zn, mass, up_ref, down_ref = refs[:5]
        ib, r_out, d_out, y_out, s0, s1, s2, s3, zone, terms = refs[5:]
        y = y_ref[...] + received(lists, (g0, g1, g2, g3), 4)
        pad = lax.broadcasted_iota(jnp.int32, (ROWS, WIDE), 0) == 31
        inv_bound = 1.0 / jnp.where(pad, 1.0, y[96:])
        ib[...] = inv_bound
        r = y[:96]
    else:
        ib, lists, zn, mass, up_ref, down_ref = refs[:6]
        r_out, d_out, y_out, s0, s1, s2, s3, zone, terms = refs[6:]
        r = y_ref[...] + received(lists, (g0, g1, g2, g3), 3)
        inv_bound = ib[...]
    r_out[...] = r
    d_out[...] = r * three(inv_bound) * (1.0 / THETA)
    apply_mass(zn, mass, up_ref, down_ref, d_out, y_out, zone, terms)
    send_shared(lists, y_out, (s0, s1, s2, s3), 3)


def sweep_kernel(
    g0, g1, g2, g3, y_ref, r_ref, d_ref, a_ref, ib_ref, lists, zn, mass, mass_up, mass_down,
    r_out, d_out, a_out, y_out, s0, s1, s2, s3, zone, terms, *, step,
):
    y = y_ref[...] + received(lists, (g0, g1, g2, g3), 3)
    r, d, a = update(y, r_ref, d_ref, a_ref, ib_ref, step)
    r_out[...] = r
    d_out[...] = d
    a_out[...] = a
    apply_mass(zn, mass, mass_up, mass_down, d_out, y_out, zone, terms)
    send_shared(lists, y_out, (s0, s1, s2, s3), 3)


def second_kernel(
    g0, g1, g2, g3, y_ref, r_ref, d_ref, a_ref, ib_ref, lists, zn, mass, jac, inv, en, ehalf, vel,
    grad_up, grad_down, bern_up, bern_down, spread, gather,
    en_out, y_out, s0, s1, s2, s3, vhalf, vz, terms, work,
):
    cst = dict(grad_up=grad_up, grad_down=grad_down, bern_up=bern_up, bern_down=bern_down,
               spread=spread, gather=gather)
    y = y_ref[...] + received(lists, (g0, g1, g2, g3), 3)
    _, _, a = update(y, r_ref, d_ref, a_ref, ib_ref, SWEEPS - 1)
    vhalf[...] = vel[...] + 0.5 * STEP_SIZE * a
    gather_zones(zn, vhalf, vz)
    rhs_e = force(vz, ehalf[...], jac, mass[...], terms, work, cst)
    y_out[...] = scatter_zones(zn, terms, 3)
    send_shared(lists, y_out, (s0, s1, s2, s3), 3)
    en_out[...] = en[...] + STEP_SIZE * energy_change(rhs_e, inv[...], cst)


def last_kernel(g0, g1, g2, g3, y_ref, r_ref, d_ref, a_ref, ib_ref, lists, vel, out):
    y = y_ref[...] + received(lists, (g0, g1, g2, g3), 3)
    _, _, a = update(y, r_ref, d_ref, a_ref, ib_ref, SWEEPS - 1)
    v = vel[...] + STEP_SIZE * a
    for c in range(3):
        for r in range(31):
            out[c : c + 1, r * WIDE : (r + 1) * WIDE] = v[c * ROWS + r : c * ROWS + r + 1]


VM = pl.BlockSpec(memory_space=pltpu.VMEM)
SM = pl.BlockSpec(memory_space=pltpu.SMEM)


def call(kernel, args, outs, scratch=(), scalars=0, limit=24, name=None):
    shapes = [jax.ShapeDtypeStruct(s, F32) for s in outs]
    return pl.pallas_call(
        kernel,
        out_shape=shapes,
        in_specs=[SM] * scalars + [VM] * (len(args) - scalars),
        out_specs=[VM] * len(outs),
        scratch_shapes=[pltpu.VMEM(s, F32) for s in scratch],
        compiler_params=pltpu.CompilerParams(vmem_limit_bytes=limit * 1024 * 1024),
        name=name,
    )(*args)


def paired(first, size):
    return [p for i in range(first, size - 1, 2) for p in ((i, i + 1), (i + 1, i))]


def exchange(sends):
    n_curve, n_split = lax.axis_size("curve"), lax.axis_size("split")
    return [
        lax.ppermute(sends[0], "curve", paired(0, n_curve)),
        lax.ppermute(sends[1], "curve", paired(1, n_curve)),
        lax.ppermute(sends[2], "split", paired(0, n_split)),
        lax.ppermute(sends[3], "split", paired(1, n_split)),
    ]


def per_device(velocity, energy, mass, jac, inv, send_rows, arrive_rows, zone_nodes, shared_nodes):
    cst = {k: jnp.asarray(v) for k, v in constants().items()}
    n_curve, n_split = lax.axis_size("curve"), lax.axis_size("split")
    devices = n_curve * n_split
    lists = shared_nodes[0].reshape(4, 2, HALF)
    odd_c, odd_s = lax.axis_index("curve") % 2 == 1, lax.axis_index("split") % 2 == 1
    swap = lambda odd, x: jnp.where(odd, x[::-1], x)
    lists = jnp.concatenate([swap(odd_c, lists[:2]), swap(odd_s, lists[2:])], 0).reshape(8, HALF)

    zones, node, msg = (WIDE,), (96, WIDE), (8, MSG + TAIL)
    send = [(8, HALF)] * 4
    zscr = [(3, NPZ, WIDE), (3, NPZ, WIDE)]
    msgs = call(pack_kernel, (send_rows, jac, mass, inv, energy), [msg] * 4, [(40, WIDE)], 1, name="pack")
    came = []
    for p, off in enumerate((1, -1, 2, -2)):
        pairs = [(i, i + off) for i in range(devices) if 0 <= i + off < devices]
        came.append(lax.ppermute(msgs[p], AXES, pairs))
    fc = [cst[k] for k in ("grad_up", "grad_down", "bern_up", "bern_down", "spread", "gather")]
    mc = [cst["mass_up"], cst["mass_down"]]
    jac, mass, inv, en, vel, ehalf, y, *sends = call(
        first_kernel,
        (arrive_rows, *came, jac, mass, inv, energy, velocity, zone_nodes, lists,
         cst["limit"], *fc),
        [(9 * QP,) + zones, (QP,) + zones, (LD * LD,) + zones, (LD,) + zones, node, (LD,) + zones,
         (128, WIDE)] + send,
        [(48, WIDE), (48, MSG), (3, NPZ, WIDE), (4, NPZ, WIDE), (QP, WIDE)],
        1, limit=32, name="force_one",
    )
    ib = None
    for section in range(2):
        got = exchange(sends)
        outs = [node, node, node] + send
        tail = (lists, zone_nodes, mass, *mc)
        if section == 0:
            ib, r, d, y, *sends = call(
                functools.partial(start_kernel, first=True), (*got, y, *tail),
                [(ROWS, WIDE)] + outs, zscr, name="mass_start",
            )
        else:
            r, d, y, *sends = call(
                functools.partial(start_kernel, first=False), (*got, y, ib, *tail), outs, zscr,
                name="mass_start_two",
            )
        a = d
        for step in range(SWEEPS - 1):
            got = exchange(sends)
            r, d, a, y, *sends = call(
                functools.partial(sweep_kernel, step=step), (*got, y, r, d, a, ib, *tail),
                [node] + outs, zscr, name="mass_sweep",
            )
        got = exchange(sends)
        if section == 0:
            energy_next, y, *sends = call(
                second_kernel,
                (*got, y, r, d, a, ib, lists, zone_nodes, mass, jac, inv, en, ehalf, vel, *fc),
                [(LD,) + zones, node] + send,
                [node, (3, NPZ, WIDE), (3, NPZ, WIDE), (QP, WIDE)], limit=32, name="force_two",
            )
        else:
            (velocity_next,) = call(
                last_kernel, (*got, y, r, d, a, ib, lists, vel), [velocity.shape], name="finish"
            )
    return velocity_next, energy_next


def solution(mesh):
    both = P(None, AXES)
    rows = P(AXES, None)
    return jax.shard_map(
        per_device,
        mesh=mesh,
        in_specs=(both, both, both, both, both, rows, rows, both, P(AXES, None, None)),
        out_specs=(both, both),
        check_vma=False,
    )
```

time: 2040 us -> 194 us (0.10)
  other arithmetic: 1040 us -> 0.77 us
  local copies, waits for them, and re-layouts: 710 us -> 16.6 us
  starting transfers between devices: 196 us -> 73.4 us
  Pallas kernels: 0 us -> 82.9 us
  matrix products: 71.4 us -> 0 us
    scatter-add x45 -> x0, other arithmetic: 1010 us -> none  [the longest x9 804 us: scatter_nodes(): jnp.zeros((terms.shape[0], node_count), jnp.float32).at[:, connect]]
    gather x30 -> x0, local copies, waits for them, and re-layouts: 555 us -> none  [the longest x12 375 us: zone_mass(): dir_zone = direction_nodes[:, connect].reshape(3, H1D, H1D, H1D, zone_count)]
    ppermute x52 -> x36, starting transfers between devices: 196 us -> 73.4 us  [the longest x8 27.3 us: exchange(): lax.ppermute(sends[1], 'curve', paired(1, n_curve))]
    pallas_call x0 -> x10, Pallas kernels: none -> 82.9 us  [call(): pl.pallas_call(kernel, out_shape=shapes, in_specs=[SM] * scalars + [VM] *...]
    dot_general x85 -> x0, matrix products: 71.4 us -> none  [apply_along(): return jnp.einsum(einsum_forms[which_axis], matrix, tensor, precision=HIGH)]
    reshape x36 -> x0, local copies, waits for them, and re-layouts: 69.9 us -> none  [the longest x12 38.4 us: zone_mass(): back.reshape(3, H1D ** 3, zone_count)]
    scatter-add x8 -> x0, local copies, waits for them, and re-layouts: 26.3 us -> none  [assemble(): result.at[:, lists[3]].add(split_got[:, 0]).at[:, lists[2]]]
  transfers between devices with their start and end apart: 52 -> 36, of which waited for: 0 -> 16; matrix products, arithmetic and copies ran while one was open for 55% -> 2% of each run, Pallas kernels for 0% -> 0%
where the time goes in v1:
time: 194 us; the launch traced here: 193 us
  Pallas kernels  82.9 us (43%)
  starting transfers between devices  73.4 us (38%)
  waiting for transfers between devices  18 us (9%)
  local copies, waits for them, and re-layouts  16.6 us (9%)
    pallas_call x10, Pallas kernels, call(): pl.pallas_call(kernel, out_shape=shapes, in_specs=[SM] * scalars + [VM] *...  82.9 us
    ppermute x8, starting transfers between devices, exchange(): lax.ppermute(sends[1], 'curve', paired(1, n_curve))  27.3 us
    ppermute x8, starting transfers between devices, exchange(): lax.ppermute(sends[3], 'split', paired(1, n_split))  26.5 us
    ppermute x4, starting transfers between devices, per_device(): came.append(lax.ppermute(msgs[p], AXES, pairs))  15.9 us
    ppermute x8, waiting for transfers between devices, exchange(): lax.ppermute(sends[3], 'split', paired(1, n_split))  14.4 us
    unnamed x50, local copies, waits for them, and re-layouts  12.7 us
  transfers between devices with their start and end apart: 36, of which 16 were waited for; matrix products, arithmetic and copies ran while one was open for 2% of the time, Pallas kernels for 0%

profile of v1, /device:TPU:26, one launch (start us, length us, event | category | flops | bytes accessed | tf_op | source)
XLA Modules:
  0.0 192.9 jit_solution(8356595461938955787)
XLA Ops:
  5.7 2.8 %pack.1 = (f32[8,3712]{1,0:T(8,128)}, f32[8,3712]{1,0:T(8,128)}, f32[8,3712]{1,0:T(8,128)}, f32[8,3712]{1,0:T(8,128)}) custom-call(s32[1,36]{1,0:T(1,128)S(1)} %copy-done.23, f32[1944,256]{1,0:T(8,128)S(1)} %copy-done, f32[216,256]{1,0:T(8,128)S(1)} %copy-done.9, f32[729,256]{1,0:T(8,128)S(1)} %copy-done.4, f32[27,256]{1,0:T(8,128)S(1)} %copy-done.18), custom_call_target="tpu_custom_call" | custom-call | tf_op jit(solution)/shard_map/pack/pallas_call | solution.py:408
  8.5 3.4 %collective-permute-start = (f32[8,3712]{1,0:T(8,128)}, f32[8,3712]{1,0:T(8,128)S(1)}, u32[]{:S(2)}, u32[]{:S(2)}) collective-permute-start(f32[8,3712]{1,0:T(8,128)} %get-tuple-element.70), channel_id=1, source_target_pairs={{0,1},{1,2},{2,3},{3,4},{4,5},{5,6},{6,7},{7,8},{8,9},{9,10},{10,1... | collective-permute-start | bytes 356360 | tf_op jit(solution)/shard_map/ppermute | solution.py:449
  11.9 2.4 %collective-permute-start.1 = (f32[8,3712]{1,0:T(8,128)}, f32[8,3712]{1,0:T(8,128)S(1)}, u32[]{:S(2)}, u32[]{:S(2)}) collective-permute-start(f32[8,3712]{1,0:T(8,128)} %get-tuple-element.71), channel_id=1, source_target_pairs={{1,0},{2,1},{3,2},{4,3},{5,4},{6,5},{7,6},{8,7},{9,8},{10,9},{11,1... | collective-permute-start | bytes 356360 | tf_op jit(solution)/shard_map/ppermute | solution.py:449
  14.3 4.0 %collective-permute-start.2 = (f32[8,3712]{1,0:T(8,128)}, f32[8,3712]{1,0:T(8,128)S(1)}, u32[]{:S(2)}, u32[]{:S(2)}) collective-permute-start(f32[8,3712]{1,0:T(8,128)} %get-tuple-element.72), channel_id=1, source_target_pairs={{0,2},{1,3},{2,4},{3,5},{4,6},{5,7},{6,8},{7,9},{8,10},{9,11},{10,... | collective-permute-start | bytes 356360 | tf_op jit(solution)/shard_map/ppermute | solution.py:449
  18.4 6.0 %collective-permute-start.3 = (f32[8,3712]{1,0:T(8,128)}, f32[8,3712]{1,0:T(8,128)S(1)}, u32[]{:S(2)}, u32[]{:S(2)}) collective-permute-start(f32[8,3712]{1,0:T(8,128)} %get-tuple-element.73), channel_id=1, source_target_pairs={{2,0},{3,1},{4,2},{5,3},{6,4},{7,5},{8,6},{9,7},{10,8},{11,9},{12,... | collective-permute-start | bytes 356360 | tf_op jit(solution)/shard_map/ppermute | solution.py:449
  36.8 11.5 %force_one.1 = (f32[1944,256]{1,0:T(8,128)S(1)}, f32[216,256]{1,0:T(8,128)S(1)}, f32[729,256]{1,0:T(8,128)S(1)}, f32[27,256]{1,0:T(8,128)S(1)}, f32[96,256]{1,0:...) custom-call(s32[1,36]{1,0:T(1,128)S(1)} %copy-done.24, ...), custom_call_target="tpu_custom_call" | custom-call | tf_op jit(solution)/shard_map/force_one/pallas_call | solution.py:408
  48.4 4.1 %collective-permute-start.5 = (f32[8,128]{1,0:T(8,128)S(1)}, f32[8,128]{1,0:T(8,128)S(1)}, u32[]{:S(2)}, u32[]{:S(2)}) collective-permute-start(f32[8,128]{1,0:T(8,128)S(1)} %get-tuple-element.75), channel_id=1, source_target_pairs={{4,8},{8,4},{12,16},{16,12},{20,24},{24,20},{28,32},{32,28},{36,40... | collective-permute-start | bytes 12296 | tf_op jit(solution)/shard_map/ppermute | solution.py:427
  52.5 2.5 %collective-permute-start.6 = (f32[8,128]{1,0:T(8,128)S(1)}, f32[8,128]{1,0:T(8,128)S(1)}, u32[]{:S(2)}, u32[]{:S(2)}) collective-permute-start(f32[8,128]{1,0:T(8,128)S(1)} %get-tuple-element.76), channel_id=1, source_target_pairs={{0,1},{1,0},{2,3},{3,2},{4,5},{5,4},{6,7},{7,6},{8,9},{9,8},{10,11... | collective-permute-start | bytes 12296 | tf_op jit(solution)/shard_map/ppermute | solution.py:428
  55.0 4.6 %collective-permute-start.7 = (f32[8,128]{1,0:T(8,128)S(1)}, f32[8,128]{1,0:T(8,128)S(1)}, u32[]{:S(2)}, u32[]{:S(2)}) collective-permute-start(f32[8,128]{1,0:T(8,128)S(1)} %get-tuple-element.77), channel_id=1, source_target_pairs={{1,2},{2,1},{5,6},{6,5},{9,10},{10,9},{13,14},{14,13},{17,18},{18,... | collective-permute-start | bytes 12296 | tf_op jit(solution)/shard_map/ppermute | solution.py:429
  61.2 9.5 %mass_start.1 = (f32[32,256]{1,0:T(8,128)S(1)}, f32[96,256]{1,0:T(8,128)S(1)}, f32[96,256]{1,0:T(8,128)S(1)}, f32[96,256]{1,0:T(8,128)S(1)}, f32[8,128]{1,0:T(8,...) custom-call(f32[8,128]{1,0:T(8,128)S(1)} %collective-permute-done.4.g0, ...), custom_call_target="tpu_custom_call" | custom-call | tf_op jit(solution)/shard_map/mass_start/pallas_call | solution.py:408
  70.8 3.6 %collective-permute-start.9 = (f32[8,128]{1,0:T(8,128)S(1)}, f32[8,128]{1,0:T(8,128)S(1)}, u32[]{:S(2)}, u32[]{:S(2)}) collective-permute-start(f32[8,128]{1,0:T(8,128)S(1)} %get-tuple-element.81), channel_id=1, source_target_pairs={{4,8},{8,4},{12,16},{16,12},{20,24},{24,20},{28,32},{32,28},{36,40... | collective-permute-start | bytes 12296 | tf_op jit(solution)/shard_map/ppermute | solution.py:427
  74.5 2.6 %collective-permute-start.11 = (f32[8,128]{1,0:T(8,128)S(1)}, f32[8,128]{1,0:T(8,128)S(1)}, u32[]{:S(2)}, u32[]{:S(2)}) collective-permute-start(f32[8,128]{1,0:T(8,128)S(1)} %get-tuple-element.83), channel_id=1, source_target_pairs={{1,2},{2,1},{5,6},{6,5},{9,10},{10,9},{13,14},{14,13},{17,18},{18,... | collective-permute-start | bytes 12296 | tf_op jit(solution)/shard_map/ppermute | solution.py:429
  78.1 1.9 collective-permute-done.11.g3
  80.0 9.4 %mass_sweep.4 = (f32[96,256]{1,0:T(8,128)S(1)}, f32[96,256]{1,0:T(8,128)S(1)}, f32[96,256]{1,0:T(8,128)S(1)}, f32[96,256]{1,0:T(8,128)S(1)}, f32[8,128]{1,0:T(8,...) custom-call(f32[8,128]{1,0:T(8,128)S(1)} %collective-permute-done.8.g0, ...), custom_call_target="tpu_custom_call" | custom-call | tf_op jit(solution)/shard_map/mass_sweep/pallas_call | solution.py:408
  89.5 3.2 %collective-permute-start.13 = (f32[8,128]{1,0:T(8,128)S(1)}, f32[8,128]{1,0:T(8,128)S(1)}, u32[]{:S(2)}, u32[]{:S(2)}) collective-permute-start(f32[8,128]{1,0:T(8,128)S(1)} %get-tuple-element.89), channel_id=1, source_target_pairs={{4,8},{8,4},{12,16},{16,12},{20,24},{24,20},{28,32},{32,28},{36,40... | collective-permute-start | bytes 12296 | tf_op jit(solution)/shard_map/ppermute | solution.py:427
  92.8 3.6 %collective-permute-start.15 = (f32[8,128]{1,0:T(8,128)S(1)}, f32[8,128]{1,0:T(8,128)S(1)}, u32[]{:S(2)}, u32[]{:S(2)}) collective-permute-start(f32[8,128]{1,0:T(8,128)S(1)} %get-tuple-element.91), channel_id=1, source_target_pairs={{1,2},{2,1},{5,6},{6,5},{9,10},{10,9},{13,14},{14,13},{17,18},{18,... | collective-permute-start | bytes 12296 | tf_op jit(solution)/shard_map/ppermute | solution.py:429
  98.3 9.5 %mass_sweep.5 = (f32[96,256]{1,0:T(8,128)S(1)}, f32[96,256]{1,0:T(8,128)S(1)}, f32[96,256]{1,0:T(8,128)S(1)}, f32[96,256]{1,0:T(8,128)S(1)}, f32[8,128]{1,0:T(8,...) custom-call(f32[8,128]{1,0:T(8,128)S(1)} %collective-permute-done.12.g0, ...), custom_call_target="tpu_custom_call" | custom-call | tf_op jit(solution)/shard_map/mass_sweep/pallas_call | solution.py:408
  107.9 3.3 %collective-permute-start.17 = (f32[8,128]{1,0:T(8,128)S(1)}, f32[8,128]{1,0:T(8,128)S(1)}, u32[]{:S(2)}, u32[]{:S(2)}) collective-permute-start(f32[8,128]{1,0:T(8,128)S(1)} %get-tuple-element.97), channel_id=1, source_target_pairs={{4,8},{8,4},{12,16},{16,12},{20,24},{24,20},{28,32},{32,28},{36,40... | collective-permute-start | bytes 12296 | tf_op jit(solution)/shard_map/ppermute | solution.py:427
  111.3 2.9 %collective-permute-start.19 = (f32[8,128]{1,0:T(8,128)S(1)}, f32[8,128]{1,0:T(8,128)S(1)}, u32[]{:S(2)}, u32[]{:S(2)}) collective-permute-start(f32[8,128]{1,0:T(8,128)S(1)} %get-tuple-element.99), channel_id=1, source_target_pairs={{1,2},{2,1},{5,6},{6,5},{9,10},{10,9},{13,14},{14,13},{17,18},{18,... | collective-permute-start | bytes 12296 | tf_op jit(solution)/shard_map/ppermute | solution.py:429
  114.9 1.9 collective-permute-done.19.g3
  116.8 11.0 %force_two.1 = (f32[27,256]{1,0:T(8,128)}, f32[96,256]{1,0:T(8,128)S(1)}, f32[8,128]{1,0:T(8,128)S(1)}, f32[8,128]{1,0:T(8,128)S(1)}, f32[8,128]{1,0:T(8,128)S(1)}, /*index=5*/f32[8,128]{1,0:T(8,128)S(1)}) custom-call(f32[8,128]{1,0:T(8,128)S(1)} %collective-permute-done.16.g0, f32[8,128]{1,0:T(8,128)S(1)} %collective-permute-done.17.g1, ...), custom_call_target="tpu_custom_call" | custom-call | tf_op jit(solution)/shard_map/force_two/pallas_call | solution.py:408
  127.8 3.2 %collective-permute-start.21 = (f32[8,128]{1,0:T(8,128)S(1)}, f32[8,128]{1,0:T(8,128)S(1)}, u32[]{:S(2)}, u32[]{:S(2)}) collective-permute-start(f32[8,128]{1,0:T(8,128)S(1)} %get-tuple-element.110), channel_id=1, source_target_pairs={{4,8},{8,4},{12,16},{16,12},{20,24},{24,20},{28,32},{32,28},{36,40... | collective-permute-start | bytes 12296 | tf_op jit(solution)/shard_map/ppermute | solution.py:427
  131.1 3.6 %collective-permute-start.23 = (f32[8,128]{1,0:T(8,128)S(1)}, f32[8,128]{1,0:T(8,128)S(1)}, u32[]{:S(2)}, u32[]{:S(2)}) collective-permute-start(f32[8,128]{1,0:T(8,128)S(1)} %get-tuple-element.112), channel_id=1, source_target_pairs={{1,2},{2,1},{5,6},{6,5},{9,10},{10,9},{13,14},{14,13},{17,18},{18,... | collective-permute-start | bytes 12296 | tf_op jit(solution)/shard_map/ppermute | solution.py:429
  136.6 9.4 %mass_start_two.1 = (f32[96,256]{1,0:T(8,128)S(1)}, f32[96,256]{1,0:T(8,128)S(1)}, f32[96,256]{1,0:T(8,128)S(1)}, f32[8,128]{1,0:T(8,128)S(1)}, f32[8,128]{1,0:T...) custom-call(f32[8,128]{1,0:T(8,128)S(1)} %collective-permute-done.20.g0, ...), custom_call_target="tpu_custom_call" | custom-call | tf_op jit(solution)/shard_map/mass_start_two/pallas_call | solution.py:408
  146.1 3.3 %collective-permute-start.25 = (f32[8,128]{1,0:T(8,128)S(1)}, f32[8,128]{1,0:T(8,128)S(1)}, u32[]{:S(2)}, u32[]{:S(2)}) collective-permute-start(f32[8,128]{1,0:T(8,128)S(1)} %get-tuple-element.115), channel_id=1, source_target_pairs={{4,8},{8,4},{12,16},{16,12},{20,24},{24,20},{28,32},{32,28},{36,40... | collective-permute-start | bytes 12296 | tf_op jit(solution)/shard_map/ppermute | solution.py:427
  149.5 2.7 %collective-permute-start.27 = (f32[8,128]{1,0:T(8,128)S(1)}, f32[8,128]{1,0:T(8,128)S(1)}, u32[]{:S(2)}, u32[]{:S(2)}) collective-permute-start(f32[8,128]{1,0:T(8,128)S(1)} %get-tuple-element.117), channel_id=1, source_target_pairs={{1,2},{2,1},{5,6},{6,5},{9,10},{10,9},{13,14},{14,13},{17,18},{18,... | collective-permute-start | bytes 12296 | tf_op jit(solution)/shard_map/ppermute | solution.py:429
  155.0 9.4 %mass_sweep.6 = (f32[96,256]{1,0:T(8,128)S(1)}, f32[96,256]{1,0:T(8,128)S(1)}, f32[96,256]{1,0:T(8,128)S(1)}, f32[96,256]{1,0:T(8,128)S(1)}, f32[8,128]{1,0:T(8,...) custom-call(f32[8,128]{1,0:T(8,128)S(1)} %collective-permute-done.24.g0, ...), custom_call_target="tpu_custom_call" | custom-call | tf_op jit(solution)/shard_map/mass_sweep/pallas_call | solution.py:408
  164.6 3.2 %collective-permute-start.29 = (f32[8,128]{1,0:T(8,128)S(1)}, f32[8,128]{1,0:T(8,128)S(1)}, u32[]{:S(2)}, u32[]{:S(2)}) collective-permute-start(f32[8,128]{1,0:T(8,128)S(1)} %get-tuple-element.122), channel_id=1, source_target_pairs={{4,8},{8,4},{12,16},{16,12},{20,24},{24,20},{28,32},{32,28},{36,40... | collective-permute-start | bytes 12296 | tf_op jit(solution)/shard_map/ppermute | solution.py:427
  167.9 3.6 %collective-permute-start.31 = (f32[8,128]{1,0:T(8,128)S(1)}, f32[8,128]{1,0:T(8,128)S(1)}, u32[]{:S(2)}, u32[]{:S(2)}) collective-permute-start(f32[8,128]{1,0:T(8,128)S(1)} %get-tuple-element.124), channel_id=1, source_target_pairs={{1,2},{2,1},{5,6},{6,5},{9,10},{10,9},{13,14},{14,13},{17,18},{18,... | collective-permute-start | bytes 12296 | tf_op jit(solution)/shard_map/ppermute | solution.py:429
  173.4 9.4 %mass_sweep.7 = (f32[96,256]{1,0:T(8,128)S(1)}, f32[96,256]{1,0:T(8,128)S(1)}, f32[96,256]{1,0:T(8,128)S(1)}, f32[96,256]{1,0:T(8,128)S(1)}, f32[8,128]{1,0:T(8,...) custom-call(f32[8,128]{1,0:T(8,128)S(1)} %collective-permute-done.28.g0, ...), custom_call_target="tpu_custom_call" | custom-call | tf_op jit(solution)/shard_map/mass_sweep/pallas_call | solution.py:408
  182.9 3.3 %collective-permute-start.33 = (f32[8,128]{1,0:T(8,128)S(1)}, f32[8,128]{1,0:T(8,128)S(1)}, u32[]{:S(2)}, u32[]{:S(2)}) collective-permute-start(f32[8,128]{1,0:T(8,128)S(1)} %get-tuple-element.130), channel_id=1, source_target_pairs={{4,8},{8,4},{12,16},{16,12},{20,24},{24,20},{28,32},{32,28},{36,40... | collective-permute-start | bytes 12296 | tf_op jit(solution)/shard_map/ppermute | solution.py:427
  186.3 2.7 %collective-permute-start.35 = (f32[8,128]{1,0:T(8,128)S(1)}, f32[8,128]{1,0:T(8,128)S(1)}, u32[]{:S(2)}, u32[]{:S(2)}) collective-permute-start(f32[8,128]{1,0:T(8,128)S(1)} %get-tuple-element.132), channel_id=1, source_target_pairs={{1,2},{2,1},{5,6},{6,5},{9,10},{10,9},{13,14},{14,13},{17,18},{18,... | collective-permute-start | bytes 12296 | tf_op jit(solution)/shard_map/ppermute | solution.py:429
  (105 shorter events, 33.8 us)
Async XLA Ops:
  8.5 20.6 %collective-permute-start = (f32[8,3712]{1,0:T(8,128)}, f32[8,3712]{1,0:T(8,128)S(1)}, u32[]{:S(2)}, u32[]{:S(2)}) collective-permute-start(f32[8,3712]{1,0:T(8,128)} %get-tuple-element.70), channel_id=1, source_target_pairs={{0,1},{1,2},{2,3},{3,4},{4,5},{5,6},{6,7},{7,8},{8,9},{9,10},{10,1... | collective-permute-start | bytes 356360 | tf_op jit(solution)/shard_map/ppermute | solution.py:449
  11.9 17.2 %collective-permute-start.1 = (f32[8,3712]{1,0:T(8,128)}, f32[8,3712]{1,0:T(8,128)S(1)}, u32[]{:S(2)}, u32[]{:S(2)}) collective-permute-start(f32[8,3712]{1,0:T(8,128)} %get-tuple-element.71), channel_id=1, source_target_pairs={{1,0},{2,1},{3,2},{4,3},{5,4},{6,5},{7,6},{8,7},{9,8},{10,9},{11,1... | collective-permute-start | bytes 356360 | tf_op jit(solution)/shard_map/ppermute | solution.py:449
  14.3 14.8 %collective-permute-start.2 = (f32[8,3712]{1,0:T(8,128)}, f32[8,3712]{1,0:T(8,128)S(1)}, u32[]{:S(2)}, u32[]{:S(2)}) collective-permute-start(f32[8,3712]{1,0:T(8,128)} %get-tuple-element.72), channel_id=1, source_target_pairs={{0,2},{1,3},{2,4},{3,5},{4,6},{5,7},{6,8},{7,9},{8,10},{9,11},{10,... | collective-permute-start | bytes 356360 | tf_op jit(solution)/shard_map/ppermute | solution.py:449
  18.4 10.7 %collective-permute-start.3 = (f32[8,3712]{1,0:T(8,128)}, f32[8,3712]{1,0:T(8,128)S(1)}, u32[]{:S(2)}, u32[]{:S(2)}) collective-permute-start(f32[8,3712]{1,0:T(8,128)} %get-tuple-element.73), channel_id=1, source_target_pairs={{2,0},{3,1},{4,2},{5,3},{6,4},{7,5},{8,6},{9,7},{10,8},{11,9},{12,... | collective-permute-start | bytes 356360 | tf_op jit(solution)/shard_map/ppermute | solution.py:449
  48.3 11.4 %collective-permute-start.4 = (f32[8,128]{1,0:T(8,128)S(1)}, f32[8,128]{1,0:T(8,128)S(1)}, u32[]{:S(2)}, u32[]{:S(2)}) collective-permute-start(f32[8,128]{1,0:T(8,128)S(1)} %get-tuple-element.74), channel_id=1, source_target_pairs={{0,4},{4,0},{8,12},{12,8},{16,20},{20,16},{24,28},{28,24},{32,36},... | collective-permute-start | bytes 12296 | tf_op jit(solution)/shard_map/ppermute | solution.py:426
  48.4 11.3 %collective-permute-start.5 = (f32[8,128]{1,0:T(8,128)S(1)}, f32[8,128]{1,0:T(8,128)S(1)}, u32[]{:S(2)}, u32[]{:S(2)}) collective-permute-start(f32[8,128]{1,0:T(8,128)S(1)} %get-tuple-element.75), channel_id=1, source_target_pairs={{4,8},{8,4},{12,16},{16,12},{20,24},{24,20},{28,32},{32,28},{36,40... | collective-permute-start | bytes 12296 | tf_op jit(solution)/shard_map/ppermute | solution.py:427
  52.5 7.2 %collective-permute-start.6 = (f32[8,128]{1,0:T(8,128)S(1)}, f32[8,128]{1,0:T(8,128)S(1)}, u32[]{:S(2)}, u32[]{:S(2)}) collective-permute-start(f32[8,128]{1,0:T(8,128)S(1)} %get-tuple-element.76), channel_id=1, source_target_pairs={{0,1},{1,0},{2,3},{3,2},{4,5},{5,4},{6,7},{7,6},{8,9},{9,8},{10,11... | collective-permute-start | bytes 12296 | tf_op jit(solution)/shard_map/ppermute | solution.py:428
  55.0 6.2 %collective-permute-start.7 = (f32[8,128]{1,0:T(8,128)S(1)}, f32[8,128]{1,0:T(8,128)S(1)}, u32[]{:S(2)}, u32[]{:S(2)}) collective-permute-start(f32[8,128]{1,0:T(8,128)S(1)} %get-tuple-element.77), channel_id=1, source_target_pairs={{1,2},{2,1},{5,6},{6,5},{9,10},{10,9},{13,14},{14,13},{17,18},{18,... | collective-permute-start | bytes 12296 | tf_op jit(solution)/shard_map/ppermute | solution.py:429
  70.7 6.4 %collective-permute-start.8 = (f32[8,128]{1,0:T(8,128)S(1)}, f32[8,128]{1,0:T(8,128)S(1)}, u32[]{:S(2)}, u32[]{:S(2)}) collective-permute-start(f32[8,128]{1,0:T(8,128)S(1)} %get-tuple-element.80), channel_id=1, source_target_pairs={{0,4},{4,0},{8,12},{12,8},{16,20},{20,16},{24,28},{28,24},{32,36},... | collective-permute-start | bytes 12296 | tf_op jit(solution)/shard_map/ppermute | solution.py:426
  70.8 7.0 %collective-permute-start.9 = (f32[8,128]{1,0:T(8,128)S(1)}, f32[8,128]{1,0:T(8,128)S(1)}, u32[]{:S(2)}, u32[]{:S(2)}) collective-permute-start(f32[8,128]{1,0:T(8,128)S(1)} %get-tuple-element.81), channel_id=1, source_target_pairs={{4,8},{8,4},{12,16},{16,12},{20,24},{24,20},{28,32},{32,28},{36,40... | collective-permute-start | bytes 12296 | tf_op jit(solution)/shard_map/ppermute | solution.py:427
  74.5 5.5 %collective-permute-start.11 = (f32[8,128]{1,0:T(8,128)S(1)}, f32[8,128]{1,0:T(8,128)S(1)}, u32[]{:S(2)}, u32[]{:S(2)}) collective-permute-start(f32[8,128]{1,0:T(8,128)S(1)} %get-tuple-element.83), channel_id=1, source_target_pairs={{1,2},{2,1},{5,6},{6,5},{9,10},{10,9},{13,14},{14,13},{17,18},{18,... | collective-permute-start | bytes 12296 | tf_op jit(solution)/shard_map/ppermute | solution.py:429
  89.4 7.1 %collective-permute-start.12 = (f32[8,128]{1,0:T(8,128)S(1)}, f32[8,128]{1,0:T(8,128)S(1)}, u32[]{:S(2)}, u32[]{:S(2)}) collective-permute-start(f32[8,128]{1,0:T(8,128)S(1)} %get-tuple-element.88), channel_id=1, source_target_pairs={{0,4},{4,0},{8,12},{12,8},{16,20},{20,16},{24,28},{28,24},{32,36},... | collective-permute-start | bytes 12296 | tf_op jit(solution)/shard_map/ppermute | solution.py:426
  89.5 7.0 %collective-permute-start.13 = (f32[8,128]{1,0:T(8,128)S(1)}, f32[8,128]{1,0:T(8,128)S(1)}, u32[]{:S(2)}, u32[]{:S(2)}) collective-permute-start(f32[8,128]{1,0:T(8,128)S(1)} %get-tuple-element.89), channel_id=1, source_target_pairs={{4,8},{8,4},{12,16},{16,12},{20,24},{24,20},{28,32},{32,28},{36,40... | collective-permute-start | bytes 12296 | tf_op jit(solution)/shard_map/ppermute | solution.py:427
  92.7 3.8 %collective-permute-start.14 = (f32[8,128]{1,0:T(8,128)S(1)}, f32[8,128]{1,0:T(8,128)S(1)}, u32[]{:S(2)}, u32[]{:S(2)}) collective-permute-start(f32[8,128]{1,0:T(8,128)S(1)} %get-tuple-element.90), channel_id=1, source_target_pairs={{0,1},{1,0},{2,3},{3,2},{4,5},{5,4},{6,7},{7,6},{8,9},{9,8},{10,11... | collective-permute-start | bytes 12296 | tf_op jit(solution)/shard_map/ppermute | solution.py:428
  92.8 5.5 %collective-permute-start.15 = (f32[8,128]{1,0:T(8,128)S(1)}, f32[8,128]{1,0:T(8,128)S(1)}, u32[]{:S(2)}, u32[]{:S(2)}) collective-permute-start(f32[8,128]{1,0:T(8,128)S(1)} %get-tuple-element.91), channel_id=1, source_target_pairs={{1,2},{2,1},{5,6},{6,5},{9,10},{10,9},{13,14},{14,13},{17,18},{18,... | collective-permute-start | bytes 12296 | tf_op jit(solution)/shard_map/ppermute | solution.py:429
  107.8 6.4 %collective-permute-start.16 = (f32[8,128]{1,0:T(8,128)S(1)}, f32[8,128]{1,0:T(8,128)S(1)}, u32[]{:S(2)}, u32[]{:S(2)}) collective-permute-start(f32[8,128]{1,0:T(8,128)S(1)} %get-tuple-element.96), channel_id=1, source_target_pairs={{0,4},{4,0},{8,12},{12,8},{16,20},{20,16},{24,28},{28,24},{32,36},... | collective-permute-start | bytes 12296 | tf_op jit(solution)/shard_map/ppermute | solution.py:426
  107.9 7.0 %collective-permute-start.17 = (f32[8,128]{1,0:T(8,128)S(1)}, f32[8,128]{1,0:T(8,128)S(1)}, u32[]{:S(2)}, u32[]{:S(2)}) collective-permute-start(f32[8,128]{1,0:T(8,128)S(1)} %get-tuple-element.97), channel_id=1, source_target_pairs={{4,8},{8,4},{12,16},{16,12},{20,24},{24,20},{28,32},{32,28},{36,40... | collective-permute-start | bytes 12296 | tf_op jit(solution)/shard_map/ppermute | solution.py:427
  111.3 5.5 %collective-permute-start.19 = (f32[8,128]{1,0:T(8,128)S(1)}, f32[8,128]{1,0:T(8,128)S(1)}, u32[]{:S(2)}, u32[]{:S(2)}) collective-permute-start(f32[8,128]{1,0:T(8,128)S(1)} %get-tuple-element.99), channel_id=1, source_target_pairs={{1,2},{2,1},{5,6},{6,5},{9,10},{10,9},{13,14},{14,13},{17,18},{18,... | collective-permute-start | bytes 12296 | tf_op jit(solution)/shard_map/ppermute | solution.py:429
  127.8 7.0 %collective-permute-start.20 = (f32[8,128]{1,0:T(8,128)S(1)}, f32[8,128]{1,0:T(8,128)S(1)}, u32[]{:S(2)}, u32[]{:S(2)}) collective-permute-start(f32[8,128]{1,0:T(8,128)S(1)} %get-tuple-element.109), channel_id=1, source_target_pairs={{0,4},{4,0},{8,12},{12,8},{16,20},{20,16},{24,28},{28,24},{32,36},... | collective-permute-start | bytes 12296 | tf_op jit(solution)/shard_map/ppermute | solution.py:426
  127.8 7.0 %collective-permute-start.21 = (f32[8,128]{1,0:T(8,128)S(1)}, f32[8,128]{1,0:T(8,128)S(1)}, u32[]{:S(2)}, u32[]{:S(2)}) collective-permute-start(f32[8,128]{1,0:T(8,128)S(1)} %get-tuple-element.110), channel_id=1, source_target_pairs={{4,8},{8,4},{12,16},{16,12},{20,24},{24,20},{28,32},{32,28},{36,40... | collective-permute-start | bytes 12296 | tf_op jit(solution)/shard_map/ppermute | solution.py:427
  131.0 3.8 %collective-permute-start.22 = (f32[8,128]{1,0:T(8,128)S(1)}, f32[8,128]{1,0:T(8,128)S(1)}, u32[]{:S(2)}, u32[]{:S(2)}) collective-permute-start(f32[8,128]{1,0:T(8,128)S(1)} %get-tuple-element.111), channel_id=1, source_target_pairs={{0,1},{1,0},{2,3},{3,2},{4,5},{5,4},{6,7},{7,6},{8,9},{9,8},{10,11... | collective-permute-start | bytes 12296 | tf_op jit(solution)/shard_map/ppermute | solution.py:428
  131.1 5.5 %collective-permute-start.23 = (f32[8,128]{1,0:T(8,128)S(1)}, f32[8,128]{1,0:T(8,128)S(1)}, u32[]{:S(2)}, u32[]{:S(2)}) collective-permute-start(f32[8,128]{1,0:T(8,128)S(1)} %get-tuple-element.112), channel_id=1, source_target_pairs={{1,2},{2,1},{5,6},{6,5},{9,10},{10,9},{13,14},{14,13},{17,18},{18,... | collective-permute-start | bytes 12296 | tf_op jit(solution)/shard_map/ppermute | solution.py:429
  146.0 6.3 %collective-permute-start.24 = (f32[8,128]{1,0:T(8,128)S(1)}, f32[8,128]{1,0:T(8,128)S(1)}, u32[]{:S(2)}, u32[]{:S(2)}) collective-permute-start(f32[8,128]{1,0:T(8,128)S(1)} %get-tuple-element.114), channel_id=1, source_target_pairs={{0,4},{4,0},{8,12},{12,8},{16,20},{20,16},{24,28},{28,24},{32,36},... | collective-permute-start | bytes 12296 | tf_op jit(solution)/shard_map/ppermute | solution.py:426
  146.1 7.0 %collective-permute-start.25 = (f32[8,128]{1,0:T(8,128)S(1)}, f32[8,128]{1,0:T(8,128)S(1)}, u32[]{:S(2)}, u32[]{:S(2)}) collective-permute-start(f32[8,128]{1,0:T(8,128)S(1)} %get-tuple-element.115), channel_id=1, source_target_pairs={{4,8},{8,4},{12,16},{16,12},{20,24},{24,20},{28,32},{32,28},{36,40... | collective-permute-start | bytes 12296 | tf_op jit(solution)/shard_map/ppermute | solution.py:427
  149.5 5.5 %collective-permute-start.27 = (f32[8,128]{1,0:T(8,128)S(1)}, f32[8,128]{1,0:T(8,128)S(1)}, u32[]{:S(2)}, u32[]{:S(2)}) collective-permute-start(f32[8,128]{1,0:T(8,128)S(1)} %get-tuple-element.117), channel_id=1, source_target_pairs={{1,2},{2,1},{5,6},{6,5},{9,10},{10,9},{13,14},{14,13},{17,18},{18,... | collective-permute-start | bytes 12296 | tf_op jit(solution)/shard_map/ppermute | solution.py:429
  164.5 7.1 %collective-permute-start.28 = (f32[8,128]{1,0:T(8,128)S(1)}, f32[8,128]{1,0:T(8,128)S(1)}, u32[]{:S(2)}, u32[]{:S(2)}) collective-permute-start(f32[8,128]{1,0:T(8,128)S(1)} %get-tuple-element.121), channel_id=1, source_target_pairs={{0,4},{4,0},{8,12},{12,8},{16,20},{20,16},{24,28},{28,24},{32,36},... | collective-permute-start | bytes 12296 | tf_op jit(solution)/shard_map/ppermute | solution.py:426
  164.6 7.0 %collective-permute-start.29 = (f32[8,128]{1,0:T(8,128)S(1)}, f32[8,128]{1,0:T(8,128)S(1)}, u32[]{:S(2)}, u32[]{:S(2)}) collective-permute-start(f32[8,128]{1,0:T(8,128)S(1)} %get-tuple-element.122), channel_id=1, source_target_pairs={{4,8},{8,4},{12,16},{16,12},{20,24},{24,20},{28,32},{32,28},{36,40... | collective-permute-start | bytes 12296 | tf_op jit(solution)/shard_map/ppermute | solution.py:427
  167.8 3.8 %collective-permute-start.30 = (f32[8,128]{1,0:T(8,128)S(1)}, f32[8,128]{1,0:T(8,128)S(1)}, u32[]{:S(2)}, u32[]{:S(2)}) collective-permute-start(f32[8,128]{1,0:T(8,128)S(1)} %get-tuple-element.123), channel_id=1, source_target_pairs={{0,1},{1,0},{2,3},{3,2},{4,5},{5,4},{6,7},{7,6},{8,9},{9,8},{10,11... | collective-permute-start | bytes 12296 | tf_op jit(solution)/shard_map/ppermute | solution.py:428
  167.9 5.5 %collective-permute-start.31 = (f32[8,128]{1,0:T(8,128)S(1)}, f32[8,128]{1,0:T(8,128)S(1)}, u32[]{:S(2)}, u32[]{:S(2)}) collective-permute-start(f32[8,128]{1,0:T(8,128)S(1)} %get-tuple-element.124), channel_id=1, source_target_pairs={{1,2},{2,1},{5,6},{6,5},{9,10},{10,9},{13,14},{14,13},{17,18},{18,... | collective-permute-start | bytes 12296 | tf_op jit(solution)/shard_map/ppermute | solution.py:429
  182.8 6.3 %collective-permute-start.32 = (f32[8,128]{1,0:T(8,128)S(1)}, f32[8,128]{1,0:T(8,128)S(1)}, u32[]{:S(2)}, u32[]{:S(2)}) collective-permute-start(f32[8,128]{1,0:T(8,128)S(1)} %get-tuple-element.129), channel_id=1, source_target_pairs={{0,4},{4,0},{8,12},{12,8},{16,20},{20,16},{24,28},{28,24},{32,36},... | collective-permute-start | bytes 12296 | tf_op jit(solution)/shard_map/ppermute | solution.py:426
  182.9 7.0 %collective-permute-start.33 = (f32[8,128]{1,0:T(8,128)S(1)}, f32[8,128]{1,0:T(8,128)S(1)}, u32[]{:S(2)}, u32[]{:S(2)}) collective-permute-start(f32[8,128]{1,0:T(8,128)S(1)} %get-tuple-element.130), channel_id=1, source_target_pairs={{4,8},{8,4},{12,16},{16,12},{20,24},{24,20},{28,32},{32,28},{36,40... | collective-permute-start | bytes 12296 | tf_op jit(solution)/shard_map/ppermute | solution.py:427
  186.3 5.5 %collective-permute-start.35 = (f32[8,128]{1,0:T(8,128)S(1)}, f32[8,128]{1,0:T(8,128)S(1)}, u32[]{:S(2)}, u32[]{:S(2)}) collective-permute-start(f32[8,128]{1,0:T(8,128)S(1)} %get-tuple-element.132), channel_id=1, source_target_pairs={{1,2},{2,1},{5,6},{6,5},{9,10},{10,9},{13,14},{14,13},{17,18},{18,... | collective-permute-start | bytes 12296 | tf_op jit(solution)/shard_map/ppermute | solution.py:429
  (29 other events, 467.9 us)

commit v2 on v1

v2 whole, which is shorter than its diff:
```python
import functools
import math

import jax
import jax.numpy as jnp
import numpy as np
from jax import lax
from jax.experimental import pallas as pl
from jax.experimental.pallas import tpu as pltpu
from jax.sharding import PartitionSpec as P

H1D, Q1D, L1D, SWEEPS = 4, 6, 3, 3
NPZ, QP, LD = 64, 216, 27
GAMMA_LESS = 0.4
STEP_SIZE = 0.25
THETA, DELTA = 0.575, 0.425
SIGMA = THETA / DELTA
AXES = ("curve", "split")
CAP = 9
HALF = 128
WIDE = 256
ROWS = 32
AT_JAC, AT_MASS, AT_INV, AT_EN, AT_FLAG, MSG = 0, 2048, 2304, 3072, 3100, 3200
TAIL = 512
BF, F32 = jnp.bfloat16, jnp.float32
NT = (((1,), (1,)), ((), ()))
TN = (((0,), (0,)), ((), ()))


def line_tables():
    on_line = [-0.9324695142031521, -0.6612093864662645, -0.2386191860831909]
    on_line = on_line + [-v for v in reversed(on_line)]
    points = [0.5 * (v + 1.0) for v in on_line]
    lobatto = [0.5 * (v + 1.0) for v in [-1.0, -0.4472135954999579, 0.4472135954999579, 1.0]]
    value, slope, bern = np.zeros((Q1D, H1D)), np.zeros((Q1D, H1D)), np.zeros((Q1D, L1D))
    for i in range(H1D):
        others = [lobatto[j] for j in range(H1D) if j != i]
        scaling = np.prod([lobatto[i] - o for o in others])
        for q, t in enumerate(points):
            value[q, i] = np.prod([t - o for o in others]) / scaling
            slope[q, i] = sum(
                np.prod([t - others[n] for n in range(3) if n != m]) for m in range(3)
            ) / scaling
    for q, t in enumerate(points):
        for j in range(L1D):
            bern[q, j] = math.comb(2, j) * t**j * (1.0 - t) ** (2 - j)
    return [np.float32(t).astype(np.float64) for t in (value, slope, bern)]


def halves(table):
    high = table.astype(np.float32).astype(BF)
    low = (table - high.astype(np.float64)).astype(np.float32).astype(BF)
    return high, low


def beside(table):
    high, low = halves(table)
    return np.concatenate([high, high, low], 1)


def above(table):
    return np.concatenate(halves(table), 0)


def stacked(tables):
    places, blocks, at = {}, [], 0
    for name, table in tables.items():
        rows, columns = table.shape
        places[name] = (at, rows, columns)
        room = -(-rows // 16) * 16
        block = np.zeros((room, WIDE), BF)
        block[:rows, :columns] = table
        blocks.append(block)
        at += room
    return np.concatenate(blocks, 0), places


def constants():
    b, g, p = line_tables()
    kron = lambda x, y, z: np.kron(np.kron(x, y), z)
    bbb, ppp = kron(b, b, b), kron(p, p, p)
    grads = [kron(g, b, b), kron(b, g, b), kron(b, b, g)]
    r = np.abs(b).sum(1, keepdims=True)
    limit = kron(np.abs(b), np.abs(b), np.abs(b)) * kron(r, r, r)
    spread = np.kron(np.ones((LD, 1)), np.eye(LD)).astype(BF)
    collect = np.kron(np.eye(LD), np.ones((1, LD))).astype(BF)
    force = dict(
        bern_up_high=halves(ppp)[0],
        bern_up_low=halves(ppp)[1],
        bern_down_high=halves(ppp.T)[0],
        bern_down_low=halves(ppp.T)[1],
        spread=spread,
        limit=above(limit.T),
    )
    for k, t in enumerate(grads):
        force["up%d" % k] = beside(t)
        force["down%d" % k] = above(t.T)
    for k in range(0, LD * LD, 243):
        force["collect%d" % k] = collect[:, k : k + 243]
    return stacked(force), stacked(dict(up=beside(bbb), down=above(bbb.T)))


(FORCE_TABLES, FORCE_AT), (MASS_TABLES, MASS_AT) = constants()


def entry(ref, places, name):
    at, rows, columns = places[name]
    return ref[at : at + rows, :columns]


def split2(x):
    high = x.astype(BF)
    return high, (x - high.astype(F32)).astype(BF)


def split3(x):
    high = x.astype(BF)
    rest = x - high.astype(F32)
    mid = rest.astype(BF)
    return high, mid, (rest - mid.astype(F32)).astype(BF)


def dot(a, b, dims=None):
    if dims is None:
        return jnp.dot(a, b, preferred_element_type=F32)
    return lax.dot_general(a, b, dims, preferred_element_type=F32)


def up(table, x):
    high, low = split2(x)
    return dot(table, jnp.concatenate([high, low, high], 0))


def down(table, x):
    high, low = split2(x)
    half = table.shape[0] // 2
    both = dot(table, high)
    return both[:half] + both[half:] + dot(table[:half], low)


def pick(tables, chunk_of, lane_of, shape, kind=F32):
    acc = [jnp.zeros(shape, kind) for _ in tables]
    for k in range(62):
        here = chunk_of == k
        for c, row in enumerate(tables):
            got = jnp.take_along_axis(jnp.broadcast_to(row(k), shape), lane_of, axis=1)
            acc[c] = jnp.where(here, got, acc[c])
    return acc


def table_rows(ref, count):
    def row(c, k):
        return ref[c * ROWS + k // 2 : c * ROWS + k // 2 + 1, (k % 2) * HALF : (k % 2 + 1) * HALF]

    return [functools.partial(row, c) for c in range(count)]


def gather_zones(idx_ref, tab_ref, word_ref, out_ref):
    x = tab_ref[...]
    scale = jnp.max(jnp.abs(x), keepdims=True)
    per_unit = 1000000.0 / jnp.maximum(scale, 1e-30)
    step = jnp.maximum(scale, 1e-30) * 1e-6
    q = jnp.round(x * per_unit).astype(jnp.int32) + (1 << 20)
    word_ref[:ROWS] = (q[:ROWS] << 11) | (q[2 * ROWS :] >> 10)
    word_ref[ROWS:] = (q[ROWS : 2 * ROWS] << 11) | (q[2 * ROWS :] & 1023)

    @pl.loop(0, 8)
    def _(t):
        r0 = pl.multiple_of(t * 8, 8)
        for h in range(2):
            lanes = slice(h * HALF, (h + 1) * HALF)
            idx = idx_ref[pl.ds(r0, 8), lanes]
            w0, w1 = pick(table_rows(word_ref, 2), idx >> 7, idx & 127, (8, HALF), jnp.int32)
            back = (
                lax.shift_right_logical(w0, 11),
                lax.shift_right_logical(w1, 11),
                ((w0 & 2047) << 10) | (w1 & 1023),
            )
            for c in range(3):
                out_ref[c, pl.ds(r0, 8), lanes] = (back[c] - (1 << 20)).astype(F32) * step


def scatter_tile(acc, idx, rows):
    lane = jnp.where(
        lax.broadcasted_iota(jnp.int32, (WIDE, WIDE), 0) == (idx & 255), 1.0, 0.0
    ).astype(BF)
    here = lax.broadcasted_iota(jnp.int32, (ROWS, WIDE), 0) == (idx >> 8)
    parts = []
    for x in rows:
        high = x.astype(BF).astype(F32)
        for part in (high, x - high):
            parts.append(jnp.where(here, part, 0.0).astype(BF))
    return acc + dot(jnp.concatenate(parts, 0), lane, NT)


def joined(acc):
    acc = acc.reshape(acc.shape[0] // (2 * ROWS), 2, ROWS, WIDE)
    return (acc[:, 0] + acc[:, 1]).reshape(-1, WIDE)


def scatter_zones(idx_ref, term_ref, count):
    def eight(t, acc):
        r0 = pl.multiple_of(t * 8, 8)
        idx = idx_ref[pl.ds(r0, 8), :]
        terms = [term_ref[c, pl.ds(r0, 8), :] for c in range(count)]
        for a in range(8):
            acc = scatter_tile(acc, idx[a : a + 1], [x[a : a + 1] for x in terms])
        return acc

    return joined(lax.fori_loop(0, 8, eight, jnp.zeros((2 * ROWS * count, WIDE), F32)))


def flat_row(ref, first):
    return jnp.concatenate([ref[first : first + 1, :], ref[first + 1 : first + 2, :]], 1)


def received(lists_ref, got_refs, count):
    acc = jnp.zeros((2 * ROWS * count, WIDE), F32)
    for k, got in enumerate(got_refs):
        acc = scatter_tile(acc, flat_row(lists_ref, 2 * k), [flat_row(got, 2 * c) for c in range(count)])
    return joined(acc)


def send_shared(lists_ref, tab_ref, send_refs, count):
    idx = lists_ref[...]
    got = pick(table_rows(tab_ref, count), idx >> 7, idx & 127, (8, HALF))
    for k, send in enumerate(send_refs):
        send[...] = jnp.concatenate(
            [got[min(c, count - 1)][2 * k : 2 * k + 2] for c in range(4)], 0
        )


def force(v_ref, en, jac_ref, mass, t_ref, work_ref, tables):
    get = functools.partial(entry, tables, FORCE_AT)
    eh, el = split2(en)
    e_q = dot(get("bern_up_high"), eh) + dot(get("bern_up_high"), el) + dot(get("bern_up_low"), eh)
    pressure = GAMMA_LESS * e_q * mass
    for c in range(3):
        high, low = split2(v_ref[c])
        vc = jnp.concatenate([high, low, high], 0)
        term = jnp.zeros((NPZ, WIDE), F32)
        for k in range(3):
            w = jac_ref[(3 * k + c) * QP : (3 * k + c + 1) * QP, :] * pressure
            dv = dot(get("up%d" % k), vc)
            if c == 0 and k == 0:
                work_ref[...] = w * dv
            else:
                work_ref[...] += w * dv
            term = term + down(get("down%d" % k), w)
        t_ref[c] = term
    wh, wl = split2(work_ref[...])
    high, low = get("bern_down_high"), get("bern_down_low")
    return -(dot(high, wh) + dot(high, wl) + dot(low, wh))


def energy_change(rhs_e, inv_ref, tables):
    get = functools.partial(entry, tables, FORCE_AT)
    rh, rl = split2(rhs_e)
    prod = inv_ref[...] * (dot(get("spread"), rh) + dot(get("spread"), rl))
    total = jnp.zeros((LD, WIDE), F32)
    for k in range(0, LD * LD, 243):
        for part in split2(prod[k : k + 243]):
            total = total + dot(get("collect%d" % k), part)
    return total


def nodes_in(vel_ref, tab_ref):
    for c in range(3):
        for r in range(31):
            tab_ref[c * ROWS + r : c * ROWS + r + 1, :] = vel_ref[c : c + 1, r * WIDE : (r + 1) * WIDE]
        tab_ref[c * ROWS + 31 : (c + 1) * ROWS, :] = jnp.zeros((1, WIDE), F32)


def fetch(pairs, sems):
    copies = [pltpu.make_async_copy(a, b, sems.at[i]) for i, (a, b) in enumerate(pairs)]
    for copy in copies:
        copy.start()
    return copies


def split_side():
    return lax.axis_index("split")


def sent_block(k):
    s = split_side()
    return (s % 2, 1 - s % 2, 2 + s // 2, 3 - s // 2)[k]


def landing_block(k):
    s = split_side()
    return (1 - s % 2, s % 2, 3 - s // 2, 2 + s // 2)[k]


def pack_kernel(send_ref, shared_ref, jac_hbm, mass_hbm, inv_hbm, en_hbm, *refs):
    msgs, (lists, oh, jac_ref, mass_ref, inv_ref, en_ref, sems) = refs[:4], refs[4:]
    copies = fetch(
        ((mass_hbm, mass_ref), (inv_hbm, inv_ref), (en_hbm, en_ref), (jac_hbm, jac_ref)), sems
    )
    lane = lax.broadcasted_iota(jnp.int32, (1, WIDE), 1)
    for k in range(4):
        first = sent_block(k) * CAP
        for j in range(CAP):
            at = k * 8 + j if j < 8 else 32 + k
            oh[at : at + 1, :] = jnp.where(lane == send_ref[0, first + j], 1.0, 0.0)
    oh[36:40, :] = jnp.zeros((4, WIDE), F32)
    hot = oh[...].astype(BF)
    odds = (lax.axis_index("curve") % 2, split_side() % 2)
    for k in range(4):
        other = k ^ 1
        row = jnp.where(odds[k // 2] == 1, shared_ref[0, other : other + 1, :], shared_ref[0, k : k + 1, :])
        lists[2 * k : 2 * k + 1, :] = row[:, :HALF]
        lists[2 * k + 1 : 2 * k + 2, :] = row[:, HALF:]

    def put(at, n, block):
        for p in range(4):
            msgs[p][:, at : at + n] = block[p * 8 : (p + 1) * 8]
            done = 0
            while done < n:
                piece, off = divmod(at + done, TAIL)
                step = min(n - done, TAIL - off)
                msgs[p][piece : piece + 1, MSG + off : MSG + off + step] = block[
                    32 + p : 33 + p, done : done + step
                ]
                done += step

    places = ((mass_ref, AT_MASS), (inv_ref, AT_INV), (en_ref, AT_EN), (jac_ref, AT_JAC))
    for copy, (ref, at) in zip(copies, places):
        copy.wait()
        total = ref.shape[0]
        for i in range(0, total, WIDE):
            n = min(WIDE, total - i)
            parts = split3(ref[i : i + n, :])
            put(at + i, n, sum(dot(hot, part, NT) for part in parts))
    for p in range(4):
        msgs[p][:, AT_FLAG:MSG] = jnp.ones((8, MSG - AT_FLAG), F32)


def first_kernel(
    arrive_ref, m0, m1, m2, m3, lists_ref, jac_hbm, mass_hbm, inv_hbm, en_hbm, vel_hbm, zn_hbm, tables_hbm,
    jac_out, mass_out, inv_out, en_out, vel_out, ehalf_out, y_out, s0, s1, s2, s3,
    oh, arr, vz, terms, work, words, jac_ref, mass_ref, inv_ref, en_ref, vel_ref, zn_ref, tables, sems,
):
    copies = fetch(
        ((vel_hbm, vel_ref), (zn_hbm, zn_ref), (jac_hbm, jac_ref), (mass_hbm, mass_ref),
         (inv_hbm, inv_ref), (en_hbm, en_ref), (tables_hbm, tables)), sems,
    )
    msgs = (m0, m1, m2, m3)
    lane = lax.broadcasted_iota(jnp.int32, (1, WIDE), 1)
    oh[...] = jnp.zeros(oh.shape, F32)
    for k in range(4):
        first = landing_block(k) * CAP
        flag = msgs[k][0:1, AT_FLAG : AT_FLAG + 1]
        for j in range(CAP):
            at = k * 8 + j if j < 8 else 32 + k
            oh[at : at + 1, :] = jnp.where(lane == arrive_ref[0, first + j], 1.0, 0.0) * flag
    lands = jnp.sum(oh[...], axis=0, keepdims=True) > 0.5
    hot = oh[...].astype(BF)
    hot3 = jnp.concatenate([hot, hot, hot], 0)
    for p in range(4):
        arr[p * 8 : (p + 1) * 8, :] = msgs[p][:, :MSG]
        for piece in range(7):
            n = min(TAIL, MSG - piece * TAIL)
            arr[32 + p : 33 + p, piece * TAIL : piece * TAIL + n] = msgs[p][
                piece : piece + 1, MSG : MSG + n
            ]
    arr[36:48, :] = jnp.zeros((12, MSG), F32)
    copies[0].wait()
    nodes_in(vel_ref, vel_out)
    copies[1].wait()
    gather_zones(zn_ref, vel_out, words, vz)
    for copy in copies[2:]:
        copy.wait()
    for ref, out, at in (
        (jac_ref, jac_out, AT_JAC), (mass_ref, mass_out, AT_MASS),
        (inv_ref, inv_out, AT_INV), (en_ref, en_out, AT_EN),
    ):
        total = ref.shape[0]
        for i in range(0, total, WIDE):
            n = min(WIDE, total - i)
            wide = min(WIDE, -(-n // HALF) * HALF)
            came = jnp.concatenate(split3(arr[:, at + i : at + i + wide]), 0)
            out[i : i + n, :] = jnp.where(lands, dot(came, hot3, TN)[:n], ref[i : i + n, :])
    mass = mass_out[...]
    rhs_e = force(vz, en_out[...], jac_out, mass, terms, work, tables)
    terms[3] = down(entry(tables, FORCE_AT, "limit"), mass)
    ehalf_out[...] = en_out[...] + 0.5 * STEP_SIZE * energy_change(rhs_e, inv_out, tables)
    y_out[...] = scatter_zones(zn_ref, terms, 4)
    send_shared(lists_ref, y_out, (s0, s1, s2, s3), 4)


def rhos():
    rho, out = 1.0 / SIGMA, []
    for _ in range(SWEEPS):
        new = 1.0 / (2.0 * SIGMA - rho)
        out.append((new * rho, 2.0 * new / DELTA))
        rho = new
    return out


def three(x):
    return jnp.concatenate([x, x, x], 0)


def update(y, r_ref, d_ref, a_ref, ib_ref, step):
    keep, add = rhos()[step]
    r = r_ref[...] - y
    d = keep * d_ref[...] + add * (r * three(ib_ref[...]))
    return r, d, a_ref[...] + d


def apply_mass(zn_ref, mass_ref, tables, d_ref, y_out, zone, terms, words):
    gather_zones(zn_ref, d_ref, words, zone)
    mass = mass_ref[...]
    for c in range(3):
        at_points = up(entry(tables, MASS_AT, "up"), zone[c])
        terms[c] = down(entry(tables, MASS_AT, "down"), at_points * mass)
    y_out[...] = scatter_zones(zn_ref, terms, 3)


def start_kernel(g0, g1, g2, g3, y_ref, *refs, first):
    if first:
        lists, zn, mass, tables = refs[:4]
        ib, r_out, d_out, y_out, s0, s1, s2, s3, *scratch = refs[4:]
        y = y_ref[...] + received(lists, (g0, g1, g2, g3), 4)
        pad = lax.broadcasted_iota(jnp.int32, (ROWS, WIDE), 0) == 31
        inv_bound = 1.0 / jnp.where(pad, 1.0, y[96:])
        ib[...] = inv_bound
        r = y[:96]
    else:
        ib, lists, zn, mass, tables = refs[:5]
        r_out, d_out, y_out, s0, s1, s2, s3, *scratch = refs[5:]
        r = y_ref[...] + received(lists, (g0, g1, g2, g3), 3)
        inv_bound = ib[...]
    r_out[...] = r
    d_out[...] = r * three(inv_bound) * (1.0 / THETA)
    apply_mass(zn, mass, tables, d_out, y_out, *scratch)
    send_shared(lists, y_out, (s0, s1, s2, s3), 3)


def sweep_kernel(
    g0, g1, g2, g3, y_ref, r_ref, d_ref, a_ref, ib_ref, lists, zn, mass, tables,
    r_out, d_out, a_out, y_out, s0, s1, s2, s3, *scratch, step,
):
    y = y_ref[...] + received(lists, (g0, g1, g2, g3), 3)
    r, d, a = update(y, r_ref, d_ref, a_ref, ib_ref, step)
    r_out[...] = r
    d_out[...] = d
    a_out[...] = a
    apply_mass(zn, mass, tables, d_out, y_out, *scratch)
    send_shared(lists, y_out, (s0, s1, s2, s3), 3)


def second_kernel(
    g0, g1, g2, g3, y_ref, r_ref, d_ref, a_ref, ib_ref, lists, zn, mass, jac, inv, en, ehalf, vel, tables,
    en_out, y_out, s0, s1, s2, s3, vhalf, vz, terms, work, words,
):
    y = y_ref[...] + received(lists, (g0, g1, g2, g3), 3)
    _, _, a = update(y, r_ref, d_ref, a_ref, ib_ref, SWEEPS - 1)
    vhalf[...] = vel[...] + 0.5 * STEP_SIZE * a
    gather_zones(zn, vhalf, words, vz)
    rhs_e = force(vz, ehalf[...], jac, mass[...], terms, work, tables)
    y_out[...] = scatter_zones(zn, terms, 3)
    send_shared(lists, y_out, (s0, s1, s2, s3), 3)
    en_out[...] = en[...] + STEP_SIZE * energy_change(rhs_e, inv, tables)


def last_kernel(g0, g1, g2, g3, y_ref, r_ref, d_ref, a_ref, ib_ref, lists, vel, out):
    y = y_ref[...] + received(lists, (g0, g1, g2, g3), 3)
    _, _, a = update(y, r_ref, d_ref, a_ref, ib_ref, SWEEPS - 1)
    v = vel[...] + STEP_SIZE * a
    for c in range(3):
        for r in range(31):
            out[c : c + 1, r * WIDE : (r + 1) * WIDE] = v[c * ROWS + r : c * ROWS + r + 1]


VM = pl.BlockSpec(memory_space=pltpu.VMEM)
SM = pl.BlockSpec(memory_space=pltpu.SMEM)
HB = pl.BlockSpec(memory_space=pl.ANY)


def shape_of(s):
    return s if isinstance(s, jax.ShapeDtypeStruct) else jax.ShapeDtypeStruct(s, F32)


def call(kernel, args, outs, scratch=(), specs=None, limit=16, copies=0, name=None):
    scratch = [pltpu.VMEM(shape_of(s).shape, shape_of(s).dtype) for s in scratch]
    return pl.pallas_call(
        kernel,
        out_shape=[shape_of(s) for s in outs],
        in_specs=specs or [VM] * len(args),
        out_specs=[VM] * len(outs),
        scratch_shapes=scratch + ([pltpu.SemaphoreType.DMA((copies,))] if copies else []),
        compiler_params=pltpu.CompilerParams(vmem_limit_bytes=limit * 1024 * 1024),
        name=name,
    )(*args)


def paired(first, size, hop=1):
    low = [i for i in range(size - hop) if (i // hop) % 2 == first]
    return [p for i in low for p in ((i, i + hop), (i + hop, i))]


def exchange(sends):
    n_curve, n_split = lax.axis_size("curve"), lax.axis_size("split")
    return [
        lax.ppermute(sends[0], "curve", paired(0, n_curve)),
        lax.ppermute(sends[1], "curve", paired(1, n_curve)),
        lax.ppermute(sends[2], "split", paired(0, n_split)),
        lax.ppermute(sends[3], "split", paired(1, n_split)),
    ]


def per_device(velocity, energy, mass, jac, inv, send_rows, arrive_rows, zone_nodes, shared_nodes):
    force_tables, mass_tables = jnp.asarray(FORCE_TABLES), jnp.asarray(MASS_TABLES)
    devices = lax.axis_size("curve") * lax.axis_size("split")
    ints = lambda *s: jax.ShapeDtypeStruct(s, jnp.int32)
    half = lambda *s: jax.ShapeDtypeStruct(s, BF)
    node, msg = (96, WIDE), (8, MSG + TAIL)
    fields = [(9 * QP, WIDE), (QP, WIDE), (LD * LD, WIDE), (LD, WIDE)]
    send = [(8, HALF)] * 4
    zone = (3, NPZ, WIDE)
    words = ints(2 * ROWS, WIDE)
    *msgs, lists = call(
        pack_kernel, (send_rows, shared_nodes, jac, mass, inv, energy), [msg] * 4 + [ints(8, HALF)],
        [(40, WIDE)] + fields, [SM, VM] + [HB] * 4, copies=4, name="pack",
    )
    came = []
    for k, m in enumerate(msgs):
        came.append(lax.ppermute(m, AXES, paired(k % 2, devices, 1 + k // 2)))
    jac, mass, inv, en, vel, ehalf, y, *sends = call(
        first_kernel,
        (arrive_rows, *came, lists, jac, mass, inv, energy, velocity, zone_nodes, force_tables),
        fields + [node, (LD, WIDE), (128, WIDE)] + send,
        [(48, WIDE), (48, MSG), zone, (4, NPZ, WIDE), (QP, WIDE), words] + fields
        + [velocity.shape, ints(NPZ, WIDE), half(*FORCE_TABLES.shape)],
        [SM] + [VM] * 5 + [HB] * 7, limit=24, copies=7, name="force_one",
    )
    scratch = [zone, zone, words]
    for section in range(2):
        got = exchange(sends)
        outs = [node, node, node] + send
        tail = (lists, zone_nodes, mass, mass_tables)
        if section == 0:
            ib, r, d, y, *sends = call(
                functools.partial(start_kernel, first=True), (*got, y, *tail),
                [(ROWS, WIDE)] + outs, scratch, name="mass_start",
            )
        else:
            r, d, y, *sends = call(
                functools.partial(start_kernel, first=False), (*got, y, ib, *tail), outs, scratch,
                name="mass_start_two",
            )
        a = d
        for step in range(SWEEPS - 1):
            got = exchange(sends)
            r, d, a, y, *sends = call(
                functools.partial(sweep_kernel, step=step), (*got, y, r, d, a, ib, *tail),
                [node] + outs, scratch, name="mass_sweep",
            )
        got = exchange(sends)
        if section == 0:
            energy_next, y, *sends = call(
                second_kernel,
                (*got, y, r, d, a, ib, lists, zone_nodes, mass, jac, inv, en, ehalf, vel, force_tables),
                [(LD, WIDE), node] + send, [node, zone, zone, (QP, WIDE), words], limit=24,
                name="force_two",
            )
        else:
            (velocity_next,) = call(
                last_kernel, (*got, y, r, d, a, ib, lists, vel), [velocity.shape], name="finish"
            )
    return velocity_next, energy_next


def solution(mesh):
    both = P(None, AXES)
    rows = P(AXES, None)
    return jax.shard_map(
        per_device,
        mesh=mesh,
        in_specs=(both, both, both, both, both, rows, rows, both, P(AXES, None, None)),
        out_specs=(both, both),
        check_vma=False,
    )
```

time: 194 us -> 179 us (0.923)
  local copies, waits for them, and re-layouts: 16.6 us -> 7.98 us
  starting transfers between devices: 73.4 us -> 68.5 us
  waiting for transfers between devices: 18 us -> 22.4 us
  Pallas kernels: 82.9 us -> 78.6 us
    unnamed x50 -> x32, local copies, waits for them, and re-layouts: 12.7 us -> 7.98 us
    pallas_call x10, Pallas kernels: 82.9 us -> 78.6 us  [call(): pl.pallas_call(kernel, out_shape=[shape_of(s) for s in outs], in_specs=sp...]
    ppermute x4, waiting for transfers between devices: 0.01 us -> 4.01 us  [per_device(): came.append(lax.ppermute(m, AXES, paired(k % 2, devices, 1 + k // 2)))]
    slice x3 -> x0, local copies, waits for them, and re-layouts: 3.87 us -> none  [the longest x2 2.62 us: per_device(): lists[:2]]
    ppermute x4, starting transfers between devices: 15.9 us -> 12.4 us  [per_device(): came.append(lax.ppermute(m, AXES, paired(k % 2, devices, 1 + k // 2)))]
  transfers between devices with their start and end apart: 36 -> 36, of which waited for: 16 -> 18; matrix products, arithmetic and copies ran while one was open for 2% -> 0% of each run, Pallas kernels for 0% -> 0%
where the time goes in v2:
time: 179 us
  Pallas kernels  78.6 us (44%)
  starting transfers between devices  68.5 us (38%)
  waiting for transfers between devices  22.4 us (13%)
  local copies, waits for them, and re-layouts  7.98 us (4%)
    pallas_call x10, Pallas kernels, call(): pl.pallas_call(kernel, out_shape=[shape_of(s) for s in outs], in_specs=sp...  78.6 us
    ppermute x8, starting transfers between devices, exchange(): lax.ppermute(sends[1], 'curve', paired(1, n_curve))  27.2 us
    ppermute x8, starting transfers between devices, exchange(): lax.ppermute(sends[3], 'split', paired(1, n_split))  26.2 us
    ppermute x8, waiting for transfers between devices, exchange(): lax.ppermute(sends[3], 'split', paired(1, n_split))  14.4 us
    ppermute x4, starting transfers between devices, per_device(): came.append(lax.ppermute(m, AXES, paired(k % 2, devices, 1 + k // 2)))  12.4 us
    unnamed x32, local copies, waits for them, and re-layouts  7.98 us
    ppermute x4, waiting for transfers between devices, per_device(): came.append(lax.ppermute(m, AXES, paired(k % 2, devices, 1 + k // 2)))  4.01 us
  transfers between devices with their start and end apart: 36, of which 18 were waited for; matrix products, arithmetic and copies ran while one was open for 0% of the time, Pallas kernels for 0%

profile of v2, /device:TPU:26, one launch (start us, length us, event | category | flops | bytes accessed | tf_op | source)
XLA Modules:
  0.0 178.6 jit_solution(14312011777903863269)
XLA Ops:
  6.4 3.7 %pack.1 = (f32[8,3712]{1,0:T(8,128)S(1)}, f32[8,3712]{1,0:T(8,128)S(1)}, f32[8,3712]{1,0:T(8,128)S(1)}, f32[8,3712]{1,0:T(8,128)S(1)}, s32[8,128]{1,0:T(8,128)S(1)}) custom-call(s32[1,36]{1,0:T(1,128)S(1)} %copy-done.14, s32[1,4,256]{2,1,0:T(4,128)S(1)} %copy-done.13, f32[1944,256]{1,0:T(8,128)S(1)} %copy-done, f32[216,256]{1,0:T(8,128)S(1)} %copy-done.8, ...), custom_call_target="tpu_custom_call" | custom-call | tf_op jit(solution)/shard_map/pack/pallas_call | solution.py:488
  10.7 4.0 %collective-permute-start.1 = (f32[8,3712]{1,0:T(8,128)S(1)}, f32[8,3712]{1,0:T(8,128)S(1)}, u32[]{:S(2)}, u32[]{:S(2)}) collective-permute-start(f32[8,3712]{1,0:T(8,128)S(1)} %get-tuple-element.72), channel_id=1, source_target_pairs={{1,2},{2,1},{3,4},{4,3},{5,6},{6,5},{7,8},{8,7},{9,10},{10,9},{11,... | collective-permute-start | bytes 356360 | tf_op jit(solution)/shard_map/ppermute | solution.py:530
  15.4 7.1 %collective-permute-start.3 = (f32[8,3712]{1,0:T(8,128)S(1)}, f32[8,3712]{1,0:T(8,128)S(1)}, u32[]{:S(2)}, u32[]{:S(2)}) collective-permute-start(f32[8,3712]{1,0:T(8,128)S(1)} %get-tuple-element.74), channel_id=1, source_target_pairs={{2,4},{4,2},{3,5},{5,3},{6,8},{8,6},{7,9},{9,7},{10,12},{12,10},{1... | collective-permute-start | bytes 356360 | tf_op jit(solution)/shard_map/ppermute | solution.py:530
  22.5 4.0 %collective-permute-done.3.m3 = f32[8,3712]{1,0:T(8,128)S(1)} collective-permute-done((f32[8,3712]{1,0:T(8,128)S(1)}, f32[8,3712]{1,0:T(8,128)S(1)}, u32[]{:S(2)}, u32[]{:S(2)}) %collective-permute-start.3) | collective-permute-done | bytes 118816 | tf_op jit(solution)/shard_map/ppermute | solution.py:530
  28.8 12.4 %force_one.1 = (f32[1944,256]{1,0:T(8,128)S(1)}, f32[216,256]{1,0:T(8,128)S(1)}, f32[729,256]{1,0:T(8,128)S(1)}, f32[27,256]{1,0:T(8,128)S(1)}, f32[96,256]{1,0:...) custom-call(s32[1,36]{1,0:T(1,128)S(1)} %copy-done.15, ...), custom_call_target="tpu_custom_call" | custom-call | tf_op jit(solution)/shard_map/force_one/pallas_call | solution.py:488
  41.3 4.0 %collective-permute-start.5 = (f32[8,128]{1,0:T(8,128)S(1)}, f32[8,128]{1,0:T(8,128)S(1)}, u32[]{:S(2)}, u32[]{:S(2)}) collective-permute-start(f32[8,128]{1,0:T(8,128)S(1)} %get-tuple-element.77), channel_id=1, source_target_pairs={{4,8},{8,4},{12,16},{16,12},{20,24},{24,20},{28,32},{32,28},{36,40... | collective-permute-start | bytes 12296 | tf_op jit(solution)/shard_map/ppermute | solution.py:508
  46.7 4.6 %collective-permute-start.7 = (f32[8,128]{1,0:T(8,128)S(1)}, f32[8,128]{1,0:T(8,128)S(1)}, u32[]{:S(2)}, u32[]{:S(2)}) collective-permute-start(f32[8,128]{1,0:T(8,128)S(1)} %get-tuple-element.79), channel_id=1, source_target_pairs={{1,2},{2,1},{5,6},{6,5},{9,10},{10,9},{13,14},{14,13},{17,18},{18,... | collective-permute-start | bytes 12296 | tf_op jit(solution)/shard_map/ppermute | solution.py:510
  52.9 8.6 %mass_start.1 = (f32[32,256]{1,0:T(8,128)S(1)}, f32[96,256]{1,0:T(8,128)S(1)}, f32[96,256]{1,0:T(8,128)S(1)}, f32[96,256]{1,0:T(8,128)S(1)}, f32[8,128]{1,0:T(8,...) custom-call(f32[8,128]{1,0:T(8,128)S(1)} %collective-permute-done.4.g0, ...), custom_call_target="tpu_custom_call" | custom-call | tf_op jit(solution)/shard_map/mass_start/pallas_call | solution.py:488
  61.6 3.6 %collective-permute-start.9 = (f32[8,128]{1,0:T(8,128)S(1)}, f32[8,128]{1,0:T(8,128)S(1)}, u32[]{:S(2)}, u32[]{:S(2)}) collective-permute-start(f32[8,128]{1,0:T(8,128)S(1)} %get-tuple-element.83), channel_id=1, source_target_pairs={{4,8},{8,4},{12,16},{16,12},{20,24},{24,20},{28,32},{32,28},{36,40... | collective-permute-start | bytes 12296 | tf_op jit(solution)/shard_map/ppermute | solution.py:508
  65.3 2.5 %collective-permute-start.11 = (f32[8,128]{1,0:T(8,128)S(1)}, f32[8,128]{1,0:T(8,128)S(1)}, u32[]{:S(2)}, u32[]{:S(2)}) collective-permute-start(f32[8,128]{1,0:T(8,128)S(1)} %get-tuple-element.85), channel_id=1, source_target_pairs={{1,2},{2,1},{5,6},{6,5},{9,10},{10,9},{13,14},{14,13},{17,18},{18,... | collective-permute-start | bytes 12296 | tf_op jit(solution)/shard_map/ppermute | solution.py:510
  68.9 1.9 %collective-permute-done.11.g3 = f32[8,128]{1,0:T(8,128)S(1)} collective-permute-done((f32[8,128]{1,0:T(8,128)S(1)}, f32[8,128]{1,0:T(8,128)S(1)}, u32[]{:S(2)}, u32[]{:S(2)}) %collective-permute-start.11) | collective-permute-done | bytes 4128 | tf_op jit(solution)/shard_map/ppermute | solution.py:510
  70.8 8.6 %mass_sweep.4 = (f32[96,256]{1,0:T(8,128)S(1)}, f32[96,256]{1,0:T(8,128)S(1)}, f32[96,256]{1,0:T(8,128)S(1)}, f32[96,256]{1,0:T(8,128)S(1)}, f32[8,128]{1,0:T(8,...) custom-call(f32[8,128]{1,0:T(8,128)S(1)} %collective-permute-done.8.g0, ...), custom_call_target="tpu_custom_call" | custom-call | tf_op jit(solution)/shard_map/mass_sweep/pallas_call | solution.py:488
  79.5 3.2 %collective-permute-start.13 = (f32[8,128]{1,0:T(8,128)S(1)}, f32[8,128]{1,0:T(8,128)S(1)}, u32[]{:S(2)}, u32[]{:S(2)}) collective-permute-start(f32[8,128]{1,0:T(8,128)S(1)} %get-tuple-element.91), channel_id=1, source_target_pairs={{4,8},{8,4},{12,16},{16,12},{20,24},{24,20},{28,32},{32,28},{36,40... | collective-permute-start | bytes 12296 | tf_op jit(solution)/shard_map/ppermute | solution.py:508
  82.8 3.6 %collective-permute-start.15 = (f32[8,128]{1,0:T(8,128)S(1)}, f32[8,128]{1,0:T(8,128)S(1)}, u32[]{:S(2)}, u32[]{:S(2)}) collective-permute-start(f32[8,128]{1,0:T(8,128)S(1)} %get-tuple-element.93), channel_id=1, source_target_pairs={{1,2},{2,1},{5,6},{6,5},{9,10},{10,9},{13,14},{14,13},{17,18},{18,... | collective-permute-start | bytes 12296 | tf_op jit(solution)/shard_map/ppermute | solution.py:510
  88.3 8.6 %mass_sweep.5 = (f32[96,256]{1,0:T(8,128)S(1)}, f32[96,256]{1,0:T(8,128)S(1)}, f32[96,256]{1,0:T(8,128)S(1)}, f32[96,256]{1,0:T(8,128)S(1)}, f32[8,128]{1,0:T(8,...) custom-call(f32[8,128]{1,0:T(8,128)S(1)} %collective-permute-done.12.g0, ...), custom_call_target="tpu_custom_call" | custom-call | tf_op jit(solution)/shard_map/mass_sweep/pallas_call | solution.py:488
  96.9 3.4 %collective-permute-start.17 = (f32[8,128]{1,0:T(8,128)S(1)}, f32[8,128]{1,0:T(8,128)S(1)}, u32[]{:S(2)}, u32[]{:S(2)}) collective-permute-start(f32[8,128]{1,0:T(8,128)S(1)} %get-tuple-element.99), channel_id=1, source_target_pairs={{4,8},{8,4},{12,16},{16,12},{20,24},{24,20},{28,32},{32,28},{36,40... | collective-permute-start | bytes 12296 | tf_op jit(solution)/shard_map/ppermute | solution.py:508
  100.6 2.7 %collective-permute-start.19 = (f32[8,128]{1,0:T(8,128)S(1)}, f32[8,128]{1,0:T(8,128)S(1)}, u32[]{:S(2)}, u32[]{:S(2)}) collective-permute-start(f32[8,128]{1,0:T(8,128)S(1)} %get-tuple-element.101), channel_id=1, source_target_pairs={{1,2},{2,1},{5,6},{6,5},{9,10},{10,9},{13,14},{14,13},{17,18},{18,... | collective-permute-start | bytes 12296 | tf_op jit(solution)/shard_map/ppermute | solution.py:510
  104.2 1.9 %collective-permute-done.19.g3 = f32[8,128]{1,0:T(8,128)S(1)} collective-permute-done((f32[8,128]{1,0:T(8,128)S(1)}, f32[8,128]{1,0:T(8,128)S(1)}, u32[]{:S(2)}, u32[]{:S(2)}) %collective-permute-start.19) | collective-permute-done | bytes 4128 | tf_op jit(solution)/shard_map/ppermute | solution.py:510
  106.1 10.0 %force_two.1 = (f32[27,256]{1,0:T(8,128)}, f32[96,256]{1,0:T(8,128)S(1)}, f32[8,128]{1,0:T(8,128)S(1)}, f32[8,128]{1,0:T(8,128)S(1)}, f32[8,128]{1,0:T(8,128)S(1)}, /*index=5*/f32[8,128]{1,0:T(8,128)S(1)}) custom-call(f32[8,128]{1,0:T(8,128)S(1)} %collective-permute-done.16.g0, f32[8,128]{1,0:T(8,128)S(1)} %collective-permute-done.17.g1, ...), custom_call_target="tpu_custom_call" | custom-call | tf_op jit(solution)/shard_map/force_two/pallas_call | solution.py:488
  116.1 3.2 %collective-permute-start.21 = (f32[8,128]{1,0:T(8,128)S(1)}, f32[8,128]{1,0:T(8,128)S(1)}, u32[]{:S(2)}, u32[]{:S(2)}) collective-permute-start(f32[8,128]{1,0:T(8,128)S(1)} %get-tuple-element.112), channel_id=1, source_target_pairs={{4,8},{8,4},{12,16},{16,12},{20,24},{24,20},{28,32},{32,28},{36,40... | collective-permute-start | bytes 12296 | tf_op jit(solution)/shard_map/ppermute | solution.py:508
  119.4 3.6 %collective-permute-start.23 = (f32[8,128]{1,0:T(8,128)S(1)}, f32[8,128]{1,0:T(8,128)S(1)}, u32[]{:S(2)}, u32[]{:S(2)}) collective-permute-start(f32[8,128]{1,0:T(8,128)S(1)} %get-tuple-element.114), channel_id=1, source_target_pairs={{1,2},{2,1},{5,6},{6,5},{9,10},{10,9},{13,14},{14,13},{17,18},{18,... | collective-permute-start | bytes 12296 | tf_op jit(solution)/shard_map/ppermute | solution.py:510
  124.9 8.6 %mass_start_two.1 = (f32[96,256]{1,0:T(8,128)S(1)}, f32[96,256]{1,0:T(8,128)S(1)}, f32[96,256]{1,0:T(8,128)S(1)}, f32[8,128]{1,0:T(8,128)S(1)}, f32[8,128]{1,0:T...) custom-call(f32[8,128]{1,0:T(8,128)S(1)} %collective-permute-done.20.g0, ...), custom_call_target="tpu_custom_call" | custom-call | tf_op jit(solution)/shard_map/mass_start_two/pallas_call | solution.py:488
  133.5 3.3 %collective-permute-start.25 = (f32[8,128]{1,0:T(8,128)S(1)}, f32[8,128]{1,0:T(8,128)S(1)}, u32[]{:S(2)}, u32[]{:S(2)}) collective-permute-start(f32[8,128]{1,0:T(8,128)S(1)} %get-tuple-element.117), channel_id=1, source_target_pairs={{4,8},{8,4},{12,16},{16,12},{20,24},{24,20},{28,32},{32,28},{36,40... | collective-permute-start | bytes 12296 | tf_op jit(solution)/shard_map/ppermute | solution.py:508
  137.0 2.7 %collective-permute-start.27 = (f32[8,128]{1,0:T(8,128)S(1)}, f32[8,128]{1,0:T(8,128)S(1)}, u32[]{:S(2)}, u32[]{:S(2)}) collective-permute-start(f32[8,128]{1,0:T(8,128)S(1)} %get-tuple-element.119), channel_id=1, source_target_pairs={{1,2},{2,1},{5,6},{6,5},{9,10},{10,9},{13,14},{14,13},{17,18},{18,... | collective-permute-start | bytes 12296 | tf_op jit(solution)/shard_map/ppermute | solution.py:510
  140.6 1.9 %collective-permute-done.27.g3 = f32[8,128]{1,0:T(8,128)S(1)} collective-permute-done((f32[8,128]{1,0:T(8,128)S(1)}, f32[8,128]{1,0:T(8,128)S(1)}, u32[]{:S(2)}, u32[]{:S(2)}) %collective-permute-start.27) | collective-permute-done | bytes 4128 | tf_op jit(solution)/shard_map/ppermute | solution.py:510
  142.5 8.6 %mass_sweep.6 = (f32[96,256]{1,0:T(8,128)S(1)}, f32[96,256]{1,0:T(8,128)S(1)}, f32[96,256]{1,0:T(8,128)S(1)}, f32[96,256]{1,0:T(8,128)S(1)}, f32[8,128]{1,0:T(8,...) custom-call(f32[8,128]{1,0:T(8,128)S(1)} %collective-permute-done.24.g0, ...), custom_call_target="tpu_custom_call" | custom-call | tf_op jit(solution)/shard_map/mass_sweep/pallas_call | solution.py:488
  151.2 3.2 %collective-permute-start.29 = (f32[8,128]{1,0:T(8,128)S(1)}, f32[8,128]{1,0:T(8,128)S(1)}, u32[]{:S(2)}, u32[]{:S(2)}) collective-permute-start(f32[8,128]{1,0:T(8,128)S(1)} %get-tuple-element.124), channel_id=1, source_target_pairs={{4,8},{8,4},{12,16},{16,12},{20,24},{24,20},{28,32},{32,28},{36,40... | collective-permute-start | bytes 12296 | tf_op jit(solution)/shard_map/ppermute | solution.py:508
  154.4 3.6 %collective-permute-start.31 = (f32[8,128]{1,0:T(8,128)S(1)}, f32[8,128]{1,0:T(8,128)S(1)}, u32[]{:S(2)}, u32[]{:S(2)}) collective-permute-start(f32[8,128]{1,0:T(8,128)S(1)} %get-tuple-element.126), channel_id=1, source_target_pairs={{1,2},{2,1},{5,6},{6,5},{9,10},{10,9},{13,14},{14,13},{17,18},{18,... | collective-permute-start | bytes 12296 | tf_op jit(solution)/shard_map/ppermute | solution.py:510
  159.9 8.6 %mass_sweep.7 = (f32[96,256]{1,0:T(8,128)S(1)}, f32[96,256]{1,0:T(8,128)S(1)}, f32[96,256]{1,0:T(8,128)S(1)}, f32[96,256]{1,0:T(8,128)S(1)}, f32[8,128]{1,0:T(8,...) custom-call(f32[8,128]{1,0:T(8,128)S(1)} %collective-permute-done.28.g0, ...), custom_call_target="tpu_custom_call" | custom-call | tf_op jit(solution)/shard_map/mass_sweep/pallas_call | solution.py:488
  168.6 3.4 %collective-permute-start.33 = (f32[8,128]{1,0:T(8,128)S(1)}, f32[8,128]{1,0:T(8,128)S(1)}, u32[]{:S(2)}, u32[]{:S(2)}) collective-permute-start(f32[8,128]{1,0:T(8,128)S(1)} %get-tuple-element.132), channel_id=1, source_target_pairs={{4,8},{8,4},{12,16},{16,12},{20,24},{24,20},{28,32},{32,28},{36,40... | collective-permute-start | bytes 12296 | tf_op jit(solution)/shard_map/ppermute | solution.py:508
  172.1 2.7 %collective-permute-start.35 = (f32[8,128]{1,0:T(8,128)S(1)}, f32[8,128]{1,0:T(8,128)S(1)}, u32[]{:S(2)}, u32[]{:S(2)}) collective-permute-start(f32[8,128]{1,0:T(8,128)S(1)} %get-tuple-element.134), channel_id=1, source_target_pairs={{1,2},{2,1},{5,6},{6,5},{9,10},{10,9},{13,14},{14,13},{17,18},{18,... | collective-permute-start | bytes 12296 | tf_op jit(solution)/shard_map/ppermute | solution.py:510
  175.7 1.9 %collective-permute-done.35.g3 = f32[8,128]{1,0:T(8,128)S(1)} collective-permute-done((f32[8,128]{1,0:T(8,128)S(1)}, f32[8,128]{1,0:T(8,128)S(1)}, u32[]{:S(2)}, u32[]{:S(2)}) %collective-permute-start.35) | collective-permute-done | bytes 4128 | tf_op jit(solution)/shard_map/ppermute | solution.py:510
  (82 shorter events, 23.7 us)
Async XLA Ops:
  10.1 12.4 %collective-permute-start = (f32[8,3712]{1,0:T(8,128)S(1)}, f32[8,3712]{1,0:T(8,128)S(1)}, u32[]{:S(2)}, u32[]{:S(2)}) collective-permute-start(f32[8,3712]{1,0:T(8,128)S(1)} %get-tuple-element.71), channel_id=1, source_target_pairs={{0,1},{1,0},{2,3},{3,2},{4,5},{5,4},{6,7},{7,6},{8,9},{9,8},{10,11... | collective-permute-start | bytes 356360 | tf_op jit(solution)/shard_map/ppermute | solution.py:530
  10.7 11.8 %collective-permute-start.1 = (f32[8,3712]{1,0:T(8,128)S(1)}, f32[8,3712]{1,0:T(8,128)S(1)}, u32[]{:S(2)}, u32[]{:S(2)}) collective-permute-start(f32[8,3712]{1,0:T(8,128)S(1)} %get-tuple-element.72), channel_id=1, source_target_pairs={{1,2},{2,1},{3,4},{4,3},{5,6},{6,5},{7,8},{8,7},{9,10},{10,9},{11,... | collective-permute-start | bytes 356360 | tf_op jit(solution)/shard_map/ppermute | solution.py:530
  14.7 7.8 %collective-permute-start.2 = (f32[8,3712]{1,0:T(8,128)S(1)}, f32[8,3712]{1,0:T(8,128)S(1)}, u32[]{:S(2)}, u32[]{:S(2)}) collective-permute-start(f32[8,3712]{1,0:T(8,128)S(1)} %get-tuple-element.73), channel_id=1, source_target_pairs={{0,2},{2,0},{1,3},{3,1},{4,6},{6,4},{5,7},{7,5},{8,10},{10,8},{9,1... | collective-permute-start | bytes 356360 | tf_op jit(solution)/shard_map/ppermute | solution.py:530
  15.4 11.2 %collective-permute-start.3 = (f32[8,3712]{1,0:T(8,128)S(1)}, f32[8,3712]{1,0:T(8,128)S(1)}, u32[]{:S(2)}, u32[]{:S(2)}) collective-permute-start(f32[8,3712]{1,0:T(8,128)S(1)} %get-tuple-element.74), channel_id=1, source_target_pairs={{2,4},{4,2},{3,5},{5,3},{6,8},{8,6},{7,9},{9,7},{10,12},{12,10},{1... | collective-permute-start | bytes 356360 | tf_op jit(solution)/shard_map/ppermute | solution.py:530
  41.2 10.1 %collective-permute-start.4 = (f32[8,128]{1,0:T(8,128)S(1)}, f32[8,128]{1,0:T(8,128)S(1)}, u32[]{:S(2)}, u32[]{:S(2)}) collective-permute-start(f32[8,128]{1,0:T(8,128)S(1)} %get-tuple-element.76), channel_id=1, source_target_pairs={{0,4},{4,0},{8,12},{12,8},{16,20},{20,16},{24,28},{28,24},{32,36},... | collective-permute-start | bytes 12296 | tf_op jit(solution)/shard_map/ppermute | solution.py:507
  41.3 10.0 %collective-permute-start.5 = (f32[8,128]{1,0:T(8,128)S(1)}, f32[8,128]{1,0:T(8,128)S(1)}, u32[]{:S(2)}, u32[]{:S(2)}) collective-permute-start(f32[8,128]{1,0:T(8,128)S(1)} %get-tuple-element.77), channel_id=1, source_target_pairs={{4,8},{8,4},{12,16},{16,12},{20,24},{24,20},{28,32},{32,28},{36,40... | collective-permute-start | bytes 12296 | tf_op jit(solution)/shard_map/ppermute | solution.py:508
  45.4 6.0 %collective-permute-start.6 = (f32[8,128]{1,0:T(8,128)S(1)}, f32[8,128]{1,0:T(8,128)S(1)}, u32[]{:S(2)}, u32[]{:S(2)}) collective-permute-start(f32[8,128]{1,0:T(8,128)S(1)} %get-tuple-element.78), channel_id=1, source_target_pairs={{0,1},{1,0},{2,3},{3,2},{4,5},{5,4},{6,7},{7,6},{8,9},{9,8},{10,11... | collective-permute-start | bytes 12296 | tf_op jit(solution)/shard_map/ppermute | solution.py:509
  46.7 6.2 %collective-permute-start.7 = (f32[8,128]{1,0:T(8,128)S(1)}, f32[8,128]{1,0:T(8,128)S(1)}, u32[]{:S(2)}, u32[]{:S(2)}) collective-permute-start(f32[8,128]{1,0:T(8,128)S(1)} %get-tuple-element.79), channel_id=1, source_target_pairs={{1,2},{2,1},{5,6},{6,5},{9,10},{10,9},{13,14},{14,13},{17,18},{18,... | collective-permute-start | bytes 12296 | tf_op jit(solution)/shard_map/ppermute | solution.py:510
  61.5 6.4 %collective-permute-start.8 = (f32[8,128]{1,0:T(8,128)S(1)}, f32[8,128]{1,0:T(8,128)S(1)}, u32[]{:S(2)}, u32[]{:S(2)}) collective-permute-start(f32[8,128]{1,0:T(8,128)S(1)} %get-tuple-element.82), channel_id=1, source_target_pairs={{0,4},{4,0},{8,12},{12,8},{16,20},{20,16},{24,28},{28,24},{32,36},... | collective-permute-start | bytes 12296 | tf_op jit(solution)/shard_map/ppermute | solution.py:507
  61.6 7.0 %collective-permute-start.9 = (f32[8,128]{1,0:T(8,128)S(1)}, f32[8,128]{1,0:T(8,128)S(1)}, u32[]{:S(2)}, u32[]{:S(2)}) collective-permute-start(f32[8,128]{1,0:T(8,128)S(1)} %get-tuple-element.83), channel_id=1, source_target_pairs={{4,8},{8,4},{12,16},{16,12},{20,24},{24,20},{28,32},{32,28},{36,40... | collective-permute-start | bytes 12296 | tf_op jit(solution)/shard_map/ppermute | solution.py:508
  65.3 5.5 %collective-permute-start.11 = (f32[8,128]{1,0:T(8,128)S(1)}, f32[8,128]{1,0:T(8,128)S(1)}, u32[]{:S(2)}, u32[]{:S(2)}) collective-permute-start(f32[8,128]{1,0:T(8,128)S(1)} %get-tuple-element.85), channel_id=1, source_target_pairs={{1,2},{2,1},{5,6},{6,5},{9,10},{10,9},{13,14},{14,13},{17,18},{18,... | collective-permute-start | bytes 12296 | tf_op jit(solution)/shard_map/ppermute | solution.py:510
  79.4 7.0 %collective-permute-start.12 = (f32[8,128]{1,0:T(8,128)S(1)}, f32[8,128]{1,0:T(8,128)S(1)}, u32[]{:S(2)}, u32[]{:S(2)}) collective-permute-start(f32[8,128]{1,0:T(8,128)S(1)} %get-tuple-element.90), channel_id=1, source_target_pairs={{0,4},{4,0},{8,12},{12,8},{16,20},{20,16},{24,28},{28,24},{32,36},... | collective-permute-start | bytes 12296 | tf_op jit(solution)/shard_map/ppermute | solution.py:507
  79.5 7.0 %collective-permute-start.13 = (f32[8,128]{1,0:T(8,128)S(1)}, f32[8,128]{1,0:T(8,128)S(1)}, u32[]{:S(2)}, u32[]{:S(2)}) collective-permute-start(f32[8,128]{1,0:T(8,128)S(1)} %get-tuple-element.91), channel_id=1, source_target_pairs={{4,8},{8,4},{12,16},{16,12},{20,24},{24,20},{28,32},{32,28},{36,40... | collective-permute-start | bytes 12296 | tf_op jit(solution)/shard_map/ppermute | solution.py:508
  82.7 3.8 %collective-permute-start.14 = (f32[8,128]{1,0:T(8,128)S(1)}, f32[8,128]{1,0:T(8,128)S(1)}, u32[]{:S(2)}, u32[]{:S(2)}) collective-permute-start(f32[8,128]{1,0:T(8,128)S(1)} %get-tuple-element.92), channel_id=1, source_target_pairs={{0,1},{1,0},{2,3},{3,2},{4,5},{5,4},{6,7},{7,6},{8,9},{9,8},{10,11... | collective-permute-start | bytes 12296 | tf_op jit(solution)/shard_map/ppermute | solution.py:509
  82.8 5.5 %collective-permute-start.15 = (f32[8,128]{1,0:T(8,128)S(1)}, f32[8,128]{1,0:T(8,128)S(1)}, u32[]{:S(2)}, u32[]{:S(2)}) collective-permute-start(f32[8,128]{1,0:T(8,128)S(1)} %get-tuple-element.93), channel_id=1, source_target_pairs={{1,2},{2,1},{5,6},{6,5},{9,10},{10,9},{13,14},{14,13},{17,18},{18,... | collective-permute-start | bytes 12296 | tf_op jit(solution)/shard_map/ppermute | solution.py:510
  96.8 6.4 %collective-permute-start.16 = (f32[8,128]{1,0:T(8,128)S(1)}, f32[8,128]{1,0:T(8,128)S(1)}, u32[]{:S(2)}, u32[]{:S(2)}) collective-permute-start(f32[8,128]{1,0:T(8,128)S(1)} %get-tuple-element.98), channel_id=1, source_target_pairs={{0,4},{4,0},{8,12},{12,8},{16,20},{20,16},{24,28},{28,24},{32,36},... | collective-permute-start | bytes 12296 | tf_op jit(solution)/shard_map/ppermute | solution.py:507
  96.9 7.0 %collective-permute-start.17 = (f32[8,128]{1,0:T(8,128)S(1)}, f32[8,128]{1,0:T(8,128)S(1)}, u32[]{:S(2)}, u32[]{:S(2)}) collective-permute-start(f32[8,128]{1,0:T(8,128)S(1)} %get-tuple-element.99), channel_id=1, source_target_pairs={{4,8},{8,4},{12,16},{16,12},{20,24},{24,20},{28,32},{32,28},{36,40... | collective-permute-start | bytes 12296 | tf_op jit(solution)/shard_map/ppermute | solution.py:508
  100.3 3.9 %collective-permute-start.18 = (f32[8,128]{1,0:T(8,128)S(1)}, f32[8,128]{1,0:T(8,128)S(1)}, u32[]{:S(2)}, u32[]{:S(2)}) collective-permute-start(f32[8,128]{1,0:T(8,128)S(1)} %get-tuple-element.100), channel_id=1, source_target_pairs={{0,1},{1,0},{2,3},{3,2},{4,5},{5,4},{6,7},{7,6},{8,9},{9,8},{10,11... | collective-permute-start | bytes 12296 | tf_op jit(solution)/shard_map/ppermute | solution.py:509
  100.6 5.5 %collective-permute-start.19 = (f32[8,128]{1,0:T(8,128)S(1)}, f32[8,128]{1,0:T(8,128)S(1)}, u32[]{:S(2)}, u32[]{:S(2)}) collective-permute-start(f32[8,128]{1,0:T(8,128)S(1)} %get-tuple-element.101), channel_id=1, source_target_pairs={{1,2},{2,1},{5,6},{6,5},{9,10},{10,9},{13,14},{14,13},{17,18},{18,... | collective-permute-start | bytes 12296 | tf_op jit(solution)/shard_map/ppermute | solution.py:510
  116.1 6.9 %collective-permute-start.20 = (f32[8,128]{1,0:T(8,128)S(1)}, f32[8,128]{1,0:T(8,128)S(1)}, u32[]{:S(2)}, u32[]{:S(2)}) collective-permute-start(f32[8,128]{1,0:T(8,128)S(1)} %get-tuple-element.111), channel_id=1, source_target_pairs={{0,4},{4,0},{8,12},{12,8},{16,20},{20,16},{24,28},{28,24},{32,36},... | collective-permute-start | bytes 12296 | tf_op jit(solution)/shard_map/ppermute | solution.py:507
  116.1 7.0 %collective-permute-start.21 = (f32[8,128]{1,0:T(8,128)S(1)}, f32[8,128]{1,0:T(8,128)S(1)}, u32[]{:S(2)}, u32[]{:S(2)}) collective-permute-start(f32[8,128]{1,0:T(8,128)S(1)} %get-tuple-element.112), channel_id=1, source_target_pairs={{4,8},{8,4},{12,16},{16,12},{20,24},{24,20},{28,32},{32,28},{36,40... | collective-permute-start | bytes 12296 | tf_op jit(solution)/shard_map/ppermute | solution.py:508
  119.4 5.5 %collective-permute-start.23 = (f32[8,128]{1,0:T(8,128)S(1)}, f32[8,128]{1,0:T(8,128)S(1)}, u32[]{:S(2)}, u32[]{:S(2)}) collective-permute-start(f32[8,128]{1,0:T(8,128)S(1)} %get-tuple-element.114), channel_id=1, source_target_pairs={{1,2},{2,1},{5,6},{6,5},{9,10},{10,9},{13,14},{14,13},{17,18},{18,... | collective-permute-start | bytes 12296 | tf_op jit(solution)/shard_map/ppermute | solution.py:510
  133.5 6.2 %collective-permute-start.24 = (f32[8,128]{1,0:T(8,128)S(1)}, f32[8,128]{1,0:T(8,128)S(1)}, u32[]{:S(2)}, u32[]{:S(2)}) collective-permute-start(f32[8,128]{1,0:T(8,128)S(1)} %get-tuple-element.116), channel_id=1, source_target_pairs={{0,4},{4,0},{8,12},{12,8},{16,20},{20,16},{24,28},{28,24},{32,36},... | collective-permute-start | bytes 12296 | tf_op jit(solution)/shard_map/ppermute | solution.py:507
  133.5 7.0 %collective-permute-start.25 = (f32[8,128]{1,0:T(8,128)S(1)}, f32[8,128]{1,0:T(8,128)S(1)}, u32[]{:S(2)}, u32[]{:S(2)}) collective-permute-start(f32[8,128]{1,0:T(8,128)S(1)} %get-tuple-element.117), channel_id=1, source_target_pairs={{4,8},{8,4},{12,16},{16,12},{20,24},{24,20},{28,32},{32,28},{36,40... | collective-permute-start | bytes 12296 | tf_op jit(solution)/shard_map/ppermute | solution.py:508
  137.0 5.5 %collective-permute-start.27 = (f32[8,128]{1,0:T(8,128)S(1)}, f32[8,128]{1,0:T(8,128)S(1)}, u32[]{:S(2)}, u32[]{:S(2)}) collective-permute-start(f32[8,128]{1,0:T(8,128)S(1)} %get-tuple-element.119), channel_id=1, source_target_pairs={{1,2},{2,1},{5,6},{6,5},{9,10},{10,9},{13,14},{14,13},{17,18},{18,... | collective-permute-start | bytes 12296 | tf_op jit(solution)/shard_map/ppermute | solution.py:510
  151.1 7.0 %collective-permute-start.28 = (f32[8,128]{1,0:T(8,128)S(1)}, f32[8,128]{1,0:T(8,128)S(1)}, u32[]{:S(2)}, u32[]{:S(2)}) collective-permute-start(f32[8,128]{1,0:T(8,128)S(1)} %get-tuple-element.123), channel_id=1, source_target_pairs={{0,4},{4,0},{8,12},{12,8},{16,20},{20,16},{24,28},{28,24},{32,36},... | collective-permute-start | bytes 12296 | tf_op jit(solution)/shard_map/ppermute | solution.py:507
  151.2 7.0 %collective-permute-start.29 = (f32[8,128]{1,0:T(8,128)S(1)}, f32[8,128]{1,0:T(8,128)S(1)}, u32[]{:S(2)}, u32[]{:S(2)}) collective-permute-start(f32[8,128]{1,0:T(8,128)S(1)} %get-tuple-element.124), channel_id=1, source_target_pairs={{4,8},{8,4},{12,16},{16,12},{20,24},{24,20},{28,32},{32,28},{36,40... | collective-permute-start | bytes 12296 | tf_op jit(solution)/shard_map/ppermute | solution.py:508
  154.4 3.8 %collective-permute-start.30 = (f32[8,128]{1,0:T(8,128)S(1)}, f32[8,128]{1,0:T(8,128)S(1)}, u32[]{:S(2)}, u32[]{:S(2)}) collective-permute-start(f32[8,128]{1,0:T(8,128)S(1)} %get-tuple-element.125), channel_id=1, source_target_pairs={{0,1},{1,0},{2,3},{3,2},{4,5},{5,4},{6,7},{7,6},{8,9},{9,8},{10,11... | collective-permute-start | bytes 12296 | tf_op jit(solution)/shard_map/ppermute | solution.py:509
  154.4 5.5 %collective-permute-start.31 = (f32[8,128]{1,0:T(8,128)S(1)}, f32[8,128]{1,0:T(8,128)S(1)}, u32[]{:S(2)}, u32[]{:S(2)}) collective-permute-start(f32[8,128]{1,0:T(8,128)S(1)} %get-tuple-element.126), channel_id=1, source_target_pairs={{1,2},{2,1},{5,6},{6,5},{9,10},{10,9},{13,14},{14,13},{17,18},{18,... | collective-permute-start | bytes 12296 | tf_op jit(solution)/shard_map/ppermute | solution.py:510
  168.5 6.3 %collective-permute-start.32 = (f32[8,128]{1,0:T(8,128)S(1)}, f32[8,128]{1,0:T(8,128)S(1)}, u32[]{:S(2)}, u32[]{:S(2)}) collective-permute-start(f32[8,128]{1,0:T(8,128)S(1)} %get-tuple-element.131), channel_id=1, source_target_pairs={{0,4},{4,0},{8,12},{12,8},{16,20},{20,16},{24,28},{28,24},{32,36},... | collective-permute-start | bytes 12296 | tf_op jit(solution)/shard_map/ppermute | solution.py:507
  168.6 7.0 %collective-permute-start.33 = (f32[8,128]{1,0:T(8,128)S(1)}, f32[8,128]{1,0:T(8,128)S(1)}, u32[]{:S(2)}, u32[]{:S(2)}) collective-permute-start(f32[8,128]{1,0:T(8,128)S(1)} %get-tuple-element.132), channel_id=1, source_target_pairs={{4,8},{8,4},{12,16},{16,12},{20,24},{24,20},{28,32},{32,28},{36,40... | collective-permute-start | bytes 12296 | tf_op jit(solution)/shard_map/ppermute | solution.py:508
  172.1 5.5 %collective-permute-start.35 = (f32[8,128]{1,0:T(8,128)S(1)}, f32[8,128]{1,0:T(8,128)S(1)}, u32[]{:S(2)}, u32[]{:S(2)}) collective-permute-start(f32[8,128]{1,0:T(8,128)S(1)} %get-tuple-element.134), channel_id=1, source_target_pairs={{1,2},{2,1},{5,6},{6,5},{9,10},{10,9},{13,14},{14,13},{17,18},{18,... | collective-permute-start | bytes 12296 | tf_op jit(solution)/shard_map/ppermute | solution.py:510
  (20 other events, 233.0 us)

commit v3 on v2

--- a/solution.py
+++ b/solution.py
@@ -180,17 +180,21 @@
                 out_ref[c, pl.ds(r0, 8), lanes] = (back[c] - (1 << 20)).astype(F32) * step
 
 
-def scatter_tile(acc, idx, rows):
-    lane = jnp.where(
-        lax.broadcasted_iota(jnp.int32, (WIDE, WIDE), 0) == (idx & 255), 1.0, 0.0
-    ).astype(BF)
+def spread_rows(idx, rows):
     here = lax.broadcasted_iota(jnp.int32, (ROWS, WIDE), 0) == (idx >> 8)
     parts = []
     for x in rows:
         high = x.astype(BF).astype(F32)
         for part in (high, x - high):
             parts.append(jnp.where(here, part, 0.0).astype(BF))
-    return acc + dot(jnp.concatenate(parts, 0), lane, NT)
+    return jnp.concatenate(parts, 0)
+
+
+def scatter_tile(acc, idx, rows):
+    lane = jnp.where(
+        lax.broadcasted_iota(jnp.int32, (WIDE, WIDE), 0) == (idx & 255), 1.0, 0.0
+    ).astype(BF)
+    return acc + dot(spread_rows(idx, rows), lane, NT)
 
 
 def joined(acc):
@@ -198,13 +202,13 @@
     return (acc[:, 0] + acc[:, 1]).reshape(-1, WIDE)
 
 
-def scatter_zones(idx_ref, term_ref, count):
+def scatter_zones(idx_ref, lane_ref, term_ref, count):
     def eight(t, acc):
         r0 = pl.multiple_of(t * 8, 8)
         idx = idx_ref[pl.ds(r0, 8), :]
         terms = [term_ref[c, pl.ds(r0, 8), :] for c in range(count)]
         for a in range(8):
-            acc = scatter_tile(acc, idx[a : a + 1], [x[a : a + 1] for x in terms])
+            acc = acc + dot(spread_rows(idx[a : a + 1], [x[a : a + 1] for x in terms]), lane_ref[r0 + a])
         return acc
 
     return joined(lax.fori_loop(0, 8, eight, jnp.zeros((2 * ROWS * count, WIDE), F32)))
@@ -336,15 +340,24 @@
         msgs[p][:, AT_FLAG:MSG] = jnp.ones((8, MSG - AT_FLAG), F32)
 
 
+def prep_kernel(vel_ref, zn_ref, _lists, _arrive, _en, _tables, vel_out, vz, lane_out, words, column):
+    nodes_in(vel_ref, vel_out)
+    gather_zones(zn_ref, vel_out, words, vz)
+    column[:, :NPZ] = jnp.transpose((zn_ref[...] & 255).astype(F32), (1, 0))
+    lane = lax.broadcasted_iota(jnp.int32, (16, WIDE), 1).astype(F32)
+
+    @pl.loop(0, 16)
+    def _(t):
+        r0 = pl.multiple_of(t * 16, 16)
+        rows = column[pl.ds(r0, 16), :]
+        for a in range(NPZ):
+            lane_out[a, pl.ds(r0, 16), :] = jnp.where(lane == rows[:, a : a + 1], 1.0, 0.0).astype(BF)
+
+
 def first_kernel(
-    arrive_ref, m0, m1, m2, m3, lists_ref, jac_hbm, mass_hbm, inv_hbm, en_hbm, vel_hbm, zn_hbm, tables_hbm,
-    jac_out, mass_out, inv_out, en_out, vel_out, ehalf_out, y_out, s0, s1, s2, s3,
-    oh, arr, vz, terms, work, words, jac_ref, mass_ref, inv_ref, en_ref, vel_ref, zn_ref, tables, sems,
+    arrive_ref, m0, m1, m2, m3, lists_ref, jac_ref, mass_ref, inv_ref, en_ref, zn_ref, tables, vz, lanes,
+    jac_out, mass_out, inv_out, en_out, ehalf_out, y_out, s0, s1, s2, s3, oh, arr, terms, work,
 ):
-    copies = fetch(
-        ((vel_hbm, vel_ref), (zn_hbm, zn_ref), (jac_hbm, jac_ref), (mass_hbm, mass_ref),
-         (inv_hbm, inv_ref), (en_hbm, en_ref), (tables_hbm, tables)), sems,
-    )
     msgs = (m0, m1, m2, m3)
     lane = lax.broadcasted_iota(jnp.int32, (1, WIDE), 1)
     oh[...] = jnp.zeros(oh.shape, F32)
@@ -365,12 +378,6 @@
                 piece : piece + 1, MSG : MSG + n
             ]
     arr[36:48, :] = jnp.zeros((12, MSG), F32)
-    copies[0].wait()
-    nodes_in(vel_ref, vel_out)
-    copies[1].wait()
-    gather_zones(zn_ref, vel_out, words, vz)
-    for copy in copies[2:]:
-        copy.wait()
     for ref, out, at in (
         (jac_ref, jac_out, AT_JAC), (mass_ref, mass_out, AT_MASS),
         (inv_ref, inv_out, AT_INV), (en_ref, en_out, AT_EN),
@@ -385,7 +392,7 @@
     rhs_e = force(vz, en_out[...], jac_out, mass, terms, work, tables)
     terms[3] = down(entry(tables, FORCE_AT, "limit"), mass)
     ehalf_out[...] = en_out[...] + 0.5 * STEP_SIZE * energy_change(rhs_e, inv_out, tables)
-    y_out[...] = scatter_zones(zn_ref, terms, 4)
+    y_out[...] = scatter_zones(zn_ref, lanes, terms, 4)
     send_shared(lists_ref, y_out, (s0, s1, s2, s3), 4)
 
 
@@ -409,37 +416,37 @@
     return r, d, a_ref[...] + d
 
 
-def apply_mass(zn_ref, mass_ref, tables, d_ref, y_out, zone, terms, words):
+def apply_mass(zn_ref, lanes, mass_ref, tables, d_ref, y_out, zone, terms, words):
     gather_zones(zn_ref, d_ref, words, zone)
     mass = mass_ref[...]
     for c in range(3):
         at_points = up(entry(tables, MASS_AT, "up"), zone[c])
         terms[c] = down(entry(tables, MASS_AT, "down"), at_points * mass)
-    y_out[...] = scatter_zones(zn_ref, terms, 3)
+    y_out[...] = scatter_zones(zn_ref, lanes, terms, 3)
 
 
 def start_kernel(g0, g1, g2, g3, y_ref, *refs, first):
     if first:
-        lists, zn, mass, tables = refs[:4]
-        ib, r_out, d_out, y_out, s0, s1, s2, s3, *scratch = refs[4:]
+        lists, zn, lanes, mass, tables = refs[:5]
+        ib, r_out, d_out, y_out, s0, s1, s2, s3, *scratch = refs[5:]
         y = y_ref[...] + received(lists, (g0, g1, g2, g3), 4)
         pad = lax.broadcasted_iota(jnp.int32, (ROWS, WIDE), 0) == 31
         inv_bound = 1.0 / jnp.where(pad, 1.0, y[96:])
         ib[...] = inv_bound
         r = y[:96]
     else:
-        ib, lists, zn, mass, tables = refs[:5]
-        r_out, d_out, y_out, s0, s1, s2, s3, *scratch = refs[5:]
+        ib, lists, zn, lanes, mass, tables = refs[:6]
+        r_out, d_out, y_out, s0, s1, s2, s3, *scratch = refs[6:]
         r = y_ref[...] + received(lists, (g0, g1, g2, g3), 3)
         inv_bound = ib[...]
     r_out[...] = r
     d_out[...] = r * three(inv_bound) * (1.0 / THETA)
-    apply_mass(zn, mass, tables, d_out, y_out, *scratch)
+    apply_mass(zn, lanes, mass, tables, d_out, y_out, *scratch)
     send_shared(lists, y_out, (s0, s1, s2, s3), 3)
 
 
 def sweep_kernel(
-    g0, g1, g2, g3, y_ref, r_ref, d_ref, a_ref, ib_ref, lists, zn, mass, tables,
+    g0, g1, g2, g3, y_ref, r_ref, d_ref, a_ref, ib_ref, lists, zn, lanes, mass, tables,
     r_out, d_out, a_out, y_out, s0, s1, s2, s3, *scratch, step,
 ):
     y = y_ref[...] + received(lists, (g0, g1, g2, g3), 3)
@@ -447,12 +454,12 @@
     r_out[...] = r
     d_out[...] = d
     a_out[...] = a
-    apply_mass(zn, mass, tables, d_out, y_out, *scratch)
+    apply_mass(zn, lanes, mass, tables, d_out, y_out, *scratch)
     send_shared(lists, y_out, (s0, s1, s2, s3), 3)
 
 
 def second_kernel(
-    g0, g1, g2, g3, y_ref, r_ref, d_ref, a_ref, ib_ref, lists, zn, mass, jac, inv, en, ehalf, vel, tables,
+    g0, g1, g2, g3, y_ref, r_ref, d_ref, a_ref, ib_ref, lists, zn, lanes, mass, jac, inv, en, ehalf, vel, tables,
     en_out, y_out, s0, s1, s2, s3, vhalf, vz, terms, work, words,
 ):
     y = y_ref[...] + received(lists, (g0, g1, g2, g3), 3)
@@ -460,7 +467,7 @@
     vhalf[...] = vel[...] + 0.5 * STEP_SIZE * a
     gather_zones(zn, vhalf, words, vz)
     rhs_e = force(vz, ehalf[...], jac, mass[...], terms, work, tables)
-    y_out[...] = scatter_zones(zn, terms, 3)
+    y_out[...] = scatter_zones(zn, lanes, terms, 3)
     send_shared(lists, y_out, (s0, s1, s2, s3), 3)
     en_out[...] = en[...] + STEP_SIZE * energy_change(rhs_e, inv, tables)
 
@@ -476,7 +483,7 @@
 
 VM = pl.BlockSpec(memory_space=pltpu.VMEM)
 SM = pl.BlockSpec(memory_space=pltpu.SMEM)
-HB = pl.BlockSpec(memory_space=pl.ANY)
+HB = pl.BlockSpec(memory_space=pltpu.HBM)
 
 
 def shape_of(s):
@@ -523,24 +530,27 @@
     words = ints(2 * ROWS, WIDE)
     *msgs, lists = call(
         pack_kernel, (send_rows, shared_nodes, jac, mass, inv, energy), [msg] * 4 + [ints(8, HALF)],
-        [(40, WIDE)] + fields, [SM, VM] + [HB] * 4, copies=4, name="pack",
+        [(40, WIDE)] + fields, [SM, VM] + [HB] * 4, limit=58, copies=4, name="pack",
     )
     came = []
     for k, m in enumerate(msgs):
         came.append(lax.ppermute(m, AXES, paired(k % 2, devices, 1 + k // 2)))
-    jac, mass, inv, en, vel, ehalf, y, *sends = call(
+    vel, vz, lanes = call(
+        prep_kernel, (velocity, zone_nodes, lists, arrive_rows, energy, force_tables),
+        [node, zone, half(NPZ, WIDE, WIDE)], [words, (WIDE, HALF)], [VM, VM, VM, SM, VM, VM], name="prep",
+    )
+    jac, mass, inv, en, ehalf, y, *sends = call(
         first_kernel,
-        (arrive_rows, *came, lists, jac, mass, inv, energy, velocity, zone_nodes, force_tables),
-        fields + [node, (LD, WIDE), (128, WIDE)] + send,
-        [(48, WIDE), (48, MSG), zone, (4, NPZ, WIDE), (QP, WIDE), words] + fields
-        + [velocity.shape, ints(NPZ, WIDE), half(*FORCE_TABLES.shape)],
-        [SM] + [VM] * 5 + [HB] * 7, limit=24, copies=7, name="force_one",
+        (arrive_rows, *came, lists, jac, mass, inv, energy, zone_nodes, force_tables, vz, lanes),
+        fields + [(LD, WIDE), (128, WIDE)] + send,
+        [(48, WIDE), (48, MSG), (4, NPZ, WIDE), (QP, WIDE)],
+        [SM] + [VM] * 13, name="force_one",
     )
     scratch = [zone, zone, words]
     for section in range(2):
         got = exchange(sends)
         outs = [node, node, node] + send
-        tail = (lists, zone_nodes, mass, mass_tables)
+        tail = (lists, zone_nodes, lanes, mass, mass_tables)
         if section == 0:
             ib, r, d, y, *sends = call(
                 functools.partial(start_kernel, first=True), (*got, y, *tail),
@@ -562,7 +572,7 @@
         if section == 0:
             energy_next, y, *sends = call(
                 second_kernel,
-                (*got, y, r, d, a, ib, lists, zone_nodes, mass, jac, inv, en, ehalf, vel, force_tables),
+                (*got, y, r, d, a, ib, lists, zone_nodes, lanes, mass, jac, inv, en, ehalf, vel, force_tables),
                 [(LD, WIDE), node] + send, [node, zone, zone, (QP, WIDE), words], limit=24,
                 name="force_two",
             )

time: 179 us -> 168 us (0.939)
  starting transfers between devices: 68.5 us -> 60.5 us
  Pallas kernels: 78.6 us -> 75.2 us
  local copies, waits for them, and re-layouts: 7.98 us -> 4.79 us
  waiting for transfers between devices: 22.4 us -> 25.2 us
    ppermute x8, starting transfers between devices: 26.2 us -> 18.7 us  [exchange(): lax.ppermute(sends[3], 'split', paired(1, n_split))]
    ppermute x8, waiting for transfers between devices: 3.47 us -> 8.7 us  [exchange(): lax.ppermute(sends[1], 'curve', paired(1, n_curve))]
    ppermute x4, waiting for transfers between devices: 4.01 us -> 0.01 us  [per_device(): came.append(lax.ppermute(m, AXES, paired(k % 2, devices, 1 + k // 2)))]
    pallas_call x10 -> x11, Pallas kernels: 78.6 us -> 75.2 us  [call(): pl.pallas_call(kernel, out_shape=[shape_of(s) for s in outs], in_specs=sp...]
    unnamed x32 -> x24, local copies, waits for them, and re-layouts: 7.98 us -> 4.79 us
  transfers between devices with their start and end apart: 36 -> 36, of which waited for: 18 -> 20; matrix products, arithmetic and copies ran while one was open for 0% -> 0% of each run, Pallas kernels for 0% -> 5%
where the time goes in v3:
time: 168 us; the launch traced here: 167 us
  Pallas kernels  75.2 us (45%)
  starting transfers between devices  60.5 us (36%)
  waiting for transfers between devices  25.2 us (15%)
  local copies, waits for them, and re-layouts  4.79 us (3%)
    pallas_call x11, Pallas kernels, call(): pl.pallas_call(kernel, out_shape=[shape_of(s) for s in outs], in_specs=sp...  75.2 us
    ppermute x8, starting transfers between devices, exchange(): lax.ppermute(sends[1], 'curve', paired(1, n_curve))  27 us
    ppermute x8, starting transfers between devices, exchange(): lax.ppermute(sends[3], 'split', paired(1, n_split))  18.7 us
    ppermute x8, waiting for transfers between devices, exchange(): lax.ppermute(sends[3], 'split', paired(1, n_split))  14.3 us
    ppermute x4, starting transfers between devices, per_device(): came.append(lax.ppermute(m, AXES, paired(k % 2, devices, 1 + k // 2)))  12.4 us
    ppermute x8, waiting for transfers between devices, exchange(): lax.ppermute(sends[1], 'curve', paired(1, n_curve))  8.7 us
    unnamed x24, local copies, waits for them, and re-layouts  4.79 us
  transfers between devices with their start and end apart: 36, of which 20 were waited for; matrix products, arithmetic and copies ran while one was open for 0% of the time, Pallas kernels for 5%

profile of v3, /device:TPU:26, one launch (start us, length us, event | category | flops | bytes accessed | tf_op | source)
XLA Modules:
  0.0 166.7 jit_solution(8327352203158711328)
XLA Ops:
  0.7 4.8 %pack.1 = (f32[8,3712]{1,0:T(8,128)}, f32[8,3712]{1,0:T(8,128)}, f32[8,3712]{1,0:T(8,128)}, f32[8,3712]{1,0:T(8,128)}, s32[8,128]{1,0:T(8,128)}) custom-call(s32[1,36]{1,0:T(1,128)} %send_ref.1, s32[1,4,256]{2,1,0:T(4,128)} %shared_ref.1, f32[1944,256]{1,0:T(8,128)} %jac_ref.1, f32[216,256]{1,0:T(8,128)} %mass_ref.1, f32[729,256]{1,0:T(8,128)} %inv_ref.1, ...), custom_call_target="tpu_custom_call" | custom-call | tf_op jit(solution)/shard_map/pack/pallas_call | solution.py:495
  6.1 4.0 %collective-permute-start.1 = (f32[8,3712]{1,0:T(8,128)}, f32[8,3712]{1,0:T(8,128)S(1)}, u32[]{:S(2)}, u32[]{:S(2)}) collective-permute-start(f32[8,3712]{1,0:T(8,128)} %get-tuple-element.74), channel_id=1, source_target_pairs={{1,2},{2,1},{3,4},{4,3},{5,6},{6,5},{7,8},{8,7},{9,10},{10,9},{11,... | collective-permute-start | bytes 356360 | tf_op jit(solution)/shard_map/ppermute | solution.py:537
  10.8 7.1 %collective-permute-start.3 = (f32[8,3712]{1,0:T(8,128)}, f32[8,3712]{1,0:T(8,128)S(1)}, u32[]{:S(2)}, u32[]{:S(2)}) collective-permute-start(f32[8,3712]{1,0:T(8,128)} %get-tuple-element.76), channel_id=1, source_target_pairs={{2,4},{4,2},{3,5},{5,3},{6,8},{8,6},{7,9},{9,7},{10,12},{12,10},{1... | collective-permute-start | bytes 356360 | tf_op jit(solution)/shard_map/ppermute | solution.py:537
  21.7 8.1 %prep.1 = (f32[96,256]{1,0:T(8,128)S(1)}, f32[3,64,256]{2,1,0:T(8,128)S(1)}, bf16[64,256,256]{2,1,0:T(8,128)(2,1)S(1)}) custom-call(f32[3,7936]{1,0:T(4,128)S(1)} %copy-done.10, s32[64,256]{1,0:T(8,128)S(1)} %copy-done.3, s32[8,128]{1,0:T(8,128)S(1)} %copy-done.7, s32[1,36]{1,0:T(1,128)S(1)} %copy-done.11, f32[27,256]{1,0:T(8,128)S(1)} %copy-done.9, ...), custom_call_target="tpu_custom_call" | custom-call | tf_op jit(solution)/shard_map/prep/pallas_call | solution.py:495
  30.8 7.2 %force_one.1 = (f32[1944,256]{1,0:T(8,128)S(1)}, f32[216,256]{1,0:T(8,128)S(1)}, f32[729,256]{1,0:T(8,128)S(1)}, f32[27,256]{1,0:T(8,128)S(1)}, f32[27,256]{1,0:...) custom-call(s32[1,36]{1,0:T(1,128)S(1)} %copy-done.11, ...), custom_call_target="tpu_custom_call" | custom-call | tf_op jit(solution)/shard_map/force_one/pallas_call | solution.py:495
  38.1 3.6 %collective-permute-start.5 = (f32[8,128]{1,0:T(8,128)S(1)}, f32[8,128]{1,0:T(8,128)S(1)}, u32[]{:S(2)}, u32[]{:S(2)}) collective-permute-start(f32[8,128]{1,0:T(8,128)S(1)} %get-tuple-element.81), channel_id=1, source_target_pairs={{4,8},{8,4},{12,16},{16,12},{20,24},{24,20},{28,32},{32,28},{36,40... | collective-permute-start | bytes 12296 | tf_op jit(solution)/shard_map/ppermute | solution.py:515
  42.9 2.4 %collective-permute-start.7 = (f32[8,128]{1,0:T(8,128)S(1)}, f32[8,128]{1,0:T(8,128)S(1)}, u32[]{:S(2)}, u32[]{:S(2)}) collective-permute-start(f32[8,128]{1,0:T(8,128)S(1)} %get-tuple-element.83), channel_id=1, source_target_pairs={{1,2},{2,1},{5,6},{6,5},{9,10},{10,9},{13,14},{14,13},{17,18},{18,... | collective-permute-start | bytes 12296 | tf_op jit(solution)/shard_map/ppermute | solution.py:517
  45.4 3.0 %collective-permute-done.7.g3 = f32[8,128]{1,0:T(8,128)S(1)} collective-permute-done((f32[8,128]{1,0:T(8,128)S(1)}, f32[8,128]{1,0:T(8,128)S(1)}, u32[]{:S(2)}, u32[]{:S(2)}) %collective-permute-start.7) | collective-permute-done | bytes 4128 | tf_op jit(solution)/shard_map/ppermute | solution.py:517
  48.4 7.5 %mass_start.1 = (f32[32,256]{1,0:T(8,128)S(1)}, f32[96,256]{1,0:T(8,128)S(1)}, f32[96,256]{1,0:T(8,128)S(1)}, f32[96,256]{1,0:T(8,128)S(1)}, f32[8,128]{1,0:T(8,...) custom-call(f32[8,128]{1,0:T(8,128)S(1)} %collective-permute-done.4.g0, ...), custom_call_target="tpu_custom_call" | custom-call | tf_op jit(solution)/shard_map/mass_start/pallas_call | solution.py:495
  56.0 3.8 %collective-permute-start.9 = (f32[8,128]{1,0:T(8,128)S(1)}, f32[8,128]{1,0:T(8,128)S(1)}, u32[]{:S(2)}, u32[]{:S(2)}) collective-permute-start(f32[8,128]{1,0:T(8,128)S(1)} %get-tuple-element.87), channel_id=1, source_target_pairs={{4,8},{8,4},{12,16},{16,12},{20,24},{24,20},{28,32},{32,28},{36,40... | collective-permute-start | bytes 12296 | tf_op jit(solution)/shard_map/ppermute | solution.py:515
  59.9 2.2 %collective-permute-start.11 = (f32[8,128]{1,0:T(8,128)S(1)}, f32[8,128]{1,0:T(8,128)S(1)}, u32[]{:S(2)}, u32[]{:S(2)}) collective-permute-start(f32[8,128]{1,0:T(8,128)S(1)} %get-tuple-element.89), channel_id=1, source_target_pairs={{1,2},{2,1},{5,6},{6,5},{9,10},{10,9},{13,14},{14,13},{17,18},{18,... | collective-permute-start | bytes 12296 | tf_op jit(solution)/shard_map/ppermute | solution.py:517
  63.5 1.9 %collective-permute-done.11.g3 = f32[8,128]{1,0:T(8,128)S(1)} collective-permute-done((f32[8,128]{1,0:T(8,128)S(1)}, f32[8,128]{1,0:T(8,128)S(1)}, u32[]{:S(2)}, u32[]{:S(2)}) %collective-permute-start.11) | collective-permute-done | bytes 4128 | tf_op jit(solution)/shard_map/ppermute | solution.py:517
  65.4 7.5 %mass_sweep.4 = (f32[96,256]{1,0:T(8,128)S(1)}, f32[96,256]{1,0:T(8,128)S(1)}, f32[96,256]{1,0:T(8,128)S(1)}, f32[96,256]{1,0:T(8,128)S(1)}, f32[8,128]{1,0:T(8,...) custom-call(f32[8,128]{1,0:T(8,128)S(1)} %collective-permute-done.8.g0, ...), custom_call_target="tpu_custom_call" | custom-call | tf_op jit(solution)/shard_map/mass_sweep/pallas_call | solution.py:495
  73.1 2.7 %collective-permute-start.13 = (f32[8,128]{1,0:T(8,128)S(1)}, f32[8,128]{1,0:T(8,128)S(1)}, u32[]{:S(2)}, u32[]{:S(2)}) collective-permute-start(f32[8,128]{1,0:T(8,128)S(1)} %get-tuple-element.95), channel_id=1, source_target_pairs={{4,8},{8,4},{12,16},{16,12},{20,24},{24,20},{28,32},{32,28},{36,40... | collective-permute-start | bytes 12296 | tf_op jit(solution)/shard_map/ppermute | solution.py:515
  75.8 2.4 %collective-permute-start.15 = (f32[8,128]{1,0:T(8,128)S(1)}, f32[8,128]{1,0:T(8,128)S(1)}, u32[]{:S(2)}, u32[]{:S(2)}) collective-permute-start(f32[8,128]{1,0:T(8,128)S(1)} %get-tuple-element.97), channel_id=1, source_target_pairs={{1,2},{2,1},{5,6},{6,5},{9,10},{10,9},{13,14},{14,13},{17,18},{18,... | collective-permute-start | bytes 12296 | tf_op jit(solution)/shard_map/ppermute | solution.py:517
  81.3 7.5 %mass_sweep.5 = (f32[96,256]{1,0:T(8,128)S(1)}, f32[96,256]{1,0:T(8,128)S(1)}, f32[96,256]{1,0:T(8,128)S(1)}, f32[96,256]{1,0:T(8,128)S(1)}, f32[8,128]{1,0:T(8,...) custom-call(f32[8,128]{1,0:T(8,128)S(1)} %collective-permute-done.12.g0, ...), custom_call_target="tpu_custom_call" | custom-call | tf_op jit(solution)/shard_map/mass_sweep/pallas_call | solution.py:495
  89.0 3.9 %collective-permute-start.17 = (f32[8,128]{1,0:T(8,128)S(1)}, f32[8,128]{1,0:T(8,128)S(1)}, u32[]{:S(2)}, u32[]{:S(2)}) collective-permute-start(f32[8,128]{1,0:T(8,128)S(1)} %get-tuple-element.103), channel_id=1, source_target_pairs={{4,8},{8,4},{12,16},{16,12},{20,24},{24,20},{28,32},{32,28},{36,40... | collective-permute-start | bytes 12296 | tf_op jit(solution)/shard_map/ppermute | solution.py:515
  92.9 2.4 %collective-permute-start.19 = (f32[8,128]{1,0:T(8,128)S(1)}, f32[8,128]{1,0:T(8,128)S(1)}, u32[]{:S(2)}, u32[]{:S(2)}) collective-permute-start(f32[8,128]{1,0:T(8,128)S(1)} %get-tuple-element.105), channel_id=1, source_target_pairs={{1,2},{2,1},{5,6},{6,5},{9,10},{10,9},{13,14},{14,13},{17,18},{18,... | collective-permute-start | bytes 12296 | tf_op jit(solution)/shard_map/ppermute | solution.py:517
  96.5 1.9 %collective-permute-done.19.g3 = f32[8,128]{1,0:T(8,128)S(1)} collective-permute-done((f32[8,128]{1,0:T(8,128)S(1)}, f32[8,128]{1,0:T(8,128)S(1)}, u32[]{:S(2)}, u32[]{:S(2)}) %collective-permute-start.19) | collective-permute-done | bytes 4128 | tf_op jit(solution)/shard_map/ppermute | solution.py:517
  98.4 8.9 %force_two.1 = (f32[27,256]{1,0:T(8,128)}, f32[96,256]{1,0:T(8,128)S(1)}, f32[8,128]{1,0:T(8,128)S(1)}, f32[8,128]{1,0:T(8,128)S(1)}, f32[8,128]{1,0:T(8,128)S(1)}, /*index=5*/f32[8,128]{1,0:T(8,128)S(1)}) custom-call(f32[8,128]{1,0:T(8,128)S(1)} %collective-permute-done.16.g0, f32[8,128]{1,0:T(8,128)S(1)} %collective-permute-done.17.g1, ...), custom_call_target="tpu_custom_call" | custom-call | tf_op jit(solution)/shard_map/force_two/pallas_call | solution.py:495
  107.4 2.6 %collective-permute-start.21 = (f32[8,128]{1,0:T(8,128)S(1)}, f32[8,128]{1,0:T(8,128)S(1)}, u32[]{:S(2)}, u32[]{:S(2)}) collective-permute-start(f32[8,128]{1,0:T(8,128)S(1)} %get-tuple-element.116), channel_id=1, source_target_pairs={{4,8},{8,4},{12,16},{16,12},{20,24},{24,20},{28,32},{32,28},{36,40... | collective-permute-start | bytes 12296 | tf_op jit(solution)/shard_map/ppermute | solution.py:515
  110.1 2.4 %collective-permute-start.23 = (f32[8,128]{1,0:T(8,128)S(1)}, f32[8,128]{1,0:T(8,128)S(1)}, u32[]{:S(2)}, u32[]{:S(2)}) collective-permute-start(f32[8,128]{1,0:T(8,128)S(1)} %get-tuple-element.118), channel_id=1, source_target_pairs={{1,2},{2,1},{5,6},{6,5},{9,10},{10,9},{13,14},{14,13},{17,18},{18,... | collective-permute-start | bytes 12296 | tf_op jit(solution)/shard_map/ppermute | solution.py:517
  115.6 7.5 %mass_start_two.1 = (f32[96,256]{1,0:T(8,128)S(1)}, f32[96,256]{1,0:T(8,128)S(1)}, f32[96,256]{1,0:T(8,128)S(1)}, f32[8,128]{1,0:T(8,128)S(1)}, f32[8,128]{1,0:T...) custom-call(f32[8,128]{1,0:T(8,128)S(1)} %collective-permute-done.20.g0, ...), custom_call_target="tpu_custom_call" | custom-call | tf_op jit(solution)/shard_map/mass_start_two/pallas_call | solution.py:495
  123.2 3.9 %collective-permute-start.25 = (f32[8,128]{1,0:T(8,128)S(1)}, f32[8,128]{1,0:T(8,128)S(1)}, u32[]{:S(2)}, u32[]{:S(2)}) collective-permute-start(f32[8,128]{1,0:T(8,128)S(1)} %get-tuple-element.121), channel_id=1, source_target_pairs={{4,8},{8,4},{12,16},{16,12},{20,24},{24,20},{28,32},{32,28},{36,40... | collective-permute-start | bytes 12296 | tf_op jit(solution)/shard_map/ppermute | solution.py:515
  127.2 2.2 %collective-permute-start.27 = (f32[8,128]{1,0:T(8,128)S(1)}, f32[8,128]{1,0:T(8,128)S(1)}, u32[]{:S(2)}, u32[]{:S(2)}) collective-permute-start(f32[8,128]{1,0:T(8,128)S(1)} %get-tuple-element.123), channel_id=1, source_target_pairs={{1,2},{2,1},{5,6},{6,5},{9,10},{10,9},{13,14},{14,13},{17,18},{18,... | collective-permute-start | bytes 12296 | tf_op jit(solution)/shard_map/ppermute | solution.py:517
  130.8 1.9 %collective-permute-done.27.g3 = f32[8,128]{1,0:T(8,128)S(1)} collective-permute-done((f32[8,128]{1,0:T(8,128)S(1)}, f32[8,128]{1,0:T(8,128)S(1)}, u32[]{:S(2)}, u32[]{:S(2)}) %collective-permute-start.27) | collective-permute-done | bytes 4128 | tf_op jit(solution)/shard_map/ppermute | solution.py:517
  132.7 7.5 %mass_sweep.6 = (f32[96,256]{1,0:T(8,128)S(1)}, f32[96,256]{1,0:T(8,128)S(1)}, f32[96,256]{1,0:T(8,128)S(1)}, f32[96,256]{1,0:T(8,128)S(1)}, f32[8,128]{1,0:T(8,...) custom-call(f32[8,128]{1,0:T(8,128)S(1)} %collective-permute-done.24.g0, ...), custom_call_target="tpu_custom_call" | custom-call | tf_op jit(solution)/shard_map/mass_sweep/pallas_call | solution.py:495
  140.3 2.7 %collective-permute-start.29 = (f32[8,128]{1,0:T(8,128)S(1)}, f32[8,128]{1,0:T(8,128)S(1)}, u32[]{:S(2)}, u32[]{:S(2)}) collective-permute-start(f32[8,128]{1,0:T(8,128)S(1)} %get-tuple-element.128), channel_id=1, source_target_pairs={{4,8},{8,4},{12,16},{16,12},{20,24},{24,20},{28,32},{32,28},{36,40... | collective-permute-start | bytes 12296 | tf_op jit(solution)/shard_map/ppermute | solution.py:515
  143.1 2.4 %collective-permute-start.31 = (f32[8,128]{1,0:T(8,128)S(1)}, f32[8,128]{1,0:T(8,128)S(1)}, u32[]{:S(2)}, u32[]{:S(2)}) collective-permute-start(f32[8,128]{1,0:T(8,128)S(1)} %get-tuple-element.130), channel_id=1, source_target_pairs={{1,2},{2,1},{5,6},{6,5},{9,10},{10,9},{13,14},{14,13},{17,18},{18,... | collective-permute-start | bytes 12296 | tf_op jit(solution)/shard_map/ppermute | solution.py:517
  148.6 7.5 %mass_sweep.7 = (f32[96,256]{1,0:T(8,128)S(1)}, f32[96,256]{1,0:T(8,128)S(1)}, f32[96,256]{1,0:T(8,128)S(1)}, f32[96,256]{1,0:T(8,128)S(1)}, f32[8,128]{1,0:T(8,...) custom-call(f32[8,128]{1,0:T(8,128)S(1)} %collective-permute-done.28.g0, ...), custom_call_target="tpu_custom_call" | custom-call | tf_op jit(solution)/shard_map/mass_sweep/pallas_call | solution.py:495
  156.2 3.9 %collective-permute-start.33 = (f32[8,128]{1,0:T(8,128)S(1)}, f32[8,128]{1,0:T(8,128)S(1)}, u32[]{:S(2)}, u32[]{:S(2)}) collective-permute-start(f32[8,128]{1,0:T(8,128)S(1)} %get-tuple-element.136), channel_id=1, source_target_pairs={{4,8},{8,4},{12,16},{16,12},{20,24},{24,20},{28,32},{32,28},{36,40... | collective-permute-start | bytes 12296 | tf_op jit(solution)/shard_map/ppermute | solution.py:515
  160.2 2.2 %collective-permute-start.35 = (f32[8,128]{1,0:T(8,128)S(1)}, f32[8,128]{1,0:T(8,128)S(1)}, u32[]{:S(2)}, u32[]{:S(2)}) collective-permute-start(f32[8,128]{1,0:T(8,128)S(1)} %get-tuple-element.138), channel_id=1, source_target_pairs={{1,2},{2,1},{5,6},{6,5},{9,10},{10,9},{13,14},{14,13},{17,18},{18,... | collective-permute-start | bytes 12296 | tf_op jit(solution)/shard_map/ppermute | solution.py:517
  (75 shorter events, 25.9 us)
Async XLA Ops:
  5.4 24.4 %collective-permute-start = (f32[8,3712]{1,0:T(8,128)}, f32[8,3712]{1,0:T(8,128)S(1)}, u32[]{:S(2)}, u32[]{:S(2)}) collective-permute-start(f32[8,3712]{1,0:T(8,128)} %get-tuple-element.73), channel_id=1, source_target_pairs={{0,1},{1,0},{2,3},{3,2},{4,5},{5,4},{6,7},{7,6},{8,9},{9,8},{10,11... | collective-permute-start | bytes 356360 | tf_op jit(solution)/shard_map/ppermute | solution.py:537
  6.1 23.8 %collective-permute-start.1 = (f32[8,3712]{1,0:T(8,128)}, f32[8,3712]{1,0:T(8,128)S(1)}, u32[]{:S(2)}, u32[]{:S(2)}) collective-permute-start(f32[8,3712]{1,0:T(8,128)} %get-tuple-element.74), channel_id=1, source_target_pairs={{1,2},{2,1},{3,4},{4,3},{5,6},{6,5},{7,8},{8,7},{9,10},{10,9},{11,... | collective-permute-start | bytes 356360 | tf_op jit(solution)/shard_map/ppermute | solution.py:537
  10.1 19.7 %collective-permute-start.2 = (f32[8,3712]{1,0:T(8,128)}, f32[8,3712]{1,0:T(8,128)S(1)}, u32[]{:S(2)}, u32[]{:S(2)}) collective-permute-start(f32[8,3712]{1,0:T(8,128)} %get-tuple-element.75), channel_id=1, source_target_pairs={{0,2},{2,0},{1,3},{3,1},{4,6},{6,4},{5,7},{7,5},{8,10},{10,8},{9,1... | collective-permute-start | bytes 356360 | tf_op jit(solution)/shard_map/ppermute | solution.py:537
  10.8 19.1 %collective-permute-start.3 = (f32[8,3712]{1,0:T(8,128)}, f32[8,3712]{1,0:T(8,128)S(1)}, u32[]{:S(2)}, u32[]{:S(2)}) collective-permute-start(f32[8,3712]{1,0:T(8,128)} %get-tuple-element.76), channel_id=1, source_target_pairs={{2,4},{4,2},{3,5},{5,3},{6,8},{8,6},{7,9},{9,7},{10,12},{12,10},{1... | collective-permute-start | bytes 356360 | tf_op jit(solution)/shard_map/ppermute | solution.py:537
  38.0 7.2 %collective-permute-start.4 = (f32[8,128]{1,0:T(8,128)S(1)}, f32[8,128]{1,0:T(8,128)S(1)}, u32[]{:S(2)}, u32[]{:S(2)}) collective-permute-start(f32[8,128]{1,0:T(8,128)S(1)} %get-tuple-element.80), channel_id=1, source_target_pairs={{0,4},{4,0},{8,12},{12,8},{16,20},{20,16},{24,28},{28,24},{32,36},... | collective-permute-start | bytes 12296 | tf_op jit(solution)/shard_map/ppermute | solution.py:514
  38.1 7.2 %collective-permute-start.5 = (f32[8,128]{1,0:T(8,128)S(1)}, f32[8,128]{1,0:T(8,128)S(1)}, u32[]{:S(2)}, u32[]{:S(2)}) collective-permute-start(f32[8,128]{1,0:T(8,128)S(1)} %get-tuple-element.81), channel_id=1, source_target_pairs={{4,8},{8,4},{12,16},{16,12},{20,24},{24,20},{28,32},{32,28},{36,40... | collective-permute-start | bytes 12296 | tf_op jit(solution)/shard_map/ppermute | solution.py:515
  41.7 3.7 %collective-permute-start.6 = (f32[8,128]{1,0:T(8,128)S(1)}, f32[8,128]{1,0:T(8,128)S(1)}, u32[]{:S(2)}, u32[]{:S(2)}) collective-permute-start(f32[8,128]{1,0:T(8,128)S(1)} %get-tuple-element.82), channel_id=1, source_target_pairs={{0,1},{1,0},{2,3},{3,2},{4,5},{5,4},{6,7},{7,6},{8,9},{9,8},{10,11... | collective-permute-start | bytes 12296 | tf_op jit(solution)/shard_map/ppermute | solution.py:516
  42.9 5.5 %collective-permute-start.7 = (f32[8,128]{1,0:T(8,128)S(1)}, f32[8,128]{1,0:T(8,128)S(1)}, u32[]{:S(2)}, u32[]{:S(2)}) collective-permute-start(f32[8,128]{1,0:T(8,128)S(1)} %get-tuple-element.83), channel_id=1, source_target_pairs={{1,2},{2,1},{5,6},{6,5},{9,10},{10,9},{13,14},{14,13},{17,18},{18,... | collective-permute-start | bytes 12296 | tf_op jit(solution)/shard_map/ppermute | solution.py:517
  55.9 6.3 %collective-permute-start.8 = (f32[8,128]{1,0:T(8,128)S(1)}, f32[8,128]{1,0:T(8,128)S(1)}, u32[]{:S(2)}, u32[]{:S(2)}) collective-permute-start(f32[8,128]{1,0:T(8,128)S(1)} %get-tuple-element.86), channel_id=1, source_target_pairs={{0,4},{4,0},{8,12},{12,8},{16,20},{20,16},{24,28},{28,24},{32,36},... | collective-permute-start | bytes 12296 | tf_op jit(solution)/shard_map/ppermute | solution.py:514
  56.0 7.0 %collective-permute-start.9 = (f32[8,128]{1,0:T(8,128)S(1)}, f32[8,128]{1,0:T(8,128)S(1)}, u32[]{:S(2)}, u32[]{:S(2)}) collective-permute-start(f32[8,128]{1,0:T(8,128)S(1)} %get-tuple-element.87), channel_id=1, source_target_pairs={{4,8},{8,4},{12,16},{16,12},{20,24},{24,20},{28,32},{32,28},{36,40... | collective-permute-start | bytes 12296 | tf_op jit(solution)/shard_map/ppermute | solution.py:515
  59.9 5.5 %collective-permute-start.11 = (f32[8,128]{1,0:T(8,128)S(1)}, f32[8,128]{1,0:T(8,128)S(1)}, u32[]{:S(2)}, u32[]{:S(2)}) collective-permute-start(f32[8,128]{1,0:T(8,128)S(1)} %get-tuple-element.89), channel_id=1, source_target_pairs={{1,2},{2,1},{5,6},{6,5},{9,10},{10,9},{13,14},{14,13},{17,18},{18,... | collective-permute-start | bytes 12296 | tf_op jit(solution)/shard_map/ppermute | solution.py:517
  73.0 5.3 %collective-permute-start.12 = (f32[8,128]{1,0:T(8,128)S(1)}, f32[8,128]{1,0:T(8,128)S(1)}, u32[]{:S(2)}, u32[]{:S(2)}) collective-permute-start(f32[8,128]{1,0:T(8,128)S(1)} %get-tuple-element.94), channel_id=1, source_target_pairs={{0,4},{4,0},{8,12},{12,8},{16,20},{20,16},{24,28},{28,24},{32,36},... | collective-permute-start | bytes 12296 | tf_op jit(solution)/shard_map/ppermute | solution.py:514
  73.1 7.0 %collective-permute-start.13 = (f32[8,128]{1,0:T(8,128)S(1)}, f32[8,128]{1,0:T(8,128)S(1)}, u32[]{:S(2)}, u32[]{:S(2)}) collective-permute-start(f32[8,128]{1,0:T(8,128)S(1)} %get-tuple-element.95), channel_id=1, source_target_pairs={{4,8},{8,4},{12,16},{16,12},{20,24},{24,20},{28,32},{32,28},{36,40... | collective-permute-start | bytes 12296 | tf_op jit(solution)/shard_map/ppermute | solution.py:515
  75.7 4.4 %collective-permute-start.14 = (f32[8,128]{1,0:T(8,128)S(1)}, f32[8,128]{1,0:T(8,128)S(1)}, u32[]{:S(2)}, u32[]{:S(2)}) collective-permute-start(f32[8,128]{1,0:T(8,128)S(1)} %get-tuple-element.96), channel_id=1, source_target_pairs={{0,1},{1,0},{2,3},{3,2},{4,5},{5,4},{6,7},{7,6},{8,9},{9,8},{10,11... | collective-permute-start | bytes 12296 | tf_op jit(solution)/shard_map/ppermute | solution.py:516
  75.8 5.5 %collective-permute-start.15 = (f32[8,128]{1,0:T(8,128)S(1)}, f32[8,128]{1,0:T(8,128)S(1)}, u32[]{:S(2)}, u32[]{:S(2)}) collective-permute-start(f32[8,128]{1,0:T(8,128)S(1)} %get-tuple-element.97), channel_id=1, source_target_pairs={{1,2},{2,1},{5,6},{6,5},{9,10},{10,9},{13,14},{14,13},{17,18},{18,... | collective-permute-start | bytes 12296 | tf_op jit(solution)/shard_map/ppermute | solution.py:517
  88.9 6.5 %collective-permute-start.16 = (f32[8,128]{1,0:T(8,128)S(1)}, f32[8,128]{1,0:T(8,128)S(1)}, u32[]{:S(2)}, u32[]{:S(2)}) collective-permute-start(f32[8,128]{1,0:T(8,128)S(1)} %get-tuple-element.102), channel_id=1, source_target_pairs={{0,4},{4,0},{8,12},{12,8},{16,20},{20,16},{24,28},{28,24},{32,36},... | collective-permute-start | bytes 12296 | tf_op jit(solution)/shard_map/ppermute | solution.py:514
  89.0 7.0 %collective-permute-start.17 = (f32[8,128]{1,0:T(8,128)S(1)}, f32[8,128]{1,0:T(8,128)S(1)}, u32[]{:S(2)}, u32[]{:S(2)}) collective-permute-start(f32[8,128]{1,0:T(8,128)S(1)} %get-tuple-element.103), channel_id=1, source_target_pairs={{4,8},{8,4},{12,16},{16,12},{20,24},{24,20},{28,32},{32,28},{36,40... | collective-permute-start | bytes 12296 | tf_op jit(solution)/shard_map/ppermute | solution.py:515
  92.9 5.5 %collective-permute-start.19 = (f32[8,128]{1,0:T(8,128)S(1)}, f32[8,128]{1,0:T(8,128)S(1)}, u32[]{:S(2)}, u32[]{:S(2)}) collective-permute-start(f32[8,128]{1,0:T(8,128)S(1)} %get-tuple-element.105), channel_id=1, source_target_pairs={{1,2},{2,1},{5,6},{6,5},{9,10},{10,9},{13,14},{14,13},{17,18},{18,... | collective-permute-start | bytes 12296 | tf_op jit(solution)/shard_map/ppermute | solution.py:517
  107.4 5.2 %collective-permute-start.20 = (f32[8,128]{1,0:T(8,128)S(1)}, f32[8,128]{1,0:T(8,128)S(1)}, u32[]{:S(2)}, u32[]{:S(2)}) collective-permute-start(f32[8,128]{1,0:T(8,128)S(1)} %get-tuple-element.115), channel_id=1, source_target_pairs={{0,4},{4,0},{8,12},{12,8},{16,20},{20,16},{24,28},{28,24},{32,36},... | collective-permute-start | bytes 12296 | tf_op jit(solution)/shard_map/ppermute | solution.py:514
  107.4 7.0 %collective-permute-start.21 = (f32[8,128]{1,0:T(8,128)S(1)}, f32[8,128]{1,0:T(8,128)S(1)}, u32[]{:S(2)}, u32[]{:S(2)}) collective-permute-start(f32[8,128]{1,0:T(8,128)S(1)} %get-tuple-element.116), channel_id=1, source_target_pairs={{4,8},{8,4},{12,16},{16,12},{20,24},{24,20},{28,32},{32,28},{36,40... | collective-permute-start | bytes 12296 | tf_op jit(solution)/shard_map/ppermute | solution.py:515
  110.0 4.4 %collective-permute-start.22 = (f32[8,128]{1,0:T(8,128)S(1)}, f32[8,128]{1,0:T(8,128)S(1)}, u32[]{:S(2)}, u32[]{:S(2)}) collective-permute-start(f32[8,128]{1,0:T(8,128)S(1)} %get-tuple-element.117), channel_id=1, source_target_pairs={{0,1},{1,0},{2,3},{3,2},{4,5},{5,4},{6,7},{7,6},{8,9},{9,8},{10,11... | collective-permute-start | bytes 12296 | tf_op jit(solution)/shard_map/ppermute | solution.py:516
  110.1 5.5 %collective-permute-start.23 = (f32[8,128]{1,0:T(8,128)S(1)}, f32[8,128]{1,0:T(8,128)S(1)}, u32[]{:S(2)}, u32[]{:S(2)}) collective-permute-start(f32[8,128]{1,0:T(8,128)S(1)} %get-tuple-element.118), channel_id=1, source_target_pairs={{1,2},{2,1},{5,6},{6,5},{9,10},{10,9},{13,14},{14,13},{17,18},{18,... | collective-permute-start | bytes 12296 | tf_op jit(solution)/shard_map/ppermute | solution.py:517
  123.1 6.3 %collective-permute-start.24 = (f32[8,128]{1,0:T(8,128)S(1)}, f32[8,128]{1,0:T(8,128)S(1)}, u32[]{:S(2)}, u32[]{:S(2)}) collective-permute-start(f32[8,128]{1,0:T(8,128)S(1)} %get-tuple-element.120), channel_id=1, source_target_pairs={{0,4},{4,0},{8,12},{12,8},{16,20},{20,16},{24,28},{28,24},{32,36},... | collective-permute-start | bytes 12296 | tf_op jit(solution)/shard_map/ppermute | solution.py:514
  123.2 7.0 %collective-permute-start.25 = (f32[8,128]{1,0:T(8,128)S(1)}, f32[8,128]{1,0:T(8,128)S(1)}, u32[]{:S(2)}, u32[]{:S(2)}) collective-permute-start(f32[8,128]{1,0:T(8,128)S(1)} %get-tuple-element.121), channel_id=1, source_target_pairs={{4,8},{8,4},{12,16},{16,12},{20,24},{24,20},{28,32},{32,28},{36,40... | collective-permute-start | bytes 12296 | tf_op jit(solution)/shard_map/ppermute | solution.py:515
  127.2 5.5 %collective-permute-start.27 = (f32[8,128]{1,0:T(8,128)S(1)}, f32[8,128]{1,0:T(8,128)S(1)}, u32[]{:S(2)}, u32[]{:S(2)}) collective-permute-start(f32[8,128]{1,0:T(8,128)S(1)} %get-tuple-element.123), channel_id=1, source_target_pairs={{1,2},{2,1},{5,6},{6,5},{9,10},{10,9},{13,14},{14,13},{17,18},{18,... | collective-permute-start | bytes 12296 | tf_op jit(solution)/shard_map/ppermute | solution.py:517
  140.2 5.3 %collective-permute-start.28 = (f32[8,128]{1,0:T(8,128)S(1)}, f32[8,128]{1,0:T(8,128)S(1)}, u32[]{:S(2)}, u32[]{:S(2)}) collective-permute-start(f32[8,128]{1,0:T(8,128)S(1)} %get-tuple-element.127), channel_id=1, source_target_pairs={{0,4},{4,0},{8,12},{12,8},{16,20},{20,16},{24,28},{28,24},{32,36},... | collective-permute-start | bytes 12296 | tf_op jit(solution)/shard_map/ppermute | solution.py:514
  140.3 7.0 %collective-permute-start.29 = (f32[8,128]{1,0:T(8,128)S(1)}, f32[8,128]{1,0:T(8,128)S(1)}, u32[]{:S(2)}, u32[]{:S(2)}) collective-permute-start(f32[8,128]{1,0:T(8,128)S(1)} %get-tuple-element.128), channel_id=1, source_target_pairs={{4,8},{8,4},{12,16},{16,12},{20,24},{24,20},{28,32},{32,28},{36,40... | collective-permute-start | bytes 12296 | tf_op jit(solution)/shard_map/ppermute | solution.py:515
  143.0 4.4 %collective-permute-start.30 = (f32[8,128]{1,0:T(8,128)S(1)}, f32[8,128]{1,0:T(8,128)S(1)}, u32[]{:S(2)}, u32[]{:S(2)}) collective-permute-start(f32[8,128]{1,0:T(8,128)S(1)} %get-tuple-element.129), channel_id=1, source_target_pairs={{0,1},{1,0},{2,3},{3,2},{4,5},{5,4},{6,7},{7,6},{8,9},{9,8},{10,11... | collective-permute-start | bytes 12296 | tf_op jit(solution)/shard_map/ppermute | solution.py:516
  143.1 5.5 %collective-permute-start.31 = (f32[8,128]{1,0:T(8,128)S(1)}, f32[8,128]{1,0:T(8,128)S(1)}, u32[]{:S(2)}, u32[]{:S(2)}) collective-permute-start(f32[8,128]{1,0:T(8,128)S(1)} %get-tuple-element.130), channel_id=1, source_target_pairs={{1,2},{2,1},{5,6},{6,5},{9,10},{10,9},{13,14},{14,13},{17,18},{18,... | collective-permute-start | bytes 12296 | tf_op jit(solution)/shard_map/ppermute | solution.py:517
  156.1 6.3 %collective-permute-start.32 = (f32[8,128]{1,0:T(8,128)S(1)}, f32[8,128]{1,0:T(8,128)S(1)}, u32[]{:S(2)}, u32[]{:S(2)}) collective-permute-start(f32[8,128]{1,0:T(8,128)S(1)} %get-tuple-element.135), channel_id=1, source_target_pairs={{0,4},{4,0},{8,12},{12,8},{16,20},{20,16},{24,28},{28,24},{32,36},... | collective-permute-start | bytes 12296 | tf_op jit(solution)/shard_map/ppermute | solution.py:514
  156.2 7.0 %collective-permute-start.33 = (f32[8,128]{1,0:T(8,128)S(1)}, f32[8,128]{1,0:T(8,128)S(1)}, u32[]{:S(2)}, u32[]{:S(2)}) collective-permute-start(f32[8,128]{1,0:T(8,128)S(1)} %get-tuple-element.136), channel_id=1, source_target_pairs={{4,8},{8,4},{12,16},{16,12},{20,24},{24,20},{28,32},{32,28},{36,40... | collective-permute-start | bytes 12296 | tf_op jit(solution)/shard_map/ppermute | solution.py:515
  160.2 5.5 %collective-permute-start.35 = (f32[8,128]{1,0:T(8,128)S(1)}, f32[8,128]{1,0:T(8,128)S(1)}, u32[]{:S(2)}, u32[]{:S(2)}) collective-permute-start(f32[8,128]{1,0:T(8,128)S(1)} %get-tuple-element.138), channel_id=1, source_target_pairs={{1,2},{2,1},{5,6},{6,5},{9,10},{10,9},{13,14},{14,13},{17,18},{18,... | collective-permute-start | bytes 12296 | tf_op jit(solution)/shard_map/ppermute | solution.py:517
  (16 other events, 125.8 us)

commit v4 on v3

--- a/solution.py
+++ b/solution.py
@@ -17,6 +17,7 @@
 SIGMA = THETA / DELTA
 AXES = ("curve", "split")
 CAP = 9
+COMPONENTS = 6
 HALF = 128
 WIDE = 256
 ROWS = 32
@@ -155,14 +156,16 @@
     return [functools.partial(row, c) for c in range(count)]
 
 
-def gather_zones(idx_ref, tab_ref, word_ref, out_ref):
-    x = tab_ref[...]
-    scale = jnp.max(jnp.abs(x), keepdims=True)
-    per_unit = 1000000.0 / jnp.maximum(scale, 1e-30)
-    step = jnp.maximum(scale, 1e-30) * 1e-6
-    q = jnp.round(x * per_unit).astype(jnp.int32) + (1 << 20)
-    word_ref[:ROWS] = (q[:ROWS] << 11) | (q[2 * ROWS :] >> 10)
-    word_ref[ROWS:] = (q[ROWS : 2 * ROWS] << 11) | (q[2 * ROWS :] & 1023)
+def gather_zones(idx_ref, tab_ref, word_ref, out_ref, groups=1):
+    steps = []
+    for g in range(groups):
+        x = tab_ref[3 * g * ROWS : 3 * (g + 1) * ROWS, :]
+        scale = jnp.maximum(jnp.max(jnp.abs(x), keepdims=True), 1e-30)
+        steps.append(scale * 1e-6)
+        q = jnp.round(x * (1000000.0 / scale)).astype(jnp.int32) + (1 << 20)
+        at = 2 * g * ROWS
+        word_ref[at : at + ROWS] = (q[:ROWS] << 11) | (q[2 * ROWS :] >> 10)
+        word_ref[at + ROWS : at + 2 * ROWS] = (q[ROWS : 2 * ROWS] << 11) | (q[2 * ROWS :] & 1023)
 
     @pl.loop(0, 8)
     def _(t):
@@ -170,14 +173,17 @@
         for h in range(2):
             lanes = slice(h * HALF, (h + 1) * HALF)
             idx = idx_ref[pl.ds(r0, 8), lanes]
-            w0, w1 = pick(table_rows(word_ref, 2), idx >> 7, idx & 127, (8, HALF), jnp.int32)
-            back = (
-                lax.shift_right_logical(w0, 11),
-                lax.shift_right_logical(w1, 11),
-                ((w0 & 2047) << 10) | (w1 & 1023),
-            )
-            for c in range(3):
-                out_ref[c, pl.ds(r0, 8), lanes] = (back[c] - (1 << 20)).astype(F32) * step
+            words = pick(table_rows(word_ref, 2 * groups), idx >> 7, idx & 127, (8, HALF), jnp.int32)
+            for g in range(groups):
+                w0, w1 = words[2 * g : 2 * g + 2]
+                back = (
+                    lax.shift_right_logical(w0, 11),
+                    lax.shift_right_logical(w1, 11),
+                    ((w0 & 2047) << 10) | (w1 & 1023),
+                )
+                for c in range(3):
+                    value = (back[c] - (1 << 20)).astype(F32) * steps[g]
+                    out_ref[3 * g + c, pl.ds(r0, 8), lanes] = value
 
 
 def spread_rows(idx, rows):
@@ -229,29 +235,39 @@
     idx = lists_ref[...]
     got = pick(table_rows(tab_ref, count), idx >> 7, idx & 127, (8, HALF))
     for k, send in enumerate(send_refs):
-        send[...] = jnp.concatenate(
-            [got[min(c, count - 1)][2 * k : 2 * k + 2] for c in range(4)], 0
-        )
-
-
-def force(v_ref, en, jac_ref, mass, t_ref, work_ref, tables):
+        for c in range(count):
+            send[2 * c : 2 * c + 2, :] = got[c][2 * k : 2 * k + 2]
+        send[2 * count :, :] = jnp.zeros((16 - 2 * count, HALF), F32)
+
+
+def pressure_at(en, mass, tables):
     get = functools.partial(entry, tables, FORCE_AT)
     eh, el = split2(en)
     e_q = dot(get("bern_up_high"), eh) + dot(get("bern_up_high"), el) + dot(get("bern_up_low"), eh)
-    pressure = GAMMA_LESS * e_q * mass
+    return GAMMA_LESS * e_q * mass
+
+
+def force(pressure, jac_ref, tables, t_ref=None, at=0, v_ref=None, work_ref=None):
+    get = functools.partial(entry, tables, FORCE_AT)
     for c in range(3):
-        high, low = split2(v_ref[c])
-        vc = jnp.concatenate([high, low, high], 0)
+        if v_ref is not None:
+            high, low = split2(v_ref[c])
+            vc = jnp.concatenate([high, low, high], 0)
         term = jnp.zeros((NPZ, WIDE), F32)
         for k in range(3):
             w = jac_ref[(3 * k + c) * QP : (3 * k + c + 1) * QP, :] * pressure
-            dv = dot(get("up%d" % k), vc)
-            if c == 0 and k == 0:
-                work_ref[...] = w * dv
-            else:
-                work_ref[...] += w * dv
-            term = term + down(get("down%d" % k), w)
-        t_ref[c] = term
+            if v_ref is not None:
+                dv = dot(get("up%d" % k), vc)
+                if c == 0 and k == 0:
+                    work_ref[...] = w * dv
+                else:
+                    work_ref[...] += w * dv
+            if t_ref is not None:
+                term = term + down(get("down%d" % k), w)
+        if t_ref is not None:
+            t_ref[at + c] = term
+    if v_ref is None:
+        return None
     wh, wl = split2(work_ref[...])
     high, low = get("bern_down_high"), get("bern_down_low")
     return -(dot(high, wh) + dot(high, wl) + dot(low, wh))
@@ -389,11 +405,12 @@
             came = jnp.concatenate(split3(arr[:, at + i : at + i + wide]), 0)
             out[i : i + n, :] = jnp.where(lands, dot(came, hot3, TN)[:n], ref[i : i + n, :])
     mass = mass_out[...]
-    rhs_e = force(vz, en_out[...], jac_out, mass, terms, work, tables)
-    terms[3] = down(entry(tables, FORCE_AT, "limit"), mass)
+    rhs_e = force(pressure_at(en_out[...], mass, tables), jac_out, tables, terms, 0, vz, work)
     ehalf_out[...] = en_out[...] + 0.5 * STEP_SIZE * energy_change(rhs_e, inv_out, tables)
-    y_out[...] = scatter_zones(zn_ref, lanes, terms, 4)
-    send_shared(lists_ref, y_out, (s0, s1, s2, s3), 4)
+    force(pressure_at(ehalf_out[...], mass, tables), jac_out, tables, terms, 3)
+    terms[6] = down(entry(tables, FORCE_AT, "limit"), mass)
+    y_out[...] = scatter_zones(zn_ref, lanes, terms, 7)
+    send_shared(lists_ref, y_out, (s0, s1, s2, s3), 7)
 
 
 def rhos():
@@ -405,80 +422,67 @@
     return out
 
 
-def three(x):
-    return jnp.concatenate([x, x, x], 0)
+def each(x):
+    return jnp.concatenate([x] * COMPONENTS, 0)
 
 
 def update(y, r_ref, d_ref, a_ref, ib_ref, step):
     keep, add = rhos()[step]
     r = r_ref[...] - y
-    d = keep * d_ref[...] + add * (r * three(ib_ref[...]))
+    d = keep * d_ref[...] + add * (r * each(ib_ref[...]))
     return r, d, a_ref[...] + d
 
 
 def apply_mass(zn_ref, lanes, mass_ref, tables, d_ref, y_out, zone, terms, words):
-    gather_zones(zn_ref, d_ref, words, zone)
-    mass = mass_ref[...]
-    for c in range(3):
+    gather_zones(zn_ref, d_ref, words, zone, COMPONENTS // 3)
+    for c in range(COMPONENTS):
         at_points = up(entry(tables, MASS_AT, "up"), zone[c])
-        terms[c] = down(entry(tables, MASS_AT, "down"), at_points * mass)
-    y_out[...] = scatter_zones(zn_ref, lanes, terms, 3)
-
-
-def start_kernel(g0, g1, g2, g3, y_ref, *refs, first):
-    if first:
-        lists, zn, lanes, mass, tables = refs[:5]
-        ib, r_out, d_out, y_out, s0, s1, s2, s3, *scratch = refs[5:]
-        y = y_ref[...] + received(lists, (g0, g1, g2, g3), 4)
-        pad = lax.broadcasted_iota(jnp.int32, (ROWS, WIDE), 0) == 31
-        inv_bound = 1.0 / jnp.where(pad, 1.0, y[96:])
-        ib[...] = inv_bound
-        r = y[:96]
-    else:
-        ib, lists, zn, lanes, mass, tables = refs[:6]
-        r_out, d_out, y_out, s0, s1, s2, s3, *scratch = refs[6:]
-        r = y_ref[...] + received(lists, (g0, g1, g2, g3), 3)
-        inv_bound = ib[...]
+        terms[c] = down(entry(tables, MASS_AT, "down"), at_points * mass_ref[...])
+    y_out[...] = scatter_zones(zn_ref, lanes, terms, COMPONENTS)
+
+
+def start_kernel(
+    g0, g1, g2, g3, y_ref, lists, zn, lanes, mass, tables, ib, r_out, d_out, y_out, s0, s1, s2, s3, *scratch
+):
+    y = y_ref[...] + received(lists, (g0, g1, g2, g3), COMPONENTS + 1)
+    pad = lax.broadcasted_iota(jnp.int32, (ROWS, WIDE), 0) == 31
+    inv_bound = 1.0 / jnp.where(pad, 1.0, y[COMPONENTS * ROWS :])
+    ib[...] = inv_bound
+    r = y[: COMPONENTS * ROWS]
     r_out[...] = r
-    d_out[...] = r * three(inv_bound) * (1.0 / THETA)
+    d_out[...] = r * each(inv_bound) * (1.0 / THETA)
     apply_mass(zn, lanes, mass, tables, d_out, y_out, *scratch)
-    send_shared(lists, y_out, (s0, s1, s2, s3), 3)
+    send_shared(lists, y_out, (s0, s1, s2, s3), COMPONENTS)
 
 
 def sweep_kernel(
     g0, g1, g2, g3, y_ref, r_ref, d_ref, a_ref, ib_ref, lists, zn, lanes, mass, tables,
     r_out, d_out, a_out, y_out, s0, s1, s2, s3, *scratch, step,
 ):
-    y = y_ref[...] + received(lists, (g0, g1, g2, g3), 3)
+    y = y_ref[...] + received(lists, (g0, g1, g2, g3), COMPONENTS)
     r, d, a = update(y, r_ref, d_ref, a_ref, ib_ref, step)
     r_out[...] = r
     d_out[...] = d
     a_out[...] = a
     apply_mass(zn, lanes, mass, tables, d_out, y_out, *scratch)
-    send_shared(lists, y_out, (s0, s1, s2, s3), 3)
-
-
-def second_kernel(
-    g0, g1, g2, g3, y_ref, r_ref, d_ref, a_ref, ib_ref, lists, zn, lanes, mass, jac, inv, en, ehalf, vel, tables,
-    en_out, y_out, s0, s1, s2, s3, vhalf, vz, terms, work, words,
+    send_shared(lists, y_out, (s0, s1, s2, s3), COMPONENTS)
+
+
+def last_kernel(
+    g0, g1, g2, g3, y_ref, r_ref, d_ref, a_ref, ib_ref, lists, zn, mass, jac, inv, en, ehalf, vel, tables,
+    en_out, vel_out, vhalf, vz, work, words,
 ):
-    y = y_ref[...] + received(lists, (g0, g1, g2, g3), 3)
+    y = y_ref[...] + received(lists, (g0, g1, g2, g3), COMPONENTS)
     _, _, a = update(y, r_ref, d_ref, a_ref, ib_ref, SWEEPS - 1)
-    vhalf[...] = vel[...] + 0.5 * STEP_SIZE * a
-    gather_zones(zn, vhalf, words, vz)
-    rhs_e = force(vz, ehalf[...], jac, mass[...], terms, work, tables)
-    y_out[...] = scatter_zones(zn, lanes, terms, 3)
-    send_shared(lists, y_out, (s0, s1, s2, s3), 3)
-    en_out[...] = en[...] + STEP_SIZE * energy_change(rhs_e, inv, tables)
-
-
-def last_kernel(g0, g1, g2, g3, y_ref, r_ref, d_ref, a_ref, ib_ref, lists, vel, out):
-    y = y_ref[...] + received(lists, (g0, g1, g2, g3), 3)
-    _, _, a = update(y, r_ref, d_ref, a_ref, ib_ref, SWEEPS - 1)
-    v = vel[...] + STEP_SIZE * a
+    vhalf[...] = vel[...] + 0.5 * STEP_SIZE * a[: 3 * ROWS]
+    v = vel[...] + STEP_SIZE * a[3 * ROWS :]
     for c in range(3):
         for r in range(31):
-            out[c : c + 1, r * WIDE : (r + 1) * WIDE] = v[c * ROWS + r : c * ROWS + r + 1]
+            vel_out[c : c + 1, r * WIDE : (r + 1) * WIDE] = v[c * ROWS + r : c * ROWS + r + 1]
+    gather_zones(zn, vhalf, words, vz)
+    pressure = pressure_at(ehalf[...], mass[...], tables)
+    rhs_e = force(pressure, jac, tables, v_ref=vz, work_ref=work)
+    en_out[...] = en[...] + STEP_SIZE * energy_change(rhs_e, inv, tables)
 
 
 VM = pl.BlockSpec(memory_space=pltpu.VMEM)
@@ -523,63 +527,46 @@
     devices = lax.axis_size("curve") * lax.axis_size("split")
     ints = lambda *s: jax.ShapeDtypeStruct(s, jnp.int32)
     half = lambda *s: jax.ShapeDtypeStruct(s, BF)
-    node, msg = (96, WIDE), (8, MSG + TAIL)
+    node, nodes, msg = (3 * ROWS, WIDE), (COMPONENTS * ROWS, WIDE), (8, MSG + TAIL)
     fields = [(9 * QP, WIDE), (QP, WIDE), (LD * LD, WIDE), (LD, WIDE)]
-    send = [(8, HALF)] * 4
-    zone = (3, NPZ, WIDE)
-    words = ints(2 * ROWS, WIDE)
+    send = [(16, HALF)] * 4
+    zone = lambda count: (count, NPZ, WIDE)
+    words = lambda groups: ints(2 * groups * ROWS, WIDE)
     *msgs, lists = call(
         pack_kernel, (send_rows, shared_nodes, jac, mass, inv, energy), [msg] * 4 + [ints(8, HALF)],
-        [(40, WIDE)] + fields, [SM, VM] + [HB] * 4, limit=58, copies=4, name="pack",
+        [(40, WIDE)] + fields, [SM, VM] + [HB] * 4, limit=61, copies=4, name="pack",
     )
     came = []
     for k, m in enumerate(msgs):
         came.append(lax.ppermute(m, AXES, paired(k % 2, devices, 1 + k // 2)))
     vel, vz, lanes = call(
         prep_kernel, (velocity, zone_nodes, lists, arrive_rows, energy, force_tables),
-        [node, zone, half(NPZ, WIDE, WIDE)], [words, (WIDE, HALF)], [VM, VM, VM, SM, VM, VM], name="prep",
+        [node, zone(3), half(NPZ, WIDE, WIDE)], [words(1), (WIDE, HALF)], [VM, VM, VM, SM, VM, VM], name="prep",
     )
     jac, mass, inv, en, ehalf, y, *sends = call(
         first_kernel,
         (arrive_rows, *came, lists, jac, mass, inv, energy, zone_nodes, force_tables, vz, lanes),
-        fields + [(LD, WIDE), (128, WIDE)] + send,
-        [(48, WIDE), (48, MSG), (4, NPZ, WIDE), (QP, WIDE)],
+        fields + [(LD, WIDE), ((COMPONENTS + 1) * ROWS, WIDE)] + send,
+        [(48, WIDE), (48, MSG), zone(COMPONENTS + 1), (QP, WIDE)],
         [SM] + [VM] * 13, name="force_one",
     )
-    scratch = [zone, zone, words]
-    for section in range(2):
-        got = exchange(sends)
-        outs = [node, node, node] + send
-        tail = (lists, zone_nodes, lanes, mass, mass_tables)
-        if section == 0:
-            ib, r, d, y, *sends = call(
-                functools.partial(start_kernel, first=True), (*got, y, *tail),
-                [(ROWS, WIDE)] + outs, scratch, name="mass_start",
-            )
-        else:
-            r, d, y, *sends = call(
-                functools.partial(start_kernel, first=False), (*got, y, ib, *tail), outs, scratch,
-                name="mass_start_two",
-            )
-        a = d
-        for step in range(SWEEPS - 1):
-            got = exchange(sends)
-            r, d, a, y, *sends = call(
-                functools.partial(sweep_kernel, step=step), (*got, y, r, d, a, ib, *tail),
-                [node] + outs, scratch, name="mass_sweep",
-            )
-        got = exchange(sends)
-        if section == 0:
-            energy_next, y, *sends = call(
-                second_kernel,
-                (*got, y, r, d, a, ib, lists, zone_nodes, lanes, mass, jac, inv, en, ehalf, vel, force_tables),
-                [(LD, WIDE), node] + send, [node, zone, zone, (QP, WIDE), words], limit=24,
-                name="force_two",
-            )
-        else:
-            (velocity_next,) = call(
-                last_kernel, (*got, y, r, d, a, ib, lists, vel), [velocity.shape], name="finish"
-            )
+    scratch = [zone(COMPONENTS), zone(COMPONENTS), words(COMPONENTS // 3)]
+    tail = (lists, zone_nodes, lanes, mass, mass_tables)
+    ib, r, d, y, *sends = call(
+        start_kernel, (*exchange(sends), y, *tail), [(ROWS, WIDE), nodes, nodes, nodes] + send, scratch,
+        name="mass_start",
+    )
+    a = d
+    for step in range(SWEEPS - 1):
+        r, d, a, y, *sends = call(
+            functools.partial(sweep_kernel, step=step), (*exchange(sends), y, r, d, a, ib, *tail),
+            [nodes] * 4 + send, scratch, name="mass_sweep",
+        )
+    energy_next, velocity_next = call(
+        last_kernel,
+        (*exchange(sends), y, r, d, a, ib, lists, zone_nodes, mass, jac, inv, en, ehalf, vel, force_tables),
+        [(LD, WIDE), velocity.shape], [node, zone(3), (QP, WIDE), words(1)], name="force_two",
+    )
     return velocity_next, energy_next
 
 

time: 168 us -> 120 us (0.71)
  starting transfers between devices: 60.5 us -> 37.6 us
  waiting for transfers between devices: 25.2 us -> 12.7 us
  Pallas kernels: 75.2 us -> 65.1 us
  local copies, waits for them, and re-layouts: 4.79 us -> 2.95 us
    ppermute x8 -> x4, starting transfers between devices: 27 us -> 14 us  [exchange(): lax.ppermute(sends[1], 'curve', paired(1, n_curve))]
    pallas_call x11 -> x7, Pallas kernels: 75.2 us -> 65.1 us  [call(): pl.pallas_call(kernel, out_shape=[shape_of(s) for s in outs], in_specs=sp...]
    ppermute x8 -> x4, starting transfers between devices: 18.7 us -> 9.44 us  [exchange(): lax.ppermute(sends[3], 'split', paired(1, n_split))]
    ppermute x8 -> x4, waiting for transfers between devices: 14.3 us -> 8.01 us  [exchange(): lax.ppermute(sends[3], 'split', paired(1, n_split))]
    ppermute x8 -> x4, waiting for transfers between devices: 8.7 us -> 3.48 us  [exchange(): lax.ppermute(sends[1], 'curve', paired(1, n_curve))]
    unnamed x24 -> x22, local copies, waits for them, and re-layouts: 4.79 us -> 2.95 us
  transfers between devices with their start and end apart: 36 -> 20, of which waited for: 20 -> 10; matrix products, arithmetic and copies ran while one was open for 0% -> 0% of each run, Pallas kernels for 5% -> 7%
where the time goes in v4:
time: 120 us; the launch traced here: 119 us
  Pallas kernels  65.1 us (54%)
  starting transfers between devices  37.6 us (31%)
  waiting for transfers between devices  12.7 us (11%)
  local copies, waits for them, and re-layouts  2.95 us (2%)
    pallas_call x7, Pallas kernels, call(): pl.pallas_call(kernel, out_shape=[shape_of(s) for s in outs], in_specs=sp...  65.1 us
    ppermute x4, starting transfers between devices, exchange(): lax.ppermute(sends[1], 'curve', paired(1, n_curve))  14 us
    ppermute x4, starting transfers between devices, per_device(): came.append(lax.ppermute(m, AXES, paired(k % 2, devices, 1 + k // 2)))  12.4 us
    ppermute x4, starting transfers between devices, exchange(): lax.ppermute(sends[3], 'split', paired(1, n_split))  9.44 us
    ppermute x4, waiting for transfers between devices, exchange(): lax.ppermute(sends[3], 'split', paired(1, n_split))  8.01 us
    ppermute x4, waiting for transfers between devices, exchange(): lax.ppermute(sends[1], 'curve', paired(1, n_curve))  3.48 us
    unnamed x22, local copies, waits for them, and re-layouts  2.95 us
  transfers between devices with their start and end apart: 20, of which 10 were waited for; matrix products, arithmetic and copies ran while one was open for 0% of the time, Pallas kernels for 7%

profile of v4, /device:TPU:26, one launch (start us, length us, event | category | flops | bytes accessed | tf_op | source)
XLA Modules:
  0.0 119.3 jit_solution(15339064268621013841)
XLA Ops:
  0.7 4.6 %pack.1 = (f32[8,3712]{1,0:T(8,128)}, f32[8,3712]{1,0:T(8,128)}, f32[8,3712]{1,0:T(8,128)}, f32[8,3712]{1,0:T(8,128)}, s32[8,128]{1,0:T(8,128)}) custom-call(s32[1,36]{1,0:T(1,128)} %send_ref.1, s32[1,4,256]{2,1,0:T(4,128)} %shared_ref.1, f32[1944,256]{1,0:T(8,128)} %jac_ref.1, f32[216,256]{1,0:T(8,128)} %mass_ref.1, f32[729,256]{1,0:T(8,128)} %inv_ref.1, ...), custom_call_target="tpu_custom_call" | custom-call | tf_op jit(solution)/shard_map/pack/pallas_call | solution.py:499
  5.3 0.6 collective-permute-start
  6.0 4.1 %collective-permute-start.1 = (f32[8,3712]{1,0:T(8,128)}, f32[8,3712]{1,0:T(8,128)S(1)}, u32[]{:S(2)}, u32[]{:S(2)}) collective-permute-start(f32[8,3712]{1,0:T(8,128)} %get-tuple-element.47), channel_id=1, source_target_pairs={{1,2},{2,1},{3,4},{4,3},{5,6},{6,5},{7,8},{8,7},{9,10},{10,9},{11,... | collective-permute-start | bytes 356360 | tf_op jit(solution)/shard_map/ppermute | solution.py:541
  10.0 0.6 collective-permute-start.2
  10.7 7.1 %collective-permute-start.3 = (f32[8,3712]{1,0:T(8,128)}, f32[8,3712]{1,0:T(8,128)S(1)}, u32[]{:S(2)}, u32[]{:S(2)}) collective-permute-start(f32[8,3712]{1,0:T(8,128)} %get-tuple-element.49), channel_id=1, source_target_pairs={{2,4},{4,2},{3,5},{5,3},{6,8},{8,6},{7,9},{9,7},{10,12},{12,10},{1... | collective-permute-start | bytes 356360 | tf_op jit(solution)/shard_map/ppermute | solution.py:541
  17.8 0.7 copy-done.7
  18.5 8.1 %prep.1 = (f32[96,256]{1,0:T(8,128)S(1)}, f32[3,64,256]{2,1,0:T(8,128)S(1)}, bf16[64,256,256]{2,1,0:T(8,128)(2,1)S(1)}) custom-call(f32[3,7936]{1,0:T(4,128)S(1)} %copy-done.9, s32[64,256]{1,0:T(8,128)S(1)} %copy-done.3, s32[8,128]{1,0:T(8,128)S(1)} %copy-done.7, s32[1,36]{1,0:T(1,128)S(1)} %copy-done.10, f32[27,256]{1,0:T(8,128)S(1)} %copy-done.6, ...), custom_call_target="tpu_custom_call" | custom-call | tf_op jit(solution)/shard_map/prep/pallas_call | solution.py:499
  26.7 1.5 %copy-done.1 = f32[1944,256]{1,0:T(8,128)S(1)} copy-done((f32[1944,256]{1,0:T(8,128)S(1)}, f32[1944,256]{1,0:T(8,128)}, u32[]{:S(2)}) %copy-start.1) | copy-done | bytes 1990680
  28.2 0.7 copy-done.8
  28.9 10.1 %force_one.1 = (f32[1944,256]{1,0:T(8,128)S(1)}, f32[216,256]{1,0:T(8,128)S(1)}, f32[729,256]{1,0:T(8,128)S(1)}, f32[27,256]{1,0:T(8,128)S(1)}, f32[27,256]{1,0:...) custom-call(s32[1,36]{1,0:T(1,128)S(1)} %copy-done.10, ...), custom_call_target="tpu_custom_call" | custom-call | tf_op jit(solution)/shard_map/force_one/pallas_call | solution.py:499
  39.1 3.6 %collective-permute-start.5 = (f32[16,128]{1,0:T(8,128)S(1)}, f32[16,128]{1,0:T(8,128)S(1)}, u32[]{:S(2)}, u32[]{:S(2)}) collective-permute-start(f32[16,128]{1,0:T(8,128)S(1)} %get-tuple-element.54), channel_id=1, source_target_pairs={{4,8},{8,4},{12,16},{16,12},{20,24},{24,20},{28,32},{32,28},{36,40... | collective-permute-start | bytes 24584 | tf_op jit(solution)/shard_map/ppermute | solution.py:519
  42.7 1.2 collective-permute-start.6
  43.9 2.4 %collective-permute-start.7 = (f32[16,128]{1,0:T(8,128)S(1)}, f32[16,128]{1,0:T(8,128)S(1)}, u32[]{:S(2)}, u32[]{:S(2)}) collective-permute-start(f32[16,128]{1,0:T(8,128)S(1)} %get-tuple-element.56), channel_id=1, source_target_pairs={{1,2},{2,1},{5,6},{6,5},{9,10},{10,9},{13,14},{14,13},{17,18},{18,... | collective-permute-start | bytes 24584 | tf_op jit(solution)/shard_map/ppermute | solution.py:521
  46.4 3.0 %collective-permute-done.7.g3 = f32[16,128]{1,0:T(8,128)S(1)} collective-permute-done((f32[16,128]{1,0:T(8,128)S(1)}, f32[16,128]{1,0:T(8,128)S(1)}, u32[]{:S(2)}, u32[]{:S(2)}) %collective-permute-start.7) | collective-permute-done | bytes 8224 | tf_op jit(solution)/shard_map/ppermute | solution.py:521
  49.4 12.4 %mass_start.1 = (f32[32,256]{1,0:T(8,128)S(1)}, f32[192,256]{1,0:T(8,128)S(1)}, f32[192,256]{1,0:T(8,128)S(1)}, f32[192,256]{1,0:T(8,128)S(1)}, f32[16,128]{1,0:...) custom-call(f32[16,128]{1,0:T(8,128)S(1)} %collective-permute-done.4.g0, ...), custom_call_target="tpu_custom_call" | custom-call | tf_op jit(solution)/shard_map/mass_start/pallas_call | solution.py:499
  61.9 3.8 %collective-permute-start.9 = (f32[16,128]{1,0:T(8,128)S(1)}, f32[16,128]{1,0:T(8,128)S(1)}, u32[]{:S(2)}, u32[]{:S(2)}) collective-permute-start(f32[16,128]{1,0:T(8,128)S(1)} %get-tuple-element.60), channel_id=1, source_target_pairs={{4,8},{8,4},{12,16},{16,12},{20,24},{24,20},{28,32},{32,28},{36,40... | collective-permute-start | bytes 24584 | tf_op jit(solution)/shard_map/ppermute | solution.py:519
  65.8 2.4 %collective-permute-start.11 = (f32[16,128]{1,0:T(8,128)S(1)}, f32[16,128]{1,0:T(8,128)S(1)}, u32[]{:S(2)}, u32[]{:S(2)}) collective-permute-start(f32[16,128]{1,0:T(8,128)S(1)} %get-tuple-element.62), channel_id=1, source_target_pairs={{1,2},{2,1},{5,6},{6,5},{9,10},{10,9},{13,14},{14,13},{17,18},{18,... | collective-permute-start | bytes 24584 | tf_op jit(solution)/shard_map/ppermute | solution.py:521
  68.2 0.7 collective-permute-done.9.g1
  69.0 0.5 collective-permute-done.10.g2
  69.5 1.9 %collective-permute-done.11.g3 = f32[16,128]{1,0:T(8,128)S(1)} collective-permute-done((f32[16,128]{1,0:T(8,128)S(1)}, f32[16,128]{1,0:T(8,128)S(1)}, u32[]{:S(2)}, u32[]{:S(2)}) %collective-permute-start.11) | collective-permute-done | bytes 8224 | tf_op jit(solution)/shard_map/ppermute | solution.py:521
  71.4 12.1 %mass_sweep.2 = (f32[192,256]{1,0:T(8,128)S(1)}, f32[192,256]{1,0:T(8,128)S(1)}, f32[192,256]{1,0:T(8,128)S(1)}, f32[192,256]{1,0:T(8,128)S(1)}, f32[16,128]{1,0...) custom-call(f32[16,128]{1,0:T(8,128)S(1)} %collective-permute-done.8.g0, ...), custom_call_target="tpu_custom_call" | custom-call | tf_op jit(solution)/shard_map/mass_sweep/pallas_call | solution.py:499
  83.6 2.7 %collective-permute-start.13 = (f32[16,128]{1,0:T(8,128)S(1)}, f32[16,128]{1,0:T(8,128)S(1)}, u32[]{:S(2)}, u32[]{:S(2)}) collective-permute-start(f32[16,128]{1,0:T(8,128)S(1)} %get-tuple-element.68), channel_id=1, source_target_pairs={{4,8},{8,4},{12,16},{16,12},{20,24},{24,20},{28,32},{32,28},{36,40... | collective-permute-start | bytes 24584 | tf_op jit(solution)/shard_map/ppermute | solution.py:519
  86.3 2.4 %collective-permute-start.15 = (f32[16,128]{1,0:T(8,128)S(1)}, f32[16,128]{1,0:T(8,128)S(1)}, u32[]{:S(2)}, u32[]{:S(2)}) collective-permute-start(f32[16,128]{1,0:T(8,128)S(1)} %get-tuple-element.70), channel_id=1, source_target_pairs={{1,2},{2,1},{5,6},{6,5},{9,10},{10,9},{13,14},{14,13},{17,18},{18,... | collective-permute-start | bytes 24584 | tf_op jit(solution)/shard_map/ppermute | solution.py:521
  88.8 1.9 %collective-permute-done.13.g1 = f32[16,128]{1,0:T(8,128)S(1)} collective-permute-done((f32[16,128]{1,0:T(8,128)S(1)}, f32[16,128]{1,0:T(8,128)S(1)}, u32[]{:S(2)}, u32[]{:S(2)}) %collective-permute-start.13) | collective-permute-done | bytes 8224 | tf_op jit(solution)/shard_map/ppermute | solution.py:519
  90.7 1.2 %collective-permute-done.15.g3 = f32[16,128]{1,0:T(8,128)S(1)} collective-permute-done((f32[16,128]{1,0:T(8,128)S(1)}, f32[16,128]{1,0:T(8,128)S(1)}, u32[]{:S(2)}, u32[]{:S(2)}) %collective-permute-start.15) | collective-permute-done | bytes 8224 | tf_op jit(solution)/shard_map/ppermute | solution.py:521
  91.9 12.1 %mass_sweep.3 = (f32[192,256]{1,0:T(8,128)S(1)}, f32[192,256]{1,0:T(8,128)S(1)}, f32[192,256]{1,0:T(8,128)S(1)}, f32[192,256]{1,0:T(8,128)S(1)}, f32[16,128]{1,0...) custom-call(f32[16,128]{1,0:T(8,128)S(1)} %collective-permute-done.12.g0, ...), custom_call_target="tpu_custom_call" | custom-call | tf_op jit(solution)/shard_map/mass_sweep/pallas_call | solution.py:499
  104.1 3.9 %collective-permute-start.17 = (f32[16,128]{1,0:T(8,128)S(1)}, f32[16,128]{1,0:T(8,128)S(1)}, u32[]{:S(2)}, u32[]{:S(2)}) collective-permute-start(f32[16,128]{1,0:T(8,128)S(1)} %get-tuple-element.76), channel_id=1, source_target_pairs={{4,8},{8,4},{12,16},{16,12},{20,24},{24,20},{28,32},{32,28},{36,40... | collective-permute-start | bytes 24584 | tf_op jit(solution)/shard_map/ppermute | solution.py:519
  108.1 2.2 %collective-permute-start.19 = (f32[16,128]{1,0:T(8,128)S(1)}, f32[16,128]{1,0:T(8,128)S(1)}, u32[]{:S(2)}, u32[]{:S(2)}) collective-permute-start(f32[16,128]{1,0:T(8,128)S(1)} %get-tuple-element.78), channel_id=1, source_target_pairs={{1,2},{2,1},{5,6},{6,5},{9,10},{10,9},{13,14},{14,13},{17,18},{18,... | collective-permute-start | bytes 24584 | tf_op jit(solution)/shard_map/ppermute | solution.py:521
  110.3 0.9 collective-permute-done.17.g1
  111.2 0.5 collective-permute-done.18.g2
  111.7 1.9 %collective-permute-done.19.g3 = f32[16,128]{1,0:T(8,128)S(1)} collective-permute-done((f32[16,128]{1,0:T(8,128)S(1)}, f32[16,128]{1,0:T(8,128)S(1)}, u32[]{:S(2)}, u32[]{:S(2)}) %collective-permute-start.19) | collective-permute-done | bytes 8224 | tf_op jit(solution)/shard_map/ppermute | solution.py:521
  113.6 5.7 %force_two.1 = (f32[27,256]{1,0:T(8,128)}, f32[3,7936]{1,0:T(4,128)}) custom-call(f32[16,128]{1,0:T(8,128)S(1)} %collective-permute-done.16.g0, f32[16,128]{1,0:T(8,128)S(1)} %collective-permute-done.17.g1, f32[16,128]{1,0:T(8,128)S(1)} %collective-permute-done.18.g2, f32[16,128]{1,0:T(8,128)S(1)} %collective-permute-done.19.g3, ...), custom_call_target="tpu_custom_call" | custom-call | tf_op jit(solution)/shard_map/force_two/pallas_call | solution.py:499
  (37 shorter events, 0.8 us)
Async XLA Ops:
  0.6 17.2 %copy-start = (bf16[2528,256]{1,0:T(8,128)(2,1)S(1)}, bf16[2528,256]{1,0:T(8,128)(2,1)}, u32[]{:S(2)}) copy-start(bf16[2528,256]{1,0:T(8,128)(2,1)} %constant.4.clone._tables.tables) | copy-start | bytes 3883012
  0.6 17.2 %copy-start.6 = (f32[27,256]{1,0:T(8,128)S(1)}, f32[27,256]{1,0:T(8,128)}, u32[]{:S(2)}) copy-start(f32[27,256]{1,0:T(8,128)} %en_ref.1) | copy-start | bytes 82948
  0.7 26.0 %copy-start.2 = (f32[729,256]{1,0:T(8,128)S(1)}, f32[729,256]{1,0:T(8,128)}, u32[]{:S(2)}) copy-start(f32[729,256]{1,0:T(8,128)} %inv_ref.1) | copy-start | bytes 2239492
  0.7 26.0 %copy-start.5 = (f32[216,256]{1,0:T(8,128)S(1)}, f32[216,256]{1,0:T(8,128)}, u32[]{:S(2)}) copy-start(f32[216,256]{1,0:T(8,128)} %mass_ref.1) | copy-start | bytes 663556
  0.7 17.1 %copy-start.3 = (s32[64,256]{1,0:T(8,128)S(1)}, s32[64,256]{1,0:T(8,128)}, u32[]{:S(2)}) copy-start(s32[64,256]{1,0:T(8,128)} %zn.7) | copy-start | bytes 196612
  0.7 17.1 %copy-start.10 = (s32[1,36]{1,0:T(1,128)S(1)}, s32[1,36]{1,0:T(1,128)}, u32[]{:S(2)}) copy-start(s32[1,36]{1,0:T(1,128)} %arrive_ref.1) | copy-start | bytes 436
  0.7 17.1 %copy-start.9 = (f32[3,7936]{1,0:T(4,128)S(1)}, f32[3,7936]{1,0:T(4,128)}, u32[]{:S(2)}) copy-start(f32[3,7936]{1,0:T(4,128)} %vel_ref.1) | copy-start | bytes 285700
  5.3 21.2 %collective-permute-start = (f32[8,3712]{1,0:T(8,128)}, f32[8,3712]{1,0:T(8,128)S(1)}, u32[]{:S(2)}, u32[]{:S(2)}) collective-permute-start(f32[8,3712]{1,0:T(8,128)} %get-tuple-element.46), channel_id=1, source_target_pairs={{0,1},{1,0},{2,3},{3,2},{4,5},{5,4},{6,7},{7,6},{8,9},{9,8},{10,11... | collective-permute-start | bytes 356360 | tf_op jit(solution)/shard_map/ppermute | solution.py:541
  6.0 20.6 %collective-permute-start.1 = (f32[8,3712]{1,0:T(8,128)}, f32[8,3712]{1,0:T(8,128)S(1)}, u32[]{:S(2)}, u32[]{:S(2)}) collective-permute-start(f32[8,3712]{1,0:T(8,128)} %get-tuple-element.47), channel_id=1, source_target_pairs={{1,2},{2,1},{3,4},{4,3},{5,6},{6,5},{7,8},{8,7},{9,10},{10,9},{11,... | collective-permute-start | bytes 356360 | tf_op jit(solution)/shard_map/ppermute | solution.py:541
  10.0 16.6 %collective-permute-start.2 = (f32[8,3712]{1,0:T(8,128)}, f32[8,3712]{1,0:T(8,128)S(1)}, u32[]{:S(2)}, u32[]{:S(2)}) collective-permute-start(f32[8,3712]{1,0:T(8,128)} %get-tuple-element.48), channel_id=1, source_target_pairs={{0,2},{2,0},{1,3},{3,1},{4,6},{6,4},{5,7},{7,5},{8,10},{10,8},{9,1... | collective-permute-start | bytes 356360 | tf_op jit(solution)/shard_map/ppermute | solution.py:541
  10.7 16.0 %collective-permute-start.3 = (f32[8,3712]{1,0:T(8,128)}, f32[8,3712]{1,0:T(8,128)S(1)}, u32[]{:S(2)}, u32[]{:S(2)}) collective-permute-start(f32[8,3712]{1,0:T(8,128)} %get-tuple-element.49), channel_id=1, source_target_pairs={{2,4},{4,2},{3,5},{5,3},{6,8},{8,6},{7,9},{9,7},{10,12},{12,10},{1... | collective-permute-start | bytes 356360 | tf_op jit(solution)/shard_map/ppermute | solution.py:541
  17.8 0.7 copy-start.7
  26.7 1.6 %copy-start.1 = (f32[1944,256]{1,0:T(8,128)S(1)}, f32[1944,256]{1,0:T(8,128)}, u32[]{:S(2)}) copy-start(f32[1944,256]{1,0:T(8,128)} %jac_ref.1) | copy-start | bytes 5971972
  28.2 0.7 copy-start.8
  28.9 20.5 %copy-start.4 = (bf16[352,256]{1,0:T(8,128)(2,1)S(1)}, bf16[352,256]{1,0:T(8,128)(2,1)}, u32[]{:S(2)}) copy-start(bf16[352,256]{1,0:T(8,128)(2,1)} %constant.5.clone.tables) | copy-start | bytes 540676
  39.0 7.3 %collective-permute-start.4 = (f32[16,128]{1,0:T(8,128)S(1)}, f32[16,128]{1,0:T(8,128)S(1)}, u32[]{:S(2)}, u32[]{:S(2)}) collective-permute-start(f32[16,128]{1,0:T(8,128)S(1)} %get-tuple-element.53), channel_id=1, source_target_pairs={{0,4},{4,0},{8,12},{12,8},{16,20},{20,16},{24,28},{28,24},{32,36},... | collective-permute-start | bytes 24584 | tf_op jit(solution)/shard_map/ppermute | solution.py:518
  39.1 7.2 %collective-permute-start.5 = (f32[16,128]{1,0:T(8,128)S(1)}, f32[16,128]{1,0:T(8,128)S(1)}, u32[]{:S(2)}, u32[]{:S(2)}) collective-permute-start(f32[16,128]{1,0:T(8,128)S(1)} %get-tuple-element.54), channel_id=1, source_target_pairs={{4,8},{8,4},{12,16},{16,12},{20,24},{24,20},{28,32},{32,28},{36,40... | collective-permute-start | bytes 24584 | tf_op jit(solution)/shard_map/ppermute | solution.py:519
  42.7 3.7 %collective-permute-start.6 = (f32[16,128]{1,0:T(8,128)S(1)}, f32[16,128]{1,0:T(8,128)S(1)}, u32[]{:S(2)}, u32[]{:S(2)}) collective-permute-start(f32[16,128]{1,0:T(8,128)S(1)} %get-tuple-element.55), channel_id=1, source_target_pairs={{0,1},{1,0},{2,3},{3,2},{4,5},{5,4},{6,7},{7,6},{8,9},{9,8},{10,11... | collective-permute-start | bytes 24584 | tf_op jit(solution)/shard_map/ppermute | solution.py:520
  43.9 5.5 %collective-permute-start.7 = (f32[16,128]{1,0:T(8,128)S(1)}, f32[16,128]{1,0:T(8,128)S(1)}, u32[]{:S(2)}, u32[]{:S(2)}) collective-permute-start(f32[16,128]{1,0:T(8,128)S(1)} %get-tuple-element.56), channel_id=1, source_target_pairs={{1,2},{2,1},{5,6},{6,5},{9,10},{10,9},{13,14},{14,13},{17,18},{18,... | collective-permute-start | bytes 24584 | tf_op jit(solution)/shard_map/ppermute | solution.py:521
  61.8 6.5 %collective-permute-start.8 = (f32[16,128]{1,0:T(8,128)S(1)}, f32[16,128]{1,0:T(8,128)S(1)}, u32[]{:S(2)}, u32[]{:S(2)}) collective-permute-start(f32[16,128]{1,0:T(8,128)S(1)} %get-tuple-element.59), channel_id=1, source_target_pairs={{0,4},{4,0},{8,12},{12,8},{16,20},{20,16},{24,28},{28,24},{32,36},... | collective-permute-start | bytes 24584 | tf_op jit(solution)/shard_map/ppermute | solution.py:518
  61.9 7.1 %collective-permute-start.9 = (f32[16,128]{1,0:T(8,128)S(1)}, f32[16,128]{1,0:T(8,128)S(1)}, u32[]{:S(2)}, u32[]{:S(2)}) collective-permute-start(f32[16,128]{1,0:T(8,128)S(1)} %get-tuple-element.60), channel_id=1, source_target_pairs={{4,8},{8,4},{12,16},{16,12},{20,24},{24,20},{28,32},{32,28},{36,40... | collective-permute-start | bytes 24584 | tf_op jit(solution)/shard_map/ppermute | solution.py:519
  65.7 3.7 %collective-permute-start.10 = (f32[16,128]{1,0:T(8,128)S(1)}, f32[16,128]{1,0:T(8,128)S(1)}, u32[]{:S(2)}, u32[]{:S(2)}) collective-permute-start(f32[16,128]{1,0:T(8,128)S(1)} %get-tuple-element.61), channel_id=1, source_target_pairs={{0,1},{1,0},{2,3},{3,2},{4,5},{5,4},{6,7},{7,6},{8,9},{9,8},{10,11... | collective-permute-start | bytes 24584 | tf_op jit(solution)/shard_map/ppermute | solution.py:520
  65.8 5.5 %collective-permute-start.11 = (f32[16,128]{1,0:T(8,128)S(1)}, f32[16,128]{1,0:T(8,128)S(1)}, u32[]{:S(2)}, u32[]{:S(2)}) collective-permute-start(f32[16,128]{1,0:T(8,128)S(1)} %get-tuple-element.62), channel_id=1, source_target_pairs={{1,2},{2,1},{5,6},{6,5},{9,10},{10,9},{13,14},{14,13},{17,18},{18,... | collective-permute-start | bytes 24584 | tf_op jit(solution)/shard_map/ppermute | solution.py:521
  83.5 5.3 %collective-permute-start.12 = (f32[16,128]{1,0:T(8,128)S(1)}, f32[16,128]{1,0:T(8,128)S(1)}, u32[]{:S(2)}, u32[]{:S(2)}) collective-permute-start(f32[16,128]{1,0:T(8,128)S(1)} %get-tuple-element.67), channel_id=1, source_target_pairs={{0,4},{4,0},{8,12},{12,8},{16,20},{20,16},{24,28},{28,24},{32,36},... | collective-permute-start | bytes 24584 | tf_op jit(solution)/shard_map/ppermute | solution.py:518
  83.6 7.1 %collective-permute-start.13 = (f32[16,128]{1,0:T(8,128)S(1)}, f32[16,128]{1,0:T(8,128)S(1)}, u32[]{:S(2)}, u32[]{:S(2)}) collective-permute-start(f32[16,128]{1,0:T(8,128)S(1)} %get-tuple-element.68), channel_id=1, source_target_pairs={{4,8},{8,4},{12,16},{16,12},{20,24},{24,20},{28,32},{32,28},{36,40... | collective-permute-start | bytes 24584 | tf_op jit(solution)/shard_map/ppermute | solution.py:519
  86.2 4.4 %collective-permute-start.14 = (f32[16,128]{1,0:T(8,128)S(1)}, f32[16,128]{1,0:T(8,128)S(1)}, u32[]{:S(2)}, u32[]{:S(2)}) collective-permute-start(f32[16,128]{1,0:T(8,128)S(1)} %get-tuple-element.69), channel_id=1, source_target_pairs={{0,1},{1,0},{2,3},{3,2},{4,5},{5,4},{6,7},{7,6},{8,9},{9,8},{10,11... | collective-permute-start | bytes 24584 | tf_op jit(solution)/shard_map/ppermute | solution.py:520
  86.3 5.5 %collective-permute-start.15 = (f32[16,128]{1,0:T(8,128)S(1)}, f32[16,128]{1,0:T(8,128)S(1)}, u32[]{:S(2)}, u32[]{:S(2)}) collective-permute-start(f32[16,128]{1,0:T(8,128)S(1)} %get-tuple-element.70), channel_id=1, source_target_pairs={{1,2},{2,1},{5,6},{6,5},{9,10},{10,9},{13,14},{14,13},{17,18},{18,... | collective-permute-start | bytes 24584 | tf_op jit(solution)/shard_map/ppermute | solution.py:521
  104.0 6.3 %collective-permute-start.16 = (f32[16,128]{1,0:T(8,128)S(1)}, f32[16,128]{1,0:T(8,128)S(1)}, u32[]{:S(2)}, u32[]{:S(2)}) collective-permute-start(f32[16,128]{1,0:T(8,128)S(1)} %get-tuple-element.75), channel_id=1, source_target_pairs={{0,4},{4,0},{8,12},{12,8},{16,20},{20,16},{24,28},{28,24},{32,36},... | collective-permute-start | bytes 24584 | tf_op jit(solution)/shard_map/ppermute | solution.py:518
  104.1 7.1 %collective-permute-start.17 = (f32[16,128]{1,0:T(8,128)S(1)}, f32[16,128]{1,0:T(8,128)S(1)}, u32[]{:S(2)}, u32[]{:S(2)}) collective-permute-start(f32[16,128]{1,0:T(8,128)S(1)} %get-tuple-element.76), channel_id=1, source_target_pairs={{4,8},{8,4},{12,16},{16,12},{20,24},{24,20},{28,32},{32,28},{36,40... | collective-permute-start | bytes 24584 | tf_op jit(solution)/shard_map/ppermute | solution.py:519
  108.0 3.7 %collective-permute-start.18 = (f32[16,128]{1,0:T(8,128)S(1)}, f32[16,128]{1,0:T(8,128)S(1)}, u32[]{:S(2)}, u32[]{:S(2)}) collective-permute-start(f32[16,128]{1,0:T(8,128)S(1)} %get-tuple-element.77), channel_id=1, source_target_pairs={{0,1},{1,0},{2,3},{3,2},{4,5},{5,4},{6,7},{7,6},{8,9},{9,8},{10,11... | collective-permute-start | bytes 24584 | tf_op jit(solution)/shard_map/ppermute | solution.py:520
  108.1 5.5 %collective-permute-start.19 = (f32[16,128]{1,0:T(8,128)S(1)}, f32[16,128]{1,0:T(8,128)S(1)}, u32[]{:S(2)}, u32[]{:S(2)}) collective-permute-start(f32[16,128]{1,0:T(8,128)S(1)} %get-tuple-element.78), channel_id=1, source_target_pairs={{1,2},{2,1},{5,6},{6,5},{9,10},{10,9},{13,14},{14,13},{17,18},{18,... | collective-permute-start | bytes 24584 | tf_op jit(solution)/shard_map/ppermute | solution.py:521

commit v5 on v4

--- a/solution.py
+++ b/solution.py
@@ -156,7 +156,7 @@
     return [functools.partial(row, c) for c in range(count)]
 
 
-def gather_zones(idx_ref, tab_ref, word_ref, out_ref, groups=1):
+def make_words(tab_ref, word_ref, groups):
     steps = []
     for g in range(groups):
         x = tab_ref[3 * g * ROWS : 3 * (g + 1) * ROWS, :]
@@ -166,28 +166,36 @@
         at = 2 * g * ROWS
         word_ref[at : at + ROWS] = (q[:ROWS] << 11) | (q[2 * ROWS :] >> 10)
         word_ref[at + ROWS : at + 2 * ROWS] = (q[ROWS : 2 * ROWS] << 11) | (q[2 * ROWS :] & 1023)
+    return steps
+
+
+def gather_tile(idx_ref, word_ref, out_ref, steps, t, h):
+    r0 = pl.multiple_of(t * 8, 8)
+    lanes = slice(h * HALF, (h + 1) * HALF)
+    idx = idx_ref[pl.ds(r0, 8), lanes]
+    words = pick(table_rows(word_ref, 2 * len(steps)), idx >> 7, idx & 127, (8, HALF), jnp.int32)
+    for g, step in enumerate(steps):
+        w0, w1 = words[2 * g : 2 * g + 2]
+        back = (
+            lax.shift_right_logical(w0, 11),
+            lax.shift_right_logical(w1, 11),
+            ((w0 & 2047) << 10) | (w1 & 1023),
+        )
+        for c in range(3):
+            out_ref[3 * g + c, pl.ds(r0, 8), lanes] = (back[c] - (1 << 20)).astype(F32) * step
+
+
+def gather_zones(idx_ref, tab_ref, word_ref, out_ref, groups=1):
+    steps = make_words(tab_ref, word_ref, groups)
 
     @pl.loop(0, 8)
     def _(t):
-        r0 = pl.multiple_of(t * 8, 8)
         for h in range(2):
-            lanes = slice(h * HALF, (h + 1) * HALF)
-            idx = idx_ref[pl.ds(r0, 8), lanes]
-            words = pick(table_rows(word_ref, 2 * groups), idx >> 7, idx & 127, (8, HALF), jnp.int32)
-            for g in range(groups):
-                w0, w1 = words[2 * g : 2 * g + 2]
-                back = (
-                    lax.shift_right_logical(w0, 11),
-                    lax.shift_right_logical(w1, 11),
-                    ((w0 & 2047) << 10) | (w1 & 1023),
-                )
-                for c in range(3):
-                    value = (back[c] - (1 << 20)).astype(F32) * steps[g]
-                    out_ref[3 * g + c, pl.ds(r0, 8), lanes] = value
+            gather_tile(idx_ref, word_ref, out_ref, steps, t, h)
 
 
 def spread_rows(idx, rows):
-    here = lax.broadcasted_iota(jnp.int32, (ROWS, WIDE), 0) == (idx >> 8)
+    here = lax.broadcasted_iota(jnp.int32, (ROWS, idx.shape[1]), 0) == (idx >> 8)
     parts = []
     for x in rows:
         high = x.astype(BF).astype(F32)
@@ -356,18 +364,19 @@
         msgs[p][:, AT_FLAG:MSG] = jnp.ones((8, MSG - AT_FLAG), F32)
 
 
-def prep_kernel(vel_ref, zn_ref, _lists, _arrive, _en, _tables, vel_out, vz, lane_out, words, column):
+def prep_kernel(vel_ref, zn_ref, _lists, _arrive, _en, _tables, vel_out, vz, lane_out, words):
     nodes_in(vel_ref, vel_out)
     gather_zones(zn_ref, vel_out, words, vz)
-    column[:, :NPZ] = jnp.transpose((zn_ref[...] & 255).astype(F32), (1, 0))
-    lane = lax.broadcasted_iota(jnp.int32, (16, WIDE), 1).astype(F32)
-
-    @pl.loop(0, 16)
+    down_rows = lax.broadcasted_iota(jnp.int32, (WIDE, WIDE), 0)
+    eye = jnp.where(down_rows == lax.broadcasted_iota(jnp.int32, (WIDE, WIDE), 1), 1.0, 0.0).astype(BF)
+
+    @pl.loop(0, 8)
     def _(t):
-        r0 = pl.multiple_of(t * 16, 16)
-        rows = column[pl.ds(r0, 16), :]
-        for a in range(NPZ):
-            lane_out[a, pl.ds(r0, 16), :] = jnp.where(lane == rows[:, a : a + 1], 1.0, 0.0).astype(BF)
+        r0 = pl.multiple_of(t * 8, 8)
+        lane = zn_ref[pl.ds(r0, 8), :] & 255
+        for a in range(8):
+            hot = jnp.where(down_rows == lane[a : a + 1], 1.0, 0.0).astype(BF)
+            lane_out[r0 + a] = dot(eye, hot, NT).astype(BF)
 
 
 def first_kernel(
@@ -433,12 +442,50 @@
     return r, d, a_ref[...] + d
 
 
-def apply_mass(zn_ref, lanes, mass_ref, tables, d_ref, y_out, zone, terms, words):
-    gather_zones(zn_ref, d_ref, words, zone, COMPONENTS // 3)
-    for c in range(COMPONENTS):
-        at_points = up(entry(tables, MASS_AT, "up"), zone[c])
-        terms[c] = down(entry(tables, MASS_AT, "down"), at_points * mass_ref[...])
-    y_out[...] = scatter_zones(zn_ref, lanes, terms, COMPONENTS)
+def scatter_half(idx_ref, lane_ref, term_ref, acc_ref, t, h):
+    r0 = pl.multiple_of(t * 16, 16)
+    lanes = slice(h * HALF, (h + 1) * HALF)
+    idx = idx_ref[pl.ds(r0, 16), lanes]
+    terms = [term_ref[c, pl.ds(r0, 16), lanes] for c in range(COMPONENTS)]
+    rows = [spread_rows(idx[a : a + 1], [x[a : a + 1] for x in terms]) for a in range(16)]
+    hot = [lane_ref[r0 + a, lanes, :] for a in range(16)]
+    acc_ref[...] += dot(jnp.concatenate(rows, 1), jnp.concatenate(hot, 0))
+
+
+def zone_mass(mass_ref, tables, zone, terms, h):
+    lanes = slice(h * HALF, (h + 1) * HALF)
+    mass = jnp.concatenate([mass_ref[:, lanes]] * 2, 1)
+    for c in range(0, COMPONENTS, 2):
+        x = jnp.concatenate([zone[c, :, lanes], zone[c + 1, :, lanes]], 1)
+        out = down(entry(tables, MASS_AT, "down"), up(entry(tables, MASS_AT, "up"), x) * mass)
+        terms[c, :, lanes] = out[:, :HALF]
+        terms[c + 1, :, lanes] = out[:, HALF:]
+
+
+def apply_mass(zn_ref, lanes, mass_ref, tables, d_ref, y_out, zone, terms, words, acc):
+    steps = make_words(d_ref, words, COMPONENTS // 3)
+    acc[...] = jnp.zeros(acc.shape, F32)
+
+    @pl.loop(0, 4)
+    def _(t):
+        gather_tile(zn_ref, words, zone, steps, 2 * t, 0)
+        gather_tile(zn_ref, words, zone, steps, 2 * t + 1, 0)
+
+    zone_mass(mass_ref, tables, zone, terms, 0)
+
+    @pl.loop(0, 4)
+    def _(t):
+        scatter_half(zn_ref, lanes, terms, acc, t, 0)
+        gather_tile(zn_ref, words, zone, steps, 2 * t, 1)
+        gather_tile(zn_ref, words, zone, steps, 2 * t + 1, 1)
+
+    zone_mass(mass_ref, tables, zone, terms, 1)
+
+    @pl.loop(0, 4)
+    def _(t):
+        scatter_half(zn_ref, lanes, terms, acc, t, 1)
+
+    y_out[...] = joined(acc[...])
 
 
 def start_kernel(
@@ -536,12 +583,10 @@
         pack_kernel, (send_rows, shared_nodes, jac, mass, inv, energy), [msg] * 4 + [ints(8, HALF)],
         [(40, WIDE)] + fields, [SM, VM] + [HB] * 4, limit=61, copies=4, name="pack",
     )
-    came = []
-    for k, m in enumerate(msgs):
-        came.append(lax.ppermute(m, AXES, paired(k % 2, devices, 1 + k // 2)))
+    came = [lax.ppermute(msgs[k], AXES, paired(k % 2, devices, 1 + k // 2)) for k in (3, 2, 1, 0)][::-1]
     vel, vz, lanes = call(
         prep_kernel, (velocity, zone_nodes, lists, arrive_rows, energy, force_tables),
-        [node, zone(3), half(NPZ, WIDE, WIDE)], [words(1), (WIDE, HALF)], [VM, VM, VM, SM, VM, VM], name="prep",
+        [node, zone(3), half(NPZ, WIDE, WIDE)], [words(1)], [VM, VM, VM, SM, VM, VM], name="prep",
     )
     jac, mass, inv, en, ehalf, y, *sends = call(
         first_kernel,
@@ -550,7 +595,7 @@
         [(48, WIDE), (48, MSG), zone(COMPONENTS + 1), (QP, WIDE)],
         [SM] + [VM] * 13, name="force_one",
     )
-    scratch = [zone(COMPONENTS), zone(COMPONENTS), words(COMPONENTS // 3)]
+    scratch = [zone(COMPONENTS), zone(COMPONENTS), words(COMPONENTS // 3), (2 * COMPONENTS * ROWS, WIDE)]
     tail = (lists, zone_nodes, lanes, mass, mass_tables)
     ib, r, d, y, *sends = call(
         start_kernel, (*exchange(sends), y, *tail), [(ROWS, WIDE), nodes, nodes, nodes] + send, scratch,

time: 120 us -> 113 us (0.942)
  Pallas kernels: 65.1 us -> 58.3 us
    pallas_call x7, Pallas kernels: 65.1 us -> 58.3 us  [call(): pl.pallas_call(kernel, out_shape=[shape_of(s) for s in outs], in_specs=sp...]
where the time goes in v5:
time: 113 us; the launch traced here: 112 us
  Pallas kernels  58.3 us (52%)
  starting transfers between devices  37.6 us (33%)
  waiting for transfers between devices  12.6 us (11%)
  local copies, waits for them, and re-layouts  2.95 us (3%)
    pallas_call x7, Pallas kernels, call(): pl.pallas_call(kernel, out_shape=[shape_of(s) for s in outs], in_specs=sp...  58.3 us
    ppermute x4, starting transfers between devices, exchange(): lax.ppermute(sends[1], 'curve', paired(1, n_curve))  13.9 us
    ppermute x4, starting transfers between devices, per_device(): lax.ppermute(msgs[k], AXES, paired(k % 2, devices, 1 + k // 2))  12.4 us
    ppermute x4, starting transfers between devices, exchange(): lax.ppermute(sends[3], 'split', paired(1, n_split))  9.51 us
    ppermute x4, waiting for transfers between devices, exchange(): lax.ppermute(sends[3], 'split', paired(1, n_split))  8.09 us
    ppermute x4, waiting for transfers between devices, exchange(): lax.ppermute(sends[1], 'curve', paired(1, n_curve))  3.45 us
    unnamed x22, local copies, waits for them, and re-layouts  2.95 us
  transfers between devices with their start and end apart: 20, of which 10 were waited for; matrix products, arithmetic and copies ran while one was open for 0% of the time, Pallas kernels for 7%

profile of v5, /device:TPU:26, one launch (start us, length us, event | category | flops | bytes accessed | tf_op | source)
XLA Modules:
  0.0 112.4 jit_solution(17952691831678553977)
XLA Ops:
  0.7 4.6 %pack.1 = (f32[8,3712]{1,0:T(8,128)}, f32[8,3712]{1,0:T(8,128)}, f32[8,3712]{1,0:T(8,128)}, f32[8,3712]{1,0:T(8,128)}, s32[8,128]{1,0:T(8,128)}) custom-call(s32[1,36]{1,0:T(1,128)} %send_ref.1, s32[1,4,256]{2,1,0:T(4,128)} %shared_ref.1, f32[1944,256]{1,0:T(8,128)} %jac_ref.1, f32[216,256]{1,0:T(8,128)} %mass_ref.1, f32[729,256]{1,0:T(8,128)} %inv_ref.1, ...), custom_call_target="tpu_custom_call" | custom-call | tf_op jit(solution)/shard_map/pack/pallas_call | solution.py:546
  5.3 0.6 collective-permute-start
  6.0 4.1 %collective-permute-start.1 = (f32[8,3712]{1,0:T(8,128)}, f32[8,3712]{1,0:T(8,128)S(1)}, u32[]{:S(2)}, u32[]{:S(2)}) collective-permute-start(f32[8,3712]{1,0:T(8,128)} %get-tuple-element.47), channel_id=1, source_target_pairs={{1,2},{2,1},{3,4},{4,3},{5,6},{6,5},{7,8},{8,7},{9,10},{10,9},{11,... | collective-permute-start | bytes 356360 | tf_op jit(solution)/shard_map/ppermute | solution.py:586
  10.0 0.6 collective-permute-start.2
  10.7 7.1 %collective-permute-start.3 = (f32[8,3712]{1,0:T(8,128)}, f32[8,3712]{1,0:T(8,128)S(1)}, u32[]{:S(2)}, u32[]{:S(2)}) collective-permute-start(f32[8,3712]{1,0:T(8,128)} %get-tuple-element.49), channel_id=1, source_target_pairs={{2,4},{4,2},{3,5},{5,3},{6,8},{8,6},{7,9},{9,7},{10,12},{12,10},{1... | collective-permute-start | bytes 356360 | tf_op jit(solution)/shard_map/ppermute | solution.py:586
  17.8 0.7 copy-done.7
  18.5 7.4 %prep.1 = (f32[96,256]{1,0:T(8,128)S(1)}, f32[3,64,256]{2,1,0:T(8,128)S(1)}, bf16[64,256,256]{2,1,0:T(8,128)(2,1)S(1)}) custom-call(f32[3,7936]{1,0:T(4,128)S(1)} %copy-done.9, s32[64,256]{1,0:T(8,128)S(1)} %copy-done.3, s32[8,128]{1,0:T(8,128)S(1)} %copy-done.7, s32[1,36]{1,0:T(1,128)S(1)} %copy-done.10, f32[27,256]{1,0:T(8,128)S(1)} %copy-done.6, ...), custom_call_target="tpu_custom_call" | custom-call | tf_op jit(solution)/shard_map/prep/pallas_call | solution.py:546
  26.0 1.5 %copy-done.1 = f32[1944,256]{1,0:T(8,128)S(1)} copy-done((f32[1944,256]{1,0:T(8,128)S(1)}, f32[1944,256]{1,0:T(8,128)}, u32[]{:S(2)}) %copy-start.1) | copy-done | bytes 1990680
  27.5 0.7 copy-done.8
  28.2 10.1 %force_one.1 = (f32[1944,256]{1,0:T(8,128)S(1)}, f32[216,256]{1,0:T(8,128)S(1)}, f32[729,256]{1,0:T(8,128)S(1)}, f32[27,256]{1,0:T(8,128)S(1)}, f32[27,256]{1,0:...) custom-call(s32[1,36]{1,0:T(1,128)S(1)} %copy-done.10, ...), custom_call_target="tpu_custom_call" | custom-call | tf_op jit(solution)/shard_map/force_one/pallas_call | solution.py:546
  38.4 3.6 %collective-permute-start.5 = (f32[16,128]{1,0:T(8,128)S(1)}, f32[16,128]{1,0:T(8,128)S(1)}, u32[]{:S(2)}, u32[]{:S(2)}) collective-permute-start(f32[16,128]{1,0:T(8,128)S(1)} %get-tuple-element.54), channel_id=1, source_target_pairs={{4,8},{8,4},{12,16},{16,12},{20,24},{24,20},{28,32},{32,28},{36,40... | collective-permute-start | bytes 24584 | tf_op jit(solution)/shard_map/ppermute | solution.py:566
  42.0 1.2 %collective-permute-start.6 = (f32[16,128]{1,0:T(8,128)S(1)}, f32[16,128]{1,0:T(8,128)S(1)}, u32[]{:S(2)}, u32[]{:S(2)}) collective-permute-start(f32[16,128]{1,0:T(8,128)S(1)} %get-tuple-element.55), channel_id=1, source_target_pairs={{0,1},{1,0},{2,3},{3,2},{4,5},{5,4},{6,7},{7,6},{8,9},{9,8},{10,11... | collective-permute-start | bytes 24584 | tf_op jit(solution)/shard_map/ppermute | solution.py:567
  43.2 2.4 %collective-permute-start.7 = (f32[16,128]{1,0:T(8,128)S(1)}, f32[16,128]{1,0:T(8,128)S(1)}, u32[]{:S(2)}, u32[]{:S(2)}) collective-permute-start(f32[16,128]{1,0:T(8,128)S(1)} %get-tuple-element.56), channel_id=1, source_target_pairs={{1,2},{2,1},{5,6},{6,5},{9,10},{10,9},{13,14},{14,13},{17,18},{18,... | collective-permute-start | bytes 24584 | tf_op jit(solution)/shard_map/ppermute | solution.py:568
  45.8 3.0 %collective-permute-done.7.g3 = f32[16,128]{1,0:T(8,128)S(1)} collective-permute-done((f32[16,128]{1,0:T(8,128)S(1)}, f32[16,128]{1,0:T(8,128)S(1)}, u32[]{:S(2)}, u32[]{:S(2)}) %collective-permute-start.7) | collective-permute-done | bytes 8224 | tf_op jit(solution)/shard_map/ppermute | solution.py:568
  48.7 10.2 %mass_start.1 = (f32[32,256]{1,0:T(8,128)S(1)}, f32[192,256]{1,0:T(8,128)S(1)}, f32[192,256]{1,0:T(8,128)S(1)}, f32[192,256]{1,0:T(8,128)S(1)}, f32[16,128]{1,0:...) custom-call(f32[16,128]{1,0:T(8,128)S(1)} %collective-permute-done.4.g0, ...), custom_call_target="tpu_custom_call" | custom-call | tf_op jit(solution)/shard_map/mass_start/pallas_call | solution.py:546
  59.1 3.8 %collective-permute-start.9 = (f32[16,128]{1,0:T(8,128)S(1)}, f32[16,128]{1,0:T(8,128)S(1)}, u32[]{:S(2)}, u32[]{:S(2)}) collective-permute-start(f32[16,128]{1,0:T(8,128)S(1)} %get-tuple-element.60), channel_id=1, source_target_pairs={{4,8},{8,4},{12,16},{16,12},{20,24},{24,20},{28,32},{32,28},{36,40... | collective-permute-start | bytes 24584 | tf_op jit(solution)/shard_map/ppermute | solution.py:566
  62.9 2.5 %collective-permute-start.11 = (f32[16,128]{1,0:T(8,128)S(1)}, f32[16,128]{1,0:T(8,128)S(1)}, u32[]{:S(2)}, u32[]{:S(2)}) collective-permute-start(f32[16,128]{1,0:T(8,128)S(1)} %get-tuple-element.62), channel_id=1, source_target_pairs={{1,2},{2,1},{5,6},{6,5},{9,10},{10,9},{13,14},{14,13},{17,18},{18,... | collective-permute-start | bytes 24584 | tf_op jit(solution)/shard_map/ppermute | solution.py:568
  65.4 0.7 collective-permute-done.9.g1
  66.1 0.4 collective-permute-done.10.g2
  66.6 1.9 %collective-permute-done.11.g3 = f32[16,128]{1,0:T(8,128)S(1)} collective-permute-done((f32[16,128]{1,0:T(8,128)S(1)}, f32[16,128]{1,0:T(8,128)S(1)}, u32[]{:S(2)}, u32[]{:S(2)}) %collective-permute-start.11) | collective-permute-done | bytes 8224 | tf_op jit(solution)/shard_map/ppermute | solution.py:568
  68.5 10.1 %mass_sweep.2 = (f32[192,256]{1,0:T(8,128)S(1)}, f32[192,256]{1,0:T(8,128)S(1)}, f32[192,256]{1,0:T(8,128)S(1)}, f32[192,256]{1,0:T(8,128)S(1)}, f32[16,128]{1,0...) custom-call(f32[16,128]{1,0:T(8,128)S(1)} %collective-permute-done.8.g0, ...), custom_call_target="tpu_custom_call" | custom-call | tf_op jit(solution)/shard_map/mass_sweep/pallas_call | solution.py:546
  78.7 2.7 %collective-permute-start.13 = (f32[16,128]{1,0:T(8,128)S(1)}, f32[16,128]{1,0:T(8,128)S(1)}, u32[]{:S(2)}, u32[]{:S(2)}) collective-permute-start(f32[16,128]{1,0:T(8,128)S(1)} %get-tuple-element.68), channel_id=1, source_target_pairs={{4,8},{8,4},{12,16},{16,12},{20,24},{24,20},{28,32},{32,28},{36,40... | collective-permute-start | bytes 24584 | tf_op jit(solution)/shard_map/ppermute | solution.py:566
  81.6 2.4 %collective-permute-start.15 = (f32[16,128]{1,0:T(8,128)S(1)}, f32[16,128]{1,0:T(8,128)S(1)}, u32[]{:S(2)}, u32[]{:S(2)}) collective-permute-start(f32[16,128]{1,0:T(8,128)S(1)} %get-tuple-element.70), channel_id=1, source_target_pairs={{1,2},{2,1},{5,6},{6,5},{9,10},{10,9},{13,14},{14,13},{17,18},{18,... | collective-permute-start | bytes 24584 | tf_op jit(solution)/shard_map/ppermute | solution.py:568
  83.9 1.8 %collective-permute-done.13.g1 = f32[16,128]{1,0:T(8,128)S(1)} collective-permute-done((f32[16,128]{1,0:T(8,128)S(1)}, f32[16,128]{1,0:T(8,128)S(1)}, u32[]{:S(2)}, u32[]{:S(2)}) %collective-permute-start.13) | collective-permute-done | bytes 8224 | tf_op jit(solution)/shard_map/ppermute | solution.py:566
  85.8 1.3 %collective-permute-done.15.g3 = f32[16,128]{1,0:T(8,128)S(1)} collective-permute-done((f32[16,128]{1,0:T(8,128)S(1)}, f32[16,128]{1,0:T(8,128)S(1)}, u32[]{:S(2)}, u32[]{:S(2)}) %collective-permute-start.15) | collective-permute-done | bytes 8224 | tf_op jit(solution)/shard_map/ppermute | solution.py:568
  87.1 10.1 %mass_sweep.3 = (f32[192,256]{1,0:T(8,128)S(1)}, f32[192,256]{1,0:T(8,128)S(1)}, f32[192,256]{1,0:T(8,128)S(1)}, f32[192,256]{1,0:T(8,128)S(1)}, f32[16,128]{1,0...) custom-call(f32[16,128]{1,0:T(8,128)S(1)} %collective-permute-done.12.g0, ...), custom_call_target="tpu_custom_call" | custom-call | tf_op jit(solution)/shard_map/mass_sweep/pallas_call | solution.py:546
  97.3 3.8 %collective-permute-start.17 = (f32[16,128]{1,0:T(8,128)S(1)}, f32[16,128]{1,0:T(8,128)S(1)}, u32[]{:S(2)}, u32[]{:S(2)}) collective-permute-start(f32[16,128]{1,0:T(8,128)S(1)} %get-tuple-element.76), channel_id=1, source_target_pairs={{4,8},{8,4},{12,16},{16,12},{20,24},{24,20},{28,32},{32,28},{36,40... | collective-permute-start | bytes 24584 | tf_op jit(solution)/shard_map/ppermute | solution.py:566
  101.2 2.3 %collective-permute-start.19 = (f32[16,128]{1,0:T(8,128)S(1)}, f32[16,128]{1,0:T(8,128)S(1)}, u32[]{:S(2)}, u32[]{:S(2)}) collective-permute-start(f32[16,128]{1,0:T(8,128)S(1)} %get-tuple-element.78), channel_id=1, source_target_pairs={{1,2},{2,1},{5,6},{6,5},{9,10},{10,9},{13,14},{14,13},{17,18},{18,... | collective-permute-start | bytes 24584 | tf_op jit(solution)/shard_map/ppermute | solution.py:568
  103.5 0.9 collective-permute-done.17.g1
  104.4 0.4 collective-permute-done.18.g2
  104.8 1.9 %collective-permute-done.19.g3 = f32[16,128]{1,0:T(8,128)S(1)} collective-permute-done((f32[16,128]{1,0:T(8,128)S(1)}, f32[16,128]{1,0:T(8,128)S(1)}, u32[]{:S(2)}, u32[]{:S(2)}) %collective-permute-start.19) | collective-permute-done | bytes 8224 | tf_op jit(solution)/shard_map/ppermute | solution.py:568
  106.7 5.7 %force_two.1 = (f32[27,256]{1,0:T(8,128)}, f32[3,7936]{1,0:T(4,128)}) custom-call(f32[16,128]{1,0:T(8,128)S(1)} %collective-permute-done.16.g0, f32[16,128]{1,0:T(8,128)S(1)} %collective-permute-done.17.g1, f32[16,128]{1,0:T(8,128)S(1)} %collective-permute-done.18.g2, f32[16,128]{1,0:T(8,128)S(1)} %collective-permute-done.19.g3, ...), custom_call_target="tpu_custom_call" | custom-call | tf_op jit(solution)/shard_map/force_two/pallas_call | solution.py:546
  (37 shorter events, 0.8 us)
Async XLA Ops:
  0.6 17.2 %copy-start = (bf16[2528,256]{1,0:T(8,128)(2,1)S(1)}, bf16[2528,256]{1,0:T(8,128)(2,1)}, u32[]{:S(2)}) copy-start(bf16[2528,256]{1,0:T(8,128)(2,1)} %constant.4.clone._tables.tables) | copy-start | bytes 3883012
  0.6 17.2 %copy-start.6 = (f32[27,256]{1,0:T(8,128)S(1)}, f32[27,256]{1,0:T(8,128)}, u32[]{:S(2)}) copy-start(f32[27,256]{1,0:T(8,128)} %en_ref.1) | copy-start | bytes 82948
  0.7 25.3 %copy-start.2 = (f32[729,256]{1,0:T(8,128)S(1)}, f32[729,256]{1,0:T(8,128)}, u32[]{:S(2)}) copy-start(f32[729,256]{1,0:T(8,128)} %inv_ref.1) | copy-start | bytes 2239492
  0.7 25.3 %copy-start.5 = (f32[216,256]{1,0:T(8,128)S(1)}, f32[216,256]{1,0:T(8,128)}, u32[]{:S(2)}) copy-start(f32[216,256]{1,0:T(8,128)} %mass_ref.1) | copy-start | bytes 663556
  0.7 17.1 %copy-start.3 = (s32[64,256]{1,0:T(8,128)S(1)}, s32[64,256]{1,0:T(8,128)}, u32[]{:S(2)}) copy-start(s32[64,256]{1,0:T(8,128)} %zn.7) | copy-start | bytes 196612
  0.7 17.1 %copy-start.10 = (s32[1,36]{1,0:T(1,128)S(1)}, s32[1,36]{1,0:T(1,128)}, u32[]{:S(2)}) copy-start(s32[1,36]{1,0:T(1,128)} %arrive_ref.1) | copy-start | bytes 436
  0.7 17.1 %copy-start.9 = (f32[3,7936]{1,0:T(4,128)S(1)}, f32[3,7936]{1,0:T(4,128)}, u32[]{:S(2)}) copy-start(f32[3,7936]{1,0:T(4,128)} %vel_ref.1) | copy-start | bytes 285700
  5.3 20.6 %collective-permute-start = (f32[8,3712]{1,0:T(8,128)}, f32[8,3712]{1,0:T(8,128)S(1)}, u32[]{:S(2)}, u32[]{:S(2)}) collective-permute-start(f32[8,3712]{1,0:T(8,128)} %get-tuple-element.46), channel_id=1, source_target_pairs={{0,1},{1,0},{2,3},{3,2},{4,5},{5,4},{6,7},{7,6},{8,9},{9,8},{10,11... | collective-permute-start | bytes 356360 | tf_op jit(solution)/shard_map/ppermute | solution.py:586
  6.0 20.0 %collective-permute-start.1 = (f32[8,3712]{1,0:T(8,128)}, f32[8,3712]{1,0:T(8,128)S(1)}, u32[]{:S(2)}, u32[]{:S(2)}) collective-permute-start(f32[8,3712]{1,0:T(8,128)} %get-tuple-element.47), channel_id=1, source_target_pairs={{1,2},{2,1},{3,4},{4,3},{5,6},{6,5},{7,8},{8,7},{9,10},{10,9},{11,... | collective-permute-start | bytes 356360 | tf_op jit(solution)/shard_map/ppermute | solution.py:586
  10.0 15.9 %collective-permute-start.2 = (f32[8,3712]{1,0:T(8,128)}, f32[8,3712]{1,0:T(8,128)S(1)}, u32[]{:S(2)}, u32[]{:S(2)}) collective-permute-start(f32[8,3712]{1,0:T(8,128)} %get-tuple-element.48), channel_id=1, source_target_pairs={{0,2},{2,0},{1,3},{3,1},{4,6},{6,4},{5,7},{7,5},{8,10},{10,8},{9,1... | collective-permute-start | bytes 356360 | tf_op jit(solution)/shard_map/ppermute | solution.py:586
  10.7 15.3 %collective-permute-start.3 = (f32[8,3712]{1,0:T(8,128)}, f32[8,3712]{1,0:T(8,128)S(1)}, u32[]{:S(2)}, u32[]{:S(2)}) collective-permute-start(f32[8,3712]{1,0:T(8,128)} %get-tuple-element.49), channel_id=1, source_target_pairs={{2,4},{4,2},{3,5},{5,3},{6,8},{8,6},{7,9},{9,7},{10,12},{12,10},{1... | collective-permute-start | bytes 356360 | tf_op jit(solution)/shard_map/ppermute | solution.py:586
  17.8 0.7 copy-start.7
  26.0 1.6 %copy-start.1 = (f32[1944,256]{1,0:T(8,128)S(1)}, f32[1944,256]{1,0:T(8,128)}, u32[]{:S(2)}) copy-start(f32[1944,256]{1,0:T(8,128)} %jac_ref.1) | copy-start | bytes 5971972
  27.5 0.7 copy-start.8
  28.2 20.5 %copy-start.4 = (bf16[352,256]{1,0:T(8,128)(2,1)S(1)}, bf16[352,256]{1,0:T(8,128)(2,1)}, u32[]{:S(2)}) copy-start(bf16[352,256]{1,0:T(8,128)(2,1)} %constant.5.clone.tables) | copy-start | bytes 540676
  38.3 7.2 %collective-permute-start.4 = (f32[16,128]{1,0:T(8,128)S(1)}, f32[16,128]{1,0:T(8,128)S(1)}, u32[]{:S(2)}, u32[]{:S(2)}) collective-permute-start(f32[16,128]{1,0:T(8,128)S(1)} %get-tuple-element.53), channel_id=1, source_target_pairs={{0,4},{4,0},{8,12},{12,8},{16,20},{20,16},{24,28},{28,24},{32,36},... | collective-permute-start | bytes 24584 | tf_op jit(solution)/shard_map/ppermute | solution.py:565
  38.4 7.2 %collective-permute-start.5 = (f32[16,128]{1,0:T(8,128)S(1)}, f32[16,128]{1,0:T(8,128)S(1)}, u32[]{:S(2)}, u32[]{:S(2)}) collective-permute-start(f32[16,128]{1,0:T(8,128)S(1)} %get-tuple-element.54), channel_id=1, source_target_pairs={{4,8},{8,4},{12,16},{16,12},{20,24},{24,20},{28,32},{32,28},{36,40... | collective-permute-start | bytes 24584 | tf_op jit(solution)/shard_map/ppermute | solution.py:566
  42.0 3.7 %collective-permute-start.6 = (f32[16,128]{1,0:T(8,128)S(1)}, f32[16,128]{1,0:T(8,128)S(1)}, u32[]{:S(2)}, u32[]{:S(2)}) collective-permute-start(f32[16,128]{1,0:T(8,128)S(1)} %get-tuple-element.55), channel_id=1, source_target_pairs={{0,1},{1,0},{2,3},{3,2},{4,5},{5,4},{6,7},{7,6},{8,9},{9,8},{10,11... | collective-permute-start | bytes 24584 | tf_op jit(solution)/shard_map/ppermute | solution.py:567
  43.2 5.5 %collective-permute-start.7 = (f32[16,128]{1,0:T(8,128)S(1)}, f32[16,128]{1,0:T(8,128)S(1)}, u32[]{:S(2)}, u32[]{:S(2)}) collective-permute-start(f32[16,128]{1,0:T(8,128)S(1)} %get-tuple-element.56), channel_id=1, source_target_pairs={{1,2},{2,1},{5,6},{6,5},{9,10},{10,9},{13,14},{14,13},{17,18},{18,... | collective-permute-start | bytes 24584 | tf_op jit(solution)/shard_map/ppermute | solution.py:568
  59.0 6.5 %collective-permute-start.8 = (f32[16,128]{1,0:T(8,128)S(1)}, f32[16,128]{1,0:T(8,128)S(1)}, u32[]{:S(2)}, u32[]{:S(2)}) collective-permute-start(f32[16,128]{1,0:T(8,128)S(1)} %get-tuple-element.59), channel_id=1, source_target_pairs={{0,4},{4,0},{8,12},{12,8},{16,20},{20,16},{24,28},{28,24},{32,36},... | collective-permute-start | bytes 24584 | tf_op jit(solution)/shard_map/ppermute | solution.py:565
  59.1 7.1 %collective-permute-start.9 = (f32[16,128]{1,0:T(8,128)S(1)}, f32[16,128]{1,0:T(8,128)S(1)}, u32[]{:S(2)}, u32[]{:S(2)}) collective-permute-start(f32[16,128]{1,0:T(8,128)S(1)} %get-tuple-element.60), channel_id=1, source_target_pairs={{4,8},{8,4},{12,16},{16,12},{20,24},{24,20},{28,32},{32,28},{36,40... | collective-permute-start | bytes 24584 | tf_op jit(solution)/shard_map/ppermute | solution.py:566
  62.9 3.7 %collective-permute-start.10 = (f32[16,128]{1,0:T(8,128)S(1)}, f32[16,128]{1,0:T(8,128)S(1)}, u32[]{:S(2)}, u32[]{:S(2)}) collective-permute-start(f32[16,128]{1,0:T(8,128)S(1)} %get-tuple-element.61), channel_id=1, source_target_pairs={{0,1},{1,0},{2,3},{3,2},{4,5},{5,4},{6,7},{7,6},{8,9},{9,8},{10,11... | collective-permute-start | bytes 24584 | tf_op jit(solution)/shard_map/ppermute | solution.py:567
  62.9 5.5 %collective-permute-start.11 = (f32[16,128]{1,0:T(8,128)S(1)}, f32[16,128]{1,0:T(8,128)S(1)}, u32[]{:S(2)}, u32[]{:S(2)}) collective-permute-start(f32[16,128]{1,0:T(8,128)S(1)} %get-tuple-element.62), channel_id=1, source_target_pairs={{1,2},{2,1},{5,6},{6,5},{9,10},{10,9},{13,14},{14,13},{17,18},{18,... | collective-permute-start | bytes 24584 | tf_op jit(solution)/shard_map/ppermute | solution.py:568
  78.6 5.3 %collective-permute-start.12 = (f32[16,128]{1,0:T(8,128)S(1)}, f32[16,128]{1,0:T(8,128)S(1)}, u32[]{:S(2)}, u32[]{:S(2)}) collective-permute-start(f32[16,128]{1,0:T(8,128)S(1)} %get-tuple-element.67), channel_id=1, source_target_pairs={{0,4},{4,0},{8,12},{12,8},{16,20},{20,16},{24,28},{28,24},{32,36},... | collective-permute-start | bytes 24584 | tf_op jit(solution)/shard_map/ppermute | solution.py:565
  78.7 7.1 %collective-permute-start.13 = (f32[16,128]{1,0:T(8,128)S(1)}, f32[16,128]{1,0:T(8,128)S(1)}, u32[]{:S(2)}, u32[]{:S(2)}) collective-permute-start(f32[16,128]{1,0:T(8,128)S(1)} %get-tuple-element.68), channel_id=1, source_target_pairs={{4,8},{8,4},{12,16},{16,12},{20,24},{24,20},{28,32},{32,28},{36,40... | collective-permute-start | bytes 24584 | tf_op jit(solution)/shard_map/ppermute | solution.py:566
  81.5 4.3 %collective-permute-start.14 = (f32[16,128]{1,0:T(8,128)S(1)}, f32[16,128]{1,0:T(8,128)S(1)}, u32[]{:S(2)}, u32[]{:S(2)}) collective-permute-start(f32[16,128]{1,0:T(8,128)S(1)} %get-tuple-element.69), channel_id=1, source_target_pairs={{0,1},{1,0},{2,3},{3,2},{4,5},{5,4},{6,7},{7,6},{8,9},{9,8},{10,11... | collective-permute-start | bytes 24584 | tf_op jit(solution)/shard_map/ppermute | solution.py:567
  81.6 5.5 %collective-permute-start.15 = (f32[16,128]{1,0:T(8,128)S(1)}, f32[16,128]{1,0:T(8,128)S(1)}, u32[]{:S(2)}, u32[]{:S(2)}) collective-permute-start(f32[16,128]{1,0:T(8,128)S(1)} %get-tuple-element.70), channel_id=1, source_target_pairs={{1,2},{2,1},{5,6},{6,5},{9,10},{10,9},{13,14},{14,13},{17,18},{18,... | collective-permute-start | bytes 24584 | tf_op jit(solution)/shard_map/ppermute | solution.py:568
  97.2 6.3 %collective-permute-start.16 = (f32[16,128]{1,0:T(8,128)S(1)}, f32[16,128]{1,0:T(8,128)S(1)}, u32[]{:S(2)}, u32[]{:S(2)}) collective-permute-start(f32[16,128]{1,0:T(8,128)S(1)} %get-tuple-element.75), channel_id=1, source_target_pairs={{0,4},{4,0},{8,12},{12,8},{16,20},{20,16},{24,28},{28,24},{32,36},... | collective-permute-start | bytes 24584 | tf_op jit(solution)/shard_map/ppermute | solution.py:565
  97.3 7.1 %collective-permute-start.17 = (f32[16,128]{1,0:T(8,128)S(1)}, f32[16,128]{1,0:T(8,128)S(1)}, u32[]{:S(2)}, u32[]{:S(2)}) collective-permute-start(f32[16,128]{1,0:T(8,128)S(1)} %get-tuple-element.76), channel_id=1, source_target_pairs={{4,8},{8,4},{12,16},{16,12},{20,24},{24,20},{28,32},{32,28},{36,40... | collective-permute-start | bytes 24584 | tf_op jit(solution)/shard_map/ppermute | solution.py:566
  101.1 3.7 %collective-permute-start.18 = (f32[16,128]{1,0:T(8,128)S(1)}, f32[16,128]{1,0:T(8,128)S(1)}, u32[]{:S(2)}, u32[]{:S(2)}) collective-permute-start(f32[16,128]{1,0:T(8,128)S(1)} %get-tuple-element.77), channel_id=1, source_target_pairs={{0,1},{1,0},{2,3},{3,2},{4,5},{5,4},{6,7},{7,6},{8,9},{9,8},{10,11... | collective-permute-start | bytes 24584 | tf_op jit(solution)/shard_map/ppermute | solution.py:567
  101.2 5.5 %collective-permute-start.19 = (f32[16,128]{1,0:T(8,128)S(1)}, f32[16,128]{1,0:T(8,128)S(1)}, u32[]{:S(2)}, u32[]{:S(2)}) collective-permute-start(f32[16,128]{1,0:T(8,128)S(1)} %get-tuple-element.78), channel_id=1, source_target_pairs={{1,2},{2,1},{5,6},{6,5},{9,10},{10,9},{13,14},{14,13},{17,18},{18,... | collective-permute-start | bytes 24584 | tf_op jit(solution)/shard_map/ppermute | solution.py:568

commit v6 on v5

--- a/solution.py
+++ b/solution.py
@@ -312,18 +312,22 @@
 
 def sent_block(k):
     s = split_side()
-    return (s % 2, 1 - s % 2, 2 + s // 2, 3 - s // 2)[k]
+    return (3 - s // 2, 2 + s // 2, 1 - s % 2, s % 2)[k]
 
 
 def landing_block(k):
     s = split_side()
-    return (1 - s % 2, s % 2, 3 - s // 2, 2 + s // 2)[k]
+    return (2 + s // 2, 3 - s // 2, s % 2, 1 - s % 2)[k]
 
 
 def pack_kernel(send_ref, shared_ref, jac_hbm, mass_hbm, inv_hbm, en_hbm, *refs):
     msgs, (lists, oh, jac_ref, mass_ref, inv_ref, en_ref, sems) = refs[:4], refs[4:]
+    chunks = [(i, min(2 * WIDE, 9 * QP - i)) for i in range(0, 9 * QP, 2 * WIDE)]
     copies = fetch(
-        ((mass_hbm, mass_ref), (inv_hbm, inv_ref), (en_hbm, en_ref), (jac_hbm, jac_ref)), sems
+        ((mass_hbm, mass_ref), (en_hbm, en_ref))
+        + tuple((jac_hbm.at[pl.ds(i, n), :], jac_ref.at[pl.ds(i, n), :]) for i, n in chunks)
+        + ((inv_hbm, inv_ref),),
+        sems,
     )
     lane = lax.broadcasted_iota(jnp.int32, (1, WIDE), 1)
     for k in range(4):
@@ -352,12 +356,12 @@
                 ]
                 done += step
 
-    places = ((mass_ref, AT_MASS), (inv_ref, AT_INV), (en_ref, AT_EN), (jac_ref, AT_JAC))
-    for copy, (ref, at) in zip(copies, places):
+    places = [(mass_ref, AT_MASS, 0, QP), (en_ref, AT_EN, 0, LD)]
+    places += [(jac_ref, AT_JAC, i, n) for i, n in chunks] + [(inv_ref, AT_INV, 0, LD * LD)]
+    for copy, (ref, at, first, total) in zip(copies, places):
         copy.wait()
-        total = ref.shape[0]
-        for i in range(0, total, WIDE):
-            n = min(WIDE, total - i)
+        for i in range(first, first + total, WIDE):
+            n = min(WIDE, first + total - i)
             parts = split3(ref[i : i + n, :])
             put(at + i, n, sum(dot(hot, part, NT) for part in parts))
     for p in range(4):
@@ -366,7 +370,7 @@
 
 def prep_kernel(vel_ref, zn_ref, _lists, _arrive, _en, _tables, vel_out, vz, lane_out, words):
     nodes_in(vel_ref, vel_out)
-    gather_zones(zn_ref, vel_out, words, vz)
+    steps = make_words(vel_out, words, 1)
     down_rows = lax.broadcasted_iota(jnp.int32, (WIDE, WIDE), 0)
     eye = jnp.where(down_rows == lax.broadcasted_iota(jnp.int32, (WIDE, WIDE), 1), 1.0, 0.0).astype(BF)
 
@@ -377,6 +381,8 @@
         for a in range(8):
             hot = jnp.where(down_rows == lane[a : a + 1], 1.0, 0.0).astype(BF)
             lane_out[r0 + a] = dot(eye, hot, NT).astype(BF)
+        for h in range(2):
+            gather_tile(zn_ref, words, vz, steps, t, h)
 
 
 def first_kernel(
@@ -541,7 +547,7 @@
     return s if isinstance(s, jax.ShapeDtypeStruct) else jax.ShapeDtypeStruct(s, F32)
 
 
-def call(kernel, args, outs, scratch=(), specs=None, limit=16, copies=0, name=None):
+def call(kernel, args, outs, scratch=(), specs=None, limit=16, copies=0, us=10, name=None):
     scratch = [pltpu.VMEM(shape_of(s).shape, shape_of(s).dtype) for s in scratch]
     return pl.pallas_call(
         kernel,
@@ -550,6 +556,7 @@
         out_specs=[VM] * len(outs),
         scratch_shapes=scratch + ([pltpu.SemaphoreType.DMA((copies,))] if copies else []),
         compiler_params=pltpu.CompilerParams(vmem_limit_bytes=limit * 1024 * 1024),
+        cost_estimate=pl.CostEstimate(flops=us * 10**9, bytes_accessed=us * 10**5, transcendentals=0),
         name=name,
     )(*args)
 
@@ -581,9 +588,10 @@
     words = lambda groups: ints(2 * groups * ROWS, WIDE)
     *msgs, lists = call(
         pack_kernel, (send_rows, shared_nodes, jac, mass, inv, energy), [msg] * 4 + [ints(8, HALF)],
-        [(40, WIDE)] + fields, [SM, VM] + [HB] * 4, limit=61, copies=4, name="pack",
-    )
-    came = [lax.ppermute(msgs[k], AXES, paired(k % 2, devices, 1 + k // 2)) for k in (3, 2, 1, 0)][::-1]
+        [(40, WIDE)] + fields, [SM, VM] + [HB] * 4, limit=61, copies=7, us=4, name="pack",
+    )
+    rounds = ((1, 2), (0, 2), (1, 1), (0, 1))
+    came = [lax.ppermute(m, AXES, paired(first, devices, hop)) for m, (first, hop) in zip(msgs, rounds)]
     vel, vz, lanes = call(
         prep_kernel, (velocity, zone_nodes, lists, arrive_rows, energy, force_tables),
         [node, zone(3), half(NPZ, WIDE, WIDE)], [words(1)], [VM, VM, VM, SM, VM, VM], name="prep",

time: 113 us -> 108 us (0.956)
  waiting for transfers between devices: 12.6 us -> 7.42 us
  starting transfers between devices: 37.6 us -> 42.3 us
  Pallas kernels: 58.3 us -> 55.9 us
  local copies, waits for them, and re-layouts: 2.95 us -> 0.72 us
    ppermute x4, starting transfers between devices: 9.51 us -> 15.8 us  [exchange(): lax.ppermute(sends[3], 'split', paired(1, n_split))]
    pallas_call x7, Pallas kernels: 58.3 us -> 55.9 us  [call(): pl.pallas_call(kernel, out_shape=[shape_of(s) for s in outs], in_specs=sp...]
    unnamed x22 -> x20, local copies, waits for them, and re-layouts: 2.95 us -> 0.72 us
    ppermute x4, starting transfers between devices: 13.9 us -> 11.8 us  [exchange(): lax.ppermute(sends[1], 'curve', paired(1, n_curve))]
    ppermute x4, waiting for transfers between devices: 8.09 us -> 5.98 us  [exchange(): lax.ppermute(sends[3], 'split', paired(1, n_split))]
    ppermute x4, waiting for transfers between devices: 3.45 us -> 1.4 us  [exchange(): lax.ppermute(sends[1], 'curve', paired(1, n_curve))]
    ppermute x4, starting transfers between devices: 12.4 us -> 13.9 us  [per_device(): lax.ppermute(m, AXES, paired(first, devices, hop))]
  transfers between devices with their start and end apart: 20 -> 20, of which waited for: 10 -> 6; matrix products, arithmetic and copies ran while one was open for 0% -> 0% of each run, Pallas kernels for 7% -> 4%
where the time goes in v6:
time: 108 us; the launch traced here: 107 us
  Pallas kernels  55.9 us (52%)
  starting transfers between devices  42.3 us (39%)
  waiting for transfers between devices  7.42 us (7%)
    pallas_call x7, Pallas kernels, call(): pl.pallas_call(kernel, out_shape=[shape_of(s) for s in outs], in_specs=sp...  55.9 us
    ppermute x4, starting transfers between devices, exchange(): lax.ppermute(sends[3], 'split', paired(1, n_split))  15.8 us
    ppermute x4, starting transfers between devices, per_device(): lax.ppermute(m, AXES, paired(first, devices, hop))  13.9 us
    ppermute x4, starting transfers between devices, exchange(): lax.ppermute(sends[1], 'curve', paired(1, n_curve))  11.8 us
    ppermute x4, waiting for transfers between devices, exchange(): lax.ppermute(sends[3], 'split', paired(1, n_split))  5.98 us
  transfers between devices with their start and end apart: 20, of which 6 were waited for; matrix products, arithmetic and copies ran while one was open for 0% of the time, Pallas kernels for 4%

profile of v6, /device:TPU:26, one launch (start us, length us, event | category | flops | bytes accessed | tf_op | source)
XLA Modules:
  0.0 107.4 jit_solution(16783992226771513834)
XLA Ops:
  0.7 5.0 %pack.1 = (f32[8,3712]{1,0:T(8,128)}, f32[8,3712]{1,0:T(8,128)}, f32[8,3712]{1,0:T(8,128)}, f32[8,3712]{1,0:T(8,128)}, s32[8,128]{1,0:T(8,128)}) custom-call(s32[1,36]{1,0:T(1,128)} %send_ref.1, s32[1,4,256]{2,1,0:T(4,128)} %shared_ref.1, f32[1944,256]{1,0:T(8,128)} %jac_ref.1, f32[216,256]{1,0:T(8,128)} %mass_ref.1, f32[729,256]{1,0:T(8,128)} %inv_ref.1, ...), custom_call_target="tpu_custom_call" | custom-call | flops 4000000000 | bytes 400000 | tf_op jit(solution)/shard_map/pack/pallas_call | solution.py:552
  5.7 7.1 %collective-permute-start = (f32[8,3712]{1,0:T(8,128)}, f32[8,3712]{1,0:T(8,128)S(1)}, u32[]{:S(2)}, u32[]{:S(2)}) collective-permute-start(f32[8,3712]{1,0:T(8,128)} %get-tuple-element.46), channel_id=1, source_target_pairs={{2,4},{4,2},{3,5},{5,3},{6,8},{8,6},{7,9},{9,7},{10,12},{12,10},{1... | collective-permute-start | bytes 356360 | tf_op jit(solution)/shard_map/ppermute | solution.py:594
  12.9 4.8 %collective-permute-start.2 = (f32[8,3712]{1,0:T(8,128)}, f32[8,3712]{1,0:T(8,128)S(1)}, u32[]{:S(2)}, u32[]{:S(2)}) collective-permute-start(f32[8,3712]{1,0:T(8,128)} %get-tuple-element.48), channel_id=1, source_target_pairs={{1,2},{2,1},{3,4},{4,3},{5,6},{6,5},{7,8},{8,7},{9,10},{10,9},{11,... | collective-permute-start | bytes 356360 | tf_op jit(solution)/shard_map/ppermute | solution.py:594
  17.7 1.9 %collective-permute-start.3 = (f32[8,3712]{1,0:T(8,128)}, f32[8,3712]{1,0:T(8,128)S(1)}, u32[]{:S(2)}, u32[]{:S(2)}) collective-permute-start(f32[8,3712]{1,0:T(8,128)} %get-tuple-element.49), channel_id=1, source_target_pairs={{0,1},{1,0},{2,3},{3,2},{4,5},{5,4},{6,7},{7,6},{8,9},{9,8},{10,11... | collective-permute-start | bytes 356360 | tf_op jit(solution)/shard_map/ppermute | solution.py:594
  19.6 0.7 copy-done.9
  20.3 4.6 %prep.1 = (f32[96,256]{1,0:T(8,128)S(1)}, f32[3,64,256]{2,1,0:T(8,128)S(1)}, bf16[64,256,256]{2,1,0:T(8,128)(2,1)S(1)}) custom-call(f32[3,7936]{1,0:T(4,128)S(1)} %copy-done.3, s32[64,256]{1,0:T(8,128)S(1)} %copy-done.4, s32[8,128]{1,0:T(8,128)S(1)} %copy-done.9, s32[1,36]{1,0:T(1,128)S(1)} %copy-done.6, f32[27,256]{1,0:T(8,128)S(1)} %copy-done.5, ...), custom_call_target="tpu_custom_call" | custom-call | flops 10000000000 | bytes 1000000 | tf_op jit(solution)/shard_map/prep/pallas_call | solution.py:552
  25.0 10.1 %force_one.1 = (f32[1944,256]{1,0:T(8,128)S(1)}, f32[216,256]{1,0:T(8,128)S(1)}, f32[729,256]{1,0:T(8,128)S(1)}, f32[27,256]{1,0:T(8,128)S(1)}, f32[27,256]{1,0:...) custom-call(s32[1,36]{1,0:T(1,128)S(1)} %copy-done.6, ...), custom_call_target="tpu_custom_call" | custom-call | flops 10000000000 | bytes 1000000 | tf_op jit(solution)/shard_map/force_one/pallas_call | solution.py:552
  35.2 0.1 collective-permute-start.4
  35.3 2.4 %collective-permute-start.5 = (f32[16,128]{1,0:T(8,128)S(1)}, f32[16,128]{1,0:T(8,128)S(1)}, u32[]{:S(2)}, u32[]{:S(2)}) collective-permute-start(f32[16,128]{1,0:T(8,128)S(1)} %get-tuple-element.54), channel_id=1, source_target_pairs={{4,8},{8,4},{12,16},{16,12},{20,24},{24,20},{28,32},{32,28},{36,40... | collective-permute-start | bytes 24584 | tf_op jit(solution)/shard_map/ppermute | solution.py:573
  37.7 0.3 collective-permute-start.6
  38.0 5.0 %collective-permute-start.7 = (f32[16,128]{1,0:T(8,128)S(1)}, f32[16,128]{1,0:T(8,128)S(1)}, u32[]{:S(2)}, u32[]{:S(2)}) collective-permute-start(f32[16,128]{1,0:T(8,128)S(1)} %get-tuple-element.56), channel_id=1, source_target_pairs={{1,2},{2,1},{5,6},{6,5},{9,10},{10,9},{13,14},{14,13},{17,18},{18,... | collective-permute-start | bytes 24584 | tf_op jit(solution)/shard_map/ppermute | solution.py:575
  43.0 1.6 %collective-permute-done.7.g3 = f32[16,128]{1,0:T(8,128)S(1)} collective-permute-done((f32[16,128]{1,0:T(8,128)S(1)}, f32[16,128]{1,0:T(8,128)S(1)}, u32[]{:S(2)}, u32[]{:S(2)}) %collective-permute-start.7) | collective-permute-done | bytes 8224 | tf_op jit(solution)/shard_map/ppermute | solution.py:575
  44.6 10.2 %mass_start.1 = (f32[32,256]{1,0:T(8,128)S(1)}, f32[192,256]{1,0:T(8,128)S(1)}, f32[192,256]{1,0:T(8,128)S(1)}, f32[192,256]{1,0:T(8,128)S(1)}, f32[16,128]{1,0:...) custom-call(f32[16,128]{1,0:T(8,128)S(1)} %collective-permute-done.4.g0, ...), custom_call_target="tpu_custom_call" | custom-call | flops 10000000000 | bytes 1000000 | tf_op jit(solution)/shard_map/mass_start/pallas_call | solution.py:552
  54.8 0.1 collective-permute-start.8
  54.9 2.8 %collective-permute-start.9 = (f32[16,128]{1,0:T(8,128)S(1)}, f32[16,128]{1,0:T(8,128)S(1)}, u32[]{:S(2)}, u32[]{:S(2)}) collective-permute-start(f32[16,128]{1,0:T(8,128)S(1)} %get-tuple-element.60), channel_id=1, source_target_pairs={{4,8},{8,4},{12,16},{16,12},{20,24},{24,20},{28,32},{32,28},{36,40... | collective-permute-start | bytes 24584 | tf_op jit(solution)/shard_map/ppermute | solution.py:573
  57.8 0.1 collective-permute-start.10
  57.9 3.6 %collective-permute-start.11 = (f32[16,128]{1,0:T(8,128)S(1)}, f32[16,128]{1,0:T(8,128)S(1)}, u32[]{:S(2)}, u32[]{:S(2)}) collective-permute-start(f32[16,128]{1,0:T(8,128)S(1)} %get-tuple-element.62), channel_id=1, source_target_pairs={{1,2},{2,1},{5,6},{6,5},{9,10},{10,9},{13,14},{14,13},{17,18},{18,... | collective-permute-start | bytes 24584 | tf_op jit(solution)/shard_map/ppermute | solution.py:575
  61.5 0.5 collective-permute-done.9.g1
  62.0 1.4 %collective-permute-done.11.g3 = f32[16,128]{1,0:T(8,128)S(1)} collective-permute-done((f32[16,128]{1,0:T(8,128)S(1)}, f32[16,128]{1,0:T(8,128)S(1)}, u32[]{:S(2)}, u32[]{:S(2)}) %collective-permute-start.11) | collective-permute-done | bytes 8224 | tf_op jit(solution)/shard_map/ppermute | solution.py:575
  63.4 10.1 %mass_sweep.2 = (f32[192,256]{1,0:T(8,128)S(1)}, f32[192,256]{1,0:T(8,128)S(1)}, f32[192,256]{1,0:T(8,128)S(1)}, f32[192,256]{1,0:T(8,128)S(1)}, f32[16,128]{1,0...) custom-call(f32[16,128]{1,0:T(8,128)S(1)} %collective-permute-done.8.g0, ...), custom_call_target="tpu_custom_call" | custom-call | flops 10000000000 | bytes 1000000 | tf_op jit(solution)/shard_map/mass_sweep/pallas_call | solution.py:552
  73.5 0.1 collective-permute-start.12
  73.6 4.0 %collective-permute-start.13 = (f32[16,128]{1,0:T(8,128)S(1)}, f32[16,128]{1,0:T(8,128)S(1)}, u32[]{:S(2)}, u32[]{:S(2)}) collective-permute-start(f32[16,128]{1,0:T(8,128)S(1)} %get-tuple-element.68), channel_id=1, source_target_pairs={{4,8},{8,4},{12,16},{16,12},{20,24},{24,20},{28,32},{32,28},{36,40... | collective-permute-start | bytes 24584 | tf_op jit(solution)/shard_map/ppermute | solution.py:573
  77.6 0.1 collective-permute-start.14
  77.7 3.6 %collective-permute-start.15 = (f32[16,128]{1,0:T(8,128)S(1)}, f32[16,128]{1,0:T(8,128)S(1)}, u32[]{:S(2)}, u32[]{:S(2)}) collective-permute-start(f32[16,128]{1,0:T(8,128)S(1)} %get-tuple-element.70), channel_id=1, source_target_pairs={{1,2},{2,1},{5,6},{6,5},{9,10},{10,9},{13,14},{14,13},{17,18},{18,... | collective-permute-start | bytes 24584 | tf_op jit(solution)/shard_map/ppermute | solution.py:575
  81.4 1.9 %collective-permute-done.15.g3 = f32[16,128]{1,0:T(8,128)S(1)} collective-permute-done((f32[16,128]{1,0:T(8,128)S(1)}, f32[16,128]{1,0:T(8,128)S(1)}, u32[]{:S(2)}, u32[]{:S(2)}) %collective-permute-start.15) | collective-permute-done | bytes 8224 | tf_op jit(solution)/shard_map/ppermute | solution.py:575
  83.2 10.1 %mass_sweep.3 = (f32[192,256]{1,0:T(8,128)S(1)}, f32[192,256]{1,0:T(8,128)S(1)}, f32[192,256]{1,0:T(8,128)S(1)}, f32[192,256]{1,0:T(8,128)S(1)}, f32[16,128]{1,0...) custom-call(f32[16,128]{1,0:T(8,128)S(1)} %collective-permute-done.12.g0, ...), custom_call_target="tpu_custom_call" | custom-call | flops 10000000000 | bytes 1000000 | tf_op jit(solution)/shard_map/mass_sweep/pallas_call | solution.py:552
  93.4 0.1 collective-permute-start.16
  93.5 2.6 %collective-permute-start.17 = (f32[16,128]{1,0:T(8,128)S(1)}, f32[16,128]{1,0:T(8,128)S(1)}, u32[]{:S(2)}, u32[]{:S(2)}) collective-permute-start(f32[16,128]{1,0:T(8,128)S(1)} %get-tuple-element.76), channel_id=1, source_target_pairs={{4,8},{8,4},{12,16},{16,12},{20,24},{24,20},{28,32},{32,28},{36,40... | collective-permute-start | bytes 24584 | tf_op jit(solution)/shard_map/ppermute | solution.py:573
  96.2 3.5 %collective-permute-start.19 = (f32[16,128]{1,0:T(8,128)S(1)}, f32[16,128]{1,0:T(8,128)S(1)}, u32[]{:S(2)}, u32[]{:S(2)}) collective-permute-start(f32[16,128]{1,0:T(8,128)S(1)} %get-tuple-element.78), channel_id=1, source_target_pairs={{1,2},{2,1},{5,6},{6,5},{9,10},{10,9},{13,14},{14,13},{17,18},{18,... | collective-permute-start | bytes 24584 | tf_op jit(solution)/shard_map/ppermute | solution.py:575
  99.6 0.9 collective-permute-done.17.g1
  100.6 1.1 %collective-permute-done.19.g3 = f32[16,128]{1,0:T(8,128)S(1)} collective-permute-done((f32[16,128]{1,0:T(8,128)S(1)}, f32[16,128]{1,0:T(8,128)S(1)}, u32[]{:S(2)}, u32[]{:S(2)}) %collective-permute-start.19) | collective-permute-done | bytes 8224 | tf_op jit(solution)/shard_map/ppermute | solution.py:575
  101.7 5.7 %force_two.1 = (f32[27,256]{1,0:T(8,128)}, f32[3,7936]{1,0:T(4,128)}) custom-call(f32[16,128]{1,0:T(8,128)S(1)} %collective-permute-done.16.g0, f32[16,128]{1,0:T(8,128)S(1)} %collective-permute-done.17.g1, f32[16,128]{1,0:T(8,128)S(1)} %collective-permute-done.18.g2, f32[16,128]{1,0:T(8,128)S(1)} %collective-permute-done.19.g3, ...), custom_call_target="tpu_custom_call" | custom-call | flops 10000000000 | bytes 1000000 | tf_op jit(solution)/shard_map/force_two/pallas_call | solution.py:552
  (35 shorter events, 0.3 us)
Async XLA Ops:
  0.6 19.0 %copy-start.7 = (bf16[2528,256]{1,0:T(8,128)(2,1)S(1)}, bf16[2528,256]{1,0:T(8,128)(2,1)}, u32[]{:S(2)}) copy-start(bf16[2528,256]{1,0:T(8,128)(2,1)} %constant.4.clone._tables.tables) | copy-start | bytes 3883012
  0.6 18.9 %copy-start.5 = (f32[27,256]{1,0:T(8,128)S(1)}, f32[27,256]{1,0:T(8,128)}, u32[]{:S(2)}) copy-start(f32[27,256]{1,0:T(8,128)} %en_ref.1) | copy-start | bytes 82948
  0.7 18.9 %copy-start.4 = (s32[64,256]{1,0:T(8,128)S(1)}, s32[64,256]{1,0:T(8,128)}, u32[]{:S(2)}) copy-start(s32[64,256]{1,0:T(8,128)} %zn.7) | copy-start | bytes 196612
  0.7 18.9 %copy-start.6 = (s32[1,36]{1,0:T(1,128)S(1)}, s32[1,36]{1,0:T(1,128)}, u32[]{:S(2)}) copy-start(s32[1,36]{1,0:T(1,128)} %arrive_ref.1) | copy-start | bytes 436
  0.7 18.9 %copy-start.3 = (f32[3,7936]{1,0:T(4,128)S(1)}, f32[3,7936]{1,0:T(4,128)}, u32[]{:S(2)}) copy-start(f32[3,7936]{1,0:T(4,128)} %vel_ref.1) | copy-start | bytes 285700
  5.7 19.3 %collective-permute-start = (f32[8,3712]{1,0:T(8,128)}, f32[8,3712]{1,0:T(8,128)S(1)}, u32[]{:S(2)}, u32[]{:S(2)}) collective-permute-start(f32[8,3712]{1,0:T(8,128)} %get-tuple-element.46), channel_id=1, source_target_pairs={{2,4},{4,2},{3,5},{5,3},{6,8},{8,6},{7,9},{9,7},{10,12},{12,10},{1... | collective-permute-start | bytes 356360 | tf_op jit(solution)/shard_map/ppermute | solution.py:594
  12.8 12.1 %collective-permute-start.1 = (f32[8,3712]{1,0:T(8,128)}, f32[8,3712]{1,0:T(8,128)S(1)}, u32[]{:S(2)}, u32[]{:S(2)}) collective-permute-start(f32[8,3712]{1,0:T(8,128)} %get-tuple-element.47), channel_id=1, source_target_pairs={{0,2},{2,0},{1,3},{3,1},{4,6},{6,4},{5,7},{7,5},{8,10},{10,8},{9,1... | collective-permute-start | bytes 356360 | tf_op jit(solution)/shard_map/ppermute | solution.py:594
  12.9 12.1 %collective-permute-start.2 = (f32[8,3712]{1,0:T(8,128)}, f32[8,3712]{1,0:T(8,128)S(1)}, u32[]{:S(2)}, u32[]{:S(2)}) collective-permute-start(f32[8,3712]{1,0:T(8,128)} %get-tuple-element.48), channel_id=1, source_target_pairs={{1,2},{2,1},{3,4},{4,3},{5,6},{6,5},{7,8},{8,7},{9,10},{10,9},{11,... | collective-permute-start | bytes 356360 | tf_op jit(solution)/shard_map/ppermute | solution.py:594
  17.7 7.3 %collective-permute-start.3 = (f32[8,3712]{1,0:T(8,128)}, f32[8,3712]{1,0:T(8,128)S(1)}, u32[]{:S(2)}, u32[]{:S(2)}) collective-permute-start(f32[8,3712]{1,0:T(8,128)} %get-tuple-element.49), channel_id=1, source_target_pairs={{0,1},{1,0},{2,3},{3,2},{4,5},{5,4},{6,7},{7,6},{8,9},{9,8},{10,11... | collective-permute-start | bytes 356360 | tf_op jit(solution)/shard_map/ppermute | solution.py:594
  19.6 0.7 copy-start.9
  20.3 4.7 %copy-start = (f32[1944,256]{1,0:T(8,128)S(1)}, f32[1944,256]{1,0:T(8,128)}, u32[]{:S(2)}) copy-start(f32[1944,256]{1,0:T(8,128)} %jac_ref.1) | copy-start | bytes 5971972
  20.3 4.7 %copy-start.1 = (f32[729,256]{1,0:T(8,128)S(1)}, f32[729,256]{1,0:T(8,128)}, u32[]{:S(2)}) copy-start(f32[729,256]{1,0:T(8,128)} %inv_ref.1) | copy-start | bytes 2239492
  20.3 4.7 %copy-start.2 = (f32[216,256]{1,0:T(8,128)S(1)}, f32[216,256]{1,0:T(8,128)}, u32[]{:S(2)}) copy-start(f32[216,256]{1,0:T(8,128)} %mass_ref.1) | copy-start | bytes 663556
  25.0 19.6 %copy-start.8 = (bf16[352,256]{1,0:T(8,128)(2,1)S(1)}, bf16[352,256]{1,0:T(8,128)(2,1)}, u32[]{:S(2)}) copy-start(bf16[352,256]{1,0:T(8,128)(2,1)} %constant.5.clone.tables) | copy-start | bytes 540676
  35.2 7.8 %collective-permute-start.4 = (f32[16,128]{1,0:T(8,128)S(1)}, f32[16,128]{1,0:T(8,128)S(1)}, u32[]{:S(2)}, u32[]{:S(2)}) collective-permute-start(f32[16,128]{1,0:T(8,128)S(1)} %get-tuple-element.53), channel_id=1, source_target_pairs={{0,4},{4,0},{8,12},{12,8},{16,20},{20,16},{24,28},{28,24},{32,36},... | collective-permute-start | bytes 24584 | tf_op jit(solution)/shard_map/ppermute | solution.py:572
  35.3 7.7 %collective-permute-start.5 = (f32[16,128]{1,0:T(8,128)S(1)}, f32[16,128]{1,0:T(8,128)S(1)}, u32[]{:S(2)}, u32[]{:S(2)}) collective-permute-start(f32[16,128]{1,0:T(8,128)S(1)} %get-tuple-element.54), channel_id=1, source_target_pairs={{4,8},{8,4},{12,16},{16,12},{20,24},{24,20},{28,32},{32,28},{36,40... | collective-permute-start | bytes 24584 | tf_op jit(solution)/shard_map/ppermute | solution.py:573
  37.7 5.3 %collective-permute-start.6 = (f32[16,128]{1,0:T(8,128)S(1)}, f32[16,128]{1,0:T(8,128)S(1)}, u32[]{:S(2)}, u32[]{:S(2)}) collective-permute-start(f32[16,128]{1,0:T(8,128)S(1)} %get-tuple-element.55), channel_id=1, source_target_pairs={{0,1},{1,0},{2,3},{3,2},{4,5},{5,4},{6,7},{7,6},{8,9},{9,8},{10,11... | collective-permute-start | bytes 24584 | tf_op jit(solution)/shard_map/ppermute | solution.py:574
  38.0 6.6 %collective-permute-start.7 = (f32[16,128]{1,0:T(8,128)S(1)}, f32[16,128]{1,0:T(8,128)S(1)}, u32[]{:S(2)}, u32[]{:S(2)}) collective-permute-start(f32[16,128]{1,0:T(8,128)S(1)} %get-tuple-element.56), channel_id=1, source_target_pairs={{1,2},{2,1},{5,6},{6,5},{9,10},{10,9},{13,14},{14,13},{17,18},{18,... | collective-permute-start | bytes 24584 | tf_op jit(solution)/shard_map/ppermute | solution.py:575
  54.8 6.7 %collective-permute-start.8 = (f32[16,128]{1,0:T(8,128)S(1)}, f32[16,128]{1,0:T(8,128)S(1)}, u32[]{:S(2)}, u32[]{:S(2)}) collective-permute-start(f32[16,128]{1,0:T(8,128)S(1)} %get-tuple-element.59), channel_id=1, source_target_pairs={{0,4},{4,0},{8,12},{12,8},{16,20},{20,16},{24,28},{28,24},{32,36},... | collective-permute-start | bytes 24584 | tf_op jit(solution)/shard_map/ppermute | solution.py:572
  54.9 7.1 %collective-permute-start.9 = (f32[16,128]{1,0:T(8,128)S(1)}, f32[16,128]{1,0:T(8,128)S(1)}, u32[]{:S(2)}, u32[]{:S(2)}) collective-permute-start(f32[16,128]{1,0:T(8,128)S(1)} %get-tuple-element.60), channel_id=1, source_target_pairs={{4,8},{8,4},{12,16},{16,12},{20,24},{24,20},{28,32},{32,28},{36,40... | collective-permute-start | bytes 24584 | tf_op jit(solution)/shard_map/ppermute | solution.py:573
  57.8 4.2 %collective-permute-start.10 = (f32[16,128]{1,0:T(8,128)S(1)}, f32[16,128]{1,0:T(8,128)S(1)}, u32[]{:S(2)}, u32[]{:S(2)}) collective-permute-start(f32[16,128]{1,0:T(8,128)S(1)} %get-tuple-element.61), channel_id=1, source_target_pairs={{0,1},{1,0},{2,3},{3,2},{4,5},{5,4},{6,7},{7,6},{8,9},{9,8},{10,11... | collective-permute-start | bytes 24584 | tf_op jit(solution)/shard_map/ppermute | solution.py:574
  57.9 5.5 %collective-permute-start.11 = (f32[16,128]{1,0:T(8,128)S(1)}, f32[16,128]{1,0:T(8,128)S(1)}, u32[]{:S(2)}, u32[]{:S(2)}) collective-permute-start(f32[16,128]{1,0:T(8,128)S(1)} %get-tuple-element.62), channel_id=1, source_target_pairs={{1,2},{2,1},{5,6},{6,5},{9,10},{10,9},{13,14},{14,13},{17,18},{18,... | collective-permute-start | bytes 24584 | tf_op jit(solution)/shard_map/ppermute | solution.py:575
  73.5 7.8 %collective-permute-start.12 = (f32[16,128]{1,0:T(8,128)S(1)}, f32[16,128]{1,0:T(8,128)S(1)}, u32[]{:S(2)}, u32[]{:S(2)}) collective-permute-start(f32[16,128]{1,0:T(8,128)S(1)} %get-tuple-element.67), channel_id=1, source_target_pairs={{0,4},{4,0},{8,12},{12,8},{16,20},{20,16},{24,28},{28,24},{32,36},... | collective-permute-start | bytes 24584 | tf_op jit(solution)/shard_map/ppermute | solution.py:572
  73.6 7.7 %collective-permute-start.13 = (f32[16,128]{1,0:T(8,128)S(1)}, f32[16,128]{1,0:T(8,128)S(1)}, u32[]{:S(2)}, u32[]{:S(2)}) collective-permute-start(f32[16,128]{1,0:T(8,128)S(1)} %get-tuple-element.68), channel_id=1, source_target_pairs={{4,8},{8,4},{12,16},{16,12},{20,24},{24,20},{28,32},{32,28},{36,40... | collective-permute-start | bytes 24584 | tf_op jit(solution)/shard_map/ppermute | solution.py:573
  77.6 3.8 %collective-permute-start.14 = (f32[16,128]{1,0:T(8,128)S(1)}, f32[16,128]{1,0:T(8,128)S(1)}, u32[]{:S(2)}, u32[]{:S(2)}) collective-permute-start(f32[16,128]{1,0:T(8,128)S(1)} %get-tuple-element.69), channel_id=1, source_target_pairs={{0,1},{1,0},{2,3},{3,2},{4,5},{5,4},{6,7},{7,6},{8,9},{9,8},{10,11... | collective-permute-start | bytes 24584 | tf_op jit(solution)/shard_map/ppermute | solution.py:574
  77.7 5.5 %collective-permute-start.15 = (f32[16,128]{1,0:T(8,128)S(1)}, f32[16,128]{1,0:T(8,128)S(1)}, u32[]{:S(2)}, u32[]{:S(2)}) collective-permute-start(f32[16,128]{1,0:T(8,128)S(1)} %get-tuple-element.70), channel_id=1, source_target_pairs={{1,2},{2,1},{5,6},{6,5},{9,10},{10,9},{13,14},{14,13},{17,18},{18,... | collective-permute-start | bytes 24584 | tf_op jit(solution)/shard_map/ppermute | solution.py:575
  93.4 6.2 %collective-permute-start.16 = (f32[16,128]{1,0:T(8,128)S(1)}, f32[16,128]{1,0:T(8,128)S(1)}, u32[]{:S(2)}, u32[]{:S(2)}) collective-permute-start(f32[16,128]{1,0:T(8,128)S(1)} %get-tuple-element.75), channel_id=1, source_target_pairs={{0,4},{4,0},{8,12},{12,8},{16,20},{20,16},{24,28},{28,24},{32,36},... | collective-permute-start | bytes 24584 | tf_op jit(solution)/shard_map/ppermute | solution.py:572
  93.5 7.1 %collective-permute-start.17 = (f32[16,128]{1,0:T(8,128)S(1)}, f32[16,128]{1,0:T(8,128)S(1)}, u32[]{:S(2)}, u32[]{:S(2)}) collective-permute-start(f32[16,128]{1,0:T(8,128)S(1)} %get-tuple-element.76), channel_id=1, source_target_pairs={{4,8},{8,4},{12,16},{16,12},{20,24},{24,20},{28,32},{32,28},{36,40... | collective-permute-start | bytes 24584 | tf_op jit(solution)/shard_map/ppermute | solution.py:573
  96.1 4.5 %collective-permute-start.18 = (f32[16,128]{1,0:T(8,128)S(1)}, f32[16,128]{1,0:T(8,128)S(1)}, u32[]{:S(2)}, u32[]{:S(2)}) collective-permute-start(f32[16,128]{1,0:T(8,128)S(1)} %get-tuple-element.77), channel_id=1, source_target_pairs={{0,1},{1,0},{2,3},{3,2},{4,5},{5,4},{6,7},{7,6},{8,9},{9,8},{10,11... | collective-permute-start | bytes 24584 | tf_op jit(solution)/shard_map/ppermute | solution.py:574
  96.2 5.5 %collective-permute-start.19 = (f32[16,128]{1,0:T(8,128)S(1)}, f32[16,128]{1,0:T(8,128)S(1)}, u32[]{:S(2)}, u32[]{:S(2)}) collective-permute-start(f32[16,128]{1,0:T(8,128)S(1)} %get-tuple-element.78), channel_id=1, source_target_pairs={{1,2},{2,1},{5,6},{6,5},{9,10},{10,9},{13,14},{14,13},{17,18},{18,... | collective-permute-start | bytes 24584 | tf_op jit(solution)/shard_map/ppermute | solution.py:575

commit v7 on v6

--- a/solution.py
+++ b/solution.py
@@ -114,13 +114,6 @@
     return high, (x - high.astype(F32)).astype(BF)
 
 
-def split3(x):
-    high = x.astype(BF)
-    rest = x - high.astype(F32)
-    mid = rest.astype(BF)
-    return high, mid, (rest - mid.astype(F32)).astype(BF)
-
-
 def dot(a, b, dims=None):
     if dims is None:
         return jnp.dot(a, b, preferred_element_type=F32)
@@ -216,16 +209,24 @@
     return (acc[:, 0] + acc[:, 1]).reshape(-1, WIDE)
 
 
-def scatter_zones(idx_ref, lane_ref, term_ref, count):
-    def eight(t, acc):
-        r0 = pl.multiple_of(t * 8, 8)
-        idx = idx_ref[pl.ds(r0, 8), :]
-        terms = [term_ref[c, pl.ds(r0, 8), :] for c in range(count)]
-        for a in range(8):
-            acc = acc + dot(spread_rows(idx[a : a + 1], [x[a : a + 1] for x in terms]), lane_ref[r0 + a])
-        return acc
-
-    return joined(lax.fori_loop(0, 8, eight, jnp.zeros((2 * ROWS * count, WIDE), F32)))
+def add_product(acc_ref, rows, hot, step):
+    rows, hot = jnp.concatenate(rows, 1), jnp.concatenate(hot, 0)
+    for p in range(0, acc_ref.shape[0], step):
+        acc_ref[p : p + step, :] += dot(rows[p : p + step], hot)
+
+
+def scatter_zones(idx_ref, lane_ref, term_ref, acc_ref, count):
+    acc_ref[...] = jnp.zeros(acc_ref.shape, F32)
+
+    @pl.loop(0, NPZ // 16)
+    def _(t):
+        r0 = pl.multiple_of(t * 16, 8)
+        idx = idx_ref[pl.ds(r0, 16), :]
+        terms = [term_ref[c, pl.ds(r0, 16), :] for c in range(count)]
+        rows = [spread_rows(idx[a : a + 1], [x[a : a + 1] for x in terms]) for a in range(16)]
+        add_product(acc_ref, rows, [lane_ref[r0 + a] for a in range(16)], 224)
+
+    return joined(acc_ref[...])
 
 
 def flat_row(ref, first):
@@ -362,13 +363,13 @@
         copy.wait()
         for i in range(first, first + total, WIDE):
             n = min(WIDE, first + total - i)
-            parts = split3(ref[i : i + n, :])
+            parts = split2(ref[i : i + n, :])
             put(at + i, n, sum(dot(hot, part, NT) for part in parts))
     for p in range(4):
         msgs[p][:, AT_FLAG:MSG] = jnp.ones((8, MSG - AT_FLAG), F32)
 
 
-def prep_kernel(vel_ref, zn_ref, _lists, _arrive, _en, _tables, vel_out, vz, lane_out, words):
+def prep_kernel(vel_ref, zn_ref, _arrive, _en, _tables, vel_out, vz, lane_out, words):
     nodes_in(vel_ref, vel_out)
     steps = make_words(vel_out, words, 1)
     down_rows = lax.broadcasted_iota(jnp.int32, (WIDE, WIDE), 0)
@@ -387,7 +388,7 @@
 
 def first_kernel(
     arrive_ref, m0, m1, m2, m3, lists_ref, jac_ref, mass_ref, inv_ref, en_ref, zn_ref, tables, vz, lanes,
-    jac_out, mass_out, inv_out, en_out, ehalf_out, y_out, s0, s1, s2, s3, oh, arr, terms, work,
+    jac_out, mass_out, inv_out, en_out, ehalf_out, y_out, s0, s1, s2, s3, oh, arr, terms, work, acc,
 ):
     msgs = (m0, m1, m2, m3)
     lane = lax.broadcasted_iota(jnp.int32, (1, WIDE), 1)
@@ -400,7 +401,7 @@
             oh[at : at + 1, :] = jnp.where(lane == arrive_ref[0, first + j], 1.0, 0.0) * flag
     lands = jnp.sum(oh[...], axis=0, keepdims=True) > 0.5
     hot = oh[...].astype(BF)
-    hot3 = jnp.concatenate([hot, hot, hot], 0)
+    hot2 = jnp.concatenate([hot, hot], 0)
     for p in range(4):
         arr[p * 8 : (p + 1) * 8, :] = msgs[p][:, :MSG]
         for piece in range(7):
@@ -417,14 +418,14 @@
         for i in range(0, total, WIDE):
             n = min(WIDE, total - i)
             wide = min(WIDE, -(-n // HALF) * HALF)
-            came = jnp.concatenate(split3(arr[:, at + i : at + i + wide]), 0)
-            out[i : i + n, :] = jnp.where(lands, dot(came, hot3, TN)[:n], ref[i : i + n, :])
+            came = jnp.concatenate(split2(arr[:, at + i : at + i + wide]), 0)
+            out[i : i + n, :] = jnp.where(lands, dot(came, hot2, TN)[:n], ref[i : i + n, :])
     mass = mass_out[...]
     rhs_e = force(pressure_at(en_out[...], mass, tables), jac_out, tables, terms, 0, vz, work)
     ehalf_out[...] = en_out[...] + 0.5 * STEP_SIZE * energy_change(rhs_e, inv_out, tables)
     force(pressure_at(ehalf_out[...], mass, tables), jac_out, tables, terms, 3)
     terms[6] = down(entry(tables, FORCE_AT, "limit"), mass)
-    y_out[...] = scatter_zones(zn_ref, lanes, terms, 7)
+    y_out[...] = scatter_zones(zn_ref, lanes, terms, acc, 7)
     send_shared(lists_ref, y_out, (s0, s1, s2, s3), 7)
 
 
@@ -455,7 +456,7 @@
     terms = [term_ref[c, pl.ds(r0, 16), lanes] for c in range(COMPONENTS)]
     rows = [spread_rows(idx[a : a + 1], [x[a : a + 1] for x in terms]) for a in range(16)]
     hot = [lane_ref[r0 + a, lanes, :] for a in range(16)]
-    acc_ref[...] += dot(jnp.concatenate(rows, 1), jnp.concatenate(hot, 0))
+    add_product(acc_ref, rows, hot, 192)
 
 
 def zone_mass(mass_ref, tables, zone, terms, h):
@@ -593,14 +594,14 @@
     rounds = ((1, 2), (0, 2), (1, 1), (0, 1))
     came = [lax.ppermute(m, AXES, paired(first, devices, hop)) for m, (first, hop) in zip(msgs, rounds)]
     vel, vz, lanes = call(
-        prep_kernel, (velocity, zone_nodes, lists, arrive_rows, energy, force_tables),
-        [node, zone(3), half(NPZ, WIDE, WIDE)], [words(1)], [VM, VM, VM, SM, VM, VM], name="prep",
+        prep_kernel, (velocity, zone_nodes, arrive_rows, energy, force_tables),
+        [node, zone(3), half(NPZ, WIDE, WIDE)], [words(1)], [VM, VM, SM, VM, VM], name="prep",
     )
     jac, mass, inv, en, ehalf, y, *sends = call(
         first_kernel,
         (arrive_rows, *came, lists, jac, mass, inv, energy, zone_nodes, force_tables, vz, lanes),
         fields + [(LD, WIDE), ((COMPONENTS + 1) * ROWS, WIDE)] + send,
-        [(48, WIDE), (48, MSG), zone(COMPONENTS + 1), (QP, WIDE)],
+        [(48, WIDE), (48, MSG), zone(COMPONENTS + 1), (QP, WIDE), (2 * (COMPONENTS + 1) * ROWS, WIDE)],
         [SM] + [VM] * 13, name="force_one",
     )
     scratch = [zone(COMPONENTS), zone(COMPONENTS), words(COMPONENTS // 3), (2 * COMPONENTS * ROWS, WIDE)]

time: 108 us -> 106 us (0.981)
  Pallas kernels: 55.9 us -> 54.1 us
    pallas_call x7, Pallas kernels: 55.9 us -> 54.1 us  [call(): pl.pallas_call(kernel, out_shape=[shape_of(s) for s in outs], in_specs=sp...]
where the time goes in v7:
time: 106 us; the launch traced here: 105 us
  Pallas kernels  54.1 us (51%)
  starting transfers between devices  43.2 us (41%)
  waiting for transfers between devices  7.01 us (7%)
    pallas_call x7, Pallas kernels, call(): pl.pallas_call(kernel, out_shape=[shape_of(s) for s in outs], in_specs=sp...  54.1 us
    ppermute x4, starting transfers between devices, exchange(): lax.ppermute(sends[3], 'split', paired(1, n_split))  16.3 us
    ppermute x4, starting transfers between devices, per_device(): lax.ppermute(m, AXES, paired(first, devices, hop))  13.9 us
    ppermute x4, starting transfers between devices, exchange(): lax.ppermute(sends[1], 'curve', paired(1, n_curve))  11.6 us
    ppermute x4, waiting for transfers between devices, exchange(): lax.ppermute(sends[3], 'split', paired(1, n_split))  5.57 us
  transfers between devices with their start and end apart: 20, of which 6 were waited for; matrix products, arithmetic and copies ran while one was open for 0% of the time, Pallas kernels for 4%

profile of v7, /device:TPU:26, one launch (start us, length us, event | category | flops | bytes accessed | tf_op | source)
XLA Modules:
  0.0 105.4 jit_solution(9565567786911269424)
XLA Ops:
  0.7 4.5 %pack.1 = (f32[8,3712]{1,0:T(8,128)}, f32[8,3712]{1,0:T(8,128)}, f32[8,3712]{1,0:T(8,128)}, f32[8,3712]{1,0:T(8,128)}, s32[8,128]{1,0:T(8,128)}) custom-call(s32[1,36]{1,0:T(1,128)} %send_ref.1, s32[1,4,256]{2,1,0:T(4,128)} %shared_ref.1, f32[1944,256]{1,0:T(8,128)} %jac_ref.1, f32[216,256]{1,0:T(8,128)} %mass_ref.1, f32[729,256]{1,0:T(8,128)} %inv_ref.1, ...), custom_call_target="tpu_custom_call" | custom-call | flops 4000000000 | bytes 400000 | tf_op jit(solution)/shard_map/pack/pallas_call | solution.py:553
  5.1 7.1 %collective-permute-start = (f32[8,3712]{1,0:T(8,128)}, f32[8,3712]{1,0:T(8,128)S(1)}, u32[]{:S(2)}, u32[]{:S(2)}) collective-permute-start(f32[8,3712]{1,0:T(8,128)} %get-tuple-element.46), channel_id=1, source_target_pairs={{2,4},{4,2},{3,5},{5,3},{6,8},{8,6},{7,9},{9,7},{10,12},{12,10},{1... | collective-permute-start | bytes 356360 | tf_op jit(solution)/shard_map/ppermute | solution.py:595
  12.4 4.8 %collective-permute-start.2 = (f32[8,3712]{1,0:T(8,128)}, f32[8,3712]{1,0:T(8,128)S(1)}, u32[]{:S(2)}, u32[]{:S(2)}) collective-permute-start(f32[8,3712]{1,0:T(8,128)} %get-tuple-element.48), channel_id=1, source_target_pairs={{1,2},{2,1},{3,4},{4,3},{5,6},{6,5},{7,8},{8,7},{9,10},{10,9},{11,... | collective-permute-start | bytes 356360 | tf_op jit(solution)/shard_map/ppermute | solution.py:595
  17.2 1.9 %collective-permute-start.3 = (f32[8,3712]{1,0:T(8,128)}, f32[8,3712]{1,0:T(8,128)S(1)}, u32[]{:S(2)}, u32[]{:S(2)}) collective-permute-start(f32[8,3712]{1,0:T(8,128)} %get-tuple-element.49), channel_id=1, source_target_pairs={{0,1},{1,0},{2,3},{3,2},{4,5},{5,4},{6,7},{7,6},{8,9},{9,8},{10,11... | collective-permute-start | bytes 356360 | tf_op jit(solution)/shard_map/ppermute | solution.py:595
  19.1 4.6 %prep.1 = (f32[96,256]{1,0:T(8,128)S(1)}, f32[3,64,256]{2,1,0:T(8,128)S(1)}, bf16[64,256,256]{2,1,0:T(8,128)(2,1)S(1)}) custom-call(f32[3,7936]{1,0:T(4,128)S(1)} %copy-done.3, s32[64,256]{1,0:T(8,128)S(1)} %copy-done.4, s32[1,36]{1,0:T(1,128)S(1)} %copy-done.6, f32[27,256]{1,0:T(8,128)S(1)} %copy-done.5, bf16[2528,256]{1,0:T(8,128)(2,1)S(1)} %copy-done.7), custom_call_target="tpu_custom_call" | custom-call | flops 10000000000 | bytes 1000000 | tf_op jit(solution)/shard_map/prep/pallas_call | solution.py:553
  23.9 9.2 %force_one.1 = (f32[1944,256]{1,0:T(8,128)S(1)}, f32[216,256]{1,0:T(8,128)S(1)}, f32[729,256]{1,0:T(8,128)S(1)}, f32[27,256]{1,0:T(8,128)S(1)}, f32[27,256]{1,0:...) custom-call(s32[1,36]{1,0:T(1,128)S(1)} %copy-done.6, ...), custom_call_target="tpu_custom_call" | custom-call | flops 10000000000 | bytes 1000000 | tf_op jit(solution)/shard_map/force_one/pallas_call | solution.py:553
  33.1 0.1 collective-permute-start.4
  33.1 2.4 %collective-permute-start.5 = (f32[16,128]{1,0:T(8,128)S(1)}, f32[16,128]{1,0:T(8,128)S(1)}, u32[]{:S(2)}, u32[]{:S(2)}) collective-permute-start(f32[16,128]{1,0:T(8,128)S(1)} %get-tuple-element.54), channel_id=1, source_target_pairs={{4,8},{8,4},{12,16},{16,12},{20,24},{24,20},{28,32},{32,28},{36,40... | collective-permute-start | bytes 24584 | tf_op jit(solution)/shard_map/ppermute | solution.py:574
  35.6 0.8 collective-permute-start.6
  36.4 5.1 %collective-permute-start.7 = (f32[16,128]{1,0:T(8,128)S(1)}, f32[16,128]{1,0:T(8,128)S(1)}, u32[]{:S(2)}, u32[]{:S(2)}) collective-permute-start(f32[16,128]{1,0:T(8,128)S(1)} %get-tuple-element.56), channel_id=1, source_target_pairs={{1,2},{2,1},{5,6},{6,5},{9,10},{10,9},{13,14},{14,13},{17,18},{18,... | collective-permute-start | bytes 24584 | tf_op jit(solution)/shard_map/ppermute | solution.py:576
  41.6 1.6 %collective-permute-done.7.g3 = f32[16,128]{1,0:T(8,128)S(1)} collective-permute-done((f32[16,128]{1,0:T(8,128)S(1)}, f32[16,128]{1,0:T(8,128)S(1)}, u32[]{:S(2)}, u32[]{:S(2)}) %collective-permute-start.7) | collective-permute-done | bytes 8224 | tf_op jit(solution)/shard_map/ppermute | solution.py:576
  43.1 10.1 %mass_start.1 = (f32[32,256]{1,0:T(8,128)S(1)}, f32[192,256]{1,0:T(8,128)S(1)}, f32[192,256]{1,0:T(8,128)S(1)}, f32[192,256]{1,0:T(8,128)S(1)}, f32[16,128]{1,0:...) custom-call(f32[16,128]{1,0:T(8,128)S(1)} %collective-permute-done.4.g0, ...), custom_call_target="tpu_custom_call" | custom-call | flops 10000000000 | bytes 1000000 | tf_op jit(solution)/shard_map/mass_start/pallas_call | solution.py:553
  53.2 0.1 collective-permute-start.8
  53.3 2.6 %collective-permute-start.9 = (f32[16,128]{1,0:T(8,128)S(1)}, f32[16,128]{1,0:T(8,128)S(1)}, u32[]{:S(2)}, u32[]{:S(2)}) collective-permute-start(f32[16,128]{1,0:T(8,128)S(1)} %get-tuple-element.60), channel_id=1, source_target_pairs={{4,8},{8,4},{12,16},{16,12},{20,24},{24,20},{28,32},{32,28},{36,40... | collective-permute-start | bytes 24584 | tf_op jit(solution)/shard_map/ppermute | solution.py:574
  55.9 0.1 collective-permute-start.10
  56.0 3.9 %collective-permute-start.11 = (f32[16,128]{1,0:T(8,128)S(1)}, f32[16,128]{1,0:T(8,128)S(1)}, u32[]{:S(2)}, u32[]{:S(2)}) collective-permute-start(f32[16,128]{1,0:T(8,128)S(1)} %get-tuple-element.62), channel_id=1, source_target_pairs={{1,2},{2,1},{5,6},{6,5},{9,10},{10,9},{13,14},{14,13},{17,18},{18,... | collective-permute-start | bytes 24584 | tf_op jit(solution)/shard_map/ppermute | solution.py:576
  59.9 0.5 collective-permute-done.9.g1
  60.4 1.2 %collective-permute-done.11.g3 = f32[16,128]{1,0:T(8,128)S(1)} collective-permute-done((f32[16,128]{1,0:T(8,128)S(1)}, f32[16,128]{1,0:T(8,128)S(1)}, u32[]{:S(2)}, u32[]{:S(2)}) %collective-permute-start.11) | collective-permute-done | bytes 8224 | tf_op jit(solution)/shard_map/ppermute | solution.py:576
  61.6 10.0 %mass_sweep.2 = (f32[192,256]{1,0:T(8,128)S(1)}, f32[192,256]{1,0:T(8,128)S(1)}, f32[192,256]{1,0:T(8,128)S(1)}, f32[192,256]{1,0:T(8,128)S(1)}, f32[16,128]{1,0...) custom-call(f32[16,128]{1,0:T(8,128)S(1)} %collective-permute-done.8.g0, ...), custom_call_target="tpu_custom_call" | custom-call | flops 10000000000 | bytes 1000000 | tf_op jit(solution)/shard_map/mass_sweep/pallas_call | solution.py:553
  71.6 0.1 collective-permute-start.12
  71.7 4.2 %collective-permute-start.13 = (f32[16,128]{1,0:T(8,128)S(1)}, f32[16,128]{1,0:T(8,128)S(1)}, u32[]{:S(2)}, u32[]{:S(2)}) collective-permute-start(f32[16,128]{1,0:T(8,128)S(1)} %get-tuple-element.68), channel_id=1, source_target_pairs={{4,8},{8,4},{12,16},{16,12},{20,24},{24,20},{28,32},{32,28},{36,40... | collective-permute-start | bytes 24584 | tf_op jit(solution)/shard_map/ppermute | solution.py:574
  75.9 0.1 collective-permute-start.14
  76.0 3.6 %collective-permute-start.15 = (f32[16,128]{1,0:T(8,128)S(1)}, f32[16,128]{1,0:T(8,128)S(1)}, u32[]{:S(2)}, u32[]{:S(2)}) collective-permute-start(f32[16,128]{1,0:T(8,128)S(1)} %get-tuple-element.70), channel_id=1, source_target_pairs={{1,2},{2,1},{5,6},{6,5},{9,10},{10,9},{13,14},{14,13},{17,18},{18,... | collective-permute-start | bytes 24584 | tf_op jit(solution)/shard_map/ppermute | solution.py:576
  79.7 1.9 %collective-permute-done.15.g3 = f32[16,128]{1,0:T(8,128)S(1)} collective-permute-done((f32[16,128]{1,0:T(8,128)S(1)}, f32[16,128]{1,0:T(8,128)S(1)}, u32[]{:S(2)}, u32[]{:S(2)}) %collective-permute-start.15) | collective-permute-done | bytes 8224 | tf_op jit(solution)/shard_map/ppermute | solution.py:576
  81.6 10.0 %mass_sweep.3 = (f32[192,256]{1,0:T(8,128)S(1)}, f32[192,256]{1,0:T(8,128)S(1)}, f32[192,256]{1,0:T(8,128)S(1)}, f32[192,256]{1,0:T(8,128)S(1)}, f32[16,128]{1,0...) custom-call(f32[16,128]{1,0:T(8,128)S(1)} %collective-permute-done.12.g0, ...), custom_call_target="tpu_custom_call" | custom-call | flops 10000000000 | bytes 1000000 | tf_op jit(solution)/shard_map/mass_sweep/pallas_call | solution.py:553
  91.6 0.1 collective-permute-start.16
  91.7 2.4 %collective-permute-start.17 = (f32[16,128]{1,0:T(8,128)S(1)}, f32[16,128]{1,0:T(8,128)S(1)}, u32[]{:S(2)}, u32[]{:S(2)}) collective-permute-start(f32[16,128]{1,0:T(8,128)S(1)} %get-tuple-element.76), channel_id=1, source_target_pairs={{4,8},{8,4},{12,16},{16,12},{20,24},{24,20},{28,32},{32,28},{36,40... | collective-permute-start | bytes 24584 | tf_op jit(solution)/shard_map/ppermute | solution.py:574
  94.1 0.1 collective-permute-start.18
  94.2 3.6 %collective-permute-start.19 = (f32[16,128]{1,0:T(8,128)S(1)}, f32[16,128]{1,0:T(8,128)S(1)}, u32[]{:S(2)}, u32[]{:S(2)}) collective-permute-start(f32[16,128]{1,0:T(8,128)S(1)} %get-tuple-element.78), channel_id=1, source_target_pairs={{1,2},{2,1},{5,6},{6,5},{9,10},{10,9},{13,14},{14,13},{17,18},{18,... | collective-permute-start | bytes 24584 | tf_op jit(solution)/shard_map/ppermute | solution.py:576
  97.8 0.9 collective-permute-done.17.g1
  98.8 0.9 collective-permute-done.19.g3
  99.7 5.7 %force_two.1 = (f32[27,256]{1,0:T(8,128)}, f32[3,7936]{1,0:T(4,128)}) custom-call(f32[16,128]{1,0:T(8,128)S(1)} %collective-permute-done.16.g0, f32[16,128]{1,0:T(8,128)S(1)} %collective-permute-done.17.g1, f32[16,128]{1,0:T(8,128)S(1)} %collective-permute-done.18.g2, f32[16,128]{1,0:T(8,128)S(1)} %collective-permute-done.19.g3, ...), custom_call_target="tpu_custom_call" | custom-call | flops 10000000000 | bytes 1000000 | tf_op jit(solution)/shard_map/force_two/pallas_call | solution.py:553
  (35 shorter events, 0.2 us)
Async XLA Ops:
  0.6 18.5 %copy-start.7 = (bf16[2528,256]{1,0:T(8,128)(2,1)S(1)}, bf16[2528,256]{1,0:T(8,128)(2,1)}, u32[]{:S(2)}) copy-start(bf16[2528,256]{1,0:T(8,128)(2,1)} %constant.4.clone._tables.tables) | copy-start | bytes 3883012
  0.6 18.5 %copy-start.5 = (f32[27,256]{1,0:T(8,128)S(1)}, f32[27,256]{1,0:T(8,128)}, u32[]{:S(2)}) copy-start(f32[27,256]{1,0:T(8,128)} %en_ref.1) | copy-start | bytes 82948
  0.7 18.4 %copy-start.4 = (s32[64,256]{1,0:T(8,128)S(1)}, s32[64,256]{1,0:T(8,128)}, u32[]{:S(2)}) copy-start(s32[64,256]{1,0:T(8,128)} %zn.7) | copy-start | bytes 196612
  0.7 18.4 %copy-start.6 = (s32[1,36]{1,0:T(1,128)S(1)}, s32[1,36]{1,0:T(1,128)}, u32[]{:S(2)}) copy-start(s32[1,36]{1,0:T(1,128)} %arrive_ref.1) | copy-start | bytes 436
  0.7 18.4 %copy-start.3 = (f32[3,7936]{1,0:T(4,128)S(1)}, f32[3,7936]{1,0:T(4,128)}, u32[]{:S(2)}) copy-start(f32[3,7936]{1,0:T(4,128)} %vel_ref.1) | copy-start | bytes 285700
  5.1 18.6 %collective-permute-start = (f32[8,3712]{1,0:T(8,128)}, f32[8,3712]{1,0:T(8,128)S(1)}, u32[]{:S(2)}, u32[]{:S(2)}) collective-permute-start(f32[8,3712]{1,0:T(8,128)} %get-tuple-element.46), channel_id=1, source_target_pairs={{2,4},{4,2},{3,5},{5,3},{6,8},{8,6},{7,9},{9,7},{10,12},{12,10},{1... | collective-permute-start | bytes 356360 | tf_op jit(solution)/shard_map/ppermute | solution.py:595
  12.3 11.5 %collective-permute-start.1 = (f32[8,3712]{1,0:T(8,128)}, f32[8,3712]{1,0:T(8,128)S(1)}, u32[]{:S(2)}, u32[]{:S(2)}) collective-permute-start(f32[8,3712]{1,0:T(8,128)} %get-tuple-element.47), channel_id=1, source_target_pairs={{0,2},{2,0},{1,3},{3,1},{4,6},{6,4},{5,7},{7,5},{8,10},{10,8},{9,1... | collective-permute-start | bytes 356360 | tf_op jit(solution)/shard_map/ppermute | solution.py:595
  12.4 11.4 %collective-permute-start.2 = (f32[8,3712]{1,0:T(8,128)}, f32[8,3712]{1,0:T(8,128)S(1)}, u32[]{:S(2)}, u32[]{:S(2)}) collective-permute-start(f32[8,3712]{1,0:T(8,128)} %get-tuple-element.48), channel_id=1, source_target_pairs={{1,2},{2,1},{3,4},{4,3},{5,6},{6,5},{7,8},{8,7},{9,10},{10,9},{11,... | collective-permute-start | bytes 356360 | tf_op jit(solution)/shard_map/ppermute | solution.py:595
  17.2 6.6 %copy-start = (f32[1944,256]{1,0:T(8,128)S(1)}, f32[1944,256]{1,0:T(8,128)}, u32[]{:S(2)}) copy-start(f32[1944,256]{1,0:T(8,128)} %jac_ref.1) | copy-start | bytes 5971972
  17.2 6.6 %copy-start.1 = (f32[729,256]{1,0:T(8,128)S(1)}, f32[729,256]{1,0:T(8,128)}, u32[]{:S(2)}) copy-start(f32[729,256]{1,0:T(8,128)} %inv_ref.1) | copy-start | bytes 2239492
  17.2 6.6 %copy-start.2 = (f32[216,256]{1,0:T(8,128)S(1)}, f32[216,256]{1,0:T(8,128)}, u32[]{:S(2)}) copy-start(f32[216,256]{1,0:T(8,128)} %mass_ref.1) | copy-start | bytes 663556
  17.2 6.6 %copy-start.9 = (s32[8,128]{1,0:T(8,128)S(1)}, s32[8,128]{1,0:T(8,128)}, u32[]{:S(2)}) copy-start(s32[8,128]{1,0:T(8,128)} %get-tuple-element.50.lists_ref.lists) | copy-start | bytes 12292
  17.2 6.6 %collective-permute-start.3 = (f32[8,3712]{1,0:T(8,128)}, f32[8,3712]{1,0:T(8,128)S(1)}, u32[]{:S(2)}, u32[]{:S(2)}) collective-permute-start(f32[8,3712]{1,0:T(8,128)} %get-tuple-element.49), channel_id=1, source_target_pairs={{0,1},{1,0},{2,3},{3,2},{4,5},{5,4},{6,7},{7,6},{8,9},{9,8},{10,11... | collective-permute-start | bytes 356360 | tf_op jit(solution)/shard_map/ppermute | solution.py:595
  23.8 19.3 %copy-start.8 = (bf16[352,256]{1,0:T(8,128)(2,1)S(1)}, bf16[352,256]{1,0:T(8,128)(2,1)}, u32[]{:S(2)}) copy-start(bf16[352,256]{1,0:T(8,128)(2,1)} %constant.5.clone.tables) | copy-start | bytes 540676
  33.1 8.5 %collective-permute-start.4 = (f32[16,128]{1,0:T(8,128)S(1)}, f32[16,128]{1,0:T(8,128)S(1)}, u32[]{:S(2)}, u32[]{:S(2)}) collective-permute-start(f32[16,128]{1,0:T(8,128)S(1)} %get-tuple-element.53), channel_id=1, source_target_pairs={{0,4},{4,0},{8,12},{12,8},{16,20},{20,16},{24,28},{28,24},{32,36},... | collective-permute-start | bytes 24584 | tf_op jit(solution)/shard_map/ppermute | solution.py:573
  33.1 8.4 %collective-permute-start.5 = (f32[16,128]{1,0:T(8,128)S(1)}, f32[16,128]{1,0:T(8,128)S(1)}, u32[]{:S(2)}, u32[]{:S(2)}) collective-permute-start(f32[16,128]{1,0:T(8,128)S(1)} %get-tuple-element.54), channel_id=1, source_target_pairs={{4,8},{8,4},{12,16},{16,12},{20,24},{24,20},{28,32},{32,28},{36,40... | collective-permute-start | bytes 24584 | tf_op jit(solution)/shard_map/ppermute | solution.py:574
  35.6 6.0 %collective-permute-start.6 = (f32[16,128]{1,0:T(8,128)S(1)}, f32[16,128]{1,0:T(8,128)S(1)}, u32[]{:S(2)}, u32[]{:S(2)}) collective-permute-start(f32[16,128]{1,0:T(8,128)S(1)} %get-tuple-element.55), channel_id=1, source_target_pairs={{0,1},{1,0},{2,3},{3,2},{4,5},{5,4},{6,7},{7,6},{8,9},{9,8},{10,11... | collective-permute-start | bytes 24584 | tf_op jit(solution)/shard_map/ppermute | solution.py:575
  36.4 6.8 %collective-permute-start.7 = (f32[16,128]{1,0:T(8,128)S(1)}, f32[16,128]{1,0:T(8,128)S(1)}, u32[]{:S(2)}, u32[]{:S(2)}) collective-permute-start(f32[16,128]{1,0:T(8,128)S(1)} %get-tuple-element.56), channel_id=1, source_target_pairs={{1,2},{2,1},{5,6},{6,5},{9,10},{10,9},{13,14},{14,13},{17,18},{18,... | collective-permute-start | bytes 24584 | tf_op jit(solution)/shard_map/ppermute | solution.py:576
  53.2 6.7 %collective-permute-start.8 = (f32[16,128]{1,0:T(8,128)S(1)}, f32[16,128]{1,0:T(8,128)S(1)}, u32[]{:S(2)}, u32[]{:S(2)}) collective-permute-start(f32[16,128]{1,0:T(8,128)S(1)} %get-tuple-element.59), channel_id=1, source_target_pairs={{0,4},{4,0},{8,12},{12,8},{16,20},{20,16},{24,28},{28,24},{32,36},... | collective-permute-start | bytes 24584 | tf_op jit(solution)/shard_map/ppermute | solution.py:573
  53.3 7.1 %collective-permute-start.9 = (f32[16,128]{1,0:T(8,128)S(1)}, f32[16,128]{1,0:T(8,128)S(1)}, u32[]{:S(2)}, u32[]{:S(2)}) collective-permute-start(f32[16,128]{1,0:T(8,128)S(1)} %get-tuple-element.60), channel_id=1, source_target_pairs={{4,8},{8,4},{12,16},{16,12},{20,24},{24,20},{28,32},{32,28},{36,40... | collective-permute-start | bytes 24584 | tf_op jit(solution)/shard_map/ppermute | solution.py:574
  55.9 4.5 %collective-permute-start.10 = (f32[16,128]{1,0:T(8,128)S(1)}, f32[16,128]{1,0:T(8,128)S(1)}, u32[]{:S(2)}, u32[]{:S(2)}) collective-permute-start(f32[16,128]{1,0:T(8,128)S(1)} %get-tuple-element.61), channel_id=1, source_target_pairs={{0,1},{1,0},{2,3},{3,2},{4,5},{5,4},{6,7},{7,6},{8,9},{9,8},{10,11... | collective-permute-start | bytes 24584 | tf_op jit(solution)/shard_map/ppermute | solution.py:575
  56.0 5.5 %collective-permute-start.11 = (f32[16,128]{1,0:T(8,128)S(1)}, f32[16,128]{1,0:T(8,128)S(1)}, u32[]{:S(2)}, u32[]{:S(2)}) collective-permute-start(f32[16,128]{1,0:T(8,128)S(1)} %get-tuple-element.62), channel_id=1, source_target_pairs={{1,2},{2,1},{5,6},{6,5},{9,10},{10,9},{13,14},{14,13},{17,18},{18,... | collective-permute-start | bytes 24584 | tf_op jit(solution)/shard_map/ppermute | solution.py:576
  71.6 8.0 %collective-permute-start.12 = (f32[16,128]{1,0:T(8,128)S(1)}, f32[16,128]{1,0:T(8,128)S(1)}, u32[]{:S(2)}, u32[]{:S(2)}) collective-permute-start(f32[16,128]{1,0:T(8,128)S(1)} %get-tuple-element.67), channel_id=1, source_target_pairs={{0,4},{4,0},{8,12},{12,8},{16,20},{20,16},{24,28},{28,24},{32,36},... | collective-permute-start | bytes 24584 | tf_op jit(solution)/shard_map/ppermute | solution.py:573
  71.7 8.0 %collective-permute-start.13 = (f32[16,128]{1,0:T(8,128)S(1)}, f32[16,128]{1,0:T(8,128)S(1)}, u32[]{:S(2)}, u32[]{:S(2)}) collective-permute-start(f32[16,128]{1,0:T(8,128)S(1)} %get-tuple-element.68), channel_id=1, source_target_pairs={{4,8},{8,4},{12,16},{16,12},{20,24},{24,20},{28,32},{32,28},{36,40... | collective-permute-start | bytes 24584 | tf_op jit(solution)/shard_map/ppermute | solution.py:574
  75.9 3.8 %collective-permute-start.14 = (f32[16,128]{1,0:T(8,128)S(1)}, f32[16,128]{1,0:T(8,128)S(1)}, u32[]{:S(2)}, u32[]{:S(2)}) collective-permute-start(f32[16,128]{1,0:T(8,128)S(1)} %get-tuple-element.69), channel_id=1, source_target_pairs={{0,1},{1,0},{2,3},{3,2},{4,5},{5,4},{6,7},{7,6},{8,9},{9,8},{10,11... | collective-permute-start | bytes 24584 | tf_op jit(solution)/shard_map/ppermute | solution.py:575
  76.0 5.5 %collective-permute-start.15 = (f32[16,128]{1,0:T(8,128)S(1)}, f32[16,128]{1,0:T(8,128)S(1)}, u32[]{:S(2)}, u32[]{:S(2)}) collective-permute-start(f32[16,128]{1,0:T(8,128)S(1)} %get-tuple-element.70), channel_id=1, source_target_pairs={{1,2},{2,1},{5,6},{6,5},{9,10},{10,9},{13,14},{14,13},{17,18},{18,... | collective-permute-start | bytes 24584 | tf_op jit(solution)/shard_map/ppermute | solution.py:576
  91.6 6.2 %collective-permute-start.16 = (f32[16,128]{1,0:T(8,128)S(1)}, f32[16,128]{1,0:T(8,128)S(1)}, u32[]{:S(2)}, u32[]{:S(2)}) collective-permute-start(f32[16,128]{1,0:T(8,128)S(1)} %get-tuple-element.75), channel_id=1, source_target_pairs={{0,4},{4,0},{8,12},{12,8},{16,20},{20,16},{24,28},{28,24},{32,36},... | collective-permute-start | bytes 24584 | tf_op jit(solution)/shard_map/ppermute | solution.py:573
  91.7 7.1 %collective-permute-start.17 = (f32[16,128]{1,0:T(8,128)S(1)}, f32[16,128]{1,0:T(8,128)S(1)}, u32[]{:S(2)}, u32[]{:S(2)}) collective-permute-start(f32[16,128]{1,0:T(8,128)S(1)} %get-tuple-element.76), channel_id=1, source_target_pairs={{4,8},{8,4},{12,16},{16,12},{20,24},{24,20},{28,32},{32,28},{36,40... | collective-permute-start | bytes 24584 | tf_op jit(solution)/shard_map/ppermute | solution.py:574
  94.1 4.7 %collective-permute-start.18 = (f32[16,128]{1,0:T(8,128)S(1)}, f32[16,128]{1,0:T(8,128)S(1)}, u32[]{:S(2)}, u32[]{:S(2)}) collective-permute-start(f32[16,128]{1,0:T(8,128)S(1)} %get-tuple-element.77), channel_id=1, source_target_pairs={{0,1},{1,0},{2,3},{3,2},{4,5},{5,4},{6,7},{7,6},{8,9},{9,8},{10,11... | collective-permute-start | bytes 24584 | tf_op jit(solution)/shard_map/ppermute | solution.py:575
  94.2 5.5 %collective-permute-start.19 = (f32[16,128]{1,0:T(8,128)S(1)}, f32[16,128]{1,0:T(8,128)S(1)}, u32[]{:S(2)}, u32[]{:S(2)}) collective-permute-start(f32[16,128]{1,0:T(8,128)S(1)} %get-tuple-element.78), channel_id=1, source_target_pairs={{1,2},{2,1},{5,6},{6,5},{9,10},{10,9},{13,14},{14,13},{17,18},{18,... | collective-permute-start | bytes 24584 | tf_op jit(solution)/shard_map/ppermute | solution.py:576

commit v8 on v7

--- a/solution.py
+++ b/solution.py
@@ -462,9 +462,11 @@
 def zone_mass(mass_ref, tables, zone, terms, h):
     lanes = slice(h * HALF, (h + 1) * HALF)
     mass = jnp.concatenate([mass_ref[:, lanes]] * 2, 1)
-    for c in range(0, COMPONENTS, 2):
-        x = jnp.concatenate([zone[c, :, lanes], zone[c + 1, :, lanes]], 1)
-        out = down(entry(tables, MASS_AT, "down"), up(entry(tables, MASS_AT, "up"), x) * mass)
+    pairs = range(0, COMPONENTS, 2)
+    xs = [jnp.concatenate([zone[c, :, lanes], zone[c + 1, :, lanes]], 1) for c in pairs]
+    at_points = [up(entry(tables, MASS_AT, "up"), x) * mass for x in xs]
+    outs = [down(entry(tables, MASS_AT, "down"), x) for x in at_points]
+    for c, out in zip(pairs, outs):
         terms[c, :, lanes] = out[:, :HALF]
         terms[c + 1, :, lanes] = out[:, HALF:]
 

time: 106 us -> 105 us (level)
  Pallas kernels: 54.1 us -> 53 us
    pallas_call x7, Pallas kernels: 54.1 us -> 53 us  [call(): pl.pallas_call(kernel, out_shape=[shape_of(s) for s in outs], in_specs=sp...]
where the time goes in v8:
time: 105 us; the launch traced here: 104 us
  Pallas kernels  53 us (50%)
  starting transfers between devices  43.2 us (41%)
  waiting for transfers between devices  7.02 us (7%)
    pallas_call x7, Pallas kernels, call(): pl.pallas_call(kernel, out_shape=[shape_of(s) for s in outs], in_specs=sp...  53 us
    ppermute x4, starting transfers between devices, exchange(): lax.ppermute(sends[3], 'split', paired(1, n_split))  16.3 us
    ppermute x4, starting transfers between devices, per_device(): lax.ppermute(m, AXES, paired(first, devices, hop))  13.9 us
    ppermute x4, starting transfers between devices, exchange(): lax.ppermute(sends[1], 'curve', paired(1, n_curve))  11.6 us
    ppermute x4, waiting for transfers between devices, exchange(): lax.ppermute(sends[3], 'split', paired(1, n_split))  5.56 us
  transfers between devices with their start and end apart: 20, of which 6 were waited for; matrix products, arithmetic and copies ran while one was open for 0% of the time, Pallas kernels for 4%

profile of v8, /device:TPU:26, one launch (start us, length us, event | category | flops | bytes accessed | tf_op | source)
XLA Modules:
  0.0 104.3 jit_solution(17537247521618867334)
XLA Ops:
  0.7 4.5 %pack.1 = (f32[8,3712]{1,0:T(8,128)}, f32[8,3712]{1,0:T(8,128)}, f32[8,3712]{1,0:T(8,128)}, f32[8,3712]{1,0:T(8,128)}, s32[8,128]{1,0:T(8,128)}) custom-call(s32[1,36]{1,0:T(1,128)} %send_ref.1, s32[1,4,256]{2,1,0:T(4,128)} %shared_ref.1, f32[1944,256]{1,0:T(8,128)} %jac_ref.1, f32[216,256]{1,0:T(8,128)} %mass_ref.1, f32[729,256]{1,0:T(8,128)} %inv_ref.1, ...), custom_call_target="tpu_custom_call" | custom-call | flops 4000000000 | bytes 400000 | tf_op jit(solution)/shard_map/pack/pallas_call | solution.py:555
  5.1 7.1 %collective-permute-start = (f32[8,3712]{1,0:T(8,128)}, f32[8,3712]{1,0:T(8,128)S(1)}, u32[]{:S(2)}, u32[]{:S(2)}) collective-permute-start(f32[8,3712]{1,0:T(8,128)} %get-tuple-element.46), channel_id=1, source_target_pairs={{2,4},{4,2},{3,5},{5,3},{6,8},{8,6},{7,9},{9,7},{10,12},{12,10},{1... | collective-permute-start | bytes 356360 | tf_op jit(solution)/shard_map/ppermute | solution.py:597
  12.4 4.8 %collective-permute-start.2 = (f32[8,3712]{1,0:T(8,128)}, f32[8,3712]{1,0:T(8,128)S(1)}, u32[]{:S(2)}, u32[]{:S(2)}) collective-permute-start(f32[8,3712]{1,0:T(8,128)} %get-tuple-element.48), channel_id=1, source_target_pairs={{1,2},{2,1},{3,4},{4,3},{5,6},{6,5},{7,8},{8,7},{9,10},{10,9},{11,... | collective-permute-start | bytes 356360 | tf_op jit(solution)/shard_map/ppermute | solution.py:597
  17.2 1.9 %collective-permute-start.3 = (f32[8,3712]{1,0:T(8,128)}, f32[8,3712]{1,0:T(8,128)S(1)}, u32[]{:S(2)}, u32[]{:S(2)}) collective-permute-start(f32[8,3712]{1,0:T(8,128)} %get-tuple-element.49), channel_id=1, source_target_pairs={{0,1},{1,0},{2,3},{3,2},{4,5},{5,4},{6,7},{7,6},{8,9},{9,8},{10,11... | collective-permute-start | bytes 356360 | tf_op jit(solution)/shard_map/ppermute | solution.py:597
  19.1 4.6 %prep.1 = (f32[96,256]{1,0:T(8,128)S(1)}, f32[3,64,256]{2,1,0:T(8,128)S(1)}, bf16[64,256,256]{2,1,0:T(8,128)(2,1)S(1)}) custom-call(f32[3,7936]{1,0:T(4,128)S(1)} %copy-done.3, s32[64,256]{1,0:T(8,128)S(1)} %copy-done.4, s32[1,36]{1,0:T(1,128)S(1)} %copy-done.6, f32[27,256]{1,0:T(8,128)S(1)} %copy-done.5, bf16[2528,256]{1,0:T(8,128)(2,1)S(1)} %copy-done.7), custom_call_target="tpu_custom_call" | custom-call | flops 10000000000 | bytes 1000000 | tf_op jit(solution)/shard_map/prep/pallas_call | solution.py:555
  23.9 9.2 %force_one.1 = (f32[1944,256]{1,0:T(8,128)S(1)}, f32[216,256]{1,0:T(8,128)S(1)}, f32[729,256]{1,0:T(8,128)S(1)}, f32[27,256]{1,0:T(8,128)S(1)}, f32[27,256]{1,0:...) custom-call(s32[1,36]{1,0:T(1,128)S(1)} %copy-done.6, ...), custom_call_target="tpu_custom_call" | custom-call | flops 10000000000 | bytes 1000000 | tf_op jit(solution)/shard_map/force_one/pallas_call | solution.py:555
  33.1 0.1 collective-permute-start.4
  33.1 2.4 %collective-permute-start.5 = (f32[16,128]{1,0:T(8,128)S(1)}, f32[16,128]{1,0:T(8,128)S(1)}, u32[]{:S(2)}, u32[]{:S(2)}) collective-permute-start(f32[16,128]{1,0:T(8,128)S(1)} %get-tuple-element.54), channel_id=1, source_target_pairs={{4,8},{8,4},{12,16},{16,12},{20,24},{24,20},{28,32},{32,28},{36,40... | collective-permute-start | bytes 24584 | tf_op jit(solution)/shard_map/ppermute | solution.py:576
  35.6 0.8 collective-permute-start.6
  36.4 5.1 %collective-permute-start.7 = (f32[16,128]{1,0:T(8,128)S(1)}, f32[16,128]{1,0:T(8,128)S(1)}, u32[]{:S(2)}, u32[]{:S(2)}) collective-permute-start(f32[16,128]{1,0:T(8,128)S(1)} %get-tuple-element.56), channel_id=1, source_target_pairs={{1,2},{2,1},{5,6},{6,5},{9,10},{10,9},{13,14},{14,13},{17,18},{18,... | collective-permute-start | bytes 24584 | tf_op jit(solution)/shard_map/ppermute | solution.py:578
  41.6 1.6 %collective-permute-done.7.g3 = f32[16,128]{1,0:T(8,128)S(1)} collective-permute-done((f32[16,128]{1,0:T(8,128)S(1)}, f32[16,128]{1,0:T(8,128)S(1)}, u32[]{:S(2)}, u32[]{:S(2)}) %collective-permute-start.7) | collective-permute-done | bytes 8224 | tf_op jit(solution)/shard_map/ppermute | solution.py:578
  43.1 9.7 %mass_start.1 = (f32[32,256]{1,0:T(8,128)S(1)}, f32[192,256]{1,0:T(8,128)S(1)}, f32[192,256]{1,0:T(8,128)S(1)}, f32[192,256]{1,0:T(8,128)S(1)}, f32[16,128]{1,0:...) custom-call(f32[16,128]{1,0:T(8,128)S(1)} %collective-permute-done.4.g0, ...), custom_call_target="tpu_custom_call" | custom-call | flops 10000000000 | bytes 1000000 | tf_op jit(solution)/shard_map/mass_start/pallas_call | solution.py:555
  52.9 0.1 collective-permute-start.8
  52.9 2.6 %collective-permute-start.9 = (f32[16,128]{1,0:T(8,128)S(1)}, f32[16,128]{1,0:T(8,128)S(1)}, u32[]{:S(2)}, u32[]{:S(2)}) collective-permute-start(f32[16,128]{1,0:T(8,128)S(1)} %get-tuple-element.60), channel_id=1, source_target_pairs={{4,8},{8,4},{12,16},{16,12},{20,24},{24,20},{28,32},{32,28},{36,40... | collective-permute-start | bytes 24584 | tf_op jit(solution)/shard_map/ppermute | solution.py:576
  55.6 0.1 collective-permute-start.10
  55.7 3.9 %collective-permute-start.11 = (f32[16,128]{1,0:T(8,128)S(1)}, f32[16,128]{1,0:T(8,128)S(1)}, u32[]{:S(2)}, u32[]{:S(2)}) collective-permute-start(f32[16,128]{1,0:T(8,128)S(1)} %get-tuple-element.62), channel_id=1, source_target_pairs={{1,2},{2,1},{5,6},{6,5},{9,10},{10,9},{13,14},{14,13},{17,18},{18,... | collective-permute-start | bytes 24584 | tf_op jit(solution)/shard_map/ppermute | solution.py:578
  59.5 0.5 collective-permute-done.9.g1
  60.0 1.2 %collective-permute-done.11.g3 = f32[16,128]{1,0:T(8,128)S(1)} collective-permute-done((f32[16,128]{1,0:T(8,128)S(1)}, f32[16,128]{1,0:T(8,128)S(1)}, u32[]{:S(2)}, u32[]{:S(2)}) %collective-permute-start.11) | collective-permute-done | bytes 8224 | tf_op jit(solution)/shard_map/ppermute | solution.py:578
  61.2 9.7 %mass_sweep.2 = (f32[192,256]{1,0:T(8,128)S(1)}, f32[192,256]{1,0:T(8,128)S(1)}, f32[192,256]{1,0:T(8,128)S(1)}, f32[192,256]{1,0:T(8,128)S(1)}, f32[16,128]{1,0...) custom-call(f32[16,128]{1,0:T(8,128)S(1)} %collective-permute-done.8.g0, ...), custom_call_target="tpu_custom_call" | custom-call | flops 10000000000 | bytes 1000000 | tf_op jit(solution)/shard_map/mass_sweep/pallas_call | solution.py:555
  70.9 0.1 collective-permute-start.12
  71.0 4.2 %collective-permute-start.13 = (f32[16,128]{1,0:T(8,128)S(1)}, f32[16,128]{1,0:T(8,128)S(1)}, u32[]{:S(2)}, u32[]{:S(2)}) collective-permute-start(f32[16,128]{1,0:T(8,128)S(1)} %get-tuple-element.68), channel_id=1, source_target_pairs={{4,8},{8,4},{12,16},{16,12},{20,24},{24,20},{28,32},{32,28},{36,40... | collective-permute-start | bytes 24584 | tf_op jit(solution)/shard_map/ppermute | solution.py:576
  75.2 0.1 collective-permute-start.14
  75.3 3.6 %collective-permute-start.15 = (f32[16,128]{1,0:T(8,128)S(1)}, f32[16,128]{1,0:T(8,128)S(1)}, u32[]{:S(2)}, u32[]{:S(2)}) collective-permute-start(f32[16,128]{1,0:T(8,128)S(1)} %get-tuple-element.70), channel_id=1, source_target_pairs={{1,2},{2,1},{5,6},{6,5},{9,10},{10,9},{13,14},{14,13},{17,18},{18,... | collective-permute-start | bytes 24584 | tf_op jit(solution)/shard_map/ppermute | solution.py:578
  78.9 1.9 %collective-permute-done.15.g3 = f32[16,128]{1,0:T(8,128)S(1)} collective-permute-done((f32[16,128]{1,0:T(8,128)S(1)}, f32[16,128]{1,0:T(8,128)S(1)}, u32[]{:S(2)}, u32[]{:S(2)}) %collective-permute-start.15) | collective-permute-done | bytes 8224 | tf_op jit(solution)/shard_map/ppermute | solution.py:578
  80.8 9.7 %mass_sweep.3 = (f32[192,256]{1,0:T(8,128)S(1)}, f32[192,256]{1,0:T(8,128)S(1)}, f32[192,256]{1,0:T(8,128)S(1)}, f32[192,256]{1,0:T(8,128)S(1)}, f32[16,128]{1,0...) custom-call(f32[16,128]{1,0:T(8,128)S(1)} %collective-permute-done.12.g0, ...), custom_call_target="tpu_custom_call" | custom-call | flops 10000000000 | bytes 1000000 | tf_op jit(solution)/shard_map/mass_sweep/pallas_call | solution.py:555
  90.5 0.1 collective-permute-start.16
  90.6 2.4 %collective-permute-start.17 = (f32[16,128]{1,0:T(8,128)S(1)}, f32[16,128]{1,0:T(8,128)S(1)}, u32[]{:S(2)}, u32[]{:S(2)}) collective-permute-start(f32[16,128]{1,0:T(8,128)S(1)} %get-tuple-element.76), channel_id=1, source_target_pairs={{4,8},{8,4},{12,16},{16,12},{20,24},{24,20},{28,32},{32,28},{36,40... | collective-permute-start | bytes 24584 | tf_op jit(solution)/shard_map/ppermute | solution.py:576
  93.0 0.1 collective-permute-start.18
  93.1 3.6 %collective-permute-start.19 = (f32[16,128]{1,0:T(8,128)S(1)}, f32[16,128]{1,0:T(8,128)S(1)}, u32[]{:S(2)}, u32[]{:S(2)}) collective-permute-start(f32[16,128]{1,0:T(8,128)S(1)} %get-tuple-element.78), channel_id=1, source_target_pairs={{1,2},{2,1},{5,6},{6,5},{9,10},{10,9},{13,14},{14,13},{17,18},{18,... | collective-permute-start | bytes 24584 | tf_op jit(solution)/shard_map/ppermute | solution.py:578
  96.7 0.9 collective-permute-done.17.g1
  97.7 0.9 collective-permute-done.19.g3
  98.6 5.7 %force_two.1 = (f32[27,256]{1,0:T(8,128)}, f32[3,7936]{1,0:T(4,128)}) custom-call(f32[16,128]{1,0:T(8,128)S(1)} %collective-permute-done.16.g0, f32[16,128]{1,0:T(8,128)S(1)} %collective-permute-done.17.g1, f32[16,128]{1,0:T(8,128)S(1)} %collective-permute-done.18.g2, f32[16,128]{1,0:T(8,128)S(1)} %collective-permute-done.19.g3, ...), custom_call_target="tpu_custom_call" | custom-call | flops 10000000000 | bytes 1000000 | tf_op jit(solution)/shard_map/force_two/pallas_call | solution.py:555
  (35 shorter events, 0.2 us)
Async XLA Ops:
  0.6 18.5 %copy-start.7 = (bf16[2528,256]{1,0:T(8,128)(2,1)S(1)}, bf16[2528,256]{1,0:T(8,128)(2,1)}, u32[]{:S(2)}) copy-start(bf16[2528,256]{1,0:T(8,128)(2,1)} %constant.4.clone._tables.tables) | copy-start | bytes 3883012
  0.6 18.5 %copy-start.5 = (f32[27,256]{1,0:T(8,128)S(1)}, f32[27,256]{1,0:T(8,128)}, u32[]{:S(2)}) copy-start(f32[27,256]{1,0:T(8,128)} %en_ref.1) | copy-start | bytes 82948
  0.7 18.4 %copy-start.4 = (s32[64,256]{1,0:T(8,128)S(1)}, s32[64,256]{1,0:T(8,128)}, u32[]{:S(2)}) copy-start(s32[64,256]{1,0:T(8,128)} %zn.7) | copy-start | bytes 196612
  0.7 18.4 %copy-start.6 = (s32[1,36]{1,0:T(1,128)S(1)}, s32[1,36]{1,0:T(1,128)}, u32[]{:S(2)}) copy-start(s32[1,36]{1,0:T(1,128)} %arrive_ref.1) | copy-start | bytes 436
  0.7 18.4 %copy-start.3 = (f32[3,7936]{1,0:T(4,128)S(1)}, f32[3,7936]{1,0:T(4,128)}, u32[]{:S(2)}) copy-start(f32[3,7936]{1,0:T(4,128)} %vel_ref.1) | copy-start | bytes 285700
  5.1 18.6 %collective-permute-start = (f32[8,3712]{1,0:T(8,128)}, f32[8,3712]{1,0:T(8,128)S(1)}, u32[]{:S(2)}, u32[]{:S(2)}) collective-permute-start(f32[8,3712]{1,0:T(8,128)} %get-tuple-element.46), channel_id=1, source_target_pairs={{2,4},{4,2},{3,5},{5,3},{6,8},{8,6},{7,9},{9,7},{10,12},{12,10},{1... | collective-permute-start | bytes 356360 | tf_op jit(solution)/shard_map/ppermute | solution.py:597
  12.3 11.5 %collective-permute-start.1 = (f32[8,3712]{1,0:T(8,128)}, f32[8,3712]{1,0:T(8,128)S(1)}, u32[]{:S(2)}, u32[]{:S(2)}) collective-permute-start(f32[8,3712]{1,0:T(8,128)} %get-tuple-element.47), channel_id=1, source_target_pairs={{0,2},{2,0},{1,3},{3,1},{4,6},{6,4},{5,7},{7,5},{8,10},{10,8},{9,1... | collective-permute-start | bytes 356360 | tf_op jit(solution)/shard_map/ppermute | solution.py:597
  12.4 11.4 %collective-permute-start.2 = (f32[8,3712]{1,0:T(8,128)}, f32[8,3712]{1,0:T(8,128)S(1)}, u32[]{:S(2)}, u32[]{:S(2)}) collective-permute-start(f32[8,3712]{1,0:T(8,128)} %get-tuple-element.48), channel_id=1, source_target_pairs={{1,2},{2,1},{3,4},{4,3},{5,6},{6,5},{7,8},{8,7},{9,10},{10,9},{11,... | collective-permute-start | bytes 356360 | tf_op jit(solution)/shard_map/ppermute | solution.py:597
  17.2 6.6 %copy-start = (f32[1944,256]{1,0:T(8,128)S(1)}, f32[1944,256]{1,0:T(8,128)}, u32[]{:S(2)}) copy-start(f32[1944,256]{1,0:T(8,128)} %jac_ref.1) | copy-start | bytes 5971972
  17.2 6.6 %copy-start.1 = (f32[729,256]{1,0:T(8,128)S(1)}, f32[729,256]{1,0:T(8,128)}, u32[]{:S(2)}) copy-start(f32[729,256]{1,0:T(8,128)} %inv_ref.1) | copy-start | bytes 2239492
  17.2 6.6 %copy-start.2 = (f32[216,256]{1,0:T(8,128)S(1)}, f32[216,256]{1,0:T(8,128)}, u32[]{:S(2)}) copy-start(f32[216,256]{1,0:T(8,128)} %mass_ref.1) | copy-start | bytes 663556
  17.2 6.6 %copy-start.9 = (s32[8,128]{1,0:T(8,128)S(1)}, s32[8,128]{1,0:T(8,128)}, u32[]{:S(2)}) copy-start(s32[8,128]{1,0:T(8,128)} %get-tuple-element.50.lists_ref.lists) | copy-start | bytes 12292
  17.2 6.6 %collective-permute-start.3 = (f32[8,3712]{1,0:T(8,128)}, f32[8,3712]{1,0:T(8,128)S(1)}, u32[]{:S(2)}, u32[]{:S(2)}) collective-permute-start(f32[8,3712]{1,0:T(8,128)} %get-tuple-element.49), channel_id=1, source_target_pairs={{0,1},{1,0},{2,3},{3,2},{4,5},{5,4},{6,7},{7,6},{8,9},{9,8},{10,11... | collective-permute-start | bytes 356360 | tf_op jit(solution)/shard_map/ppermute | solution.py:597
  23.8 19.3 %copy-start.8 = (bf16[352,256]{1,0:T(8,128)(2,1)S(1)}, bf16[352,256]{1,0:T(8,128)(2,1)}, u32[]{:S(2)}) copy-start(bf16[352,256]{1,0:T(8,128)(2,1)} %constant.5.clone.tables) | copy-start | bytes 540676
  33.1 8.5 %collective-permute-start.4 = (f32[16,128]{1,0:T(8,128)S(1)}, f32[16,128]{1,0:T(8,128)S(1)}, u32[]{:S(2)}, u32[]{:S(2)}) collective-permute-start(f32[16,128]{1,0:T(8,128)S(1)} %get-tuple-element.53), channel_id=1, source_target_pairs={{0,4},{4,0},{8,12},{12,8},{16,20},{20,16},{24,28},{28,24},{32,36},... | collective-permute-start | bytes 24584 | tf_op jit(solution)/shard_map/ppermute | solution.py:575
  33.1 8.4 %collective-permute-start.5 = (f32[16,128]{1,0:T(8,128)S(1)}, f32[16,128]{1,0:T(8,128)S(1)}, u32[]{:S(2)}, u32[]{:S(2)}) collective-permute-start(f32[16,128]{1,0:T(8,128)S(1)} %get-tuple-element.54), channel_id=1, source_target_pairs={{4,8},{8,4},{12,16},{16,12},{20,24},{24,20},{28,32},{32,28},{36,40... | collective-permute-start | bytes 24584 | tf_op jit(solution)/shard_map/ppermute | solution.py:576
  35.6 6.0 %collective-permute-start.6 = (f32[16,128]{1,0:T(8,128)S(1)}, f32[16,128]{1,0:T(8,128)S(1)}, u32[]{:S(2)}, u32[]{:S(2)}) collective-permute-start(f32[16,128]{1,0:T(8,128)S(1)} %get-tuple-element.55), channel_id=1, source_target_pairs={{0,1},{1,0},{2,3},{3,2},{4,5},{5,4},{6,7},{7,6},{8,9},{9,8},{10,11... | collective-permute-start | bytes 24584 | tf_op jit(solution)/shard_map/ppermute | solution.py:577
  36.4 6.8 %collective-permute-start.7 = (f32[16,128]{1,0:T(8,128)S(1)}, f32[16,128]{1,0:T(8,128)S(1)}, u32[]{:S(2)}, u32[]{:S(2)}) collective-permute-start(f32[16,128]{1,0:T(8,128)S(1)} %get-tuple-element.56), channel_id=1, source_target_pairs={{1,2},{2,1},{5,6},{6,5},{9,10},{10,9},{13,14},{14,13},{17,18},{18,... | collective-permute-start | bytes 24584 | tf_op jit(solution)/shard_map/ppermute | solution.py:578
  52.9 6.7 %collective-permute-start.8 = (f32[16,128]{1,0:T(8,128)S(1)}, f32[16,128]{1,0:T(8,128)S(1)}, u32[]{:S(2)}, u32[]{:S(2)}) collective-permute-start(f32[16,128]{1,0:T(8,128)S(1)} %get-tuple-element.59), channel_id=1, source_target_pairs={{0,4},{4,0},{8,12},{12,8},{16,20},{20,16},{24,28},{28,24},{32,36},... | collective-permute-start | bytes 24584 | tf_op jit(solution)/shard_map/ppermute | solution.py:575
  52.9 7.1 %collective-permute-start.9 = (f32[16,128]{1,0:T(8,128)S(1)}, f32[16,128]{1,0:T(8,128)S(1)}, u32[]{:S(2)}, u32[]{:S(2)}) collective-permute-start(f32[16,128]{1,0:T(8,128)S(1)} %get-tuple-element.60), channel_id=1, source_target_pairs={{4,8},{8,4},{12,16},{16,12},{20,24},{24,20},{28,32},{32,28},{36,40... | collective-permute-start | bytes 24584 | tf_op jit(solution)/shard_map/ppermute | solution.py:576
  55.6 4.5 %collective-permute-start.10 = (f32[16,128]{1,0:T(8,128)S(1)}, f32[16,128]{1,0:T(8,128)S(1)}, u32[]{:S(2)}, u32[]{:S(2)}) collective-permute-start(f32[16,128]{1,0:T(8,128)S(1)} %get-tuple-element.61), channel_id=1, source_target_pairs={{0,1},{1,0},{2,3},{3,2},{4,5},{5,4},{6,7},{7,6},{8,9},{9,8},{10,11... | collective-permute-start | bytes 24584 | tf_op jit(solution)/shard_map/ppermute | solution.py:577
  55.7 5.5 %collective-permute-start.11 = (f32[16,128]{1,0:T(8,128)S(1)}, f32[16,128]{1,0:T(8,128)S(1)}, u32[]{:S(2)}, u32[]{:S(2)}) collective-permute-start(f32[16,128]{1,0:T(8,128)S(1)} %get-tuple-element.62), channel_id=1, source_target_pairs={{1,2},{2,1},{5,6},{6,5},{9,10},{10,9},{13,14},{14,13},{17,18},{18,... | collective-permute-start | bytes 24584 | tf_op jit(solution)/shard_map/ppermute | solution.py:578
  70.9 8.0 %collective-permute-start.12 = (f32[16,128]{1,0:T(8,128)S(1)}, f32[16,128]{1,0:T(8,128)S(1)}, u32[]{:S(2)}, u32[]{:S(2)}) collective-permute-start(f32[16,128]{1,0:T(8,128)S(1)} %get-tuple-element.67), channel_id=1, source_target_pairs={{0,4},{4,0},{8,12},{12,8},{16,20},{20,16},{24,28},{28,24},{32,36},... | collective-permute-start | bytes 24584 | tf_op jit(solution)/shard_map/ppermute | solution.py:575
  71.0 8.0 %collective-permute-start.13 = (f32[16,128]{1,0:T(8,128)S(1)}, f32[16,128]{1,0:T(8,128)S(1)}, u32[]{:S(2)}, u32[]{:S(2)}) collective-permute-start(f32[16,128]{1,0:T(8,128)S(1)} %get-tuple-element.68), channel_id=1, source_target_pairs={{4,8},{8,4},{12,16},{16,12},{20,24},{24,20},{28,32},{32,28},{36,40... | collective-permute-start | bytes 24584 | tf_op jit(solution)/shard_map/ppermute | solution.py:576
  75.2 3.8 %collective-permute-start.14 = (f32[16,128]{1,0:T(8,128)S(1)}, f32[16,128]{1,0:T(8,128)S(1)}, u32[]{:S(2)}, u32[]{:S(2)}) collective-permute-start(f32[16,128]{1,0:T(8,128)S(1)} %get-tuple-element.69), channel_id=1, source_target_pairs={{0,1},{1,0},{2,3},{3,2},{4,5},{5,4},{6,7},{7,6},{8,9},{9,8},{10,11... | collective-permute-start | bytes 24584 | tf_op jit(solution)/shard_map/ppermute | solution.py:577
  75.3 5.5 %collective-permute-start.15 = (f32[16,128]{1,0:T(8,128)S(1)}, f32[16,128]{1,0:T(8,128)S(1)}, u32[]{:S(2)}, u32[]{:S(2)}) collective-permute-start(f32[16,128]{1,0:T(8,128)S(1)} %get-tuple-element.70), channel_id=1, source_target_pairs={{1,2},{2,1},{5,6},{6,5},{9,10},{10,9},{13,14},{14,13},{17,18},{18,... | collective-permute-start | bytes 24584 | tf_op jit(solution)/shard_map/ppermute | solution.py:578
  90.5 6.2 %collective-permute-start.16 = (f32[16,128]{1,0:T(8,128)S(1)}, f32[16,128]{1,0:T(8,128)S(1)}, u32[]{:S(2)}, u32[]{:S(2)}) collective-permute-start(f32[16,128]{1,0:T(8,128)S(1)} %get-tuple-element.75), channel_id=1, source_target_pairs={{0,4},{4,0},{8,12},{12,8},{16,20},{20,16},{24,28},{28,24},{32,36},... | collective-permute-start | bytes 24584 | tf_op jit(solution)/shard_map/ppermute | solution.py:575
  90.6 7.1 %collective-permute-start.17 = (f32[16,128]{1,0:T(8,128)S(1)}, f32[16,128]{1,0:T(8,128)S(1)}, u32[]{:S(2)}, u32[]{:S(2)}) collective-permute-start(f32[16,128]{1,0:T(8,128)S(1)} %get-tuple-element.76), channel_id=1, source_target_pairs={{4,8},{8,4},{12,16},{16,12},{20,24},{24,20},{28,32},{32,28},{36,40... | collective-permute-start | bytes 24584 | tf_op jit(solution)/shard_map/ppermute | solution.py:576
  93.0 4.7 %collective-permute-start.18 = (f32[16,128]{1,0:T(8,128)S(1)}, f32[16,128]{1,0:T(8,128)S(1)}, u32[]{:S(2)}, u32[]{:S(2)}) collective-permute-start(f32[16,128]{1,0:T(8,128)S(1)} %get-tuple-element.77), channel_id=1, source_target_pairs={{0,1},{1,0},{2,3},{3,2},{4,5},{5,4},{6,7},{7,6},{8,9},{9,8},{10,11... | collective-permute-start | bytes 24584 | tf_op jit(solution)/shard_map/ppermute | solution.py:577
  93.1 5.5 %collective-permute-start.19 = (f32[16,128]{1,0:T(8,128)S(1)}, f32[16,128]{1,0:T(8,128)S(1)}, u32[]{:S(2)}, u32[]{:S(2)}) collective-permute-start(f32[16,128]{1,0:T(8,128)S(1)} %get-tuple-element.78), channel_id=1, source_target_pairs={{1,2},{2,1},{5,6},{6,5},{9,10},{10,9},{13,14},{14,13},{17,18},{18,... | collective-permute-start | bytes 24584 | tf_op jit(solution)/shard_map/ppermute | solution.py:578

commit v9 on v8

--- a/solution.py
+++ b/solution.py
@@ -262,19 +262,13 @@
         if v_ref is not None:
             high, low = split2(v_ref[c])
             vc = jnp.concatenate([high, low, high], 0)
-        term = jnp.zeros((NPZ, WIDE), F32)
-        for k in range(3):
-            w = jac_ref[(3 * k + c) * QP : (3 * k + c + 1) * QP, :] * pressure
-            if v_ref is not None:
-                dv = dot(get("up%d" % k), vc)
-                if c == 0 and k == 0:
-                    work_ref[...] = w * dv
-                else:
-                    work_ref[...] += w * dv
-            if t_ref is not None:
-                term = term + down(get("down%d" % k), w)
+        ws = [jac_ref[(3 * k + c) * QP : (3 * k + c + 1) * QP, :] * pressure for k in range(3)]
+        if v_ref is not None:
+            for k in range(3):
+                work = ws[k] * dot(get("up%d" % k), vc)
+                work_ref[...] = work if c == 0 and k == 0 else work_ref[...] + work
         if t_ref is not None:
-            t_ref[at + c] = term
+            t_ref[at + c] = sum(down(get("down%d" % k), ws[k]) for k in range(3))
     if v_ref is None:
         return None
     wh, wl = split2(work_ref[...])

time: 105 us -> 105 us (level)
  no operation moved by 1% of the time
where the time goes in v9:
time: 105 us; the launch traced here: 104 us
  Pallas kernels  52.7 us (50%)
  starting transfers between devices  43.2 us (41%)
  waiting for transfers between devices  7.01 us (7%)
    pallas_call x7, Pallas kernels, call(): pl.pallas_call(kernel, out_shape=[shape_of(s) for s in outs], in_specs=sp...  52.7 us
    ppermute x4, starting transfers between devices, exchange(): lax.ppermute(sends[3], 'split', paired(1, n_split))  16.3 us
    ppermute x4, starting transfers between devices, per_device(): lax.ppermute(m, AXES, paired(first, devices, hop))  13.9 us
    ppermute x4, starting transfers between devices, exchange(): lax.ppermute(sends[1], 'curve', paired(1, n_curve))  11.6 us
    ppermute x4, waiting for transfers between devices, exchange(): lax.ppermute(sends[3], 'split', paired(1, n_split))  5.56 us
  transfers between devices with their start and end apart: 20, of which 6 were waited for; matrix products, arithmetic and copies ran while one was open for 0% of the time, Pallas kernels for 4%

profile of v9, /device:TPU:26, one launch (start us, length us, event | category | flops | bytes accessed | tf_op | source)
XLA Modules:
  0.0 104.0 jit_solution(208726799133960192)
XLA Ops:
  0.7 4.5 %pack.1 = (f32[8,3712]{1,0:T(8,128)}, f32[8,3712]{1,0:T(8,128)}, f32[8,3712]{1,0:T(8,128)}, f32[8,3712]{1,0:T(8,128)}, s32[8,128]{1,0:T(8,128)}) custom-call(s32[1,36]{1,0:T(1,128)} %send_ref.1, s32[1,4,256]{2,1,0:T(4,128)} %shared_ref.1, f32[1944,256]{1,0:T(8,128)} %jac_ref.1, f32[216,256]{1,0:T(8,128)} %mass_ref.1, f32[729,256]{1,0:T(8,128)} %inv_ref.1, ...), custom_call_target="tpu_custom_call" | custom-call | flops 4000000000 | bytes 400000 | tf_op jit(solution)/shard_map/pack/pallas_call | solution.py:549
  5.1 7.1 %collective-permute-start = (f32[8,3712]{1,0:T(8,128)}, f32[8,3712]{1,0:T(8,128)S(1)}, u32[]{:S(2)}, u32[]{:S(2)}) collective-permute-start(f32[8,3712]{1,0:T(8,128)} %get-tuple-element.46), channel_id=1, source_target_pairs={{2,4},{4,2},{3,5},{5,3},{6,8},{8,6},{7,9},{9,7},{10,12},{12,10},{1... | collective-permute-start | bytes 356360 | tf_op jit(solution)/shard_map/ppermute | solution.py:591
  12.4 4.8 %collective-permute-start.2 = (f32[8,3712]{1,0:T(8,128)}, f32[8,3712]{1,0:T(8,128)S(1)}, u32[]{:S(2)}, u32[]{:S(2)}) collective-permute-start(f32[8,3712]{1,0:T(8,128)} %get-tuple-element.48), channel_id=1, source_target_pairs={{1,2},{2,1},{3,4},{4,3},{5,6},{6,5},{7,8},{8,7},{9,10},{10,9},{11,... | collective-permute-start | bytes 356360 | tf_op jit(solution)/shard_map/ppermute | solution.py:591
  17.2 1.9 %collective-permute-start.3 = (f32[8,3712]{1,0:T(8,128)}, f32[8,3712]{1,0:T(8,128)S(1)}, u32[]{:S(2)}, u32[]{:S(2)}) collective-permute-start(f32[8,3712]{1,0:T(8,128)} %get-tuple-element.49), channel_id=1, source_target_pairs={{0,1},{1,0},{2,3},{3,2},{4,5},{5,4},{6,7},{7,6},{8,9},{9,8},{10,11... | collective-permute-start | bytes 356360 | tf_op jit(solution)/shard_map/ppermute | solution.py:591
  19.1 4.6 %prep.1 = (f32[96,256]{1,0:T(8,128)S(1)}, f32[3,64,256]{2,1,0:T(8,128)S(1)}, bf16[64,256,256]{2,1,0:T(8,128)(2,1)S(1)}) custom-call(f32[3,7936]{1,0:T(4,128)S(1)} %copy-done.3, s32[64,256]{1,0:T(8,128)S(1)} %copy-done.4, s32[1,36]{1,0:T(1,128)S(1)} %copy-done.6, f32[27,256]{1,0:T(8,128)S(1)} %copy-done.5, bf16[2528,256]{1,0:T(8,128)(2,1)S(1)} %copy-done.7), custom_call_target="tpu_custom_call" | custom-call | flops 10000000000 | bytes 1000000 | tf_op jit(solution)/shard_map/prep/pallas_call | solution.py:549
  23.9 8.9 %force_one.1 = (f32[1944,256]{1,0:T(8,128)S(1)}, f32[216,256]{1,0:T(8,128)S(1)}, f32[729,256]{1,0:T(8,128)S(1)}, f32[27,256]{1,0:T(8,128)S(1)}, f32[27,256]{1,0:...) custom-call(s32[1,36]{1,0:T(1,128)S(1)} %copy-done.6, ...), custom_call_target="tpu_custom_call" | custom-call | flops 10000000000 | bytes 1000000 | tf_op jit(solution)/shard_map/force_one/pallas_call | solution.py:549
  32.8 0.1 collective-permute-start.4
  32.9 2.4 %collective-permute-start.5 = (f32[16,128]{1,0:T(8,128)S(1)}, f32[16,128]{1,0:T(8,128)S(1)}, u32[]{:S(2)}, u32[]{:S(2)}) collective-permute-start(f32[16,128]{1,0:T(8,128)S(1)} %get-tuple-element.54), channel_id=1, source_target_pairs={{4,8},{8,4},{12,16},{16,12},{20,24},{24,20},{28,32},{32,28},{36,40... | collective-permute-start | bytes 24584 | tf_op jit(solution)/shard_map/ppermute | solution.py:570
  35.3 0.8 collective-permute-start.6
  36.1 5.1 %collective-permute-start.7 = (f32[16,128]{1,0:T(8,128)S(1)}, f32[16,128]{1,0:T(8,128)S(1)}, u32[]{:S(2)}, u32[]{:S(2)}) collective-permute-start(f32[16,128]{1,0:T(8,128)S(1)} %get-tuple-element.56), channel_id=1, source_target_pairs={{1,2},{2,1},{5,6},{6,5},{9,10},{10,9},{13,14},{14,13},{17,18},{18,... | collective-permute-start | bytes 24584 | tf_op jit(solution)/shard_map/ppermute | solution.py:572
  41.3 1.6 %collective-permute-done.7.g3 = f32[16,128]{1,0:T(8,128)S(1)} collective-permute-done((f32[16,128]{1,0:T(8,128)S(1)}, f32[16,128]{1,0:T(8,128)S(1)}, u32[]{:S(2)}, u32[]{:S(2)}) %collective-permute-start.7) | collective-permute-done | bytes 8224 | tf_op jit(solution)/shard_map/ppermute | solution.py:572
  42.9 9.7 %mass_start.1 = (f32[32,256]{1,0:T(8,128)S(1)}, f32[192,256]{1,0:T(8,128)S(1)}, f32[192,256]{1,0:T(8,128)S(1)}, f32[192,256]{1,0:T(8,128)S(1)}, f32[16,128]{1,0:...) custom-call(f32[16,128]{1,0:T(8,128)S(1)} %collective-permute-done.4.g0, ...), custom_call_target="tpu_custom_call" | custom-call | flops 10000000000 | bytes 1000000 | tf_op jit(solution)/shard_map/mass_start/pallas_call | solution.py:549
  52.6 0.1 collective-permute-start.8
  52.7 2.6 %collective-permute-start.9 = (f32[16,128]{1,0:T(8,128)S(1)}, f32[16,128]{1,0:T(8,128)S(1)}, u32[]{:S(2)}, u32[]{:S(2)}) collective-permute-start(f32[16,128]{1,0:T(8,128)S(1)} %get-tuple-element.60), channel_id=1, source_target_pairs={{4,8},{8,4},{12,16},{16,12},{20,24},{24,20},{28,32},{32,28},{36,40... | collective-permute-start | bytes 24584 | tf_op jit(solution)/shard_map/ppermute | solution.py:570
  55.3 0.1 collective-permute-start.10
  55.4 3.9 %collective-permute-start.11 = (f32[16,128]{1,0:T(8,128)S(1)}, f32[16,128]{1,0:T(8,128)S(1)}, u32[]{:S(2)}, u32[]{:S(2)}) collective-permute-start(f32[16,128]{1,0:T(8,128)S(1)} %get-tuple-element.62), channel_id=1, source_target_pairs={{1,2},{2,1},{5,6},{6,5},{9,10},{10,9},{13,14},{14,13},{17,18},{18,... | collective-permute-start | bytes 24584 | tf_op jit(solution)/shard_map/ppermute | solution.py:572
  59.3 0.5 collective-permute-done.9.g1
  59.8 1.2 %collective-permute-done.11.g3 = f32[16,128]{1,0:T(8,128)S(1)} collective-permute-done((f32[16,128]{1,0:T(8,128)S(1)}, f32[16,128]{1,0:T(8,128)S(1)}, u32[]{:S(2)}, u32[]{:S(2)}) %collective-permute-start.11) | collective-permute-done | bytes 8224 | tf_op jit(solution)/shard_map/ppermute | solution.py:572
  60.9 9.7 %mass_sweep.2 = (f32[192,256]{1,0:T(8,128)S(1)}, f32[192,256]{1,0:T(8,128)S(1)}, f32[192,256]{1,0:T(8,128)S(1)}, f32[192,256]{1,0:T(8,128)S(1)}, f32[16,128]{1,0...) custom-call(f32[16,128]{1,0:T(8,128)S(1)} %collective-permute-done.8.g0, ...), custom_call_target="tpu_custom_call" | custom-call | flops 10000000000 | bytes 1000000 | tf_op jit(solution)/shard_map/mass_sweep/pallas_call | solution.py:549
  70.6 0.1 collective-permute-start.12
  70.7 4.2 %collective-permute-start.13 = (f32[16,128]{1,0:T(8,128)S(1)}, f32[16,128]{1,0:T(8,128)S(1)}, u32[]{:S(2)}, u32[]{:S(2)}) collective-permute-start(f32[16,128]{1,0:T(8,128)S(1)} %get-tuple-element.68), channel_id=1, source_target_pairs={{4,8},{8,4},{12,16},{16,12},{20,24},{24,20},{28,32},{32,28},{36,40... | collective-permute-start | bytes 24584 | tf_op jit(solution)/shard_map/ppermute | solution.py:570
  74.9 0.1 collective-permute-start.14
  75.0 3.6 %collective-permute-start.15 = (f32[16,128]{1,0:T(8,128)S(1)}, f32[16,128]{1,0:T(8,128)S(1)}, u32[]{:S(2)}, u32[]{:S(2)}) collective-permute-start(f32[16,128]{1,0:T(8,128)S(1)} %get-tuple-element.70), channel_id=1, source_target_pairs={{1,2},{2,1},{5,6},{6,5},{9,10},{10,9},{13,14},{14,13},{17,18},{18,... | collective-permute-start | bytes 24584 | tf_op jit(solution)/shard_map/ppermute | solution.py:572
  78.7 1.9 %collective-permute-done.15.g3 = f32[16,128]{1,0:T(8,128)S(1)} collective-permute-done((f32[16,128]{1,0:T(8,128)S(1)}, f32[16,128]{1,0:T(8,128)S(1)}, u32[]{:S(2)}, u32[]{:S(2)}) %collective-permute-start.15) | collective-permute-done | bytes 8224 | tf_op jit(solution)/shard_map/ppermute | solution.py:572
  80.5 9.7 %mass_sweep.3 = (f32[192,256]{1,0:T(8,128)S(1)}, f32[192,256]{1,0:T(8,128)S(1)}, f32[192,256]{1,0:T(8,128)S(1)}, f32[192,256]{1,0:T(8,128)S(1)}, f32[16,128]{1,0...) custom-call(f32[16,128]{1,0:T(8,128)S(1)} %collective-permute-done.12.g0, ...), custom_call_target="tpu_custom_call" | custom-call | flops 10000000000 | bytes 1000000 | tf_op jit(solution)/shard_map/mass_sweep/pallas_call | solution.py:549
  90.2 0.1 collective-permute-start.16
  90.3 2.4 %collective-permute-start.17 = (f32[16,128]{1,0:T(8,128)S(1)}, f32[16,128]{1,0:T(8,128)S(1)}, u32[]{:S(2)}, u32[]{:S(2)}) collective-permute-start(f32[16,128]{1,0:T(8,128)S(1)} %get-tuple-element.76), channel_id=1, source_target_pairs={{4,8},{8,4},{12,16},{16,12},{20,24},{24,20},{28,32},{32,28},{36,40... | collective-permute-start | bytes 24584 | tf_op jit(solution)/shard_map/ppermute | solution.py:570
  92.7 0.1 collective-permute-start.18
  92.8 3.6 %collective-permute-start.19 = (f32[16,128]{1,0:T(8,128)S(1)}, f32[16,128]{1,0:T(8,128)S(1)}, u32[]{:S(2)}, u32[]{:S(2)}) collective-permute-start(f32[16,128]{1,0:T(8,128)S(1)} %get-tuple-element.78), channel_id=1, source_target_pairs={{1,2},{2,1},{5,6},{6,5},{9,10},{10,9},{13,14},{14,13},{17,18},{18,... | collective-permute-start | bytes 24584 | tf_op jit(solution)/shard_map/ppermute | solution.py:572
  96.5 0.9 collective-permute-done.17.g1
  97.4 0.9 collective-permute-done.19.g3
  98.3 5.7 %force_two.1 = (f32[27,256]{1,0:T(8,128)}, f32[3,7936]{1,0:T(4,128)}) custom-call(f32[16,128]{1,0:T(8,128)S(1)} %collective-permute-done.16.g0, f32[16,128]{1,0:T(8,128)S(1)} %collective-permute-done.17.g1, f32[16,128]{1,0:T(8,128)S(1)} %collective-permute-done.18.g2, f32[16,128]{1,0:T(8,128)S(1)} %collective-permute-done.19.g3, ...), custom_call_target="tpu_custom_call" | custom-call | flops 10000000000 | bytes 1000000 | tf_op jit(solution)/shard_map/force_two/pallas_call | solution.py:549
  (35 shorter events, 0.2 us)
Async XLA Ops:
  0.6 18.5 %copy-start.7 = (bf16[2528,256]{1,0:T(8,128)(2,1)S(1)}, bf16[2528,256]{1,0:T(8,128)(2,1)}, u32[]{:S(2)}) copy-start(bf16[2528,256]{1,0:T(8,128)(2,1)} %constant.4.clone._tables.tables) | copy-start | bytes 3883012
  0.6 18.5 %copy-start.5 = (f32[27,256]{1,0:T(8,128)S(1)}, f32[27,256]{1,0:T(8,128)}, u32[]{:S(2)}) copy-start(f32[27,256]{1,0:T(8,128)} %en_ref.1) | copy-start | bytes 82948
  0.7 18.4 %copy-start.4 = (s32[64,256]{1,0:T(8,128)S(1)}, s32[64,256]{1,0:T(8,128)}, u32[]{:S(2)}) copy-start(s32[64,256]{1,0:T(8,128)} %zn.7) | copy-start | bytes 196612
  0.7 18.4 %copy-start.6 = (s32[1,36]{1,0:T(1,128)S(1)}, s32[1,36]{1,0:T(1,128)}, u32[]{:S(2)}) copy-start(s32[1,36]{1,0:T(1,128)} %arrive_ref.1) | copy-start | bytes 436
  0.7 18.4 %copy-start.3 = (f32[3,7936]{1,0:T(4,128)S(1)}, f32[3,7936]{1,0:T(4,128)}, u32[]{:S(2)}) copy-start(f32[3,7936]{1,0:T(4,128)} %vel_ref.1) | copy-start | bytes 285700
  5.1 18.6 %collective-permute-start = (f32[8,3712]{1,0:T(8,128)}, f32[8,3712]{1,0:T(8,128)S(1)}, u32[]{:S(2)}, u32[]{:S(2)}) collective-permute-start(f32[8,3712]{1,0:T(8,128)} %get-tuple-element.46), channel_id=1, source_target_pairs={{2,4},{4,2},{3,5},{5,3},{6,8},{8,6},{7,9},{9,7},{10,12},{12,10},{1... | collective-permute-start | bytes 356360 | tf_op jit(solution)/shard_map/ppermute | solution.py:591
  12.3 11.5 %collective-permute-start.1 = (f32[8,3712]{1,0:T(8,128)}, f32[8,3712]{1,0:T(8,128)S(1)}, u32[]{:S(2)}, u32[]{:S(2)}) collective-permute-start(f32[8,3712]{1,0:T(8,128)} %get-tuple-element.47), channel_id=1, source_target_pairs={{0,2},{2,0},{1,3},{3,1},{4,6},{6,4},{5,7},{7,5},{8,10},{10,8},{9,1... | collective-permute-start | bytes 356360 | tf_op jit(solution)/shard_map/ppermute | solution.py:591
  12.4 11.4 %collective-permute-start.2 = (f32[8,3712]{1,0:T(8,128)}, f32[8,3712]{1,0:T(8,128)S(1)}, u32[]{:S(2)}, u32[]{:S(2)}) collective-permute-start(f32[8,3712]{1,0:T(8,128)} %get-tuple-element.48), channel_id=1, source_target_pairs={{1,2},{2,1},{3,4},{4,3},{5,6},{6,5},{7,8},{8,7},{9,10},{10,9},{11,... | collective-permute-start | bytes 356360 | tf_op jit(solution)/shard_map/ppermute | solution.py:591
  17.2 6.6 %copy-start = (f32[1944,256]{1,0:T(8,128)S(1)}, f32[1944,256]{1,0:T(8,128)}, u32[]{:S(2)}) copy-start(f32[1944,256]{1,0:T(8,128)} %jac_ref.1) | copy-start | bytes 5971972
  17.2 6.6 %copy-start.1 = (f32[729,256]{1,0:T(8,128)S(1)}, f32[729,256]{1,0:T(8,128)}, u32[]{:S(2)}) copy-start(f32[729,256]{1,0:T(8,128)} %inv_ref.1) | copy-start | bytes 2239492
  17.2 6.6 %copy-start.2 = (f32[216,256]{1,0:T(8,128)S(1)}, f32[216,256]{1,0:T(8,128)}, u32[]{:S(2)}) copy-start(f32[216,256]{1,0:T(8,128)} %mass_ref.1) | copy-start | bytes 663556
  17.2 6.6 %copy-start.9 = (s32[8,128]{1,0:T(8,128)S(1)}, s32[8,128]{1,0:T(8,128)}, u32[]{:S(2)}) copy-start(s32[8,128]{1,0:T(8,128)} %get-tuple-element.50.lists_ref.lists) | copy-start | bytes 12292
  17.2 6.6 %collective-permute-start.3 = (f32[8,3712]{1,0:T(8,128)}, f32[8,3712]{1,0:T(8,128)S(1)}, u32[]{:S(2)}, u32[]{:S(2)}) collective-permute-start(f32[8,3712]{1,0:T(8,128)} %get-tuple-element.49), channel_id=1, source_target_pairs={{0,1},{1,0},{2,3},{3,2},{4,5},{5,4},{6,7},{7,6},{8,9},{9,8},{10,11... | collective-permute-start | bytes 356360 | tf_op jit(solution)/shard_map/ppermute | solution.py:591
  23.8 19.0 %copy-start.8 = (bf16[352,256]{1,0:T(8,128)(2,1)S(1)}, bf16[352,256]{1,0:T(8,128)(2,1)}, u32[]{:S(2)}) copy-start(bf16[352,256]{1,0:T(8,128)(2,1)} %constant.5.clone.tables) | copy-start | bytes 540676
  32.8 8.5 %collective-permute-start.4 = (f32[16,128]{1,0:T(8,128)S(1)}, f32[16,128]{1,0:T(8,128)S(1)}, u32[]{:S(2)}, u32[]{:S(2)}) collective-permute-start(f32[16,128]{1,0:T(8,128)S(1)} %get-tuple-element.53), channel_id=1, source_target_pairs={{0,4},{4,0},{8,12},{12,8},{16,20},{20,16},{24,28},{28,24},{32,36},... | collective-permute-start | bytes 24584 | tf_op jit(solution)/shard_map/ppermute | solution.py:569
  32.9 8.4 %collective-permute-start.5 = (f32[16,128]{1,0:T(8,128)S(1)}, f32[16,128]{1,0:T(8,128)S(1)}, u32[]{:S(2)}, u32[]{:S(2)}) collective-permute-start(f32[16,128]{1,0:T(8,128)S(1)} %get-tuple-element.54), channel_id=1, source_target_pairs={{4,8},{8,4},{12,16},{16,12},{20,24},{24,20},{28,32},{32,28},{36,40... | collective-permute-start | bytes 24584 | tf_op jit(solution)/shard_map/ppermute | solution.py:570
  35.3 6.0 %collective-permute-start.6 = (f32[16,128]{1,0:T(8,128)S(1)}, f32[16,128]{1,0:T(8,128)S(1)}, u32[]{:S(2)}, u32[]{:S(2)}) collective-permute-start(f32[16,128]{1,0:T(8,128)S(1)} %get-tuple-element.55), channel_id=1, source_target_pairs={{0,1},{1,0},{2,3},{3,2},{4,5},{5,4},{6,7},{7,6},{8,9},{9,8},{10,11... | collective-permute-start | bytes 24584 | tf_op jit(solution)/shard_map/ppermute | solution.py:571
  36.1 6.8 %collective-permute-start.7 = (f32[16,128]{1,0:T(8,128)S(1)}, f32[16,128]{1,0:T(8,128)S(1)}, u32[]{:S(2)}, u32[]{:S(2)}) collective-permute-start(f32[16,128]{1,0:T(8,128)S(1)} %get-tuple-element.56), channel_id=1, source_target_pairs={{1,2},{2,1},{5,6},{6,5},{9,10},{10,9},{13,14},{14,13},{17,18},{18,... | collective-permute-start | bytes 24584 | tf_op jit(solution)/shard_map/ppermute | solution.py:572
  52.6 6.7 %collective-permute-start.8 = (f32[16,128]{1,0:T(8,128)S(1)}, f32[16,128]{1,0:T(8,128)S(1)}, u32[]{:S(2)}, u32[]{:S(2)}) collective-permute-start(f32[16,128]{1,0:T(8,128)S(1)} %get-tuple-element.59), channel_id=1, source_target_pairs={{0,4},{4,0},{8,12},{12,8},{16,20},{20,16},{24,28},{28,24},{32,36},... | collective-permute-start | bytes 24584 | tf_op jit(solution)/shard_map/ppermute | solution.py:569
  52.7 7.1 %collective-permute-start.9 = (f32[16,128]{1,0:T(8,128)S(1)}, f32[16,128]{1,0:T(8,128)S(1)}, u32[]{:S(2)}, u32[]{:S(2)}) collective-permute-start(f32[16,128]{1,0:T(8,128)S(1)} %get-tuple-element.60), channel_id=1, source_target_pairs={{4,8},{8,4},{12,16},{16,12},{20,24},{24,20},{28,32},{32,28},{36,40... | collective-permute-start | bytes 24584 | tf_op jit(solution)/shard_map/ppermute | solution.py:570
  55.3 4.5 %collective-permute-start.10 = (f32[16,128]{1,0:T(8,128)S(1)}, f32[16,128]{1,0:T(8,128)S(1)}, u32[]{:S(2)}, u32[]{:S(2)}) collective-permute-start(f32[16,128]{1,0:T(8,128)S(1)} %get-tuple-element.61), channel_id=1, source_target_pairs={{0,1},{1,0},{2,3},{3,2},{4,5},{5,4},{6,7},{7,6},{8,9},{9,8},{10,11... | collective-permute-start | bytes 24584 | tf_op jit(solution)/shard_map/ppermute | solution.py:571
  55.4 5.5 %collective-permute-start.11 = (f32[16,128]{1,0:T(8,128)S(1)}, f32[16,128]{1,0:T(8,128)S(1)}, u32[]{:S(2)}, u32[]{:S(2)}) collective-permute-start(f32[16,128]{1,0:T(8,128)S(1)} %get-tuple-element.62), channel_id=1, source_target_pairs={{1,2},{2,1},{5,6},{6,5},{9,10},{10,9},{13,14},{14,13},{17,18},{18,... | collective-permute-start | bytes 24584 | tf_op jit(solution)/shard_map/ppermute | solution.py:572
  70.6 8.0 %collective-permute-start.12 = (f32[16,128]{1,0:T(8,128)S(1)}, f32[16,128]{1,0:T(8,128)S(1)}, u32[]{:S(2)}, u32[]{:S(2)}) collective-permute-start(f32[16,128]{1,0:T(8,128)S(1)} %get-tuple-element.67), channel_id=1, source_target_pairs={{0,4},{4,0},{8,12},{12,8},{16,20},{20,16},{24,28},{28,24},{32,36},... | collective-permute-start | bytes 24584 | tf_op jit(solution)/shard_map/ppermute | solution.py:569
  70.7 8.0 %collective-permute-start.13 = (f32[16,128]{1,0:T(8,128)S(1)}, f32[16,128]{1,0:T(8,128)S(1)}, u32[]{:S(2)}, u32[]{:S(2)}) collective-permute-start(f32[16,128]{1,0:T(8,128)S(1)} %get-tuple-element.68), channel_id=1, source_target_pairs={{4,8},{8,4},{12,16},{16,12},{20,24},{24,20},{28,32},{32,28},{36,40... | collective-permute-start | bytes 24584 | tf_op jit(solution)/shard_map/ppermute | solution.py:570
  74.9 3.8 %collective-permute-start.14 = (f32[16,128]{1,0:T(8,128)S(1)}, f32[16,128]{1,0:T(8,128)S(1)}, u32[]{:S(2)}, u32[]{:S(2)}) collective-permute-start(f32[16,128]{1,0:T(8,128)S(1)} %get-tuple-element.69), channel_id=1, source_target_pairs={{0,1},{1,0},{2,3},{3,2},{4,5},{5,4},{6,7},{7,6},{8,9},{9,8},{10,11... | collective-permute-start | bytes 24584 | tf_op jit(solution)/shard_map/ppermute | solution.py:571
  75.0 5.5 %collective-permute-start.15 = (f32[16,128]{1,0:T(8,128)S(1)}, f32[16,128]{1,0:T(8,128)S(1)}, u32[]{:S(2)}, u32[]{:S(2)}) collective-permute-start(f32[16,128]{1,0:T(8,128)S(1)} %get-tuple-element.70), channel_id=1, source_target_pairs={{1,2},{2,1},{5,6},{6,5},{9,10},{10,9},{13,14},{14,13},{17,18},{18,... | collective-permute-start | bytes 24584 | tf_op jit(solution)/shard_map/ppermute | solution.py:572
  90.2 6.2 %collective-permute-start.16 = (f32[16,128]{1,0:T(8,128)S(1)}, f32[16,128]{1,0:T(8,128)S(1)}, u32[]{:S(2)}, u32[]{:S(2)}) collective-permute-start(f32[16,128]{1,0:T(8,128)S(1)} %get-tuple-element.75), channel_id=1, source_target_pairs={{0,4},{4,0},{8,12},{12,8},{16,20},{20,16},{24,28},{28,24},{32,36},... | collective-permute-start | bytes 24584 | tf_op jit(solution)/shard_map/ppermute | solution.py:569
  90.3 7.1 %collective-permute-start.17 = (f32[16,128]{1,0:T(8,128)S(1)}, f32[16,128]{1,0:T(8,128)S(1)}, u32[]{:S(2)}, u32[]{:S(2)}) collective-permute-start(f32[16,128]{1,0:T(8,128)S(1)} %get-tuple-element.76), channel_id=1, source_target_pairs={{4,8},{8,4},{12,16},{16,12},{20,24},{24,20},{28,32},{32,28},{36,40... | collective-permute-start | bytes 24584 | tf_op jit(solution)/shard_map/ppermute | solution.py:570
  92.7 4.7 %collective-permute-start.18 = (f32[16,128]{1,0:T(8,128)S(1)}, f32[16,128]{1,0:T(8,128)S(1)}, u32[]{:S(2)}, u32[]{:S(2)}) collective-permute-start(f32[16,128]{1,0:T(8,128)S(1)} %get-tuple-element.77), channel_id=1, source_target_pairs={{0,1},{1,0},{2,3},{3,2},{4,5},{5,4},{6,7},{7,6},{8,9},{9,8},{10,11... | collective-permute-start | bytes 24584 | tf_op jit(solution)/shard_map/ppermute | solution.py:571
  92.8 5.5 %collective-permute-start.19 = (f32[16,128]{1,0:T(8,128)S(1)}, f32[16,128]{1,0:T(8,128)S(1)}, u32[]{:S(2)}, u32[]{:S(2)}) collective-permute-start(f32[16,128]{1,0:T(8,128)S(1)} %get-tuple-element.78), channel_id=1, source_target_pairs={{1,2},{2,1},{5,6},{6,5},{9,10},{10,9},{13,14},{14,13},{17,18},{18,... | collective-permute-start | bytes 24584 | tf_op jit(solution)/shard_map/ppermute | solution.py:572
